TPU v7x, 32 devices: a whole 2x2x4 slice. The times are simulated.
32 devices in a mesh: dp: 8 (over y, x, core), seq: 4 (over z).
Axes of the slice: x: 2, y: 2, z: 4, core: 2. Of those that a mesh axis runs over, the one named last changes fastest.
Arguments:
- tokens: bfloat16 [28992, 768], P(('dp', 'seq')), may hold values from -6 to 6
- grad_out: bfloat16 [28992, 768], P(('dp', 'seq')), may hold values from -6 to 6
- group_ids: int32 [28992], P(('dp', 'seq')), may hold values from 0 to 63, as said below
- segment_ids: int32 [28992], P(('dp', 'seq')), may hold values from 0 to 4, as said below
- expert_ids: int32 [28992, 1], P(('dp', 'seq')), may hold values from 0 to 1, as said below
- ln1_gain: float32 [768], replicated, may hold values from 0.25 to 1.75
- ln1_bias: float32 [768], replicated, may hold values from -1.5 to 1.5
- qkv_weight: bfloat16 [768, 2304], replicated, may hold values from -0.21875 to 0.21875
- q_bias: float32 [768], replicated, may hold values from -1.5 to 1.5
- v_bias: float32 [768], replicated, may hold values from -1.5 to 1.5
- out_weight: bfloat16 [768, 768], replicated, may hold values from -0.875 to 0.875
- out_bias: float32 [768], replicated, may hold values from -1.5 to 1.5
- ln2_gain: float32 [768], replicated, may hold values from 0.25 to 1.75
- ln2_bias: float32 [768], replicated, may hold values from -1.5 to 1.5
- up_weight: bfloat16 [2, 768, 3072], replicated, may hold values from -0.21875 to 0.21875
- up_bias: float32 [2, 3072], replicated, may hold values from -2.5 to 2.5
- down_weight: bfloat16 [2, 3072, 768], replicated, may hold values from -0.109375 to 0.109375
- down_bias: float32 [2, 768], replicated, may hold values from -1.5 to 1.5
Outputs:
- mixed: bfloat16 [28992, 768], P(('dp', 'seq'))
- grad_in: bfloat16 [28992, 768], P(('dp', 'seq'))
- grad_ln1_gain: float32 [768], P(('dp', 'seq'))
- grad_ln1_bias: float32 [768], P(('dp', 'seq'))
- grad_qkv_weight: float32 [768, 2304], P(('dp', 'seq'))
- grad_q_bias: float32 [768], P(('dp', 'seq'))
- grad_v_bias: float32 [768], P(('dp', 'seq'))
- grad_out_weight: float32 [768, 768], P(('dp', 'seq'))
- grad_out_bias: float32 [768], P(('dp', 'seq'))
- grad_ln2_gain: float32 [768], P(('dp', 'seq'))
- grad_ln2_bias: float32 [768], P(('dp', 'seq'))
- grad_up_weight: float32 [2, 768, 3072], P(None, ('dp', 'seq'))
- grad_up_bias: float32 [6144], P(('dp', 'seq'))
- grad_down_weight: float32 [6144, 768], P(('dp', 'seq'))
- grad_down_bias: float32 [2, 768], P(None, ('dp', 'seq'))
Inputs may be any that keep to these rules, and one draw needn't show every extreme that they name: `group_ids`: the rows on index d of dp hold exactly the groups d * 8 to d * 8 + 7, each with 453 rows, in an order drawn from the seed. `segment_ids`: in every group 197 rows have 0 and each caption k of 1 to 4 has 64 rows with k. `expert_ids`: the expert is the row's modality: 0 (vision) where segment_ids is 0, 1 (language) on caption rows.
All inputs are finite; a program needn't handle non-finite values.
Results may differ from a plain program's by a relative error of at most 0.012.
Values may be sent and summed in bfloat16 or wider, within the bound.
A program may use at most 256 MiB of HBM per device.

v0:
```python
import jax
import jax.numpy as jnp
from jax import lax
from jax.sharding import PartitionSpec as P

HEAD_DIM = 64
GROUP_ROWS = 453


def norm_rows(value, gain, shift):
    center = value - jnp.mean(value, axis=-1, keepdims=True)
    spread = jnp.mean(center * center, axis=-1, keepdims=True)
    return center * lax.rsqrt(spread + 1e-05) * gain + shift


def exact_gelu(value):
    return jax.nn.gelu(value, approximate=False)


def contract_rows(left, right):
    return lax.dot_general(
        left, right, (((0,), (0,)), ((), ())), preferred_element_type=jnp.float32
    )


def contract_cols(left, right):
    return lax.dot_general(
        left, right, (((1,), (1,)), ((), ())), preferred_element_type=jnp.float32
    )


def pair_allowed(marks):
    return (marks[:, None, :] == 0) | (marks[:, None, :] == marks[:, :, None])


def body(
    tokens,
    grad_out,
    group_ids,
    segment_ids,
    expert_ids,
    ln1_gain,
    ln1_bias,
    qkv_weight,
    q_bias,
    v_bias,
    out_weight,
    out_bias,
    ln2_gain,
    ln2_bias,
    up_weight,
    up_bias,
    down_weight,
    down_bias,
):
    ways = lax.axis_size("seq")
    tok_rows, width = tokens.shape
    slice_width = width // ways
    head_count = slice_width // HEAD_DIM
    scale = HEAD_DIM ** (-0.5)
    rows = tokens.astype(jnp.float32)
    h1, ln1_pull = jax.vjp(norm_rows, rows, ln1_gain, ln1_bias)
    first = h1.astype(jnp.bfloat16)
    zeros = jnp.zeros_like(q_bias)
    qkv = (
        jnp.dot(first, qkv_weight, preferred_element_type=jnp.float32)
        + jnp.concatenate([q_bias, zeros, v_bias])
    ).astype(jnp.bfloat16)
    spread = lax.all_to_all(
        qkv.reshape(tok_rows, 3, ways, slice_width), "seq", split_axis=2, concat_axis=0, tiled=True
    )
    all_rows = spread.shape[0]
    groups_all, labels_all = (
        lax.all_gather(group_ids, "seq", axis=0, tiled=True),
        lax.all_gather(segment_ids, "seq", axis=0, tiled=True),
    )
    order = jnp.argsort(groups_all, stable=True)
    undo = jnp.argsort(order, stable=True)
    pairs = all_rows // (2 * GROUP_ROWS)
    heads = jnp.take(spread.reshape(all_rows, 3, head_count, HEAD_DIM), order, axis=0)
    grouped = heads.reshape(pairs, 2, GROUP_ROWS, 3, head_count, HEAD_DIM)
    grouped_labels = jnp.take(labels_all, order, axis=0).reshape(pairs, 2, GROUP_ROWS)

    def forward_pair(pack):
        piece, marks = pack
        query = piece[:, :, 0]
        keys = piece[:, :, 1]
        values = piece[:, :, 2]
        raw = jnp.einsum("gqhd,gkhd->ghqk", query, keys, preferred_element_type=jnp.float32) * scale
        scores = jnp.where(pair_allowed(marks)[:, None], raw, -1e30)
        peak = jnp.max(scores, axis=-1, keepdims=True)
        expo = jnp.exp(scores - peak)
        total = jnp.sum(expo, axis=-1, keepdims=True)
        probs = (expo / total).astype(jnp.bfloat16)
        output = jnp.einsum("ghqk,gkhd->gqhd", probs, values, preferred_element_type=jnp.float32)
        return (output.astype(jnp.bfloat16), (peak + jnp.log(total))[..., 0])

    attended_sorted, log_totals = lax.map(forward_pair, (grouped, grouped_labels))
    attended_heads = jnp.take(attended_sorted.reshape(all_rows, slice_width), undo, axis=0)
    merged = lax.all_to_all(
        attended_heads.reshape(all_rows, 1, slice_width),
        "seq",
        split_axis=0,
        concat_axis=1,
        tiled=True,
    ).reshape(tok_rows, width)
    mid = rows + jnp.dot(merged, out_weight, preferred_element_type=jnp.float32) + out_bias
    h2, ln2_pull = jax.vjp(norm_rows, mid, ln2_gain, ln2_bias)
    second = h2.astype(jnp.bfloat16)
    expert = expert_ids[:, 0]
    experts = up_weight.shape[0]
    onehot = (expert[:, None] == jnp.arange(experts, dtype=jnp.int32)[None, :]).astype(jnp.int32)
    slot = jnp.sum(onehot * (jnp.cumsum(onehot, axis=0) - 1), axis=1)
    place = expert * tok_rows + slot
    table = (
        jnp.full((experts * tok_rows,), tok_rows, jnp.int32)
        .at[place]
        .set(jnp.arange(tok_rows, dtype=jnp.int32))
    )
    packed = jnp.take(second, table, axis=0, mode="fill", fill_value=0).reshape(
        experts, tok_rows, width
    )
    pre = (
        jnp.einsum("ecd,edf->ecf", packed, up_weight, preferred_element_type=jnp.float32)
        + up_bias[:, None, :]
    )
    hidden = exact_gelu(pre).astype(jnp.bfloat16)
    result = (
        jnp.einsum("ecf,efd->ecd", hidden, down_weight, preferred_element_type=jnp.float32)
        + down_bias[:, None, :]
    )
    mixed = (mid + jnp.take(result.reshape(experts * tok_rows, width), place, axis=0)).astype(
        jnp.bfloat16
    )
    grad_rows = grad_out.astype(jnp.float32)
    grad_packed = jnp.take(grad_out, table, axis=0, mode="fill", fill_value=0).reshape(
        experts, tok_rows, width
    )
    grad_down_weight = jnp.einsum(
        "ecf,ecd->efd", hidden, grad_packed, preferred_element_type=jnp.float32
    )
    grad_down_bias = jnp.sum(grad_packed.astype(jnp.float32), axis=1)
    grad_hidden = jnp.einsum(
        "ecd,efd->ecf", grad_packed, down_weight, preferred_element_type=jnp.float32
    )
    unused, gelu_pull = jax.vjp(exact_gelu, pre)
    grad_pre = gelu_pull(grad_hidden)[0].astype(jnp.bfloat16)
    grad_up_weight = jnp.einsum(
        "ecd,ecf->edf", packed, grad_pre, preferred_element_type=jnp.float32
    )
    grad_up_bias = jnp.sum(grad_pre.astype(jnp.float32), axis=1)
    grad_packed_in = jnp.einsum(
        "ecf,edf->ecd", grad_pre, up_weight, preferred_element_type=jnp.float32
    )
    grad_second = jnp.take(grad_packed_in.reshape(experts * tok_rows, width), place, axis=0)
    grad_mid_norm, grad_ln2_gain, grad_ln2_bias = ln2_pull(grad_second)
    grad_mid = grad_rows + grad_mid_norm
    grad_branch = grad_mid.astype(jnp.bfloat16)
    grad_out_weight = contract_rows(merged, grad_branch)
    grad_out_bias = jnp.sum(grad_branch.astype(jnp.float32), axis=0)
    grad_merged = contract_cols(grad_branch, out_weight).astype(jnp.bfloat16)
    grad_heads = lax.all_to_all(
        grad_merged.reshape(tok_rows, ways, slice_width),
        "seq",
        split_axis=1,
        concat_axis=0,
        tiled=True,
    ).reshape(all_rows, head_count, HEAD_DIM)
    grad_grouped = jnp.take(grad_heads, order, axis=0).reshape(
        pairs, 2, GROUP_ROWS, head_count, HEAD_DIM
    )

    def backward_pair(pack):
        piece, marks, totals, grad_block = pack
        query = piece[:, :, 0]
        keys = piece[:, :, 1]
        values = piece[:, :, 2]
        raw = jnp.einsum("gqhd,gkhd->ghqk", query, keys, preferred_element_type=jnp.float32) * scale
        probs = jnp.where(pair_allowed(marks)[:, None], jnp.exp(raw - totals[..., None]), 0.0)
        grad_probs = jnp.einsum(
            "gqhd,gkhd->ghqk", grad_block, values, preferred_element_type=jnp.float32
        )
        inner = jnp.sum(grad_probs * probs, axis=-1, keepdims=True)
        grad_scores = (probs * (grad_probs - inner)).astype(jnp.bfloat16)
        grad_query = (
            jnp.einsum("ghqk,gkhd->gqhd", grad_scores, keys, preferred_element_type=jnp.float32)
            * scale
        )
        grad_keys = (
            jnp.einsum("ghqk,gqhd->gkhd", grad_scores, query, preferred_element_type=jnp.float32)
            * scale
        )
        grad_values = jnp.einsum(
            "ghqk,gqhd->gkhd",
            probs.astype(jnp.bfloat16),
            grad_block,
            preferred_element_type=jnp.float32,
        )
        return jnp.stack([grad_query, grad_keys, grad_values], axis=2).astype(jnp.bfloat16)

    grad_sorted = lax.map(backward_pair, (grouped, grouped_labels, log_totals, grad_grouped))
    grad_qkv = jnp.take(grad_sorted.reshape(all_rows, 3, slice_width), undo, axis=0)
    grad_qkv = grad_qkv.reshape(all_rows, 3, 1, slice_width)
    back_tokens = lax.all_to_all(grad_qkv, "seq", split_axis=0, concat_axis=2, tiled=True).reshape(
        tok_rows, 3 * width
    )
    grad_qkv_weight = contract_rows(first, back_tokens)
    column_sums = jnp.sum(back_tokens.astype(jnp.float32), axis=0)
    grad_q_bias = column_sums[:width]
    grad_v_bias = column_sums[2 * width :]
    grad_first = contract_cols(back_tokens, qkv_weight)
    grad_in_norm, grad_ln1_gain, grad_ln1_bias = ln1_pull(grad_first)
    grad_in = (grad_mid + grad_in_norm).astype(jnp.bfloat16)
    flat_up_bias = grad_up_bias.reshape(-1)
    flat_down_weight = grad_down_weight.reshape(-1, width)
    totals = (
        lax.psum_scatter(grad_ln1_gain, ("dp", "seq"), scatter_dimension=0, tiled=True),
        lax.psum_scatter(grad_ln1_bias, ("dp", "seq"), scatter_dimension=0, tiled=True),
        lax.psum_scatter(grad_qkv_weight, ("dp", "seq"), scatter_dimension=0, tiled=True),
        lax.psum_scatter(grad_q_bias, ("dp", "seq"), scatter_dimension=0, tiled=True),
        lax.psum_scatter(grad_v_bias, ("dp", "seq"), scatter_dimension=0, tiled=True),
        lax.psum_scatter(grad_out_weight, ("dp", "seq"), scatter_dimension=0, tiled=True),
        lax.psum_scatter(grad_out_bias, ("dp", "seq"), scatter_dimension=0, tiled=True),
        lax.psum_scatter(grad_ln2_gain, ("dp", "seq"), scatter_dimension=0, tiled=True),
        lax.psum_scatter(grad_ln2_bias, ("dp", "seq"), scatter_dimension=0, tiled=True),
        lax.psum_scatter(grad_up_weight, ("dp", "seq"), scatter_dimension=1, tiled=True),
        lax.psum_scatter(flat_up_bias, ("dp", "seq"), scatter_dimension=0, tiled=True),
        lax.psum_scatter(flat_down_weight, ("dp", "seq"), scatter_dimension=0, tiled=True),
        lax.psum_scatter(grad_down_bias, ("dp", "seq"), scatter_dimension=1, tiled=True),
    )
    return (
        mixed,
        grad_in,
        totals[0],
        totals[1],
        totals[2],
        totals[3],
        totals[4],
        totals[5],
        totals[6],
        totals[7],
        totals[8],
        totals[9],
        totals[10],
        totals[11],
        totals[12],
    )


def solution(mesh):
    return jax.shard_map(
        body,
        mesh=mesh,
        in_specs=(
            P(("dp", "seq"), None),
            P(("dp", "seq"), None),
            P(("dp", "seq")),
            P(("dp", "seq")),
            P(("dp", "seq"), None),
            P(),
            P(),
            P(),
            P(),
            P(),
            P(),
            P(),
            P(),
            P(),
            P(),
            P(),
            P(),
            P(),
        ),
        out_specs=(
            P(("dp", "seq"), None),
            P(("dp", "seq"), None),
            P(("dp", "seq")),
            P(("dp", "seq")),
            P(("dp", "seq"), None),
            P(("dp", "seq")),
            P(("dp", "seq")),
            P(("dp", "seq"), None),
            P(("dp", "seq")),
            P(("dp", "seq")),
            P(("dp", "seq")),
            P(None, ("dp", "seq"), None),
            P(("dp", "seq")),
            P(("dp", "seq"), None),
            P(None, ("dp", "seq")),
        ),
        check_vma=False,
    )
```

profile of v0, /device:TPU:0, one launch (start us, length us, event | category | flops | bytes accessed | tf_op | source)
XLA Modules:
  0.0 2018.0 jit_solution(17623697408679065540)
XLA Ops:
  41.7 109.9 %all-reduce.12 = (s32[3624]{0:T(1024)}, s32[3624]{0:T(1024)S(1)}) all-reduce(s32[3624]{0:T(1024)} %copy-done.26, s32[3624]{0:T(1024)} %dynamic-update-slice.1), channel_id=1, replica_groups=mesh['dp'=8,'seq'=4] {'seq'}, use_global_device_ids=true, to_apply=%add.1 | all-reduce | flops 7248 | bytes 57984
  162.9 27.7 %gather_fusion.1 = s32[3624]{0:T(1024)} fusion(s32[3624]{0:T(1024)S(1)} %get-tuple-element.182, s32[4096]{0:T(1024)} %pad_clamp_fusion.1), kind=kCustom, calls=%fused_computation.5 | custom fusion | bytes 43488 | tf_op jit(solution)/shard_map/jit(_take)/gather | solution.py:82
  201.8 12.6 copy.200
  214.5 25.8 %reshape.449 = bf16[3624,3,3,64]{3,2,1,0:T(4,128)(2,1)} reshape(bf16[4,906,3,1,192]{4,2,1,0,3:T(4,128)(2,1)} %copy.200) | data formatting | bytes 8349696 | tf_op jit(solution)/shard_map/reshape | solution.py:80
  240.2 22.7 %gather_fusion = bf16[3624,3,3,64]{3,2,1,0:T(4,128)(2,1)} fusion(bf16[3624,3,3,64]{3,2,1,0:T(4,128)(2,1)} %reshape.449, s32[4096]{0:T(1024)S(1)} %copy-done.18), kind=kCustom, calls=%fused_computation.4 | custom fusion | bytes 8364192 | tf_op jit(solution)/shard_map/jit(_take)/gather | solution.py:80
  263.0 30.8 %copy.201 = bf16[4,2,453,3,3,64]{2,1,0,5,4,3:T(2,128)(2,1)} copy(bf16[4,2,453,3,3,64]{5,4,3,2,1,0:T(4,128)(2,1)} %bitcast.174) | data formatting | bytes 8349696 | tf_op jit(solution)/shard_map/jit(_take)/gather | solution.py:80
  293.8 8.5 broadcast_select_fusion
  308.3 35.2 %while.22 = (s32[]{:T(128)}, bf16[4,2,453,3,64]{2,1,0,4,3:T(2,128)(2,1)}, f32[4,2,3,453]{3,2,1,0:T(4,128)}, bf16[4,2,453,3,3,64]{2,5,4,1,3,0:T(8,128)(2,1)}, s32[4,2,453]{2,1,0:T(2,128)}, /*index=5*/s32[]{:T(128)}) while((s32[]{:T(128)}, bf16[4,2,453,3,64]{2,1,0,4,3:T(2,128)(2,1)}, f32[4,2,3,453]{3,2,1,0:T(4,128)}, ...), condition=%wide.region_7.8_spmd, body=%wide.region_4.7_spmd.sunk | while | flops 330969056 | bytes 21681476 | solution.py:98
  352.3 11.4 gather_fusion.2
  390.8 10.1 gather_fusion.7
  416.2 8.4 copy.181
  439.6 9.9 gather_fusion.5
  461.9 24.2 %fusion.52 = (u8[906,3072]{1,0:T(8,128)(4,1)}, u8[906,3072]{1,0:T(8,128)(4,1)}, f32[2,906,3072]{2,1,0:T(8,128)}) fusion(f32[2,3072]{1,0:T(2,128)} %param.41, bf16[2,906,768]{2,1,0:T(8,128)(2,1)} %reshape.331, bf16[2,768,3072]{2,1,0:T(8,128)(2,1)} %param.40), kind=kOutput, calls=%fused_computation.91 | convolution fusion | flops 8622452736 | bytes 40077312 | tf_op jit(solution)/shard_map/ecd,edf->ecf/dot_general | solution.py:124
  486.1 69.7 %convert_reduce_fusion = (f32[2,3072]{1,0:T(2,128)}, bf16[2,906,3072]{2,1,0:T(8,128)(2,1)}, f32[2,906,3072]{2,1,0:T(8,128)S(1)}) fusion(f32[2,906,3072]{2,1,0:T(8,128)} %get-tuple-element.212, f32[2,3072]{1,0:T(2,128)} %param.41, u8[906,3072]{1,0:T(8,128)(4,1)} %get-tuple-element.151, u8[906,3072]{1,0:T(8,128)(4,1)} %get-tuple-element.150, ...), kind=kOutput, calls=%fused_computation.71 | convolution fusion | flops 8995399680 | bytes 73500672 | tf_op jit(solution)/shard_map/ecd,efd->ecf/dot_general | solution.py:143
  555.9 14.5 multiply_convert_fusion.1
  570.3 15.9 broadcast_add_fusion
  591.9 16.0 fusion.83
  613.4 8.3 gather_fusion.6
  621.7 8.3 gather_fusion.8
  651.3 36.5 %all-to-all-done.2 = bf16[906,4,192]{0,2,1:T(8,128)(2,1)} async-done(((bf16[906,4,192]{0,2,1:T(8,128)(2,1)}), bf16[906,4,192]{0,2,1:T(8,128)(2,1)}, u32[]{:S(2)}, u32[]{:S(2)}) %all-to-all-start.2) | async-done | bytes 1391648 | tf_op jit(solution)/shard_map/all_to_all | solution.py:162
  695.9 13.8 gather_fusion.3
  709.7 10.9 copy.203
  724.5 472.1 %while.23 = (s32[]{:T(128)}, bf16[4,2,453,3,3,64]{2,1,0,5,4,3:T(2,128)(2,1)}, bf16[4,2,453,3,3,64]{2,5,4,1,3,0:T(8,128)(2,1)}, s32[4,2,453]{2,1,0:T(2,128)}, f32...) while((s32[]{:T(128)}, bf16[4,2,453,3,3,64]{2,1,0,5,4,3:T(2,128)(2,1)}, ...), condition=%wide.region_18.21_spmd, body=%wide.region_16.20_spmd.sunk | while | flops 807978496 | bytes 98973272 | solution.py:201
  737.7 10.1 copy.274
  752.2 10.0 copy.271
  764.1 68.1 %multiply_convert_fusion.3 = bf16[2,3,453,453]{3,0,2,1:T(2,128)(2,1)S(1)} fusion(f32[2,3,453,453]{3,0,2,1:T(2,128)} %copy.274, f32[2,3,453]{0,2,1:T(8,128)} %bitcast.170, f32[2,3,453,453]{3,0,2,1:T(2,128)} %copy.271, pred[2,453,453]{2,0,1:T(4,128)(4,1)} %compare_or_fusion.5), kind=kOutput, calls=%fused_computation.31.clone.1 | output fusion | flops 12315710 | bytes 12733830 | tf_op jit(solution)/shard_map/while/body/eval_jaxpr/sub | solution.py:184
  855.5 10.1 copy.274
  870.1 10.0 copy.271
  882.0 68.1 %multiply_convert_fusion.3 = bf16[2,3,453,453]{3,0,2,1:T(2,128)(2,1)S(1)} fusion(f32[2,3,453,453]{3,0,2,1:T(2,128)} %copy.274, f32[2,3,453]{0,2,1:T(8,128)} %bitcast.170, f32[2,3,453,453]{3,0,2,1:T(2,128)} %copy.271, pred[2,453,453]{2,0,1:T(4,128)(4,1)} %compare_or_fusion.5), kind=kOutput, calls=%fused_computation.31.clone.1 | output fusion | flops 12315710 | bytes 12733830 | tf_op jit(solution)/shard_map/while/body/eval_jaxpr/sub | solution.py:184
  973.5 10.1 copy.274
  988.0 10.0 copy.271
  999.9 68.1 %multiply_convert_fusion.3 = bf16[2,3,453,453]{3,0,2,1:T(2,128)(2,1)S(1)} fusion(f32[2,3,453,453]{3,0,2,1:T(2,128)} %copy.274, f32[2,3,453]{0,2,1:T(8,128)} %bitcast.170, f32[2,3,453,453]{3,0,2,1:T(2,128)} %copy.271, pred[2,453,453]{2,0,1:T(4,128)(4,1)} %compare_or_fusion.5), kind=kOutput, calls=%fused_computation.31.clone.1 | output fusion | flops 12315710 | bytes 12733830 | tf_op jit(solution)/shard_map/while/body/eval_jaxpr/sub | solution.py:184
  1091.4 10.1 copy.274
  1106.0 10.0 copy.271
  1117.8 68.1 %multiply_convert_fusion.3 = bf16[2,3,453,453]{3,0,2,1:T(2,128)(2,1)S(1)} fusion(f32[2,3,453,453]{3,0,2,1:T(2,128)} %copy.274, f32[2,3,453]{0,2,1:T(8,128)} %bitcast.170, f32[2,3,453,453]{3,0,2,1:T(2,128)} %copy.271, pred[2,453,453]{2,0,1:T(4,128)(4,1)} %compare_or_fusion.5), kind=kOutput, calls=%fused_computation.31.clone.1 | output fusion | flops 12315710 | bytes 12733830 | tf_op jit(solution)/shard_map/while/body/eval_jaxpr/sub | solution.py:184
  1196.7 10.1 reshape.337
  1206.8 11.9 copy.192
  1218.7 17.1 gather_fusion.4
  1235.8 11.8 copy.193
  1252.3 11.9 copy.194
  1274.5 166.7 %all-to-all-done.3 = bf16[3624,3,1,192]{3,1,2,0:T(4,128)(2,1)} async-done(((bf16[3624,3,1,192]{3,1,2,0:T(4,128)(2,1)}), bf16[3624,3,1,192]{3,1,2,0:T(4,128)(2,1)}, u32[]{:S(2)}, u32[]{:S(2)}) %all-to-all-start.3) | async-done | bytes 4174880 | tf_op jit(solution)/shard_map/all_to_all | solution.py:204
  1441.1 13.4 copy.204
  1467.6 17.5 fusion.86
  1485.2 17.8 fusion.85
  1515.7 8.2 fusion.77
  1526.0 40.8 %all-reduce.13 = (f32[768]{0:T(1024)}, f32[768]{0:T(1024)}, f32[768]{0:T(1024)}, f32[768]{0:T(1024)}, f32[768]{0:T(1024)}, /*index=5*/f32[768]{0:T(1024)}, f32[768]{0:T(1024)}, f32[6144]{0:T(1024)}, f32[2,768]{1,0:T(2,128)}) all-reduce(f32[768]{0:T(1024)} %get-tuple-element.154, ...), channel_id=2, replica_groups=mesh['dp'=8,'seq'=4] {'dp','seq'}, use_global_device_ids=true, to_apply=%region_22.25.clone | all-reduce | flops 13056 | bytes 104448
  1587.0 213.1 %reduce-scatter.12.cloned.1.call-done = f32[192,768]{1,0:T(8,128)} async-done(((f32[6144,768]{1,0:T(8,128)}), f32[192,768]{1,0:T(8,128)}) %reduce-scatter.12.cloned.1.call-update) | async-done | bytes 589840 | tf_op jit(solution)/shard_map/reduce_scatter | solution.py:228
  1800.0 211.0 %reduce-scatter.10.cloned.1.call-done = f32[2,24,3072]{2,1,0:T(8,128)} async-done(((f32[2,768,3072]{2,1,0:T(8,128)}), f32[2,24,3072]{2,1,0:T(8,128)}) %reduce-scatter.10.cloned.1.call-update) | async-done | bytes 589840 | tf_op jit(solution)/shard_map/reduce_scatter | solution.py:226
  (386 shorter events, 401.6 us)
Async XLA Ops:
  31.0 6.5 copy-start.55
  31.0 170.8 %all-to-all-start = ((bf16[906,3,4,192]{0,3,1,2:T(8,128)(2,1)}), bf16[906,3,4,192]{0,3,1,2:T(8,128)(2,1)}, u32[]{:S(2)}, u32[]{:S(2)}) async-start(bf16[906,3,4,192]{0,3,1,2:T(8,128)(2,1)} %copy.173), calls=%async_computation | async-start | bytes 9437184 | tf_op jit(solution)/shard_map/all_to_all | solution.py:69
  214.4 25.8 %copy-start.18 = (s32[4096]{0:T(1024)S(1)}, s32[4096]{0:T(1024)}, u32[]{:S(2)}) copy-start(s32[4096]{0:T(1024)} %pad_clamp_fusion.1) | copy-start | bytes 49156
  263.0 30.8 %copy-start.22 = (pred[4,2,453]{2,1,0:T(4,128)(4,1)S(1)}, pred[4,2,453]{2,1,0:T(4,128)(4,1)}, u32[]{:S(2)}) copy-start(pred[4,2,453]{2,1,0:T(4,128)(4,1)} %broadcast_in_dim.158) | copy-start | bytes 10876
  343.6 8.7 copy-start.20
  372.3 9.0 copy-start.27
  377.0 34.0 %all-to-all-start.1 = ((bf16[4,2,86976]{2,1,0:T(2,128)(2,1)}), bf16[4,2,86976]{2,1,0:T(2,128)(2,1)}, u32[]{:S(2)}, u32[]{:S(2)}) async-start(bf16[4,2,86976]{2,1,0:T(2,128)(2,1)} %reshape.456), calls=%async_computation.1 | async-start | bytes 2785280 | tf_op jit(solution)/shard_map/all_to_all | solution.py:100
  424.6 7.4 copy-start.53
  432.0 6.0 copy-start.38
  432.0 6.0 copy-start.50
  439.6 9.9 copy-start.49
  486.1 69.7 %copy-start.45 = (f32[2,3072]{1,0:T(2,128)S(1)}, f32[2,3072]{1,0:T(2,128)}, u32[]{:S(2)}) copy-start(f32[2,3072]{1,0:T(2,128)} %param.41) | copy-start | bytes 73732
  555.9 14.5 copy-start.52
  621.7 8.4 copy-start.25
  621.7 8.4 copy-start.31
  621.7 8.4 copy-start.39
  646.9 40.8 %all-to-all-start.2 = ((bf16[906,4,192]{0,2,1:T(8,128)(2,1)}), bf16[906,4,192]{0,2,1:T(8,128)(2,1)}, u32[]{:S(2)}, u32[]{:S(2)}) async-start(bf16[906,4,192]{0,2,1:T(8,128)(2,1)} %bitcast.179), calls=%async_computation.2 | async-start | bytes 3145728 | tf_op jit(solution)/shard_map/all_to_all | solution.py:162
  687.8 8.1 copy-start.19
  709.7 10.9 copy-start.23
  764.1 69.7 %slice-start = ((s8[5566464]{0:T(1024)(128)(4,1)}), s8[4194304]{0:T(1024)(128)(4,1)S(1)}, s32[]{:S(2)}) async-start(s8[5566464]{0:T(1024)(128)(4,1)} %bitcast.168), calls=%async_computation.12 | async-start | bytes 8388608 | tf_op jit(solution)/shard_map/while
  764.1 68.1 %copy-start.3 = (bf16[2,453,3,3,64]{1,4,3,0,2:T(8,128)(2,1)S(1)}, bf16[2,453,3,3,64]{1,4,3,0,2:T(8,128)(2,1)}, u32[]{:S(2)}) copy-start(bf16[2,453,3,3,64]{1,4,3,0,2:T(8,128)(2,1)} %copy-done.2) | copy-start | bytes 3131140 | tf_op jit(solution)/shard_map/while
  764.1 69.7 %slice-start.1 = ((s8[5566464]{0:T(1024)(128)(4,1)}), s8[1372160]{0:T(1024)(128)(4,1)S(1)}, s32[]{:S(2)}) async-start(s8[5566464]{0:T(1024)(128)(4,1)} %bitcast.168), calls=%async_computation.13 | async-start | bytes 2744320 | tf_op jit(solution)/shard_map/while
  833.9 5.8 copy-start.9
  882.0 69.7 %slice-start = ((s8[5566464]{0:T(1024)(128)(4,1)}), s8[4194304]{0:T(1024)(128)(4,1)S(1)}, s32[]{:S(2)}) async-start(s8[5566464]{0:T(1024)(128)(4,1)} %bitcast.168), calls=%async_computation.12 | async-start | bytes 8388608 | tf_op jit(solution)/shard_map/while
  882.0 68.1 %copy-start.3 = (bf16[2,453,3,3,64]{1,4,3,0,2:T(8,128)(2,1)S(1)}, bf16[2,453,3,3,64]{1,4,3,0,2:T(8,128)(2,1)}, u32[]{:S(2)}) copy-start(bf16[2,453,3,3,64]{1,4,3,0,2:T(8,128)(2,1)} %copy-done.2) | copy-start | bytes 3131140 | tf_op jit(solution)/shard_map/while
  882.0 69.7 %slice-start.1 = ((s8[5566464]{0:T(1024)(128)(4,1)}), s8[1372160]{0:T(1024)(128)(4,1)S(1)}, s32[]{:S(2)}) async-start(s8[5566464]{0:T(1024)(128)(4,1)} %bitcast.168), calls=%async_computation.13 | async-start | bytes 2744320 | tf_op jit(solution)/shard_map/while
  999.9 69.7 %slice-start = ((s8[5566464]{0:T(1024)(128)(4,1)}), s8[4194304]{0:T(1024)(128)(4,1)S(1)}, s32[]{:S(2)}) async-start(s8[5566464]{0:T(1024)(128)(4,1)} %bitcast.168), calls=%async_computation.12 | async-start | bytes 8388608 | tf_op jit(solution)/shard_map/while
  999.9 68.1 %copy-start.3 = (bf16[2,453,3,3,64]{1,4,3,0,2:T(8,128)(2,1)S(1)}, bf16[2,453,3,3,64]{1,4,3,0,2:T(8,128)(2,1)}, u32[]{:S(2)}) copy-start(bf16[2,453,3,3,64]{1,4,3,0,2:T(8,128)(2,1)} %copy-done.2) | copy-start | bytes 3131140 | tf_op jit(solution)/shard_map/while
  999.9 69.7 %slice-start.1 = ((s8[5566464]{0:T(1024)(128)(4,1)}), s8[1372160]{0:T(1024)(128)(4,1)S(1)}, s32[]{:S(2)}) async-start(s8[5566464]{0:T(1024)(128)(4,1)} %bitcast.168), calls=%async_computation.13 | async-start | bytes 2744320 | tf_op jit(solution)/shard_map/while
  1117.8 69.7 %slice-start = ((s8[5566464]{0:T(1024)(128)(4,1)}), s8[4194304]{0:T(1024)(128)(4,1)S(1)}, s32[]{:S(2)}) async-start(s8[5566464]{0:T(1024)(128)(4,1)} %bitcast.168), calls=%async_computation.12 | async-start | bytes 8388608 | tf_op jit(solution)/shard_map/while
  1117.8 68.1 %copy-start.3 = (bf16[2,453,3,3,64]{1,4,3,0,2:T(8,128)(2,1)S(1)}, bf16[2,453,3,3,64]{1,4,3,0,2:T(8,128)(2,1)}, u32[]{:S(2)}) copy-start(bf16[2,453,3,3,64]{1,4,3,0,2:T(8,128)(2,1)} %copy-done.2) | copy-start | bytes 3131140 | tf_op jit(solution)/shard_map/while
  1117.8 69.7 %slice-start.1 = ((s8[5566464]{0:T(1024)(128)(4,1)}), s8[1372160]{0:T(1024)(128)(4,1)S(1)}, s32[]{:S(2)}) async-start(s8[5566464]{0:T(1024)(128)(4,1)} %bitcast.168), calls=%async_computation.13 | async-start | bytes 2744320 | tf_op jit(solution)/shard_map/while
  1206.8 11.9 copy-start.21
  1235.8 11.8 copy-start.40
  1264.2 176.9 %all-to-all-start.3 = ((bf16[3624,3,1,192]{3,1,2,0:T(4,128)(2,1)}), bf16[3624,3,1,192]{3,1,2,0:T(4,128)(2,1)}, u32[]{:S(2)}, u32[]{:S(2)}) async-start(bf16[3624,3,1,192]{3,1,2,0:T(4,128)(2,1)} %copy.194), calls=%async_computation.3 | async-start | bytes 14843904 | tf_op jit(solution)/shard_map/all_to_all | solution.py:204
  1269.7 314.2 %reduce-scatter.8.cloned.1.call-start = ((), (), s32[]{:S(2)}) async-start(), calls=%async_computation.9 | async-start | bytes 2433024 | tf_op jit(solution)/shard_map/reduce_scatter | solution.py:222
  1274.4 312.6 %reduce-scatter.6.cloned.1.call-start = ((), (), s32[]{:S(2)}) async-start(), calls=%async_computation.8 | async-start | bytes 7299072 | tf_op jit(solution)/shard_map/reduce_scatter | solution.py:219
  1454.5 6.3 copy-start.12
  1454.5 6.3 copy-start.29
  1454.5 6.3 copy-start.42
  1454.5 6.3 copy-start.46
  1454.5 6.3 copy-start.54
  1467.5 332.5 %reduce-scatter.12.cloned.1.call-start = ((), (), s32[]{:S(2)}) async-start(), calls=%async_computation.11 | async-start | bytes 19464192 | tf_op jit(solution)/shard_map/reduce_scatter | solution.py:228
  1485.1 525.9 %reduce-scatter.10.cloned.1.call-start = ((), (), s32[]{:S(2)}) async-start(), calls=%async_computation.10 | async-start | bytes 19464192 | tf_op jit(solution)/shard_map/reduce_scatter | solution.py:226
  1515.7 8.2 copy-start.34
  1515.7 8.2 copy-start.13
  1515.7 8.2 copy-start.47
  1524.0 55.0 %copy-start.44 = (f32[906]{0:T(1024)S(1)}, f32[906]{0:T(1024)}, u32[]{:S(2)}) copy-start(f32[906]{0:T(1024)} %copy-done.43) | copy-start | bytes 10876
  (42 other events, 99.0 us)
Sparse Core Ops, SparseCore 0:
  1276.4 183.2 reduce-scatter.7
  1467.7 119.2 reduce-scatter.5
  1594.0 206.0 reduce-scatter.11
  1806.9 204.1 reduce-scatter.9
where the time goes:
time: 2030 us; the launch traced here: 2020 us
  waiting for transfers between devices  638 us (31%)
  local copies, waits for them, and re-layouts  525 us (26%)
  other arithmetic  420 us (21%)
  matrix products  248 us (12%)
  blocking collectives  151 us (7%)
  starting transfers between devices  20.8 us (1%)
    sub x4, other arithmetic, backward_pair(): grad_scores = (probs * (grad_probs - inner)).astype(jnp.bfloat16)  272 us
    reduce_scatter x1, waiting for transfers between devices, body(): lax.psum_scatter(flat_down_weight, ('dp', 'seq'), scatter_dimension=0, ti...  213 us
    reduce_scatter x1, waiting for transfers between devices, body(): lax.psum_scatter(grad_up_weight, ('dp', 'seq'), scatter_dimension=1, tile...  211 us
    all_to_all x1, waiting for transfers between devices, body(): lax.all_to_all(grad_qkv, 'seq', split_axis=0, concat_axis=2, tiled=True)  167 us
    unnamed x2, blocking collectives  151 us
    dot_general x1, matrix products, body(): jnp.einsum('ecd,efd->ecf', grad_packed, down_weight, preferred_element_ty...  69.7 us
    gather x2, local copies, waits for them, and re-layouts, body(): jnp.take(spread.reshape(all_rows, 3, head_count, HEAD_DIM), order, axis=0)  53.5 us
  transfers between devices with their start and end apart: 8, of which 6 were waited for; matrix products, arithmetic and copies ran while one was open for 9% of the time, Pallas kernels for 0%

commit v1 on v0

v1 whole, which is shorter than its diff:
```python
import functools

import jax
import jax.numpy as jnp
import numpy as np
from jax import lax
from jax.experimental import pallas as pl
from jax.experimental.pallas import tpu as pltpu
from jax.sharding import PartitionSpec as P

HEAD_DIM = 64
PATCHES = 197
CAPTIONS = 4
CAP_LEN = 64
GROUP_ROWS = PATCHES + CAPTIONS * CAP_LEN
SEGS = CAPTIONS + 1
IMG = 208
CAP = CAPTIONS * CAP_LEN
SLOTS = 288
ROOM = SLOTS - 1
EPS = 1e-05
F32 = jnp.float32
BF16 = jnp.bfloat16
VMEM = pltpu.VMEM


def dot_nn(a, b):
    return lax.dot_general(a, b, (((1,), (0,)), ((), ())), preferred_element_type=F32)


def dot_nt(a, b):
    return lax.dot_general(a, b, (((1,), (1,)), ((), ())), preferred_element_type=F32)


def dot_tn(a, b):
    return lax.dot_general(a, b, (((0,), (0,)), ((), ())), preferred_element_type=F32)


def iota(shape, dim):
    return lax.broadcasted_iota(jnp.int32, shape, dim)


def params(limit=None, **kw):
    return pltpu.CompilerParams(vmem_limit_bytes=limit, **kw)


BIG = 60 * 1024 * 1024


def pack_kernel(ways, per, gid_ref, sid_ref, tok_ref, grad_ref, st_ref, sg_ref, col_ref):
    rows = gid_ref.shape[1]
    local = lax.rem(gid_ref[...], ways * per)
    dest = local // per
    key = (local - dest * per) * SEGS + sid_ref[...] + 1
    dest8 = jnp.broadcast_to(dest, (8, rows))
    onehot = (iota((8, rows), 0) == dest8).astype(F32)
    before = (iota((rows, rows), 0) < iota((rows, rows), 1)).astype(BF16)
    ranks = dot_nn(onehot.astype(BF16), before)
    rank = jnp.sum(onehot * ranks, axis=0, keepdims=True)
    over = (jnp.max(rank, axis=1, keepdims=True) > ROOM - 0.5).astype(F32)
    slot = dest.astype(F32) * SLOTS + rank
    here = iota((rows, rows), 0) == iota((rows, rows), 1)
    col_ref[...] = jnp.sum(
        jnp.where(here, jnp.broadcast_to(slot, (rows, rows)), 0.0), axis=1, keepdims=True
    ).astype(jnp.int32)
    rank = rank.astype(jnp.int32)
    keys = jnp.broadcast_to(key.astype(F32), (8, rows)).astype(BF16)
    width = tok_ref.shape[1]
    for d in range(ways):
        place = jnp.where((dest == d) & (rank < ROOM), rank, -1)
        pick = (iota((384, rows), 0) == jnp.broadcast_to(place, (384, rows))).astype(BF16)
        line = dot_nt(keys, pick)
        line = jnp.concatenate([line, jnp.zeros((8, width - 384), F32)], axis=1)[0:1]
        line = jnp.where(iota((1, width), 1) == width - 1, over, line)
        pick = pick[0:SLOTS]
        last = iota((SLOTS, width), 0) == ROOM
        out = dot_nn(pick, tok_ref[...])
        st_ref[d] = jnp.where(last, jnp.broadcast_to(line, (SLOTS, width)), out).astype(BF16)
        sg_ref[d] = dot_nn(pick, grad_ref[...]).astype(BF16)


def pack(ways, per, gid, sid, tokens, grads):
    rows, width = tokens.shape
    return pl.pallas_call(
        functools.partial(pack_kernel, ways, per),
        out_shape=(
            jax.ShapeDtypeStruct((ways, SLOTS, width), BF16),
            jax.ShapeDtypeStruct((ways, SLOTS, width), BF16),
            jax.ShapeDtypeStruct((rows, 1), jnp.int32),
        ),
        compiler_params=params(BIG),
        name="pack",
    )(gid.reshape(1, rows), sid.reshape(1, rows), tokens, grads)


def unpack_kernel(ways, per, recv_ref, x_ref, pos_ref, col_ref, flag_ref):
    total = ways * SLOTS
    width = recv_ref.shape[1]
    keys = jnp.zeros((8, total), F32)
    flag = jnp.zeros((1, 1), F32)
    for d in range(ways):
        tail = recv_ref[d * SLOTS + SLOTS - 16 : d * SLOTS + SLOTS, :].astype(F32)
        line = tail[15:16, :]
        flag = jnp.maximum(flag, line[:, width - 1 : width])
        line = jnp.where(iota((1, width), 1) < ROOM, line, 0.0)
        wide = jnp.concatenate([line, jnp.zeros((1, total - width), F32)], axis=1)
        wide = jnp.broadcast_to(wide, (8, total))
        keys = keys + (pltpu.roll(wide, d * SLOTS, 1) if d else wide)
    flag_ref[...] = jnp.broadcast_to(flag, (8, 128))
    classes = 16
    key16 = jnp.concatenate([keys, keys], axis=0)
    onehot = (key16 == (iota((classes, total), 0) + 1).astype(F32)).astype(F32)
    before = (iota((total, total), 0) < iota((total, total), 1)).astype(BF16)
    ranks = dot_nn(onehot.astype(BF16), before)
    cls = iota((classes, 1), 0)
    grp = cls // SEGS
    seg = cls - grp * SEGS
    base = jnp.where(seg == 0, grp * IMG, per * IMG + grp * CAP + (seg - 1) * CAP_LEN)
    pos = jnp.sum(onehot * (ranks + base.astype(F32) + 1.0), axis=0, keepdims=True) - 1.0
    here = iota((total, total), 0) == iota((total, total), 1)
    col_ref[...] = jnp.sum(
        jnp.where(here, jnp.broadcast_to(pos, (total, total)), 0.0), axis=1, keepdims=True
    ).astype(jnp.int32)
    pos = pos.astype(jnp.int32)
    pos_ref[...] = jnp.broadcast_to(pos, (8, total))
    rows = x_ref.shape[0]
    pick = (iota((rows, total), 0) == jnp.broadcast_to(pos, (rows, total))).astype(BF16)
    x_ref[...] = dot_nn(pick, recv_ref[...]).astype(BF16)


def unpack(ways, per, rows, recv):
    total, width = recv.shape
    return pl.pallas_call(
        functools.partial(unpack_kernel, ways, per),
        out_shape=(
            jax.ShapeDtypeStruct((rows, width), BF16),
            jax.ShapeDtypeStruct((8, total), jnp.int32),
            jax.ShapeDtypeStruct((total, 1), jnp.int32),
            jax.ShapeDtypeStruct((8, 128), F32),
        ),
        compiler_params=params(BIG),
        name="unpack",
    )(recv)


def place_kernel(pos_ref, recv_ref, x_ref):
    rows, total = x_ref.shape[0], recv_ref.shape[0]
    pick = iota((rows, total), 0) == jnp.broadcast_to(pos_ref[0:1, :], (rows, total))
    x_ref[...] = dot_nn(pick.astype(BF16), recv_ref[...]).astype(BF16)


def place(rows, pos, recv):
    return pl.pallas_call(
        place_kernel,
        out_shape=jax.ShapeDtypeStruct((rows, recv.shape[1]), BF16),
        compiler_params=params(BIG),
        name="place",
    )(pos, recv)


def choose_kernel(col_ref, value_ref, out_ref):
    rows, total = out_ref.shape[0], value_ref.shape[0]
    pick = iota((rows, total), 1) == jnp.broadcast_to(col_ref[...], (rows, total))
    out_ref[...] = dot_nn(pick.astype(BF16), value_ref[...]).astype(BF16)


def choose(col, value):
    return pl.pallas_call(
        choose_kernel,
        out_shape=jax.ShapeDtypeStruct((col.shape[0], value.shape[1]), BF16),
        compiler_params=params(BIG),
        name="choose",
    )(col, value)


def swap(blocks):
    return lax.all_to_all(blocks, "seq", split_axis=0, concat_axis=0, tiled=True)


def everyone(value, ways):
    return swap(jnp.broadcast_to(value[None], (ways,) + value.shape))


def sorted_places(per):
    spots = []
    for g in range(per):
        spots.append(g * IMG + np.arange(PATCHES))
        spots.append(per * IMG + g * CAP + np.arange(CAP))
    return np.concatenate(spots).astype(np.int32)


def slow_order(gid, sid, ways, per):
    key = lax.rem(gid, ways * per) * SEGS + sid
    return jnp.argsort(everyone(key, ways).reshape(-1), stable=True).astype(jnp.int32)


def slow_in(value, gid, sid, ways, per):
    tok_rows, width = value.shape
    order = slow_order(gid, sid, ways, per)
    mine = lax.dynamic_slice(order, (lax.axis_index("seq") * tok_rows,), (tok_rows,))
    rows = jnp.take(everyone(value, ways).reshape(-1, width), mine, axis=0)
    full = jnp.zeros((per * (IMG + CAP), width), value.dtype)
    return full.at[sorted_places(per)].set(rows)


def slow_out(value, gid, sid, ways, per):
    rows, width = value.shape
    tok_rows = gid.shape[0]
    undo = jnp.argsort(slow_order(gid, sid, ways, per), stable=True).astype(jnp.int32)
    mine = lax.dynamic_slice(undo, (lax.axis_index("seq") * tok_rows,), (tok_rows,))
    spot = (mine // tok_rows) * rows + jnp.take(
        jnp.asarray(sorted_places(per)), lax.rem(mine, tok_rows)
    )
    return jnp.take(everyone(value, ways).reshape(-1, width), spot, axis=0)


def norm_stats(value):
    center = value - jnp.mean(value, axis=-1, keepdims=True)
    spread = jnp.mean(center * center, axis=-1, keepdims=True)
    return center, lax.rsqrt(spread + EPS)


def qkv_kernel(x_ref, gain_ref, shift_ref, w_ref, qb_ref, vb_ref, first_ref, qkv_ref, keep_ref):
    j = pl.program_id(0)

    @pl.when(j == 0)
    def _():
        def step(i, c):
            at = pl.ds(pl.multiple_of(i * 16, 16), 16)
            center, r = norm_stats(x_ref[at, :].astype(F32))
            h = (center * r * gain_ref[...] + shift_ref[...]).astype(BF16)
            keep_ref[at, :] = h
            first_ref[at, :] = h
            return c

        lax.fori_loop(0, x_ref.shape[0] // 16, step, 0)

    bias = jnp.where(j == 0, qb_ref[...], jnp.where(j == 2, vb_ref[...], 0.0))
    qkv_ref[...] = (dot_nn(keep_ref[...], w_ref[...]) + bias).astype(BF16)


def qkv_call(x, gain, shift, w, qb, vb):
    rows, width = x.shape
    full = lambda r, c: pl.BlockSpec((r, c), lambda j: (0, 0))
    return pl.pallas_call(
        qkv_kernel,
        grid=(3,),
        in_specs=[
            full(rows, width),
            full(1, width),
            full(1, width),
            pl.BlockSpec((width, width), lambda j: (0, j)),
            full(1, width),
            full(1, width),
        ],
        out_specs=[full(rows, width), pl.BlockSpec((rows, width), lambda j: (0, j))],
        out_shape=(
            jax.ShapeDtypeStruct((rows, width), BF16),
            jax.ShapeDtypeStruct((rows, 3 * width), BF16),
        ),
        scratch_shapes=[VMEM((rows, width), BF16)],
        compiler_params=params(BIG),
        name="qkv",
    )(x, gain, shift, w, qb, vb)


def head_lanes(h):
    lane = iota((1, 2 * HEAD_DIM), 1)
    return (lane < HEAD_DIM) if h == 0 else (lane >= HEAD_DIM)


def only(sel, value):
    return jnp.where(sel, value, jnp.zeros_like(value))


def real_keys(cols):
    return iota((IMG, cols), 0) < PATCHES


def same_caption():
    n = 2 * CAP_LEN
    return (iota((n, n), 0) < CAP_LEN) == (iota((n, n), 1) < CAP_LEN)


def attn_fwd_kernel(per, q_ref, k_ref, v_ref, o_ref, lse_ref):
    n = 2 * CAP_LEN
    scale = HEAD_DIM ** (-0.5)
    diag = same_caption()
    for g in range(per):
        ia = pl.ds(g * IMG, IMG)
        ca = pl.ds(per * IMG + g * CAP, CAP)
        qi, qc = q_ref[ia, :] * scale, q_ref[ca, :] * scale
        ki, kc = k_ref[ia, :], k_ref[ca, :]
        vi, vc = v_ref[ia, :], v_ref[ca, :]
        out_i = jnp.zeros((n, IMG), F32)
        out_c = [jnp.zeros((n, n), F32) for _ in range(CAP // n)]
        for h in range(2):
            sel = head_lanes(h)
            kim, vim = only(sel, ki), only(sel, vi)
            kcm, vcm = only(sel, kc), only(sel, vc)
            s = jnp.where(real_keys(IMG), dot_nt(kim, qi), -1e30)
            peak = jnp.max(s, axis=0, keepdims=True)
            e = jnp.exp(s - peak)
            total = jnp.sum(e, axis=0, keepdims=True)
            probs = (e * (1.0 / total)).astype(BF16)
            out_i = out_i + dot_tn(vim, probs)
            lse_ref[0, h : h + 1, g * 256 : g * 256 + IMG] = peak + jnp.log(total)
            for p in range(CAP // n):
                pa = slice(p * n, p * n + n)
                sa = jnp.where(real_keys(n), dot_nt(kim, qc[pa]), -1e30)
                sb = jnp.where(diag, dot_nt(kcm[pa], qc[pa]), -1e30)
                peak = jnp.maximum(
                    jnp.max(sa, axis=0, keepdims=True), jnp.max(sb, axis=0, keepdims=True)
                )
                ea, eb = jnp.exp(sa - peak), jnp.exp(sb - peak)
                total = jnp.sum(ea, axis=0, keepdims=True) + jnp.sum(eb, axis=0, keepdims=True)
                inv = 1.0 / total
                out_c[p] = (
                    out_c[p]
                    + dot_tn(vim, (ea * inv).astype(BF16))
                    + dot_tn(vcm[pa], (eb * inv).astype(BF16))
                )
                at = (per + g) * 256 + p * n
                lse_ref[0, h : h + 1, at : at + n] = peak + jnp.log(total)
        o_ref[ia, :] = out_i.T.astype(BF16)
        for p in range(CAP // n):
            o_ref[pl.ds(per * IMG + g * CAP + p * n, n), :] = out_c[p].T.astype(BF16)


def attn_fwd(per, qkv):
    rows = qkv.shape[0]
    width = qkv.shape[1] // 3
    pair = 2 * HEAD_DIM
    steps = width // pair
    col = lambda k: pl.BlockSpec((rows, pair), lambda j: (0, k * steps + j))
    return pl.pallas_call(
        functools.partial(attn_fwd_kernel, per),
        grid=(steps,),
        in_specs=[col(0), col(1), col(2)],
        out_specs=[col(0), pl.BlockSpec((1, 8, 2 * per * 256), lambda j: (j, 0, 0))],
        out_shape=(
            jax.ShapeDtypeStruct((rows, width), BF16),
            jax.ShapeDtypeStruct((steps, 8, 2 * per * 256), F32),
        ),
        compiler_params=params(BIG),
        name="attn_fwd",
    )(qkv, qkv, qkv)


def attn_bwd_kernel(per, q_ref, k_ref, v_ref, do_ref, lse_ref, dq_ref, dk_ref, dv_ref):
    n = 2 * CAP_LEN
    scale = HEAD_DIM ** (-0.5)
    diag = same_caption()
    for g in range(per):
        ia = pl.ds(g * IMG, IMG)
        ca = pl.ds(per * IMG + g * CAP, CAP)
        qi, qc = q_ref[ia, :] * scale, q_ref[ca, :] * scale
        ki, kc = k_ref[ia, :] * scale, k_ref[ca, :] * scale
        vi, vc = v_ref[ia, :], v_ref[ca, :]
        doi, doc = do_ref[ia, :], do_ref[ca, :]
        dq_i = jnp.zeros((n, IMG), F32)
        dk_i = jnp.zeros((IMG, n), F32)
        dv_i = jnp.zeros((IMG, n), F32)
        dq_c = [jnp.zeros((n, n), F32) for _ in range(CAP // n)]
        dk_c = [jnp.zeros((n, n), F32) for _ in range(CAP // n)]
        dv_c = [jnp.zeros((n, n), F32) for _ in range(CAP // n)]
        for h in range(2):
            sel = head_lanes(h)
            kim, vim, qim, doim = only(sel, ki), only(sel, vi), only(sel, qi), only(sel, doi)
            kcm, vcm, qcm, docm = only(sel, kc), only(sel, vc), only(sel, qc), only(sel, doc)
            kun = only(sel, k_ref[ia, :])
            kcun = only(sel, k_ref[ca, :])
            lse = lse_ref[0, h : h + 1, g * 256 : g * 256 + IMG]
            p_ = jnp.where(real_keys(IMG), jnp.exp(dot_nt(kun, qi) - lse), 0.0)
            dp = dot_nt(vim, doi)
            delta = jnp.sum(dp * p_, axis=0, keepdims=True)
            ds = (p_ * (dp - delta)).astype(BF16)
            dq_i = dq_i + dot_tn(kim, ds)
            dk_i = dk_i + dot_nn(ds, qim)
            dv_i = dv_i + dot_nn(p_.astype(BF16), doim)
            for p in range(CAP // n):
                pa = slice(p * n, p * n + n)
                at = (per + g) * 256 + p * n
                lse = lse_ref[0, h : h + 1, at : at + n]
                wa = jnp.where(real_keys(n), jnp.exp(dot_nt(kun, qc[pa]) - lse), 0.0)
                wb = jnp.where(diag, jnp.exp(dot_nt(kcun[pa], qc[pa]) - lse), 0.0)
                da = dot_nt(vim, doc[pa])
                db = dot_nt(vcm[pa], doc[pa])
                delta = jnp.sum(da * wa, axis=0, keepdims=True) + jnp.sum(
                    db * wb, axis=0, keepdims=True
                )
                sa = (wa * (da - delta)).astype(BF16)
                sb = (wb * (db - delta)).astype(BF16)
                dq_c[p] = dq_c[p] + dot_tn(kim, sa) + dot_tn(kcm[pa], sb)
                dk_i = dk_i + dot_nn(sa, qcm[pa])
                dv_i = dv_i + dot_nn(wa.astype(BF16), docm[pa])
                dk_c[p] = dk_c[p] + dot_nn(sb, qcm[pa])
                dv_c[p] = dv_c[p] + dot_nn(wb.astype(BF16), docm[pa])
        dq_ref[ia, :] = dq_i.T.astype(BF16)
        dk_ref[ia, :] = dk_i.astype(BF16)
        dv_ref[ia, :] = dv_i.astype(BF16)
        for p in range(CAP // n):
            at = pl.ds(per * IMG + g * CAP + p * n, n)
            dq_ref[at, :] = dq_c[p].T.astype(BF16)
            dk_ref[at, :] = dk_c[p].astype(BF16)
            dv_ref[at, :] = dv_c[p].astype(BF16)


def attn_bwd(per, qkv, d_att, lse):
    rows = qkv.shape[0]
    width = qkv.shape[1] // 3
    pair = 2 * HEAD_DIM
    steps = width // pair
    col = lambda k: pl.BlockSpec((rows, pair), lambda j: (0, k * steps + j))
    return pl.pallas_call(
        functools.partial(attn_bwd_kernel, per),
        grid=(steps,),
        in_specs=[
            col(0),
            col(1),
            col(2),
            col(0),
            pl.BlockSpec((1, 8, lse.shape[2]), lambda j: (j, 0, 0)),
        ],
        out_specs=[col(0)] * 3,
        out_shape=(jax.ShapeDtypeStruct((rows, width), BF16),) * 3,
        compiler_params=params(BIG),
        name="attn_bwd",
    )(qkv, qkv, qkv, d_att, lse)


def fold8(value):
    return jnp.sum(value.reshape(value.shape[0] // 8, 8, value.shape[1]), axis=0)


def ffn_kernel(
    bounds,
    att_ref,
    x_ref,
    g_ref,
    wo_ref,
    bo_ref,
    gain_ref,
    shift_ref,
    up_ref,
    ub_ref,
    down_ref,
    db_ref,
    mixed_ref,
    dmid_ref,
    datt_ref,
    gup_ref,
    gdown_ref,
    gwo_ref,
    gub_ref,
    sums_ref,
    mid_ref,
    second_ref,
    mix_ref,
    ds_ref,
    pre_ref,
    dh_ref,
    hid_ref,
    dpre_ref,
):
    j = pl.program_id(0)
    rows, width = x_ref.shape
    steps16 = rows // 16

    @pl.when(j == 0)
    def _():
        mid_ref[...] = dot_nn(att_ref[...], wo_ref[...])

        def step(i, c):
            at = pl.ds(pl.multiple_of(i * 16, 16), 16)
            mid = x_ref[at, :].astype(F32) + mid_ref[at, :] + bo_ref[...]
            mid_ref[at, :] = mid
            center, r = norm_stats(mid)
            second_ref[at, :] = (center * r * gain_ref[...] + shift_ref[...]).astype(BF16)
            return c

        lax.fori_loop(0, steps16, step, 0)
        for e, (lo, hi) in enumerate(bounds):
            at = pl.ds(lo, hi - lo)
            mix_ref[at, :] = mid_ref[at, :] + db_ref[e : e + 1, :]
            total = jnp.sum(g_ref[at, :].astype(F32), axis=0, keepdims=True)
            sums_ref[3 + e : 4 + e, :] = total
        ds_ref[...] = jnp.zeros_like(ds_ref)

    for e, (lo, hi) in enumerate(bounds):
        at = pl.ds(lo, hi - lo)
        second = second_ref[at, :]
        g = g_ref[at, :]
        pre_ref[at, :] = dot_nn(second, up_ref[e]) + ub_ref[e : e + 1, :]
        dh_ref[at, :] = dot_nt(g, down_ref[e])

        def step(i, c):
            ch = pl.ds(pl.multiple_of(lo + i * 16, 16), 16)
            u = pre_ref[ch, :]
            cdf = 0.5 * (1.0 + lax.erf(u * (2.0**-0.5)))
            pdf = jnp.exp(-0.5 * u * u) * (1.0 / np.sqrt(2.0 * np.pi))
            hid_ref[ch, :] = (u * cdf).astype(BF16)
            d = (dh_ref[ch, :] * (cdf + u * pdf)).astype(BF16)
            dpre_ref[ch, :] = d
            d = d.astype(F32)
            return c + (d[0:8] + d[8:16])

        total = lax.fori_loop(0, (hi - lo) // 16, step, jnp.zeros((8, pre_ref.shape[1]), F32))
        gub_ref[e : e + 1, :] = jnp.sum(total, axis=0, keepdims=True)
        hid = hid_ref[at, :]
        dpre = dpre_ref[at, :]
        mix_ref[at, :] += dot_nn(hid, down_ref[e])
        ds_ref[at, :] += dot_nt(dpre, up_ref[e])
        gdown_ref[e] = dot_tn(hid, g).astype(BF16)
        gup_ref[e] = dot_tn(second, dpre).astype(BF16)

    @pl.when(j == pl.num_programs(0) - 1)
    def _():
        def step(i, c):
            at = pl.ds(pl.multiple_of(i * 16, 16), 16)
            mixed_ref[at, :] = mix_ref[at, :].astype(BF16)
            center, r = norm_stats(mid_ref[at, :])
            n = center * r
            u = ds_ref[at, :]
            un = u * n
            w = u * gain_ref[...]
            m1 = jnp.mean(w, axis=-1, keepdims=True)
            m2 = jnp.mean(w * n, axis=-1, keepdims=True)
            d = (g_ref[at, :].astype(F32) + r * (w - m1 - n * m2)).astype(BF16)
            dmid_ref[at, :] = d
            d = d.astype(F32)
            return (
                c[0] + un[0:8] + un[8:16],
                c[1] + u[0:8] + u[8:16],
                c[2] + d[0:8] + d[8:16],
            )

        zero = jnp.zeros((8, width), F32)
        total = lax.fori_loop(0, steps16, step, (zero, zero, zero))
        for i in range(3):
            sums_ref[i : i + 1, :] = jnp.sum(total[i], axis=0, keepdims=True)
        d = dmid_ref[...]
        datt_ref[...] = dot_nt(d, wo_ref[...]).astype(BF16)
        gwo_ref[...] = dot_tn(att_ref[...], d).astype(BF16)


def ffn(bounds, att, x, g, wo, bo, gain, shift, up, ub, down, db):
    rows, width = x.shape
    experts, _, hidden = up.shape
    chunk = width
    steps = hidden // chunk
    one = pl.Buffered(1)
    full = lambda r, c: pl.BlockSpec((r, c), lambda j: (0, 0), pipeline_mode=one)
    return pl.pallas_call(
        functools.partial(ffn_kernel, bounds),
        grid=(steps,),
        in_specs=[
            full(rows, width),
            full(rows, width),
            full(rows, width),
            full(width, width),
            full(1, width),
            full(1, width),
            full(1, width),
            pl.BlockSpec((experts, width, chunk), lambda j: (0, 0, j)),
            pl.BlockSpec((experts, chunk), lambda j: (0, j)),
            pl.BlockSpec((experts, chunk, width), lambda j: (0, j, 0)),
            full(experts, width),
        ],
        out_specs=[
            full(rows, width),
            full(rows, width),
            full(rows, width),
            pl.BlockSpec((experts, width, chunk), lambda j: (0, 0, j)),
            pl.BlockSpec((experts, chunk, width), lambda j: (0, j, 0)),
            full(width, width),
            pl.BlockSpec((experts, chunk), lambda j: (0, j)),
            full(8, width),
        ],
        out_shape=(
            jax.ShapeDtypeStruct((rows, width), BF16),
            jax.ShapeDtypeStruct((rows, width), BF16),
            jax.ShapeDtypeStruct((rows, width), BF16),
            jax.ShapeDtypeStruct(up.shape, BF16),
            jax.ShapeDtypeStruct(down.shape, BF16),
            jax.ShapeDtypeStruct((width, width), BF16),
            jax.ShapeDtypeStruct((experts, hidden), F32),
            jax.ShapeDtypeStruct((8, width), F32),
        ),
        scratch_shapes=[
            VMEM((rows, width), F32),
            VMEM((rows, width), BF16),
            VMEM((rows, width), F32),
            VMEM((rows, width), F32),
            VMEM((rows, chunk), F32),
            VMEM((rows, chunk), F32),
            VMEM((rows, chunk), BF16),
            VMEM((rows, chunk), BF16),
        ],
        compiler_params=params(67043328),
        name="ffn",
    )(att, x, g, wo, bo, gain, shift, up, ub, down, db)


def last_kernel(
    x_ref, first_ref, dq_ref, dk_ref, dv_ref, w_ref, gain_ref, dmid_ref, col_ref,
    back_ref, gin_ref, gw_ref, sums_ref, df_ref,
):
    rows, width = x_ref.shape
    first = first_ref[...]
    for j, d_ref in enumerate((dq_ref, dk_ref, dv_ref)):
        part = slice(j * width, (j + 1) * width)
        d = d_ref[...]
        gw_ref[:, part] = dot_tn(first, d).astype(BF16)
        term = dot_nt(d, w_ref[:, part])
        if j == 0:
            df_ref[...] = term
        else:
            df_ref[...] += term
    for j, d_ref in ((2, dq_ref), (3, dv_ref)):
        sums_ref[j : j + 1, :] = jnp.sum(d_ref[...].astype(F32), axis=0, keepdims=True)

    def step(i, c):
        at = pl.ds(pl.multiple_of(i * 16, 16), 16)
        center, r = norm_stats(x_ref[at, :].astype(F32))
        n = center * r
        u = df_ref[at, :]
        un = u * n
        w = u * gain_ref[...]
        m1 = jnp.mean(w, axis=-1, keepdims=True)
        m2 = jnp.mean(w * n, axis=-1, keepdims=True)
        gin_ref[at, :] = (dmid_ref[at, :].astype(F32) + r * (w - m1 - n * m2)).astype(BF16)
        return (c[0] + un[0:8] + un[8:16], c[1] + u[0:8] + u[8:16])

    zero = jnp.zeros((8, width), F32)
    total = lax.fori_loop(0, rows // 16, step, (zero, zero))
    for i in range(2):
        sums_ref[i : i + 1, :] = jnp.sum(total[i], axis=0, keepdims=True)
    back_ref[...] = give_back(col_ref, gin_ref)


def give_back(col_ref, value_ref):
    total, rows = col_ref.shape[0], value_ref.shape[0]
    pick = iota((total, rows), 1) == jnp.broadcast_to(col_ref[...], (total, rows))
    return dot_nn(pick.astype(BF16), value_ref[...]).astype(BF16)


def last(x, first, dq, dk, dv, w, gain, dmid, col):
    rows, width = x.shape
    return pl.pallas_call(
        last_kernel,
        out_shape=(
            jax.ShapeDtypeStruct((col.shape[0], width), BF16),
            jax.ShapeDtypeStruct((rows, width), BF16),
            jax.ShapeDtypeStruct(w.shape, BF16),
            jax.ShapeDtypeStruct((8, width), F32),
        ),
        scratch_shapes=[VMEM((rows, width), F32)],
        compiler_params=params(BIG),
        name="last",
    )(x, first, dq, dk, dv, w, gain, dmid, col)


def back_kernel(col_ref, value_ref, out_ref):
    out_ref[...] = give_back(col_ref, value_ref)


def back(col, value):
    return pl.pallas_call(
        back_kernel,
        out_shape=jax.ShapeDtypeStruct((col.shape[0], value.shape[1]), BF16),
        compiler_params=params(BIG),
        name="back",
    )(col, value)


def body(
    tokens,
    grad_out,
    group_ids,
    segment_ids,
    expert_ids,
    ln1_gain,
    ln1_bias,
    qkv_weight,
    q_bias,
    v_bias,
    out_weight,
    out_bias,
    ln2_gain,
    ln2_bias,
    up_weight,
    up_bias,
    down_weight,
    down_bias,
):
    ways = lax.axis_size("seq")
    world = ways * lax.axis_size("dp")
    tok_rows, width = tokens.shape
    per = tok_rows // GROUP_ROWS
    rows = per * (IMG + CAP)
    bounds = ((0, per * IMG), (per * IMG, rows))
    row = lambda v: v.reshape(1, width)

    send_t, send_g, slot_col = pack(ways, per, group_ids, segment_ids, tokens, grad_out)
    recv_t = swap(send_t).reshape(ways * SLOTS, width)
    recv_g = swap(send_g).reshape(ways * SLOTS, width)
    x_fast, pos_row, pos_col, flag = unpack(ways, per, rows, recv_t)
    over = flag[0, 0] > 0.5
    labels = (group_ids, segment_ids)
    x = lax.cond(over, lambda f, v: slow_in(v, *labels, ways, per), lambda f, v: f, x_fast, tokens)
    first, qkv = qkv_call(
        x, row(ln1_gain), row(ln1_bias), qkv_weight, row(q_bias), row(v_bias)
    )
    att, lse = attn_fwd(per, qkv)
    g_fast = place(rows, pos_row, recv_g)
    g = lax.cond(over, lambda f, v: slow_in(v, *labels, ways, per), lambda f, v: f, g_fast, grad_out)
    mixed_s, dmid, d_att, g_up, g_down, g_wo, g_ub, sums2 = ffn(
        bounds, att, x, g, out_weight, row(out_bias), row(ln2_gain), row(ln2_bias),
        up_weight, up_bias, down_weight, down_bias,
    )
    ret_m = swap(back(pos_col, mixed_s).reshape(ways, SLOTS, width)).reshape(-1, width)
    dq, dk, dv = attn_bwd(per, qkv, d_att, lse)
    back_g, gin_s, g_w, sums1 = last(
        x, first, dq, dk, dv, qkv_weight, row(ln1_gain), dmid, pos_col
    )
    ret_g = swap(back_g.reshape(ways, SLOTS, width)).reshape(-1, width)
    out = lambda s, f: lax.cond(
        over, lambda f_, s_: slow_out(s_, *labels, ways, per), lambda f_, s_: f_, f, s
    )
    mixed = out(mixed_s, choose(slot_col, ret_m))
    grad_in = out(gin_s, choose(slot_col, ret_g))

    axes = ("dp", "seq")
    scat = lambda v, dim: lax.psum_scatter(v, axes, scatter_dimension=dim, tiled=True).astype(F32)
    grad_up = scat(g_up, 1)
    grad_down = scat(g_down.reshape(-1, width), 0)
    grad_wo = scat(g_wo, 0)
    grad_w = scat(g_w, 0)
    piece = width // world
    vec = jnp.concatenate(
        [
            jnp.stack([sums1[0], sums1[1], sums1[2], sums1[3], sums2[2], sums2[0], sums2[1]])
            .reshape(7, world, piece)
            .transpose(1, 0, 2),
            sums2[3:5].reshape(2, world, piece).transpose(1, 0, 2),
            g_ub.reshape(world, -1, piece),
        ],
        axis=1,
    )
    vec = jnp.sum(lax.all_to_all(vec, axes, split_axis=0, concat_axis=0, tiled=True), axis=0)
    return (
        mixed,
        grad_in,
        vec[0],
        vec[1],
        grad_w,
        vec[2],
        vec[3],
        grad_wo,
        vec[4],
        vec[5],
        vec[6],
        grad_up,
        vec[9:].reshape(-1),
        grad_down,
        vec[7:9],
    )


def solution(mesh):
    both = P(("dp", "seq"))
    both2 = P(("dp", "seq"), None)
    return jax.shard_map(
        body,
        mesh=mesh,
        in_specs=(both2, both2, both, both, both2) + (P(),) * 13,
        out_specs=(
            both2,
            both2,
            both,
            both,
            both2,
            both,
            both,
            both2,
            both,
            both,
            both,
            P(None, ("dp", "seq"), None),
            both,
            both2,
            P(None, ("dp", "seq")),
        ),
        check_vma=False,
    )
```

time: 2030 us -> 739 us (0.36)
  local copies, waits for them, and re-layouts: 525 us -> 44.7 us
  other arithmetic: 420 us -> 7.46 us
  matrix products: 248 us -> 0 us
  waiting for transfers between devices: 638 us -> 416 us
  Pallas kernels: 0 us -> 205 us
  blocking collectives: 151 us -> 13.4 us
    sub x4 -> x0, other arithmetic: 272 us -> none  [backward_pair(): grad_scores = (probs * (grad_probs - inner)).astype(jnp.bfloat16)]
    reduce_scatter x4 -> x3, waiting for transfers between devices: 427 us -> 157 us  [body(): lax.psum_scatter(v, axes, scatter_dimension=dim, tiled=True).astype(F32)]
    dot_general x40 -> x0, matrix products: 248 us -> none  [the longest x1 69.7 us: body(): jnp.einsum('ecd,efd->ecf', grad_packed, down_weight, preferred_element_ty...]
    pallas_call x0 -> x11, Pallas kernels: none -> 205 us  [the longest x1 77.6 us: ffn(): pl.pallas_call(functools.partial(ffn_kernel, bounds), grid=(steps,), in_s...]
    gather x13 -> x0, local copies, waits for them, and re-layouts: 184 us -> none  [the longest x2 53.5 us: body(): jnp.take(spread.reshape(all_rows, 3, head_count, HEAD_DIM), order, axis=0)]
    unnamed x2 -> x0, blocking collectives: 151 us -> none
    unnamed x4 -> x5, waiting for transfers between devices: 0.07 us -> 140 us
    reshape x13 -> x11, local copies, waits for them, and re-layouts: 101 us -> 5.05 us  [the longest x7 4.1 us: body(): row = lambda v: v.reshape(1, width)]
  transfers between devices with their start and end apart: 8 -> 8, of which waited for: 6 -> 6; matrix products, arithmetic and copies ran while one was open for 9% -> 6% of each run, Pallas kernels for 0% -> 15%
where the time goes in v1:
time: 739 us; the launch traced here: 732 us
  waiting for transfers between devices  416 us (56%)
  Pallas kernels  205 us (28%)
  local copies, waits for them, and re-layouts  44.7 us (6%)
  starting transfers between devices  18.2 us (2%)
  between operations  15 us (2%)
  blocking collectives  13.4 us (2%)
  loops' own time  12.1 us (2%)
  other arithmetic  7.46 us (1%)
    reduce_scatter x3, waiting for transfers between devices, body(): lax.psum_scatter(v, axes, scatter_dimension=dim, tiled=True).astype(F32)  157 us
    unnamed x5, waiting for transfers between devices  140 us
    all_to_all x4, waiting for transfers between devices, swap(): lax.all_to_all(blocks, 'seq', split_axis=0, concat_axis=0, tiled=True)  119 us
    pallas_call x1, Pallas kernels, ffn(): pl.pallas_call(functools.partial(ffn_kernel, bounds), grid=(steps,), in_s...  77.6 us
    unnamed x55, local copies, waits for them, and re-layouts  36.7 us
    pallas_call x1, Pallas kernels, last(): pl.pallas_call(last_kernel, out_shape=(jax.ShapeDtypeStruct((col.shape[0]...  31.4 us
    pallas_call x1, Pallas kernels, attn_bwd(): pl.pallas_call(functools.partial(attn_bwd_kernel, per), grid=(steps,), in...  27 us
    pallas_call x1, Pallas kernels, attn_fwd(): pl.pallas_call(functools.partial(attn_fwd_kernel, per), grid=(steps,), in...  20.5 us
  transfers between devices with their start and end apart: 8, of which 6 were waited for; matrix products, arithmetic and copies ran while one was open for 6% of the time, Pallas kernels for 15%

profile of v1, /device:TPU:0, one launch (start us, length us, event | category | flops | bytes accessed | tf_op | source)
XLA Modules:
  0.0 732.2 jit_solution(11839285080937599375)
XLA Ops:
  7.2 8.4 %pack.1 = (bf16[4,288,768]{2,1,0:T(8,128)(2,1)}, bf16[4,288,768]{2,1,0:T(8,128)(2,1)}, s32[906,1]{1,0:T(8,128)}) custom-call(s32[1,906]{1,0:T(1,128)} %bitcast.46, s32[1,906]{1,0:T(1,128)} %bitcast.47, bf16[906,768]{1,0:T(8,128)(2,1)} %tok_ref.1, bf16[906,768]{1,0:T(8,128)(2,1)} %grad_ref.1), custom_call_target="tpu_custom_call" | custom-call | tf_op jit(solution)/shard_map/pack/pallas_call | solution.py:84
  15.6 6.3 all-to-all-start.8
  22.0 41.2 %all-to-all-done.8 = bf16[4,288,768]{2,1,0:T(8,128)(2,1)S(1)} async-done(((bf16[4,288,768]{2,1,0:T(8,128)(2,1)}), bf16[4,288,768]{2,1,0:T(8,128)(2,1)S(1)}, u32[]{:S(2)}, u32[]{:S(2)}) %all-to-all-start.8) | async-done | bytes 1769504 | tf_op jit(solution)/shard_map/all_to_all | solution.py:177
  63.1 1.2 copy-done.7
  64.3 4.2 unpack.1
  68.5 1.2 slice.48
  70.4 4.7 conditional.4
  75.2 3.7 all-to-all-start.9
  79.0 0.6 reshape.169.gain_ref
  79.6 0.6 reshape.170.shift_ref
  80.2 0.6 reshape.171.qb_ref
  80.7 0.6 reshape.172.vb_ref
  81.3 0.6 reshape.174.bo_ref
  81.9 0.6 reshape.175.gain_ref
  82.5 0.6 reshape.176.shift_ref
  83.1 17.3 %qkv.1 = (bf16[928,768]{1,0:T(8,128)(2,1)}, bf16[928,2304]{1,0:T(8,128)(2,1)}) custom-call(bf16[928,768]{1,0:T(8,128)(2,1)S(1)} %get-tuple-element.163.x_ref, f32[1,768]{1,0:T(1,128)} %reshape.169.gain_ref, f32[1,768]{1,0:T(1,128)} %reshape.170.shift_ref, bf16[768,2304]{1,0:T(8,128)(2,1)} %w_ref.3, f32[1,768]{1,0:T(1,128)} %reshape.171.qb_ref, ...), custom_call_target="tpu_custom_call" | custom-call | tf_op jit(solution)/shard_map/qkv/pallas_call | solution.py:245
  100.5 20.5 %attn_fwd.1 = (bf16[928,768]{1,0:T(8,128)(2,1)}, f32[6,8,1024]{2,1,0:T(8,128)}) custom-call(bf16[928,2304]{1,0:T(8,128)(2,1)} %get-tuple-element.125.q_ref.k_ref.v_ref, bf16[928,2304]{1,0:T(8,128)(2,1)} %get-tuple-element.125.q_ref.k_ref.v_ref, bf16[928,2304]{1,0:T(8,128)(2,1)} %get-tuple-element.125.q_ref.k_ref.v_ref), custom_call_target="tpu_custom_call" | custom-call | tf_op jit(solution)/shard_map/attn_fwd/pallas_call | solution.py:336
  121.0 1.2 copy-done.6
  122.2 4.7 place.1
  126.9 7.3 conditional.5
  134.2 77.6 %ffn.1 = (bf16[928,768]{1,0:T(8,128)(2,1)}, bf16[928,768]{1,0:T(8,128)(2,1)}, bf16[928,768]{1,0:T(8,128)(2,1)}, bf16[2,768,3072]{2,1,0:T(8,128)(2,1)}, bf16[2,30...) custom-call(bf16[928,768]{1,0:T(8,128)(2,1)} %get-tuple-element.126.att_ref, ...), custom_call_target="tpu_custom_call" | custom-call | tf_op jit(solution)/shard_map/ffn/pallas_call | solution.py:554
  212.2 27.0 %attn_bwd.1 = (bf16[928,768]{1,0:T(8,128)(2,1)}, bf16[928,768]{1,0:T(8,128)(2,1)}, bf16[928,768]{1,0:T(8,128)(2,1)}) custom-call(bf16[928,2304]{1,0:T(8,128)(2,1)} %get-tuple-element.125.q_ref.k_ref.v_ref, bf16[928,2304]{1,0:T(8,128)(2,1)} %get-tuple-element.125.q_ref.k_ref.v_ref, bf16[928,2304]{1,0:T(8,128)(2,1)} %get-tuple-element.125.q_ref.k_ref.v_ref, ...), custom_call_target="tpu_custom_call" | custom-call | tf_op jit(solution)/shard_map/attn_bwd/pallas_call | solution.py:415
  239.2 31.4 %last.1 = (bf16[1152,768]{1,0:T(8,128)(2,1)}, bf16[928,768]{1,0:T(8,128)(2,1)}, bf16[768,2304]{1,0:T(8,128)(2,1)}, f32[8,768]{1,0:T(8,128)}) custom-call(bf16[928,768]{1,0:T(8,128)(2,1)S(1)} %copy-done.3, bf16[928,768]{1,0:T(8,128)(2,1)} %get-tuple-element.130.first_ref, bf16[928,768]{1,0:T(8,128)(2,1)} %get-tuple-element.133.dq_ref, ...), custom_call_target="tpu_custom_call" | custom-call | tf_op jit(solution)/shard_map/last/pallas_call | solution.py:650
  270.8 18.3 %copy.44 = bf16[2,768,3072]{2,0,1:T(2,128)(2,1)} copy(bf16[2,768,3072]{2,1,0:T(8,128)(2,1)} %get-tuple-element.144) | data formatting | bytes 18874368
  289.2 10.5 %copy.46 = bf16[96,8,2,3072]{3,1,2,0:T(8,128)(2,1)} copy(bf16[96,8,2,3072]{3,2,1,0:T(2,128)(2,1)} %bitcast.35) | data formatting | bytes 18874368
  301.4 13.4 %all_to_all.65 = f32[32,1,408]{2,1,0:T(1,128)} all-to-all(f32[32,1,408]{2,1,0:T(1,128)S(1)} %reshape.297), channel_id=1, replica_groups=mesh['dp'=8,'seq'=4] {'dp','seq'}, dimensions={0} | all-to-all | bytes 104448 | tf_op jit(solution)/shard_map/all_to_all | solution.py:751
  314.8 3.7 all-to-all-start.11
  318.5 4.4 back.1
  322.9 36.8 %all-to-all-done.11 = bf16[4,288,768]{2,1,0:T(8,128)(2,1)S(1)} async-done(((bf16[4,288,768]{2,1,0:T(8,128)(2,1)}), bf16[4,288,768]{2,1,0:T(8,128)(2,1)S(1)}, u32[]{:S(2)}, u32[]{:S(2)}) %all-to-all-start.11) | async-done | bytes 1769504 | tf_op jit(solution)/shard_map/all_to_all | solution.py:177
  359.7 1.2 copy-done.4
  360.9 3.6 all-to-all-start.10
  365.0 1.6 reduce.4
  366.9 0.6 slice.82
  367.4 0.6 reshape.184
  368.1 0.5 slice_bitcast_fusion
  368.6 1.4 convert_element_type.24
  370.0 4.8 choose.3
  374.8 40.9 %all-to-all-done.10 = bf16[4,288,768]{2,1,0:T(8,128)(2,1)S(1)} async-done(((bf16[4,288,768]{2,1,0:T(8,128)(2,1)}), bf16[4,288,768]{2,1,0:T(8,128)(2,1)S(1)}, u32[]{:S(2)}, u32[]{:S(2)}) %all-to-all-start.10) | async-done | bytes 1769504 | tf_op jit(solution)/shard_map/all_to_all | solution.py:177
  415.8 1.2 copy-done.5
  416.9 4.8 choose.2
  421.9 1.2 copy-done.9
  423.1 18.4 %reduce-scatter.7.cloned.1.call-done = bf16[24,2304]{1,0:T(8,128)(2,1)} async-done(((bf16[768,2304]{1,0:T(8,128)(2,1)}), bf16[24,2304]{1,0:T(8,128)(2,1)}) %reduce-scatter.7.cloned.1.call-update) | async-done | bytes 110608 | tf_op jit(solution)/shard_map/reduce_scatter | solution.py:735
  441.5 1.6 convert_element_type.23
  443.1 139.6 %reduce-scatter.13.cloned.1.call-done = bf16[24,6144]{1,0:T(8,128)(2,1)} async-done(((bf16[768,6144]{1,0:T(8,128)(2,1)}), bf16[24,6144]{1,0:T(8,128)(2,1)}) %reduce-scatter.13.cloned.1.call-update) | async-done | bytes 294928
  582.7 1.2 reshape.272
  583.9 0.9 copy_convert_fusion
  584.8 138.9 %reduce-scatter.11.cloned.1.call-done = bf16[192,768]{1,0:T(8,128)(2,1)} async-done(((bf16[6144,768]{1,0:T(8,128)(2,1)}), bf16[192,768]{1,0:T(8,128)(2,1)}) %reduce-scatter.11.cloned.1.call-update) | async-done | bytes 294928 | tf_op jit(solution)/shard_map/reduce_scatter | solution.py:735
  723.7 1.8 convert_element_type.26
  (73 shorter events, 3.3 us)
Async XLA Ops:
  15.6 47.5 %all-to-all-start.8 = ((bf16[4,288,768]{2,1,0:T(8,128)(2,1)}), bf16[4,288,768]{2,1,0:T(8,128)(2,1)S(1)}, u32[]{:S(2)}, u32[]{:S(2)}) async-start(bf16[4,288,768]{2,1,0:T(8,128)(2,1)} %get-tuple-element.120), calls=%async_computation.8 | async-start | bytes 3538944 | tf_op jit(solution)/shard_map/all_to_all | solution.py:177
  21.9 48.4 %copy-start = (s32[906]{0:T(1024)S(1)}, s32[906]{0:T(1024)}, u32[]{:S(2)}) copy-start(s32[906]{0:T(1024)} %constant.131.clone) | copy-start | bytes 10876
  21.9 48.5 %copy-start.11 = (s32[906]{0:T(1024)S(1)}, s32[906]{0:T(1024)}, u32[]{:S(2)}) copy-start(s32[906]{0:T(1024)} %param.40) | copy-start | bytes 10876
  22.0 48.5 %copy-start.13 = (s32[906]{0:T(1024)S(1)}, s32[906]{0:T(1024)}, u32[]{:S(2)}) copy-start(s32[906]{0:T(1024)} %param.41) | copy-start | bytes 10876
  63.1 1.2 copy-start.7
  75.1 8.0 %copy-start.2 = (bf16[928,768]{1,0:T(8,128)(2,1)}, bf16[928,768]{1,0:T(8,128)(2,1)S(1)}, u32[]{:S(2)}) copy-start(bf16[928,768]{1,0:T(8,128)(2,1)S(1)} %get-tuple-element.163.x_ref) | copy-start | bytes 4276228
  75.1 3.9 copy-start.18
  75.1 4.4 copy-start.19
  75.1 5.0 copy-start.20
  75.1 5.6 copy-start.21
  75.2 6.2 copy-start.22
  75.2 6.7 copy-start.23
  75.2 7.3 copy-start.24
  75.2 45.8 %all-to-all-start.9 = ((bf16[4,288,768]{2,1,0:T(8,128)(2,1)}), bf16[4,288,768]{2,1,0:T(8,128)(2,1)S(1)}, u32[]{:S(2)}, u32[]{:S(2)}) async-start(bf16[4,288,768]{2,1,0:T(8,128)(2,1)} %get-tuple-element.128), calls=%async_computation.9 | async-start | bytes 3538944 | tf_op jit(solution)/shard_map/all_to_all | solution.py:177
  78.9 289.7 %reduce-scatter.9.cloned.1.call-start = ((), (), s32[]{:S(2)}) async-start(), calls=%async_computation.18 | async-start | bytes 1216512 | tf_op jit(solution)/shard_map/reduce_scatter | solution.py:735
  100.5 21.8 %copy-start.10 = (bf16[906,768]{1,0:T(8,128)(2,1)S(1)}, bf16[906,768]{1,0:T(8,128)(2,1)}, u32[]{:S(2)}) copy-start(bf16[906,768]{1,0:T(8,128)(2,1)} %grad_ref.1) | copy-start | bytes 4174852
  121.0 1.2 copy-start.6
  211.8 229.7 %reduce-scatter.7.cloned.1.call-start = ((), (), s32[]{:S(2)}) async-start(), calls=%async_computation.17 | async-start | bytes 3649536 | tf_op jit(solution)/shard_map/reduce_scatter | solution.py:735
  212.2 27.0 %copy-start.3 = (bf16[928,768]{1,0:T(8,128)(2,1)S(1)}, bf16[928,768]{1,0:T(8,128)(2,1)}, u32[]{:S(2)}) copy-start(bf16[928,768]{1,0:T(8,128)(2,1)} %copy-done.2) | copy-start | bytes 4276228
  270.6 312.1 %reduce-scatter.13.cloned.1.call-start = ((), (), s32[]{:S(2)}) async-start(), calls=%async_computation.20 | async-start | bytes 9732096
  299.7 424.0 %reduce-scatter.11.cloned.1.call-start = ((), (), s32[]{:S(2)}) async-start(), calls=%async_computation.19 | async-start | bytes 9732096 | tf_op jit(solution)/shard_map/reduce_scatter | solution.py:735
  299.7 0.7 copy-start.16
  299.7 0.7 copy-start.17
  299.7 1.1 copy-start.15
  314.8 3.7 copy-start.8
  314.8 44.9 %all-to-all-start.11 = ((bf16[4,288,768]{2,1,0:T(8,128)(2,1)}), bf16[4,288,768]{2,1,0:T(8,128)(2,1)S(1)}, u32[]{:S(2)}, u32[]{:S(2)}) async-start(bf16[4,288,768]{2,1,0:T(8,128)(2,1)} %bitcast.42), calls=%async_computation.11 | async-start | bytes 3538944 | tf_op jit(solution)/shard_map/all_to_all | solution.py:177
  359.7 1.2 copy-start.4
  360.9 54.9 %all-to-all-start.10 = ((bf16[4,288,768]{2,1,0:T(8,128)(2,1)}), bf16[4,288,768]{2,1,0:T(8,128)(2,1)S(1)}, u32[]{:S(2)}, u32[]{:S(2)}) async-start(bf16[4,288,768]{2,1,0:T(8,128)(2,1)} %bitcast.41), calls=%async_computation.10 | async-start | bytes 3538944 | tf_op jit(solution)/shard_map/all_to_all | solution.py:177
  370.0 46.9 %copy-start.1 = (s32[906]{0:T(1024)S(1)}, s32[906]{0:T(1024)}, u32[]{:S(2)}) copy-start(s32[906]{0:T(1024)} %constant.131.clone) | copy-start | bytes 10876
  370.0 46.9 %copy-start.12 = (s32[906]{0:T(1024)S(1)}, s32[906]{0:T(1024)}, u32[]{:S(2)}) copy-start(s32[906]{0:T(1024)} %param.40) | copy-start | bytes 10876
  370.0 46.9 %copy-start.14 = (s32[906]{0:T(1024)S(1)}, s32[906]{0:T(1024)}, u32[]{:S(2)}) copy-start(s32[906]{0:T(1024)} %param.41) | copy-start | bytes 10876
  415.8 1.2 copy-start.5
  421.7 1.4 copy-start.9
Sparse Core Ops, SparseCore 0:
  211.9 98.7 reduce-scatter.8
  316.1 125.3 reduce-scatter.6
  447.4 135.2 reduce-scatter.12
  588.5 135.1 reduce-scatter.10

commit v2 on v1

--- a/solution.py
+++ b/solution.py
@@ -47,7 +47,11 @@
 BIG = 60 * 1024 * 1024
 
 
-def pack_kernel(ways, per, gid_ref, sid_ref, tok_ref, grad_ref, st_ref, sg_ref, col_ref):
+def cost(flops):
+    return pl.CostEstimate(flops=3 * flops, bytes_accessed=1 << 20, transcendentals=0)
+
+
+def pack_kernel(ways, per, gid_ref, sid_ref, tok_ref, st_ref, row_ref, col_ref):
     rows = gid_ref.shape[1]
     local = lax.rem(gid_ref[...], ways * per)
     dest = local // per
@@ -72,28 +76,44 @@
         line = dot_nt(keys, pick)
         line = jnp.concatenate([line, jnp.zeros((8, width - 384), F32)], axis=1)[0:1]
         line = jnp.where(iota((1, width), 1) == width - 1, over, line)
-        pick = pick[0:SLOTS]
         last = iota((SLOTS, width), 0) == ROOM
-        out = dot_nn(pick, tok_ref[...])
+        out = dot_nn(pick[0:SLOTS], tok_ref[...])
         st_ref[d] = jnp.where(last, jnp.broadcast_to(line, (SLOTS, width)), out).astype(BF16)
-        sg_ref[d] = dot_nn(pick, grad_ref[...]).astype(BF16)
-
-
-def pack(ways, per, gid, sid, tokens, grads):
+        row_ref[d : d + 1, :] = place
+
+
+def pack(ways, per, gid, sid, tokens):
     rows, width = tokens.shape
     return pl.pallas_call(
         functools.partial(pack_kernel, ways, per),
         out_shape=(
             jax.ShapeDtypeStruct((ways, SLOTS, width), BF16),
-            jax.ShapeDtypeStruct((ways, SLOTS, width), BF16),
+            jax.ShapeDtypeStruct((8, rows), jnp.int32),
             jax.ShapeDtypeStruct((rows, 1), jnp.int32),
         ),
         compiler_params=params(BIG),
         name="pack",
-    )(gid.reshape(1, rows), sid.reshape(1, rows), tokens, grads)
-
-
-def unpack_kernel(ways, per, recv_ref, x_ref, pos_ref, col_ref, flag_ref):
+    )(gid.reshape(1, rows), sid.reshape(1, rows), tokens)
+
+
+def pack_more_kernel(ways, row_ref, value_ref, out_ref):
+    rows = value_ref.shape[0]
+    for d in range(ways):
+        pick = iota((SLOTS, rows), 0) == jnp.broadcast_to(row_ref[d : d + 1, :], (SLOTS, rows))
+        out_ref[d] = dot_nn(pick.astype(BF16), value_ref[...]).astype(BF16)
+
+
+def pack_more(ways, places, value):
+    return pl.pallas_call(
+        functools.partial(pack_more_kernel, ways),
+        out_shape=jax.ShapeDtypeStruct((ways, SLOTS, value.shape[1]), BF16),
+        compiler_params=params(BIG),
+        cost_estimate=cost(2 * ways * SLOTS * value.shape[0] * value.shape[1]),
+        name="pack_more",
+    )(places, value)
+
+
+def index_kernel(ways, per, recv_ref, pos_ref, col_ref, flag_ref):
     total = ways * SLOTS
     width = recv_ref.shape[1]
     keys = jnp.zeros((8, total), F32)
@@ -123,23 +143,19 @@
     ).astype(jnp.int32)
     pos = pos.astype(jnp.int32)
     pos_ref[...] = jnp.broadcast_to(pos, (8, total))
-    rows = x_ref.shape[0]
-    pick = (iota((rows, total), 0) == jnp.broadcast_to(pos, (rows, total))).astype(BF16)
-    x_ref[...] = dot_nn(pick, recv_ref[...]).astype(BF16)
-
-
-def unpack(ways, per, rows, recv):
+
+
+def index(ways, per, recv):
     total, width = recv.shape
     return pl.pallas_call(
-        functools.partial(unpack_kernel, ways, per),
+        functools.partial(index_kernel, ways, per),
         out_shape=(
-            jax.ShapeDtypeStruct((rows, width), BF16),
             jax.ShapeDtypeStruct((8, total), jnp.int32),
             jax.ShapeDtypeStruct((total, 1), jnp.int32),
             jax.ShapeDtypeStruct((8, 128), F32),
         ),
         compiler_params=params(BIG),
-        name="unpack",
+        name="index",
     )(recv)
 
 
@@ -260,6 +276,7 @@
         ),
         scratch_shapes=[VMEM((rows, width), BF16)],
         compiler_params=params(BIG),
+        cost_estimate=cost(2 * rows * width * 3 * width),
         name="qkv",
     )(x, gain, shift, w, qb, vb)
 
@@ -343,6 +360,7 @@
             jax.ShapeDtypeStruct((steps, 8, 2 * per * 256), F32),
         ),
         compiler_params=params(BIG),
+        cost_estimate=cost(7 * rows * width * width),
         name="attn_fwd",
     )(qkv, qkv, qkv)
 
@@ -425,6 +443,7 @@
         out_specs=[col(0)] * 3,
         out_shape=(jax.ShapeDtypeStruct((rows, width), BF16),) * 3,
         compiler_params=params(BIG),
+        cost_estimate=cost(9 * rows * width * width),
         name="attn_bwd",
     )(qkv, qkv, qkv, d_att, lse)
 
@@ -433,126 +452,135 @@
     return jnp.sum(value.reshape(value.shape[0] // 8, 8, value.shape[1]), axis=0)
 
 
-def ffn_kernel(
-    bounds,
-    att_ref,
-    x_ref,
-    g_ref,
-    wo_ref,
-    bo_ref,
-    gain_ref,
-    shift_ref,
-    up_ref,
-    ub_ref,
-    down_ref,
-    db_ref,
-    mixed_ref,
-    dmid_ref,
-    datt_ref,
-    gup_ref,
-    gdown_ref,
-    gwo_ref,
-    gub_ref,
-    sums_ref,
-    mid_ref,
-    second_ref,
-    mix_ref,
-    ds_ref,
-    pre_ref,
-    dh_ref,
-    hid_ref,
-    dpre_ref,
-):
+def ffn_kernel(expert, lo, hi, *refs):
     j = pl.program_id(0)
-    rows, width = x_ref.shape
-    steps16 = rows // 16
+    att_ref, x_ref, g_ref, wo_ref, bo_ref, gain_ref, shift_ref = refs[:7]
+    up_ref, ub_ref, down_ref, db_ref = refs[7:11]
+    refs = refs[11:]
+    if lo:
+        mixed0_ref, dmid0_ref, datt0_ref, sums0_ref = refs[:4]
+        refs = refs[4:]
+    mixed_ref, dmid_ref, datt_ref, gup_ref, gdown_ref, gub_ref, sums_ref = refs[:7]
+    refs = refs[7:]
+    if lo:
+        gwo_ref = refs[0]
+        refs = refs[1:]
+    mid_ref, second_ref, mix_ref, ds_ref, pre_ref, dh_ref, hid_ref, dpre_ref = refs
+    width = x_ref.shape[1]
+    span = hi - lo
+    steps16 = span // 16
+    own = slice(lo, hi)
+    here = lambda i: pl.ds(pl.multiple_of(i * 16, 16), 16)
+    there = lambda i: pl.ds(pl.multiple_of(lo + i * 16, 16), 16)
 
     @pl.when(j == 0)
     def _():
-        mid_ref[...] = dot_nn(att_ref[...], wo_ref[...])
+        mid_ref[...] = dot_nn(att_ref[own, :], wo_ref[...])
 
         def step(i, c):
-            at = pl.ds(pl.multiple_of(i * 16, 16), 16)
-            mid = x_ref[at, :].astype(F32) + mid_ref[at, :] + bo_ref[...]
-            mid_ref[at, :] = mid
+            mid = x_ref[there(i), :].astype(F32) + mid_ref[here(i), :] + bo_ref[...]
+            mid_ref[here(i), :] = mid
+            mix_ref[here(i), :] = mid + db_ref[expert : expert + 1, :]
             center, r = norm_stats(mid)
-            second_ref[at, :] = (center * r * gain_ref[...] + shift_ref[...]).astype(BF16)
+            second_ref[here(i), :] = (center * r * gain_ref[...] + shift_ref[...]).astype(BF16)
             return c
 
         lax.fori_loop(0, steps16, step, 0)
-        for e, (lo, hi) in enumerate(bounds):
-            at = pl.ds(lo, hi - lo)
-            mix_ref[at, :] = mid_ref[at, :] + db_ref[e : e + 1, :]
-            total = jnp.sum(g_ref[at, :].astype(F32), axis=0, keepdims=True)
-            sums_ref[3 + e : 4 + e, :] = total
         ds_ref[...] = jnp.zeros_like(ds_ref)
 
-    for e, (lo, hi) in enumerate(bounds):
-        at = pl.ds(lo, hi - lo)
-        second = second_ref[at, :]
-        g = g_ref[at, :]
-        pre_ref[at, :] = dot_nn(second, up_ref[e]) + ub_ref[e : e + 1, :]
-        dh_ref[at, :] = dot_nt(g, down_ref[e])
-
-        def step(i, c):
-            ch = pl.ds(pl.multiple_of(lo + i * 16, 16), 16)
-            u = pre_ref[ch, :]
-            cdf = 0.5 * (1.0 + lax.erf(u * (2.0**-0.5)))
-            pdf = jnp.exp(-0.5 * u * u) * (1.0 / np.sqrt(2.0 * np.pi))
-            hid_ref[ch, :] = (u * cdf).astype(BF16)
-            d = (dh_ref[ch, :] * (cdf + u * pdf)).astype(BF16)
-            dpre_ref[ch, :] = d
-            d = d.astype(F32)
-            return c + (d[0:8] + d[8:16])
-
-        total = lax.fori_loop(0, (hi - lo) // 16, step, jnp.zeros((8, pre_ref.shape[1]), F32))
-        gub_ref[e : e + 1, :] = jnp.sum(total, axis=0, keepdims=True)
-        hid = hid_ref[at, :]
-        dpre = dpre_ref[at, :]
-        mix_ref[at, :] += dot_nn(hid, down_ref[e])
-        ds_ref[at, :] += dot_nt(dpre, up_ref[e])
-        gdown_ref[e] = dot_tn(hid, g).astype(BF16)
-        gup_ref[e] = dot_tn(second, dpre).astype(BF16)
+    second = second_ref[...]
+    g = g_ref[own, :]
+    pre_ref[...] = dot_nn(second, up_ref[0]) + ub_ref[expert : expert + 1, :]
+    dh_ref[...] = dot_nt(g, down_ref[0])
+
+    def gelu_step(i, c):
+        u = pre_ref[here(i), :]
+        cdf = 0.5 * (1.0 + lax.erf(u * (2.0**-0.5)))
+        pdf = jnp.exp(-0.5 * u * u) * (1.0 / np.sqrt(2.0 * np.pi))
+        hid_ref[here(i), :] = (u * cdf).astype(BF16)
+        d = (dh_ref[here(i), :] * (cdf + u * pdf)).astype(BF16)
+        dpre_ref[here(i), :] = d
+        d = d.astype(F32)
+        return c + (d[0:8] + d[8:16])
+
+    total = lax.fori_loop(0, steps16, gelu_step, jnp.zeros((8, pre_ref.shape[1]), F32))
+    gub_ref[...] = jnp.sum(total, axis=0, keepdims=True)
+    hid = hid_ref[...]
+    dpre = dpre_ref[...]
+    mix_ref[...] += dot_nn(hid, down_ref[0])
+    ds_ref[...] += dot_nt(dpre, up_ref[0])
+    gdown_ref[...] = dot_tn(hid, g).astype(BF16)
+    gup_ref[...] = dot_tn(second, dpre).astype(BF16)
 
     @pl.when(j == pl.num_programs(0) - 1)
     def _():
+        out_at = there if lo else here
+
         def step(i, c):
-            at = pl.ds(pl.multiple_of(i * 16, 16), 16)
-            mixed_ref[at, :] = mix_ref[at, :].astype(BF16)
-            center, r = norm_stats(mid_ref[at, :])
+            mixed_ref[out_at(i), :] = mix_ref[here(i), :].astype(BF16)
+            center, r = norm_stats(mid_ref[here(i), :])
             n = center * r
-            u = ds_ref[at, :]
+            u = ds_ref[here(i), :]
             un = u * n
             w = u * gain_ref[...]
             m1 = jnp.mean(w, axis=-1, keepdims=True)
             m2 = jnp.mean(w * n, axis=-1, keepdims=True)
-            d = (g_ref[at, :].astype(F32) + r * (w - m1 - n * m2)).astype(BF16)
-            dmid_ref[at, :] = d
+            g16 = g_ref[there(i), :].astype(F32)
+            d = (g16 + r * (w - m1 - n * m2)).astype(BF16)
+            dmid_ref[out_at(i), :] = d
             d = d.astype(F32)
             return (
                 c[0] + un[0:8] + un[8:16],
                 c[1] + u[0:8] + u[8:16],
                 c[2] + d[0:8] + d[8:16],
+                c[3] + g16[0:8] + g16[8:16],
             )
 
         zero = jnp.zeros((8, width), F32)
-        total = lax.fori_loop(0, steps16, step, (zero, zero, zero))
-        for i in range(3):
-            sums_ref[i : i + 1, :] = jnp.sum(total[i], axis=0, keepdims=True)
-        d = dmid_ref[...]
-        datt_ref[...] = dot_nt(d, wo_ref[...]).astype(BF16)
-        gwo_ref[...] = dot_tn(att_ref[...], d).astype(BF16)
-
-
-def ffn(bounds, att, x, g, wo, bo, gain, shift, up, ub, down, db):
+        total = lax.fori_loop(0, steps16, step, (zero,) * 4)
+        line = [jnp.sum(t, axis=0, keepdims=True) for t in total]
+        pad = jnp.zeros((8 - 3, width), F32)
+        last = jnp.where(iota((8, 1), 0) == 3 + expert, line[3], 0.0)
+        sums = jnp.concatenate(line[:3] + [pad], axis=0) + last
+        if lo:
+            mixed_ref[:lo, :] = mixed0_ref[...]
+            dmid_ref[:lo, :] = dmid0_ref[...]
+            datt_ref[:lo, :] = datt0_ref[...]
+            sums = sums + sums0_ref[...]
+            gwo_ref[...] = dot_tn(att_ref[...], dmid_ref[...]).astype(BF16)
+            datt_ref[own, :] = dot_nt(dmid_ref[own, :], wo_ref[...]).astype(BF16)
+        else:
+            datt_ref[...] = dot_nt(dmid_ref[...], wo_ref[...]).astype(BF16)
+        sums_ref[...] = sums
+
+
+def ffn(expert, bounds, att, x, g, wo, bo, gain, shift, up, ub, down, db, prev=()):
+    lo, hi = bounds
     rows, width = x.shape
     experts, _, hidden = up.shape
     chunk = width
     steps = hidden // chunk
+    span = hi - lo
+    done = rows if lo else span
     one = pl.Buffered(1)
     full = lambda r, c: pl.BlockSpec((r, c), lambda j: (0, 0), pipeline_mode=one)
-    return pl.pallas_call(
-        functools.partial(ffn_kernel, bounds),
+    out_specs = [full(done, width)] * 3 + [
+        pl.BlockSpec((width, chunk), lambda j: (0, j)),
+        pl.BlockSpec((chunk, width), lambda j: (j, 0)),
+        pl.BlockSpec((1, chunk), lambda j: (0, j)),
+        full(8, width),
+    ]
+    out_shape = [jax.ShapeDtypeStruct((done, width), BF16)] * 3 + [
+        jax.ShapeDtypeStruct((width, hidden), BF16),
+        jax.ShapeDtypeStruct((hidden, width), BF16),
+        jax.ShapeDtypeStruct((1, hidden), F32),
+        jax.ShapeDtypeStruct((8, width), F32),
+    ]
+    if lo:
+        out_specs.append(full(width, width))
+        out_shape.append(jax.ShapeDtypeStruct((width, width), BF16))
+    return pl.pallas_call(
+        functools.partial(ffn_kernel, expert, lo, hi),
         grid=(steps,),
         in_specs=[
             full(rows, width),
@@ -562,63 +590,41 @@
             full(1, width),
             full(1, width),
             full(1, width),
-            pl.BlockSpec((experts, width, chunk), lambda j: (0, 0, j)),
+            pl.BlockSpec((1, width, chunk), lambda j: (expert, 0, j)),
             pl.BlockSpec((experts, chunk), lambda j: (0, j)),
-            pl.BlockSpec((experts, chunk, width), lambda j: (0, j, 0)),
+            pl.BlockSpec((1, chunk, width), lambda j: (expert, j, 0)),
             full(experts, width),
+        ]
+        + [full(*p.shape) for p in prev],
+        out_specs=out_specs,
+        out_shape=tuple(out_shape),
+        scratch_shapes=[
+            VMEM((span, width), F32),
+            VMEM((span, width), BF16),
+            VMEM((span, width), F32),
+            VMEM((span, width), F32),
+            VMEM((span, chunk), F32),
+            VMEM((span, chunk), F32),
+            VMEM((span, chunk), BF16),
+            VMEM((span, chunk), BF16),
         ],
-        out_specs=[
-            full(rows, width),
-            full(rows, width),
-            full(rows, width),
-            pl.BlockSpec((experts, width, chunk), lambda j: (0, 0, j)),
-            pl.BlockSpec((experts, chunk, width), lambda j: (0, j, 0)),
-            full(width, width),
-            pl.BlockSpec((experts, chunk), lambda j: (0, j)),
-            full(8, width),
-        ],
-        out_shape=(
-            jax.ShapeDtypeStruct((rows, width), BF16),
-            jax.ShapeDtypeStruct((rows, width), BF16),
-            jax.ShapeDtypeStruct((rows, width), BF16),
-            jax.ShapeDtypeStruct(up.shape, BF16),
-            jax.ShapeDtypeStruct(down.shape, BF16),
-            jax.ShapeDtypeStruct((width, width), BF16),
-            jax.ShapeDtypeStruct((experts, hidden), F32),
-            jax.ShapeDtypeStruct((8, width), F32),
-        ),
-        scratch_shapes=[
-            VMEM((rows, width), F32),
-            VMEM((rows, width), BF16),
-            VMEM((rows, width), F32),
-            VMEM((rows, width), F32),
-            VMEM((rows, chunk), F32),
-            VMEM((rows, chunk), F32),
-            VMEM((rows, chunk), BF16),
-            VMEM((rows, chunk), BF16),
-        ],
-        compiler_params=params(67043328),
-        name="ffn",
-    )(att, x, g, wo, bo, gain, shift, up, ub, down, db)
+        compiler_params=params(BIG),
+        cost_estimate=cost(12 * span * width * hidden),
+        name=f"ffn{expert}",
+    )(att, x, g, wo, bo, gain, shift, up, ub, down, db, *prev)
 
 
 def last_kernel(
-    x_ref, first_ref, dq_ref, dk_ref, dv_ref, w_ref, gain_ref, dmid_ref, col_ref,
-    back_ref, gin_ref, gw_ref, sums_ref, df_ref,
+    x_ref, dq_ref, dk_ref, dv_ref, w_ref, gain_ref, dmid_ref, col_ref,
+    back_ref, gin_ref, sums_ref, df_ref,
 ):
     rows, width = x_ref.shape
-    first = first_ref[...]
     for j, d_ref in enumerate((dq_ref, dk_ref, dv_ref)):
-        part = slice(j * width, (j + 1) * width)
-        d = d_ref[...]
-        gw_ref[:, part] = dot_tn(first, d).astype(BF16)
-        term = dot_nt(d, w_ref[:, part])
+        term = dot_nt(d_ref[...], w_ref[:, j * width : (j + 1) * width])
         if j == 0:
             df_ref[...] = term
         else:
             df_ref[...] += term
-    for j, d_ref in ((2, dq_ref), (3, dv_ref)):
-        sums_ref[j : j + 1, :] = jnp.sum(d_ref[...].astype(F32), axis=0, keepdims=True)
 
     def step(i, c):
         at = pl.ds(pl.multiple_of(i * 16, 16), 16)
@@ -630,13 +636,42 @@
         m1 = jnp.mean(w, axis=-1, keepdims=True)
         m2 = jnp.mean(w * n, axis=-1, keepdims=True)
         gin_ref[at, :] = (dmid_ref[at, :].astype(F32) + r * (w - m1 - n * m2)).astype(BF16)
-        return (c[0] + un[0:8] + un[8:16], c[1] + u[0:8] + u[8:16])
+        q = dq_ref[at, :].astype(F32)
+        v = dv_ref[at, :].astype(F32)
+        return (
+            c[0] + un[0:8] + un[8:16],
+            c[1] + u[0:8] + u[8:16],
+            c[2] + q[0:8] + q[8:16],
+            c[3] + v[0:8] + v[8:16],
+        )
 
     zero = jnp.zeros((8, width), F32)
-    total = lax.fori_loop(0, rows // 16, step, (zero, zero))
-    for i in range(2):
+    total = lax.fori_loop(0, rows // 16, step, (zero,) * 4)
+    for i in range(4):
         sums_ref[i : i + 1, :] = jnp.sum(total[i], axis=0, keepdims=True)
     back_ref[...] = give_back(col_ref, gin_ref)
+
+
+def wgrad_kernel(first_ref, dq_ref, dk_ref, dv_ref, gwa_ref, gwb_ref):
+    width = first_ref.shape[1]
+    half = width // 2
+    first = first_ref[...]
+    gwa_ref[:, :width] = dot_tn(first, dq_ref[...]).astype(BF16)
+    gw = dot_tn(first, dk_ref[...]).astype(BF16)
+    gwa_ref[:, width:] = gw[:, :half]
+    gwb_ref[:, :half] = gw[:, half:]
+    gwb_ref[:, half:] = dot_tn(first, dv_ref[...]).astype(BF16)
+
+
+def wgrad(first, dq, dk, dv):
+    rows, width = first.shape
+    return pl.pallas_call(
+        wgrad_kernel,
+        out_shape=(jax.ShapeDtypeStruct((width, width + width // 2), BF16),) * 2,
+        compiler_params=params(BIG),
+        cost_estimate=cost(6 * rows * width * width),
+        name="wgrad",
+    )(first, dq, dk, dv)
 
 
 def give_back(col_ref, value_ref):
@@ -645,20 +680,20 @@
     return dot_nn(pick.astype(BF16), value_ref[...]).astype(BF16)
 
 
-def last(x, first, dq, dk, dv, w, gain, dmid, col):
+def last(x, dq, dk, dv, w, gain, dmid, col):
     rows, width = x.shape
     return pl.pallas_call(
         last_kernel,
         out_shape=(
             jax.ShapeDtypeStruct((col.shape[0], width), BF16),
             jax.ShapeDtypeStruct((rows, width), BF16),
-            jax.ShapeDtypeStruct(w.shape, BF16),
             jax.ShapeDtypeStruct((8, width), F32),
         ),
         scratch_shapes=[VMEM((rows, width), F32)],
         compiler_params=params(BIG),
+        cost_estimate=cost(2 * rows * width * w.shape[1]),
         name="last",
-    )(x, first, dq, dk, dv, w, gain, dmid, col)
+    )(x, dq, dk, dv, w, gain, dmid, col)
 
 
 def back_kernel(col_ref, value_ref, out_ref):
@@ -672,6 +707,76 @@
         compiler_params=params(BIG),
         name="back",
     )(col, value)
+
+
+def bits_of(axis):
+    return [(axis, b) for b in reversed(range(lax.axis_size(axis).bit_length() - 1))]
+
+
+def pair_bit(axis, bit):
+    return (lax.axis_index(axis) >> bit) & 1
+
+
+def pass_on(value, axis, bit):
+    n = lax.axis_size(axis)
+    return lax.ppermute(value, axis, [(i, i ^ (1 << bit)) for i in range(n)])
+
+
+tie = lax.optimization_barrier
+
+
+class Shards:
+    def __init__(self, value, left):
+        self.value, self.left = value, list(left)
+
+    def cut(self, key):
+        above = 1 << self.left.index(key)
+        rows, cols = self.value.shape
+        parts = self.value.reshape(above, 2, rows // (2 * above), cols)
+        own = pair_bit(*key)
+        take = lambda k: lax.dynamic_index_in_dim(parts, k, 1, keepdims=False)
+        self.left.remove(key)
+        self.value = take(own)
+        return take(1 - own)
+
+    def add(self, got):
+        total = self.value + got
+        self.value = total.reshape(-1, total.shape[-1])
+
+
+class Joined(Shards):
+    def __init__(self, first, second):
+        self.pair, self.left = (first.value, second.value), list(first.left)
+
+    def cut(self, key):
+        if key in self.left:
+            return super().cut(key)
+        own = pair_bit(*key) == 0
+        self.value = jnp.where(own, *self.pair)
+        return jnp.where(own, *self.pair[::-1])
+
+
+class Whole:
+    def __init__(self, value):
+        self.value = value
+
+    def cut(self, key):
+        return self.value
+
+    def add(self, got):
+        self.value = self.value + got
+
+
+def launch(moves, *tied):
+    outs, tied = tie(([s.cut(key) for s, key in moves], tied))
+    return [(s, pass_on(o, *key)) for (s, key), o in zip(moves, outs)], tied
+
+
+def settle(flights, *tied):
+    gots, tied = tie(([g for _, g in flights], tied))
+    for (s, _), g in zip(flights, gots):
+        s.add(g)
+    return tied
 
 
 def body(
@@ -702,69 +807,140 @@
     bounds = ((0, per * IMG), (per * IMG, rows))
     row = lambda v: v.reshape(1, width)
 
-    send_t, send_g, slot_col = pack(ways, per, group_ids, segment_ids, tokens, grad_out)
+    labels = (group_ids, segment_ids)
+    send_t, places, slot_col = pack(ways, per, group_ids, segment_ids, tokens)
     recv_t = swap(send_t).reshape(ways * SLOTS, width)
+    send_g = pack_more(ways, places, grad_out)
+    pos_row, pos_col, flag = index(ways, per, recv_t)
+    over = flag[0, 0] > 0.5
+    enter = lambda value, recv: lax.cond(
+        over,
+        lambda v, r, p: slow_in(v, *labels, ways, per),
+        lambda v, r, p: place(rows, p, r),
+        value,
+        recv,
+        pos_row,
+    )
+    x = enter(tokens, recv_t)
+    x, send_g = tie((x, send_g))
     recv_g = swap(send_g).reshape(ways * SLOTS, width)
-    x_fast, pos_row, pos_col, flag = unpack(ways, per, rows, recv_t)
-    over = flag[0, 0] > 0.5
-    labels = (group_ids, segment_ids)
-    x = lax.cond(over, lambda f, v: slow_in(v, *labels, ways, per), lambda f, v: f, x_fast, tokens)
     first, qkv = qkv_call(
         x, row(ln1_gain), row(ln1_bias), qkv_weight, row(q_bias), row(v_bias)
     )
     att, lse = attn_fwd(per, qkv)
-    g_fast = place(rows, pos_row, recv_g)
-    g = lax.cond(over, lambda f, v: slow_in(v, *labels, ways, per), lambda f, v: f, g_fast, grad_out)
-    mixed_s, dmid, d_att, g_up, g_down, g_wo, g_ub, sums2 = ffn(
-        bounds, att, x, g, out_weight, row(out_bias), row(ln2_gain), row(ln2_bias),
+    att, recv_g = tie((att, recv_g))
+    g = enter(grad_out, recv_g)
+    weights = (
+        out_weight, row(out_bias), row(ln2_gain), row(ln2_bias),
         up_weight, up_bias, down_weight, down_bias,
     )
-    ret_m = swap(back(pos_col, mixed_s).reshape(ways, SLOTS, width)).reshape(-1, width)
-    dq, dk, dv = attn_bwd(per, qkv, d_att, lse)
-    back_g, gin_s, g_w, sums1 = last(
-        x, first, dq, dk, dv, qkv_weight, row(ln1_gain), dmid, pos_col
-    )
-    ret_g = swap(back_g.reshape(ways, SLOTS, width)).reshape(-1, width)
-    out = lambda s, f: lax.cond(
-        over, lambda f_, s_: slow_out(s_, *labels, ways, per), lambda f_, s_: f_, f, s
-    )
-    mixed = out(mixed_s, choose(slot_col, ret_m))
-    grad_in = out(gin_s, choose(slot_col, ret_g))
-
-    axes = ("dp", "seq")
-    scat = lambda v, dim: lax.psum_scatter(v, axes, scatter_dimension=dim, tiled=True).astype(F32)
-    grad_up = scat(g_up, 1)
-    grad_down = scat(g_down.reshape(-1, width), 0)
-    grad_wo = scat(g_wo, 0)
-    grad_w = scat(g_w, 0)
+    dp_bits, seq_bits = bits_of("dp"), bits_of("seq")
+    every = dp_bits + seq_bits
+    core, mids, top = dp_bits[-1], dp_bits[1:-1][::-1], dp_bits[0]
+    z0, z1 = seq_bits[::-1]
+    low_first = mids + [top]
+    high_first = [top] + mids
+
+    mixed0, dmid0, datt0, g_up0, g_down0, g_ub0, sums0 = ffn(0, bounds[0], att, x, g, *weights)
+    up0, down0 = Shards(g_up0, every), Shards(g_down0, every[1:])
+    air1, (prev,) = launch(
+        [(up0, core), (down0, core)], (mixed0, dmid0, datt0, sums0)
+    )
+    mixed_s, dmid, d_att, g_up1, g_down1, g_ub1, sums2, g_wo = ffn(
+        1, bounds[1], att, x, g, *weights, prev=prev
+    )
+    d_att, mixed_s, g_up1, g_down1, g_wo = settle(air1, d_att, mixed_s, g_up1, g_down1, g_wo)
+    up1, down1, wo = Shards(g_up1, every), Shards(g_down1, every[1:]), Shards(g_wo, every)
+    back_m = back(pos_col, mixed_s)
+    air2, (d_att, back_m) = launch(
+        [(up0, high_first[0]), (down0, low_first[0]), (up1, core), (down1, core), (wo, core)],
+        d_att,
+        back_m,
+    )
+    ret_m = swap(back_m.reshape(ways, SLOTS, width))
+    d_qkv = attn_bwd(per, qkv, d_att, lse)
+    (d_qkv,) = settle(air2, d_qkv)
+    for key in mids[1:]:
+        air, (d_qkv,) = launch([(down0, key)], d_qkv)
+        (d_qkv,) = settle(air, d_qkv)
+    air3, (d_qkv,) = launch(
+        [(up0, high_first[1]), (up1, high_first[0]), (down1, low_first[0]), (wo, low_first[0])],
+        d_qkv,
+    )
+    back_g, gin_s, sums1 = last(x, *d_qkv, qkv_weight, row(ln1_gain), dmid, pos_col)
+    back_g, d_qkv, sums1, ret_m = settle(air3, back_g, d_qkv, sums1, ret_m)
+    for key in mids[1:]:
+        air, (d_qkv,) = launch([(down1, key), (up0, key)], d_qkv)
+        (d_qkv,) = settle(air, d_qkv)
+    down = Joined(down0, down1)
+    vec = Whole(
+        jnp.concatenate(
+            [sums1[0:4], sums2[0:5], g_ub0.reshape(-1, width), g_ub1.reshape(-1, width)], axis=0
+        )
+    )
+    air4, (d_qkv, back_g) = launch(
+        [(up0, z0), (up1, high_first[1]), (down, top), (wo, low_first[1]), (vec, core)],
+        d_qkv,
+        back_g,
+    )
+    ret_g = swap(back_g.reshape(ways, SLOTS, width))
+    g_wa, g_wb = wgrad(first, *d_qkv)
+    g_wa, g_wb = settle(air4, g_wa, g_wb)
+    wa, wb = Shards(g_wa, every), Shards(g_wb, every)
+    for key in mids[1:]:
+        air, () = launch([(up1, key), (wo, low_first[low_first.index(key) + 1])])
+        settle(air)
+    air5, () = launch(
+        [(wa, core), (wb, core), (up0, z1), (up1, z0), (down, z0), (wo, z0), (vec, low_first[0])]
+    )
+    (ret_g,) = settle(air5, ret_g)
+    air6, () = launch(
+        [(wa, low_first[0]), (wb, high_first[0]), (up1, z1), (down, z1), (wo, z1)]
+        + [(vec, low_first[1])]
+    )
+    settle(air6)
+    air7, () = launch([(wa, low_first[1]), (wb, high_first[1]), (vec, z0)])
+    settle(air7)
+    for lo_key, hi_key in zip(low_first[2:], high_first[2:]):
+        air, () = launch([(wa, lo_key), (wb, hi_key), (vec, lo_key)])
+        settle(air)
+    air8, () = launch([(wa, z0), (wb, z0), (vec, z1)])
+    settle(air8)
+    air9, () = launch([(wa, z1), (wb, z1)])
+    mixed_s, gin_s, ret_m, ret_g = settle(air9, mixed_s, gin_s, ret_m, ret_g)
+    flat2 = lambda r: r.reshape(-1, width)
+    mixed, grad_in = lax.cond(
+        over,
+        lambda m, i, rm, rg, c: tuple(slow_out(v, *labels, ways, per) for v in (m, i)),
+        lambda m, i, rm, rg, c: (choose(c, flat2(rm)), choose(c, flat2(rg))),
+        mixed_s,
+        gin_s,
+        ret_m,
+        ret_g,
+        slot_col,
+    )
+
     piece = width // world
-    vec = jnp.concatenate(
-        [
-            jnp.stack([sums1[0], sums1[1], sums1[2], sums1[3], sums2[2], sums2[0], sums2[1]])
-            .reshape(7, world, piece)
-            .transpose(1, 0, 2),
-            sums2[3:5].reshape(2, world, piece).transpose(1, 0, 2),
-            g_ub.reshape(world, -1, piece),
-        ],
-        axis=1,
-    )
-    vec = jnp.sum(lax.all_to_all(vec, axes, split_axis=0, concat_axis=0, tiled=True), axis=0)
+    me = lax.axis_index("dp") * ways + lax.axis_index("seq")
+    mine = lax.dynamic_slice_in_dim(vec.value[:9], me * piece, piece, 1)
+    flat = vec.value[9:].reshape(-1)
+    ub_piece = flat.shape[0] // world
     return (
         mixed,
         grad_in,
-        vec[0],
-        vec[1],
-        grad_w,
-        vec[2],
-        vec[3],
-        grad_wo,
-        vec[4],
-        vec[5],
-        vec[6],
-        grad_up,
-        vec[9:].reshape(-1),
-        grad_down,
-        vec[7:9],
+        mine[0],
+        mine[1],
+        jnp.concatenate([wa.value, wb.value], axis=1).astype(F32),
+        mine[2],
+        mine[3],
+        wo.value.astype(F32),
+        mine[6],
+        mine[4],
+        mine[5],
+        jnp.stack([up0.value, up1.value]).astype(F32),
+        lax.dynamic_slice_in_dim(flat, me * ub_piece, ub_piece, 0),
+        down.value.astype(F32),
+        mine[7:9],
     )
 
 

time: 739 us -> 496 us (0.67)
  waiting for transfers between devices: 416 us -> 120 us
  other arithmetic: 7.46 us -> 41.5 us
  starting transfers between devices: 18.2 us -> 51 us
  blocking collectives: 13.4 us -> 0 us
  between operations: 15 us -> 2.52 us
  Pallas kernels: 205 us -> 214 us
    reduce_scatter x3 -> x0, waiting for transfers between devices: 157 us -> none  [body(): lax.psum_scatter(v, axes, scatter_dimension=dim, tiled=True).astype(F32)]
    unnamed x5 -> x0, waiting for transfers between devices: 140 us -> none
    ppermute x0 -> x37, waiting for transfers between devices: none -> 83.1 us  [pass_on(): return lax.ppermute(value, axis, [(i, i ^ 1 << bit) for i in range(n)])]
    all_to_all x4, waiting for transfers between devices: 119 us -> 37.1 us  [swap(): lax.all_to_all(blocks, 'seq', split_axis=0, concat_axis=0, tiled=True)]
    ppermute x0 -> x37, starting transfers between devices: none -> 31.2 us  [pass_on(): return lax.ppermute(value, axis, [(i, i ^ 1 << bit) for i in range(n)])]
    add x0 -> x31, other arithmetic: none -> 30.2 us  [the longest x26 29.2 us: add(): total = self.value + got]
    unnamed x55 -> x136, local copies, waits for them, and re-layouts: 36.7 us -> 11.6 us
    squeeze x1 -> x31, local copies, waits for them, and re-layouts: 0.54 us -> 23.1 us  [the longest x30 22.5 us: cut(): take = lambda k: lax.dynamic_index_in_dim(parts, k, 1, keepdims=False)]
  transfers between devices with their start and end apart: 8 -> 41, of which waited for: 6 -> 13; matrix products, arithmetic and copies ran while one was open for 6% -> 8% of each run, Pallas kernels for 15% -> 31%
where the time goes in v2:
time: 496 us; the launch traced here: 489 us
  Pallas kernels  214 us (43%)
  waiting for transfers between devices  120 us (24%)
  starting transfers between devices  51 us (10%)
  local copies, waits for them, and re-layouts  47.2 us (10%)
  other arithmetic  41.5 us (8%)
  loops' own time  12.4 us (2%)
    ppermute x37, waiting for transfers between devices, pass_on(): return lax.ppermute(value, axis, [(i, i ^ 1 << bit) for i in range(n)])  83.1 us
    pallas_call x2, Pallas kernels, ffn(): pl.pallas_call(functools.partial(ffn_kernel, expert, lo, hi), grid=(steps...  82.9 us
    all_to_all x4, waiting for transfers between devices, swap(): lax.all_to_all(blocks, 'seq', split_axis=0, concat_axis=0, tiled=True)  37.1 us
    ppermute x37, starting transfers between devices, pass_on(): return lax.ppermute(value, axis, [(i, i ^ 1 << bit) for i in range(n)])  31.2 us
    add x26, other arithmetic, add(): total = self.value + got  29.2 us
    pallas_call x1, Pallas kernels, last(): pl.pallas_call(last_kernel, out_shape=(jax.ShapeDtypeStruct((col.shape[0]...  28.5 us
    pallas_call x1, Pallas kernels, attn_bwd(): pl.pallas_call(functools.partial(attn_bwd_kernel, per), grid=(steps,), in...  26.9 us
    squeeze x30, local copies, waits for them, and re-layouts, cut(): take = lambda k: lax.dynamic_index_in_dim(parts, k, 1, keepdims=False)  22.5 us
  transfers between devices with their start and end apart: 41, of which 13 were waited for; matrix products, arithmetic and copies ran while one was open for 8% of the time, Pallas kernels for 31%

profile of v2, /device:TPU:0, one launch (start us, length us, event | category | flops | bytes accessed | tf_op | source)
XLA Modules:
  0.0 488.9 jit_solution(9159734341180461864)
XLA Ops:
  0.6 5.8 %pack.1 = (bf16[4,288,768]{2,1,0:T(8,128)(2,1)}, s32[8,906]{1,0:T(8,128)}, s32[906,1]{1,0:T(8,128)}) custom-call(s32[1,906]{1,0:T(1,128)} %bitcast.195, s32[1,906]{1,0:T(1,128)} %bitcast.196, bf16[906,768]{1,0:T(8,128)(2,1)} %tok_ref.1), custom_call_target="tpu_custom_call" | custom-call | tf_op jit(solution)/shard_map/pack/pallas_call | solution.py:87
  6.4 6.5 %all-to-all-start.7 = ((bf16[4,288,768]{2,1,0:T(8,128)(2,1)}), bf16[4,288,768]{2,1,0:T(8,128)(2,1)S(1)}, u32[]{:S(2)}, u32[]{:S(2)}) async-start(bf16[4,288,768]{2,1,0:T(8,128)(2,1)} %get-tuple-element.244), calls=%async_computation.7 | async-start | bytes 3538944 | tf_op jit(solution)/shard_map/all_to_all | solution.py:193
  12.9 4.0 pack_more.1
  16.9 37.1 %all-to-all-done.7 = bf16[4,288,768]{2,1,0:T(8,128)(2,1)S(1)} async-done(((bf16[4,288,768]{2,1,0:T(8,128)(2,1)}), bf16[4,288,768]{2,1,0:T(8,128)(2,1)S(1)}, u32[]{:S(2)}, u32[]{:S(2)}) %all-to-all-start.7) | async-done | bytes 1769504 | tf_op jit(solution)/shard_map/all_to_all | solution.py:193
  57.3 6.7 %conditional.3 = (bf16[928,768]{1,0:T(8,128)(2,1)S(1)}) conditional(s32[]{:T(128)} %bitcast.7, (s32[8,1152]{1,0:T(8,128)S(1)}, bf16[1152,768]{1,0:T(8,128)(2,1)S(1)}) %tuple.100, (s32[906]{0:T(1024)S(1)}, pred[906]{0:T(1024)(128)(4,1)S(1)}, bf16[906,768]{1,0:T(8,128)(2,1)S(1)}, s32[906]{0:T(1024)S(1)}, s32[906]{0:T(1024)S(1)}) %tuple.109), branch_computations={%region_0.0_spmd, %region_1.5_spmd} | conditional | flops 754822 | bytes 42073716 | solution.py:816
  57.3 2.0 place.2
  64.1 3.7 all-to-all-start.8
  72.0 17.3 %qkv.1 = (bf16[928,768]{1,0:T(8,128)(2,1)}, bf16[928,2304]{1,0:T(8,128)(2,1)}) custom-call(bf16[928,768]{1,0:T(8,128)(2,1)S(1)} %get-tuple-element.413.x_ref.refs_1_, f32[1,768]{1,0:T(1,128)} %reshape.236.gain_ref, f32[1,768]{1,0:T(1,128)} %reshape.237.shift_ref, bf16[768,2304]{1,0:T(8,128)(2,1)} %w_ref.3, f32[1,768]{1,0:T(1,128)} %reshape.238.qb_ref, ...), custom_call_target="tpu_custom_call" | custom-call | flops 9852420096 | bytes 1048576 | tf_op jit(solution)/shard_map/qkv/pallas_call | solution.py:261
  89.2 20.4 %attn_fwd.1 = (bf16[928,768]{1,0:T(8,128)(2,1)}, f32[6,8,1024]{2,1,0:T(8,128)}) custom-call(bf16[928,2304]{1,0:T(8,128)(2,1)} %get-tuple-element.249.q_ref.k_ref.v_ref, bf16[928,2304]{1,0:T(8,128)(2,1)} %get-tuple-element.249.q_ref.k_ref.v_ref, bf16[928,2304]{1,0:T(8,128)(2,1)} %get-tuple-element.249.q_ref.k_ref.v_ref), custom_call_target="tpu_custom_call" | custom-call | flops 11494490112 | bytes 1048576 | tf_op jit(solution)/shard_map/attn_fwd/pallas_call | solution.py:353
  109.7 10.9 %conditional.4 = (bf16[928,768]{1,0:T(8,128)(2,1)}) conditional(s32[]{:T(128)} %bitcast.7, (s32[8,1152]{1,0:T(8,128)S(1)}, bf16[1152,768]{1,0:T(8,128)(2,1)S(1)}) %tuple.101, (s32[906]{0:T(1024)S(1)}, pred[906]{0:T(1024)(128)(4,1)S(1)}, bf16[906,768]{1,0:T(8,128)(2,1)}, s32[906]{0:T(1024)S(1)}, s32[906]{0:T(1024)S(1)}) %tuple.110), branch_computations={%region_4.6_spmd, %region_5.0_spmd} | conditional | flops 754822 | bytes 42073716 | solution.py:816
  109.7 3.1 place.3
  120.6 36.9 %ffn0.1 = (bf16[416,768]{1,0:T(8,128)(2,1)}, bf16[416,768]{1,0:T(8,128)(2,1)}, bf16[416,768]{1,0:T(8,128)(2,1)}, bf16[768,3072]{1,0:T(8,128)(2,1)}, bf16[3072,76...) custom-call(bf16[928,768]{1,0:T(8,128)(2,1)} %get-tuple-element.252.refs_0_, ...), custom_call_target="tpu_custom_call" | custom-call | flops 35332816896 | bytes 1048576 | tf_op jit(solution)/shard_map/ffn0/pallas_call | solution.py:582
  157.5 3.4 dynamic-slice_bitcast_fusion.3
  160.8 1.6 dynamic-slice_bitcast_fusion.2
  162.9 46.0 %ffn1.1 = (bf16[928,768]{1,0:T(8,128)(2,1)}, bf16[928,768]{1,0:T(8,128)(2,1)}, bf16[928,768]{1,0:T(8,128)(2,1)}, bf16[768,3072]{1,0:T(8,128)(2,1)}, bf16[3072,76...) custom-call(bf16[928,768]{1,0:T(8,128)(2,1)} %get-tuple-element.252.refs_0_, ...), custom_call_target="tpu_custom_call" | custom-call | flops 43486543872 | bytes 1048576 | tf_op jit(solution)/shard_map/ffn1/pallas_call | solution.py:582
  208.9 1.9 bitcast_add_fusion.3
  210.9 3.5 bitcast_add_fusion.2
  215.5 1.6 dynamic-slice_bitcast_fusion.1
  217.1 1.6 copy-done.10
  223.4 4.9 %back.1 = bf16[1152,768]{1,0:T(8,128)(2,1)} custom-call(s32[1152,1]{1,0:T(8,128)} %get-tuple-element.277.col_ref, bf16[928,768]{1,0:T(8,128)(2,1)} %get-tuple-element.380.value_ref), custom_call_target="tpu_custom_call" | custom-call | tf_op jit(solution)/shard_map/back/pallas_call | solution.py:704
  231.8 5.0 %all-to-all-start.9 = ((bf16[4,288,768]{2,1,0:T(8,128)(2,1)}), bf16[4,288,768]{2,1,0:T(8,128)(2,1)}, u32[]{:S(2)}, u32[]{:S(2)}) async-start(bf16[4,288,768]{2,1,0:T(8,128)(2,1)} %bitcast.153), calls=%async_computation.9 | async-start | bytes 3538944 | tf_op jit(solution)/shard_map/all_to_all | solution.py:193
  236.9 26.9 %attn_bwd.1 = (bf16[928,768]{1,0:T(8,128)(2,1)}, bf16[928,768]{1,0:T(8,128)(2,1)}, bf16[928,768]{1,0:T(8,128)(2,1)}) custom-call(bf16[928,2304]{1,0:T(8,128)(2,1)} %get-tuple-element.249.q_ref.k_ref.v_ref, bf16[928,2304]{1,0:T(8,128)(2,1)} %get-tuple-element.249.q_ref.k_ref.v_ref, bf16[928,2304]{1,0:T(8,128)(2,1)} %get-tuple-element.249.q_ref.k_ref.v_ref, ...), custom_call_target="tpu_custom_call" | custom-call | flops 14778630144 | bytes 1048576 | tf_op jit(solution)/shard_map/attn_bwd/pallas_call | solution.py:433
  263.9 3.0 bitcast_add_fusion
  275.2 2.6 bitcast_add_fusion.1
  283.9 2.0 reduce.10
  289.2 28.5 %last.1 = (bf16[1152,768]{1,0:T(8,128)(2,1)}, bf16[928,768]{1,0:T(8,128)(2,1)}, f32[8,768]{1,0:T(8,128)}) custom-call(bf16[928,768]{1,0:T(8,128)(2,1)} %copy-done.28, bf16[928,768]{1,0:T(8,128)(2,1)} %get-tuple-element.326.dq_ref, bf16[928,768]{1,0:T(8,128)(2,1)} %get-tuple-element.327.dk_ref, bf16[928,768]{1,0:T(8,128)(2,1)} %get-tuple-element.328.dv_ref, ...), custom_call_target="tpu_custom_call" | custom-call | flops 9852420096 | bytes 1048576 | tf_op jit(solution)/shard_map/last/pallas_call | solution.py:685
  317.7 10.2 %collective-permute-done.10 = bf16[2,96,768]{2,1,0:T(8,128)(2,1)} collective-permute-done((bf16[2,96,768]{2,1,0:T(8,128)(2,1)}, bf16[2,96,768]{2,1,0:T(8,128)(2,1)}, u32[]{:S(2)}, u32[]{:S(2)}) %collective-permute-start.10) | collective-permute-done | bytes 294944 | tf_op jit(solution)/shard_map/ppermute | solution.py:722
  329.0 1.9 bitcast_add_fusion.5
  340.5 1.7 collective-permute-start.11
  343.3 4.5 all-to-all-start.10
  347.8 7.8 %wgrad.1 = (bf16[768,1152]{1,0:T(8,128)(2,1)}, bf16[768,1152]{1,0:T(8,128)(2,1)}) custom-call(bf16[928,768]{1,0:T(8,128)(2,1)} %get-tuple-element.325.first_ref, bf16[928,768]{1,0:T(8,128)(2,1)} %get-tuple-element.326.dq_ref, bf16[928,768]{1,0:T(8,128)(2,1)} %get-tuple-element.327.dk_ref, bf16[928,768]{1,0:T(8,128)(2,1)} %get-tuple-element.328.dv_ref), custom_call_target="tpu_custom_call" | custom-call | flops 9852420096 | bytes 1048576 | tf_op jit(solution)/shard_map/wgrad/pallas_call | solution.py:668
  355.6 13.8 %collective-permute-done.14 = bf16[1,96,768]{2,1,0:T(8,128)(2,1)} collective-permute-done((bf16[1,96,768]{2,1,0:T(8,128)(2,1)}, bf16[1,96,768]{2,1,0:T(8,128)(2,1)}, u32[]{:S(2)}, u32[]{:S(2)}) %collective-permute-start.14) | collective-permute-done | bytes 147488 | tf_op jit(solution)/shard_map/ppermute | solution.py:722
  369.5 2.8 bitcast_add_fusion.4
  380.9 3.8 collective-permute-done.22
  386.2 23.9 %collective-permute-done.21 = bf16[2,24,768]{2,1,0:T(8,128)(2,1)} collective-permute-done((bf16[2,24,768]{2,1,0:T(8,128)(2,1)S(1)}, bf16[2,24,768]{2,1,0:T(8,128)(2,1)}, u32[]{:S(2)}, u32[]{:S(2)}) %collective-permute-start.21) | collective-permute-done | bytes 73760 | tf_op jit(solution)/shard_map/ppermute | solution.py:722
  410.1 9.1 %collective-permute-done.18 = bf16[1,24,3072]{2,1,0:T(8,128)(2,1)S(1)} collective-permute-done((bf16[1,24,3072]{2,1,0:T(8,128)(2,1)S(1)}, bf16[1,24,3072]{2,1,0:T(8,128)(2,1)S(1)}, u32[]{:S(2)}, u32[]{:S(2)}) %collective-permute-start.18) | collective-permute-done | bytes 147488 | tf_op jit(solution)/shard_map/ppermute | solution.py:722
  429.4 2.8 collective-permute-start.25
  432.6 1.9 collective-permute-start.28
  435.5 6.0 %collective-permute-done.28 = f32[17,768]{1,0:T(8,128)S(1)} collective-permute-done((f32[17,768]{1,0:T(8,128)S(1)}, f32[17,768]{1,0:T(8,128)S(1)}, u32[]{:S(2)}, u32[]{:S(2)}) %collective-permute-start.28) | collective-permute-done | bytes 52256 | tf_op jit(solution)/shard_map/ppermute | solution.py:722
  441.5 4.7 collective-permute-done.25
  446.2 5.4 %collective-permute-done.26 = bf16[1,192,768]{2,1,0:T(8,128)(2,1)S(1)} collective-permute-done((bf16[1,192,768]{2,1,0:T(8,128)(2,1)}, bf16[1,192,768]{2,1,0:T(8,128)(2,1)S(1)}, u32[]{:S(2)}, u32[]{:S(2)}) %collective-permute-start.26) | collective-permute-done | bytes 294944 | tf_op jit(solution)/shard_map/ppermute | solution.py:722
  455.7 2.6 collective-permute-done.31
  459.1 2.0 collective-permute-start.33
  463.7 2.7 collective-permute-done.34
  468.9 1.7 collective-permute-start.36
  478.8 9.2 %conditional.5 = (bf16[906,768]{1,0:T(8,128)(2,1)}, bf16[906,768]{1,0:T(8,128)(2,1)}) conditional(s32[]{:T(128)} %bitcast.7, (bf16[4,288,768]{2,1,0:T(8,128)(2,1)}, s32[906,1]{1,0:T(8,128)S(1)}, bf16[4,288,768]{2,1,0:T(8,128)(2,1)}) %tuple.104, (bf16[928,768]{1,0:T(8,128)(2,1)S(1)}, s32[906]{0:T(1024)S(1)}, s32[906]{0:T(1024)S(1)}, ...), branch_computations={%region_8.10_spmd, %region_9.15_spmd} | conditional | flops 1528782 | bytes 54242800 | solution.py:912
  478.9 4.6 choose.2
  483.4 4.6 choose.3
  (278 shorter events, 86.0 us)
Async XLA Ops:
  6.4 47.7 %all-to-all-start.7 = ((bf16[4,288,768]{2,1,0:T(8,128)(2,1)}), bf16[4,288,768]{2,1,0:T(8,128)(2,1)S(1)}, u32[]{:S(2)}, u32[]{:S(2)}) async-start(bf16[4,288,768]{2,1,0:T(8,128)(2,1)} %get-tuple-element.244), calls=%async_computation.7 | async-start | bytes 3538944 | tf_op jit(solution)/shard_map/all_to_all | solution.py:193
  16.9 40.3 %copy-start = (s32[906]{0:T(1024)S(1)}, s32[906]{0:T(1024)}, u32[]{:S(2)}) copy-start(s32[906]{0:T(1024)} %constant.301.clone) | copy-start | bytes 10876
  16.9 40.3 %copy-start.8 = (bf16[906,768]{1,0:T(8,128)(2,1)S(1)}, bf16[906,768]{1,0:T(8,128)(2,1)}, u32[]{:S(2)}) copy-start(bf16[906,768]{1,0:T(8,128)(2,1)} %tok_ref.1) | copy-start | bytes 4174852
  16.9 40.4 %copy-start.54 = (s32[906]{0:T(1024)S(1)}, s32[906]{0:T(1024)}, u32[]{:S(2)}) copy-start(s32[906]{0:T(1024)} %param.38) | copy-start | bytes 10876
  16.9 40.4 %copy-start.56 = (s32[906]{0:T(1024)S(1)}, s32[906]{0:T(1024)}, u32[]{:S(2)}) copy-start(s32[906]{0:T(1024)} %param.39) | copy-start | bytes 10876
  64.0 56.6 %copy-start.28 = (bf16[928,768]{1,0:T(8,128)(2,1)}, bf16[928,768]{1,0:T(8,128)(2,1)S(1)}, u32[]{:S(2)}) copy-start(bf16[928,768]{1,0:T(8,128)(2,1)S(1)} %get-tuple-element.413.x_ref.refs_1_) | copy-start | bytes 4276228
  64.1 45.6 %all-to-all-start.8 = ((bf16[4,288,768]{2,1,0:T(8,128)(2,1)}), bf16[4,288,768]{2,1,0:T(8,128)(2,1)S(1)}, u32[]{:S(2)}, u32[]{:S(2)}) async-start(bf16[4,288,768]{2,1,0:T(8,128)(2,1)} %pack_more.1), calls=%async_computation.8 | async-start | bytes 3538944 | tf_op jit(solution)/shard_map/all_to_all | solution.py:193
  162.4 46.5 %collective-permute-start = (bf16[4,96,3072]{2,1,0:T(8,128)(2,1)}, bf16[4,96,3072]{2,1,0:T(8,128)(2,1)S(1)}, u32[]{:S(2)}, u32[]{:S(2)}) collective-permute-start(bf16[4,96,3072]{2,1,0:T(8,128)(2,1)} %dynamic-slice_bitcast_fusion.3), channel_id=1, source_target_pairs={{0,4},{4,0},{8,12},{12,8},{16,20},{20,16},{24,28},{28,24},{1,5},{5... | collective-permute-start | bytes 7077896 | tf_op jit(solution)/shard_map/ppermute | solution.py:722
  162.4 46.5 %collective-permute-start.1 = (bf16[2,768,768]{2,1,0:T(8,128)(2,1)}, bf16[2,768,768]{2,1,0:T(8,128)(2,1)}, u32[]{:S(2)}, u32[]{:S(2)}) collective-permute-start(bf16[2,768,768]{2,1,0:T(8,128)(2,1)} %dynamic-slice_bitcast_fusion.2), channel_id=1, source_target_pairs={{0,4},{4,0},{8,12},{12,8},{16,20},{20,16},{24,28},{28,24},{1,5},{5... | collective-permute-start | bytes 7077896 | tf_op jit(solution)/shard_map/ppermute | solution.py:722
  228.3 35.5 %collective-permute-start.4 = (bf16[4,96,3072]{2,1,0:T(8,128)(2,1)}, bf16[4,96,3072]{2,1,0:T(8,128)(2,1)}, u32[]{:S(2)}, u32[]{:S(2)}) collective-permute-start(bf16[4,96,3072]{2,1,0:T(8,128)(2,1)} %dynamic-slice_bitcast_fusion.1), channel_id=1, source_target_pairs={{0,4},{4,0},{8,12},{12,8},{16,20},{20,16},{24,28},{28,24},{1,5},{5... | collective-permute-start | bytes 7077896 | tf_op jit(solution)/shard_map/ppermute | solution.py:722
  228.3 35.5 %collective-permute-start.5 = (bf16[2,768,768]{2,1,0:T(8,128)(2,1)}, bf16[2,768,768]{2,1,0:T(8,128)(2,1)}, u32[]{:S(2)}, u32[]{:S(2)}) collective-permute-start(bf16[2,768,768]{2,1,0:T(8,128)(2,1)} %dynamic-slice_bitcast_fusion), channel_id=1, source_target_pairs={{0,4},{4,0},{8,12},{12,8},{16,20},{20,16},{24,28},{28,24},{1,5},{5... | collective-permute-start | bytes 7077896 | tf_op jit(solution)/shard_map/ppermute | solution.py:722
  228.8 35.0 %collective-permute-start.2 = (bf16[1,192,3072]{2,1,0:T(8,128)(2,1)}, bf16[1,192,3072]{2,1,0:T(8,128)(2,1)}, u32[]{:S(2)}, u32[]{:S(2)}) collective-permute-start(bf16[1,192,3072]{2,1,0:T(8,128)(2,1)} %dynamic-slice_bitcast_fusion.5), channel_id=1, source_target_pairs={{0,16},{4,20},{8,24},{12,28},{16,0},{20,4},{24,8},{28,12},{1,17},{... | collective-permute-start | bytes 3538952 | tf_op jit(solution)/shard_map/ppermute | solution.py:722
  230.3 33.5 %collective-permute-start.3 = (bf16[1,768,768]{2,1,0:T(8,128)(2,1)}, bf16[1,768,768]{2,1,0:T(8,128)(2,1)S(1)}, u32[]{:S(2)}, u32[]{:S(2)}) collective-permute-start(bf16[1,768,768]{2,1,0:T(8,128)(2,1)} %constant_dynamic-slice_fusion.10), channel_id=1, source_target_pairs={{0,8},{4,12},{8,0},{12,4},{16,24},{20,28},{24,16},{28,20},{1,9},{5... | collective-permute-start | bytes 3538952 | tf_op jit(solution)/shard_map/ppermute | solution.py:722
  231.8 32.0 %collective-permute-start.6 = (bf16[4,96,768]{2,1,0:T(8,128)(2,1)}, bf16[4,96,768]{2,1,0:T(8,128)(2,1)}, u32[]{:S(2)}, u32[]{:S(2)}) collective-permute-start(bf16[4,96,768]{2,1,0:T(8,128)(2,1)} %dynamic-slice_bitcast_fusion.11), channel_id=1, source_target_pairs={{0,4},{4,0},{8,12},{12,8},{16,20},{20,16},{24,28},{28,24},{1,5},{5... | collective-permute-start | bytes 1769480 | tf_op jit(solution)/shard_map/ppermute | solution.py:722
  231.8 96.1 %all-to-all-start.9 = ((bf16[4,288,768]{2,1,0:T(8,128)(2,1)}), bf16[4,288,768]{2,1,0:T(8,128)(2,1)}, u32[]{:S(2)}, u32[]{:S(2)}) async-start(bf16[4,288,768]{2,1,0:T(8,128)(2,1)} %bitcast.153), calls=%async_computation.9 | async-start | bytes 3538944 | tf_op jit(solution)/shard_map/all_to_all | solution.py:193
  280.4 47.6 %collective-permute-start.8 = (bf16[1,192,3072]{2,1,0:T(8,128)(2,1)}, bf16[1,192,3072]{2,1,0:T(8,128)(2,1)}, u32[]{:S(2)}, u32[]{:S(2)}) collective-permute-start(bf16[1,192,3072]{2,1,0:T(8,128)(2,1)} %dynamic-slice_bitcast_fusion.4), channel_id=1, source_target_pairs={{0,16},{4,20},{8,24},{12,28},{16,0},{20,4},{24,8},{28,12},{1,17},{... | collective-permute-start | bytes 3538952 | tf_op jit(solution)/shard_map/ppermute | solution.py:722
  280.8 47.1 %collective-permute-start.9 = (bf16[1,768,768]{2,1,0:T(8,128)(2,1)}, bf16[1,768,768]{2,1,0:T(8,128)(2,1)S(1)}, u32[]{:S(2)}, u32[]{:S(2)}) collective-permute-start(bf16[1,768,768]{2,1,0:T(8,128)(2,1)} %constant_dynamic-slice_fusion.9), channel_id=1, source_target_pairs={{0,8},{4,12},{8,0},{12,4},{16,24},{20,28},{24,16},{28,20},{1,9},{5... | collective-permute-start | bytes 3538952 | tf_op jit(solution)/shard_map/ppermute | solution.py:722
  287.2 40.8 %collective-permute-start.7 = (bf16[1,96,3072]{2,1,0:T(8,128)(2,1)}, bf16[1,96,3072]{2,1,0:T(8,128)(2,1)}, u32[]{:S(2)}, u32[]{:S(2)}) collective-permute-start(bf16[1,96,3072]{2,1,0:T(8,128)(2,1)} %dynamic-slice_bitcast_fusion.10), channel_id=1, source_target_pairs={{0,8},{4,12},{8,0},{12,4},{16,24},{20,28},{24,16},{28,20},{1,9},{5... | collective-permute-start | bytes 1769480 | tf_op jit(solution)/shard_map/ppermute | solution.py:722
  288.7 39.3 %collective-permute-start.10 = (bf16[2,96,768]{2,1,0:T(8,128)(2,1)}, bf16[2,96,768]{2,1,0:T(8,128)(2,1)}, u32[]{:S(2)}, u32[]{:S(2)}) collective-permute-start(bf16[2,96,768]{2,1,0:T(8,128)(2,1)} %dynamic-slice_bitcast_fusion.16), channel_id=1, source_target_pairs={{0,8},{4,12},{8,0},{12,4},{16,24},{20,28},{24,16},{28,20},{1,9},{5... | collective-permute-start | bytes 884744 | tf_op jit(solution)/shard_map/ppermute | solution.py:722
  339.0 30.4 %collective-permute-start.13 = (bf16[768,768]{1,0:T(8,128)(2,1)}, bf16[768,768]{1,0:T(8,128)(2,1)}, u32[]{:S(2)}, u32[]{:S(2)}) collective-permute-start(bf16[768,768]{1,0:T(8,128)(2,1)} %select_bitcast_fusion), channel_id=1, source_target_pairs={{0,16},{4,20},{8,24},{12,28},{16,0},{20,4},{24,8},{28,12},{1,17},{... | collective-permute-start | bytes 3538952 | tf_op jit(solution)/shard_map/ppermute | solution.py:722
  340.5 28.9 %collective-permute-start.11 = (bf16[2,24,3072]{2,1,0:T(8,128)(2,1)}, bf16[2,24,3072]{2,1,0:T(8,128)(2,1)}, u32[]{:S(2)}, u32[]{:S(2)}) collective-permute-start(bf16[2,24,3072]{2,1,0:T(8,128)(2,1)} %dynamic-slice_bitcast_fusion.15), channel_id=1, source_target_pairs={{0,1},{1,0},{2,3},{3,2},{4,5},{5,4},{6,7},{7,6},{8,9},{9,8},{10,11... | collective-permute-start | bytes 884744 | tf_op jit(solution)/shard_map/ppermute | solution.py:722
  342.2 27.2 %collective-permute-start.12 = (bf16[1,96,3072]{2,1,0:T(8,128)(2,1)}, bf16[1,96,3072]{2,1,0:T(8,128)(2,1)}, u32[]{:S(2)}, u32[]{:S(2)}) collective-permute-start(bf16[1,96,3072]{2,1,0:T(8,128)(2,1)} %dynamic-slice_bitcast_fusion.9), channel_id=1, source_target_pairs={{0,8},{4,12},{8,0},{12,4},{16,24},{20,28},{24,16},{28,20},{1,9},{5... | collective-permute-start | bytes 1769480 | tf_op jit(solution)/shard_map/ppermute | solution.py:722
  342.8 26.6 %collective-permute-start.14 = (bf16[1,96,768]{2,1,0:T(8,128)(2,1)}, bf16[1,96,768]{2,1,0:T(8,128)(2,1)}, u32[]{:S(2)}, u32[]{:S(2)}) collective-permute-start(bf16[1,96,768]{2,1,0:T(8,128)(2,1)} %constant_dynamic-slice_fusion.8), channel_id=1, source_target_pairs={{0,16},{4,20},{8,24},{12,28},{16,0},{20,4},{24,8},{28,12},{1,17},{... | collective-permute-start | bytes 442376 | tf_op jit(solution)/shard_map/ppermute | solution.py:722
  343.3 12.3 %collective-permute-start.15 = (f32[17,768]{1,0:T(8,128)}, f32[17,768]{1,0:T(8,128)}, u32[]{:S(2)}, u32[]{:S(2)}) collective-permute-start(f32[17,768]{1,0:T(8,128)} %pad_maximum_fusion), channel_id=1, source_target_pairs={{0,4},{4,0},{8,12},{12,8},{16,20},{20,16},{24,28},{28,24},{1,5},{5... | collective-permute-start | bytes 156680 | tf_op jit(solution)/shard_map/ppermute | solution.py:722
  343.3 76.8 %all-to-all-start.10 = ((bf16[4,288,768]{2,1,0:T(8,128)(2,1)}), bf16[4,288,768]{2,1,0:T(8,128)(2,1)}, u32[]{:S(2)}, u32[]{:S(2)}) async-start(bf16[4,288,768]{2,1,0:T(8,128)(2,1)} %bitcast.178), calls=%async_computation.10 | async-start | bytes 3538944 | tf_op jit(solution)/shard_map/all_to_all | solution.py:193
  377.7 41.5 %collective-permute-start.16 = (bf16[4,96,1152]{2,1,0:T(8,128)(2,1)S(1)}, bf16[4,96,1152]{2,1,0:T(8,128)(2,1)S(1)}, u32[]{:S(2)}, u32[]{:S(2)}) collective-permute-start(bf16[4,96,1152]{2,1,0:T(8,128)(2,1)S(1)} %get-tuple-element.338), channel_id=1, source_target_pairs={{0,4},{4,0},{8,12},{12,8},{16,20},{20,16},{24,28},{28,24},{1,5},{5... | collective-permute-start | bytes 2654216 | tf_op jit(solution)/shard_map/ppermute | solution.py:722
  377.8 42.3 %collective-permute-start.17 = (bf16[4,96,1152]{2,1,0:T(8,128)(2,1)S(1)}, bf16[4,96,1152]{2,1,0:T(8,128)(2,1)S(1)}, u32[]{:S(2)}, u32[]{:S(2)}) collective-permute-start(bf16[4,96,1152]{2,1,0:T(8,128)(2,1)S(1)} %get-tuple-element.339), channel_id=1, source_target_pairs={{0,4},{4,0},{8,12},{12,8},{16,20},{20,16},{24,28},{28,24},{1,5},{5... | collective-permute-start | bytes 2654216 | tf_op jit(solution)/shard_map/ppermute | solution.py:722
  378.3 40.9 %collective-permute-start.20 = (bf16[2,192,768]{2,1,0:T(8,128)(2,1)S(1)}, bf16[2,192,768]{2,1,0:T(8,128)(2,1)S(1)}, u32[]{:S(2)}, u32[]{:S(2)}) collective-permute-start(bf16[2,192,768]{2,1,0:T(8,128)(2,1)S(1)} %dynamic-slice_bitcast_fusion.8), channel_id=1, source_target_pairs={{0,1},{1,0},{2,3},{3,2},{4,5},{5,4},{6,7},{7,6},{8,9},{9,8},{10,11... | collective-permute-start | bytes 1769480 | tf_op jit(solution)/shard_map/ppermute | solution.py:722
  379.8 39.4 %collective-permute-start.19 = (bf16[2,24,3072]{2,1,0:T(8,128)(2,1)S(1)}, bf16[2,24,3072]{2,1,0:T(8,128)(2,1)S(1)}, u32[]{:S(2)}, u32[]{:S(2)}) collective-permute-start(bf16[2,24,3072]{2,1,0:T(8,128)(2,1)S(1)} %dynamic-slice_bitcast_fusion.14), channel_id=1, source_target_pairs={{0,1},{1,0},{2,3},{3,2},{4,5},{5,4},{6,7},{7,6},{8,9},{9,8},{10,11... | collective-permute-start | bytes 884744 | tf_op jit(solution)/shard_map/ppermute | solution.py:722
  380.3 4.4 collective-permute-start.22
  384.7 25.4 %collective-permute-start.21 = (bf16[2,24,768]{2,1,0:T(8,128)(2,1)S(1)}, bf16[2,24,768]{2,1,0:T(8,128)(2,1)}, u32[]{:S(2)}, u32[]{:S(2)}) collective-permute-start(bf16[2,24,768]{2,1,0:T(8,128)(2,1)S(1)} %dynamic-slice_bitcast_fusion.20), channel_id=1, source_target_pairs={{0,1},{1,0},{2,3},{3,2},{4,5},{5,4},{6,7},{7,6},{8,9},{9,8},{10,11... | collective-permute-start | bytes 221192 | tf_op jit(solution)/shard_map/ppermute | solution.py:722
  410.1 9.1 %collective-permute-start.18 = (bf16[1,24,3072]{2,1,0:T(8,128)(2,1)S(1)}, bf16[1,24,3072]{2,1,0:T(8,128)(2,1)S(1)}, u32[]{:S(2)}, u32[]{:S(2)}) collective-permute-start(bf16[1,24,3072]{2,1,0:T(8,128)(2,1)S(1)} %constant_dynamic-slice_fusion.7), channel_id=1, source_target_pairs={{0,2},{1,3},{2,0},{3,1},{4,6},{5,7},{6,4},{7,5},{8,10},{9,11},{10,... | collective-permute-start | bytes 442376 | tf_op jit(solution)/shard_map/ppermute | solution.py:722
  427.4 5.2 %collective-permute-start.27 = (bf16[1,24,768]{2,1,0:T(8,128)(2,1)}, bf16[1,24,768]{2,1,0:T(8,128)(2,1)}, u32[]{:S(2)}, u32[]{:S(2)}) collective-permute-start(bf16[1,24,768]{2,1,0:T(8,128)(2,1)} %constant_dynamic-slice_fusion.4), channel_id=1, source_target_pairs={{0,2},{1,3},{2,0},{3,1},{4,6},{5,7},{6,4},{7,5},{8,10},{9,11},{10,... | collective-permute-start | bytes 110600 | tf_op jit(solution)/shard_map/ppermute | solution.py:722
  427.5 24.1 %collective-permute-start.23 = (bf16[2,96,1152]{2,1,0:T(8,128)(2,1)S(1)}, bf16[2,96,1152]{2,1,0:T(8,128)(2,1)S(1)}, u32[]{:S(2)}, u32[]{:S(2)}) collective-permute-start(bf16[2,96,1152]{2,1,0:T(8,128)(2,1)S(1)} %copy-done.41), channel_id=1, source_target_pairs={{0,8},{4,12},{8,0},{12,4},{16,24},{20,28},{24,16},{28,20},{1,9},{5... | collective-permute-start | bytes 1327112 | tf_op jit(solution)/shard_map/ppermute | solution.py:722
  427.9 23.7 %collective-permute-start.24 = (bf16[1,192,1152]{2,1,0:T(8,128)(2,1)}, bf16[1,192,1152]{2,1,0:T(8,128)(2,1)S(1)}, u32[]{:S(2)}, u32[]{:S(2)}) collective-permute-start(bf16[1,192,1152]{2,1,0:T(8,128)(2,1)} %dynamic-slice_bitcast_fusion.12), channel_id=1, source_target_pairs={{0,16},{4,20},{8,24},{12,28},{16,0},{20,4},{24,8},{28,12},{1,17},{... | collective-permute-start | bytes 1327112 | tf_op jit(solution)/shard_map/ppermute | solution.py:722
  429.4 16.8 %collective-permute-start.25 = (bf16[1,24,3072]{2,1,0:T(8,128)(2,1)}, bf16[1,24,3072]{2,1,0:T(8,128)(2,1)S(1)}, u32[]{:S(2)}, u32[]{:S(2)}) collective-permute-start(bf16[1,24,3072]{2,1,0:T(8,128)(2,1)} %constant_dynamic-slice_fusion.6), channel_id=1, source_target_pairs={{0,2},{1,3},{2,0},{3,1},{4,6},{5,7},{6,4},{7,5},{8,10},{9,11},{10,... | collective-permute-start | bytes 442376 | tf_op jit(solution)/shard_map/ppermute | solution.py:722
  432.2 19.3 %collective-permute-start.26 = (bf16[1,192,768]{2,1,0:T(8,128)(2,1)}, bf16[1,192,768]{2,1,0:T(8,128)(2,1)S(1)}, u32[]{:S(2)}, u32[]{:S(2)}) collective-permute-start(bf16[1,192,768]{2,1,0:T(8,128)(2,1)} %constant_dynamic-slice_fusion.5), channel_id=1, source_target_pairs={{0,2},{1,3},{2,0},{3,1},{4,6},{5,7},{6,4},{7,5},{8,10},{9,11},{10,... | collective-permute-start | bytes 884744 | tf_op jit(solution)/shard_map/ppermute | solution.py:722
  432.6 8.9 %collective-permute-start.28 = (f32[17,768]{1,0:T(8,128)S(1)}, f32[17,768]{1,0:T(8,128)S(1)}, u32[]{:S(2)}, u32[]{:S(2)}) collective-permute-start(f32[17,768]{1,0:T(8,128)S(1)} %add.308), channel_id=1, source_target_pairs={{0,16},{4,20},{8,24},{12,28},{16,0},{20,4},{24,8},{28,12},{1,17},{... | collective-permute-start | bytes 156680 | tf_op jit(solution)/shard_map/ppermute | solution.py:722
  451.8 6.6 %collective-permute-start.29 = (bf16[1,96,1152]{2,1,0:T(8,128)(2,1)S(1)}, bf16[1,96,1152]{2,1,0:T(8,128)(2,1)S(1)}, u32[]{:S(2)}, u32[]{:S(2)}) collective-permute-start(bf16[1,96,1152]{2,1,0:T(8,128)(2,1)S(1)} %constant_dynamic-slice_fusion.3), channel_id=1, source_target_pairs={{0,16},{4,20},{8,24},{12,28},{16,0},{20,4},{24,8},{28,12},{1,17},{... | collective-permute-start | bytes 663560 | tf_op jit(solution)/shard_map/ppermute | solution.py:722
  452.7 6.1 %collective-permute-start.30 = (bf16[1,96,1152]{2,1,0:T(8,128)(2,1)S(1)}, bf16[1,96,1152]{2,1,0:T(8,128)(2,1)S(1)}, u32[]{:S(2)}, u32[]{:S(2)}) collective-permute-start(bf16[1,96,1152]{2,1,0:T(8,128)(2,1)S(1)} %dynamic-slice_bitcast_fusion.17), channel_id=1, source_target_pairs={{0,8},{4,12},{8,0},{12,4},{16,24},{20,28},{24,16},{28,20},{1,9},{5... | collective-permute-start | bytes 663560 | tf_op jit(solution)/shard_map/ppermute | solution.py:722
  454.0 4.4 collective-permute-start.31
  458.8 20.0 %copy-start.27 = (bf16[928,768]{1,0:T(8,128)(2,1)S(1)}, bf16[928,768]{1,0:T(8,128)(2,1)}, u32[]{:S(2)}) copy-start(bf16[928,768]{1,0:T(8,128)(2,1)} %get-tuple-element.381) | copy-start | bytes 4276228
  458.9 19.9 %copy-start.1 = (s32[906]{0:T(1024)S(1)}, s32[906]{0:T(1024)}, u32[]{:S(2)}) copy-start(s32[906]{0:T(1024)} %constant.301.clone) | copy-start | bytes 10876
  459.0 7.3 %collective-permute-start.32 = (bf16[2,24,1152]{2,1,0:T(8,128)(2,1)S(1)}, bf16[2,24,1152]{2,1,0:T(8,128)(2,1)S(1)}, u32[]{:S(2)}, u32[]{:S(2)}) collective-permute-start(bf16[2,24,1152]{2,1,0:T(8,128)(2,1)S(1)} %dynamic-slice_bitcast_fusion.19), channel_id=1, source_target_pairs={{0,1},{1,0},{2,3},{3,2},{4,5},{5,4},{6,7},{7,6},{8,9},{9,8},{10,11... | collective-permute-start | bytes 331784 | tf_op jit(solution)/shard_map/ppermute | solution.py:722
  459.1 7.3 %collective-permute-start.33 = (bf16[2,24,1152]{2,1,0:T(8,128)(2,1)S(1)}, bf16[2,24,1152]{2,1,0:T(8,128)(2,1)S(1)}, u32[]{:S(2)}, u32[]{:S(2)}) collective-permute-start(bf16[2,24,1152]{2,1,0:T(8,128)(2,1)S(1)} %dynamic-slice_bitcast_fusion.18), channel_id=1, source_target_pairs={{0,1},{1,0},{2,3},{3,2},{4,5},{5,4},{6,7},{7,6},{8,9},{9,8},{10,11... | collective-permute-start | bytes 331784 | tf_op jit(solution)/shard_map/ppermute | solution.py:722
  461.1 5.3 %collective-permute-start.34 = (f32[17,768]{1,0:T(8,128)S(1)}, f32[17,768]{1,0:T(8,128)S(1)}, u32[]{:S(2)}, u32[]{:S(2)}) collective-permute-start(f32[17,768]{1,0:T(8,128)S(1)} %add.314), channel_id=1, source_target_pairs={{0,2},{1,3},{2,0},{3,1},{4,6},{5,7},{6,4},{7,5},{8,10},{9,11},{10,... | collective-permute-start | bytes 156680 | tf_op jit(solution)/shard_map/ppermute | solution.py:722
  467.7 8.8 %collective-permute-start.35 = (bf16[1,24,1152]{2,1,0:T(8,128)(2,1)}, bf16[1,24,1152]{2,1,0:T(8,128)(2,1)}, u32[]{:S(2)}, u32[]{:S(2)}) collective-permute-start(bf16[1,24,1152]{2,1,0:T(8,128)(2,1)} %constant_dynamic-slice_fusion.2), channel_id=1, source_target_pairs={{0,2},{1,3},{2,0},{3,1},{4,6},{5,7},{6,4},{7,5},{8,10},{9,11},{10,... | collective-permute-start | bytes 165896 | tf_op jit(solution)/shard_map/ppermute | solution.py:722
  468.9 7.6 %collective-permute-start.36 = (bf16[1,24,1152]{2,1,0:T(8,128)(2,1)}, bf16[1,24,1152]{2,1,0:T(8,128)(2,1)}, u32[]{:S(2)}, u32[]{:S(2)}) collective-permute-start(bf16[1,24,1152]{2,1,0:T(8,128)(2,1)} %constant_dynamic-slice_fusion.1), channel_id=1, source_target_pairs={{0,2},{1,3},{2,0},{3,1},{4,6},{5,7},{6,4},{7,5},{8,10},{9,11},{10,... | collective-permute-start | bytes 165896 | tf_op jit(solution)/shard_map/ppermute | solution.py:722
  (61 other events, 274.9 us)

commit v3 on v2

--- a/solution.py
+++ b/solution.py
@@ -159,19 +159,48 @@
     )(recv)
 
 
-def place_kernel(pos_ref, recv_ref, x_ref):
-    rows, total = x_ref.shape[0], recv_ref.shape[0]
+def picked(pos_ref, recv_ref, rows):
+    total = recv_ref.shape[0]
     pick = iota((rows, total), 0) == jnp.broadcast_to(pos_ref[0:1, :], (rows, total))
-    x_ref[...] = dot_nn(pick.astype(BF16), recv_ref[...]).astype(BF16)
+    return dot_nn(pick.astype(BF16), recv_ref[...]).astype(BF16)
+
+
+def place_kernel(pos_ref, recv_ref, x_ref, spare_ref):
+    x_ref[...] = picked(pos_ref, recv_ref, x_ref.shape[0])
 
 
 def place(rows, pos, recv):
+    out = jax.ShapeDtypeStruct((rows, recv.shape[1]), BF16)
     return pl.pallas_call(
         place_kernel,
-        out_shape=jax.ShapeDtypeStruct((rows, recv.shape[1]), BF16),
+        out_shape=(out, out),
+        out_specs=(pl.BlockSpec(memory_space=VMEM), pl.BlockSpec(memory_space=pl.ANY)),
         compiler_params=params(BIG),
         name="place",
     )(pos, recv)
+
+
+def place_or_kernel(flag_ref, pos_ref, recv_ref, other_ref, x_ref):
+    over = flag_ref[0] != 0
+
+    @pl.when(over)
+    def _():
+        x_ref[...] = other_ref[...]
+
+    @pl.when(jnp.logical_not(over))
+    def _():
+        x_ref[...] = picked(pos_ref, recv_ref, x_ref.shape[0])
+
+
+def place_or(flag, pos, recv, other):
+    vmem = pl.BlockSpec(memory_space=VMEM)
+    return pl.pallas_call(
+        place_or_kernel,
+        in_specs=[pl.BlockSpec(memory_space=pltpu.SMEM), vmem, vmem, vmem],
+        out_shape=jax.ShapeDtypeStruct(other.shape, BF16),
+        compiler_params=params(BIG),
+        name="place_or",
+    )(flag, pos, recv, other)
 
 
 def choose_kernel(col_ref, value_ref, out_ref):
@@ -230,6 +259,17 @@
     return jnp.take(everyone(value, ways).reshape(-1, width), spot, axis=0)
 
 
+STRIP = 32
+
+
+def fold8(value):
+    return sum(value[i : i + 8] for i in range(0, value.shape[0], 8))
+
+
+def strip(i, size, start=0):
+    return pl.ds(pl.multiple_of(start + i * size, 16), size)
+
+
 def norm_stats(value):
     center = value - jnp.mean(value, axis=-1, keepdims=True)
     spread = jnp.mean(center * center, axis=-1, keepdims=True)
@@ -242,14 +282,14 @@
     @pl.when(j == 0)
     def _():
         def step(i, c):
-            at = pl.ds(pl.multiple_of(i * 16, 16), 16)
+            at = strip(i, STRIP)
             center, r = norm_stats(x_ref[at, :].astype(F32))
             h = (center * r * gain_ref[...] + shift_ref[...]).astype(BF16)
             keep_ref[at, :] = h
             first_ref[at, :] = h
             return c
 
-        lax.fori_loop(0, x_ref.shape[0] // 16, step, 0)
+        lax.fori_loop(0, x_ref.shape[0] // STRIP, step, 0)
 
     bias = jnp.where(j == 0, qb_ref[...], jnp.where(j == 2, vb_ref[...], 0.0))
     qkv_ref[...] = (dot_nn(keep_ref[...], w_ref[...]) + bias).astype(BF16)
@@ -448,34 +488,41 @@
     )(qkv, qkv, qkv, d_att, lse)
 
 
-def fold8(value):
-    return jnp.sum(value.reshape(value.shape[0] // 8, 8, value.shape[1]), axis=0)
-
-
-def ffn_kernel(expert, lo, hi, *refs):
+def split_rows(own, value, run, keep_ref, send_ref):
+    rows, cols = value.shape
+    parts = value.reshape(rows // (2 * run), 2, run, cols)
+    even, odd = parts[:, 0], parts[:, 1]
+    mine = own == 0
+    keep_ref[...] = jnp.where(mine, even, odd).reshape(rows // 2, cols)
+    send_ref[...] = jnp.where(mine, odd, even).reshape(rows // 2, cols)
+
+
+def ffn_kernel(expert, lo, hi, run, own_ref, *refs):
     j = pl.program_id(0)
+    own = own_ref[0]
     att_ref, x_ref, g_ref, wo_ref, bo_ref, gain_ref, shift_ref = refs[:7]
     up_ref, ub_ref, down_ref, db_ref = refs[7:11]
     refs = refs[11:]
     if lo:
         mixed0_ref, dmid0_ref, datt0_ref, sums0_ref = refs[:4]
         refs = refs[4:]
-    mixed_ref, dmid_ref, datt_ref, gup_ref, gdown_ref, gub_ref, sums_ref = refs[:7]
-    refs = refs[7:]
-    if lo:
-        gwo_ref = refs[0]
-        refs = refs[1:]
+    mixed_ref, dmid_ref, datt_ref, sums_ref = refs[:4]
+    refs = refs[4:]
+    each = 2 if run else 1
+    gup_refs, gdown_refs = refs[:each], refs[each : 2 * each]
+    refs = refs[2 * each :]
     mid_ref, second_ref, mix_ref, ds_ref, pre_ref, dh_ref, hid_ref, dpre_ref = refs
     width = x_ref.shape[1]
     span = hi - lo
-    steps16 = span // 16
-    own = slice(lo, hi)
-    here = lambda i: pl.ds(pl.multiple_of(i * 16, 16), 16)
-    there = lambda i: pl.ds(pl.multiple_of(lo + i * 16, 16), 16)
+    size = 64 if span % 64 == 0 else STRIP
+    steps = span // size
+    part = slice(lo, hi)
+    here = lambda i: strip(i, size)
+    there = lambda i: strip(i, size, lo)
 
     @pl.when(j == 0)
     def _():
-        mid_ref[...] = dot_nn(att_ref[own, :], wo_ref[...])
+        mid_ref[...] = dot_nn(att_ref[part, :], wo_ref[...])
 
         def step(i, c):
             mid = x_ref[there(i), :].astype(F32) + mid_ref[here(i), :] + bo_ref[...]
@@ -485,32 +532,48 @@
             second_ref[here(i), :] = (center * r * gain_ref[...] + shift_ref[...]).astype(BF16)
             return c
 
-        lax.fori_loop(0, steps16, step, 0)
+        lax.fori_loop(0, steps, step, 0)
         ds_ref[...] = jnp.zeros_like(ds_ref)
+        sums_ref[...] = sums0_ref[...] if lo else jnp.zeros_like(sums_ref)
 
     second = second_ref[...]
-    g = g_ref[own, :]
+    g = g_ref[part, :]
     pre_ref[...] = dot_nn(second, up_ref[0]) + ub_ref[expert : expert + 1, :]
     dh_ref[...] = dot_nt(g, down_ref[0])
 
     def gelu_step(i, c):
-        u = pre_ref[here(i), :]
+        u = pre_ref[strip(i, size), :]
         cdf = 0.5 * (1.0 + lax.erf(u * (2.0**-0.5)))
         pdf = jnp.exp(-0.5 * u * u) * (1.0 / np.sqrt(2.0 * np.pi))
-        hid_ref[here(i), :] = (u * cdf).astype(BF16)
-        d = (dh_ref[here(i), :] * (cdf + u * pdf)).astype(BF16)
-        dpre_ref[here(i), :] = d
+        hid_ref[strip(i, size), :] = (u * cdf).astype(BF16)
+        d = (dh_ref[strip(i, size), :] * (cdf + u * pdf)).astype(BF16)
+        dpre_ref[strip(i, size), :] = d
         d = d.astype(F32)
-        return c + (d[0:8] + d[8:16])
-
-    total = lax.fori_loop(0, steps16, gelu_step, jnp.zeros((8, pre_ref.shape[1]), F32))
-    gub_ref[...] = jnp.sum(total, axis=0, keepdims=True)
+        return c + fold8(d)
+
+    total = lax.fori_loop(0, steps, gelu_step, jnp.zeros((8, pre_ref.shape[1]), F32))
+    spot = 8 + expert * (8 // ub_ref.shape[0]) + j
+    sums_ref[pl.ds(spot, 1), :] = jnp.sum(total, axis=0, keepdims=True)
     hid = hid_ref[...]
     dpre = dpre_ref[...]
     mix_ref[...] += dot_nn(hid, down_ref[0])
     ds_ref[...] += dot_nt(dpre, up_ref[0])
-    gdown_ref[...] = dot_tn(hid, g).astype(BF16)
-    gup_ref[...] = dot_tn(second, dpre).astype(BF16)
+    gdown = dot_tn(hid, g).astype(BF16)
+    gup = dot_tn(second, dpre).astype(BF16)
+    if run:
+        split_rows(own, gup, run, *gup_refs)
+        stay = lax.rem(j, 2) == own
+
+        @pl.when(stay)
+        def _():
+            gdown_refs[0][...] = gdown
+
+        @pl.when(jnp.logical_not(stay))
+        def _():
+            gdown_refs[1][...] = gdown
+    else:
+        gup_refs[0][...] = gup
+        gdown_refs[0][...] = gdown
 
     @pl.when(j == pl.num_programs(0) - 1)
     def _():
@@ -530,31 +593,28 @@
             dmid_ref[out_at(i), :] = d
             d = d.astype(F32)
             return (
-                c[0] + un[0:8] + un[8:16],
-                c[1] + u[0:8] + u[8:16],
-                c[2] + d[0:8] + d[8:16],
-                c[3] + g16[0:8] + g16[8:16],
+                c[0] + fold8(un),
+                c[1] + fold8(u),
+                c[2] + fold8(d),
+                c[3] + fold8(g16),
             )
 
         zero = jnp.zeros((8, width), F32)
-        total = lax.fori_loop(0, steps16, step, (zero,) * 4)
+        total = lax.fori_loop(0, steps, step, (zero,) * 4)
         line = [jnp.sum(t, axis=0, keepdims=True) for t in total]
-        pad = jnp.zeros((8 - 3, width), F32)
-        last = jnp.where(iota((8, 1), 0) == 3 + expert, line[3], 0.0)
-        sums = jnp.concatenate(line[:3] + [pad], axis=0) + last
+        spots = (0, 1, 2, 3 + expert)
+        for spot, value in zip(spots, line):
+            sums_ref[spot : spot + 1, :] += value
         if lo:
             mixed_ref[:lo, :] = mixed0_ref[...]
             dmid_ref[:lo, :] = dmid0_ref[...]
             datt_ref[:lo, :] = datt0_ref[...]
-            sums = sums + sums0_ref[...]
-            gwo_ref[...] = dot_tn(att_ref[...], dmid_ref[...]).astype(BF16)
-            datt_ref[own, :] = dot_nt(dmid_ref[own, :], wo_ref[...]).astype(BF16)
+            datt_ref[part, :] = dot_nt(dmid_ref[part, :], wo_ref[...]).astype(BF16)
         else:
             datt_ref[...] = dot_nt(dmid_ref[...], wo_ref[...]).astype(BF16)
-        sums_ref[...] = sums
-
-
-def ffn(expert, bounds, att, x, g, wo, bo, gain, shift, up, ub, down, db, prev=()):
+
+
+def ffn(expert, bounds, run, own, att, x, g, wo, bo, gain, shift, up, ub, down, db, prev=()):
     lo, hi = bounds
     rows, width = x.shape
     experts, _, hidden = up.shape
@@ -564,25 +624,25 @@
     done = rows if lo else span
     one = pl.Buffered(1)
     full = lambda r, c: pl.BlockSpec((r, c), lambda j: (0, 0), pipeline_mode=one)
-    out_specs = [full(done, width)] * 3 + [
-        pl.BlockSpec((width, chunk), lambda j: (0, j)),
-        pl.BlockSpec((chunk, width), lambda j: (j, 0)),
-        pl.BlockSpec((1, chunk), lambda j: (0, j)),
-        full(8, width),
-    ]
-    out_shape = [jax.ShapeDtypeStruct((done, width), BF16)] * 3 + [
-        jax.ShapeDtypeStruct((width, hidden), BF16),
-        jax.ShapeDtypeStruct((hidden, width), BF16),
-        jax.ShapeDtypeStruct((1, hidden), F32),
-        jax.ShapeDtypeStruct((8, width), F32),
-    ]
-    if lo:
-        out_specs.append(full(width, width))
-        out_shape.append(jax.ShapeDtypeStruct((width, width), BF16))
-    return pl.pallas_call(
-        functools.partial(ffn_kernel, expert, lo, hi),
+    each = 2 if run else 1
+    shape = jax.ShapeDtypeStruct
+    out_specs = (
+        [full(done, width)] * 3
+        + [full(16, width)]
+        + [pl.BlockSpec((width // each, chunk), lambda j: (0, j))] * each
+        + [pl.BlockSpec((chunk, width), lambda j: (j // each, 0))] * each
+    )
+    out_shape = (
+        [shape((done, width), BF16)] * 3
+        + [shape((16, width), F32)]
+        + [shape((width // each, hidden), BF16)] * each
+        + [shape((hidden // each, width), BF16)] * each
+    )
+    return pl.pallas_call(
+        functools.partial(ffn_kernel, expert, lo, hi, run),
         grid=(steps,),
         in_specs=[
+            pl.BlockSpec(memory_space=pltpu.SMEM),
             full(rows, width),
             full(rows, width),
             full(rows, width),
@@ -611,11 +671,11 @@
         compiler_params=params(BIG),
         cost_estimate=cost(12 * span * width * hidden),
         name=f"ffn{expert}",
-    )(att, x, g, wo, bo, gain, shift, up, ub, down, db, *prev)
+    )(own, att, x, g, wo, bo, gain, shift, up, ub, down, db, *prev)
 
 
 def last_kernel(
-    x_ref, dq_ref, dk_ref, dv_ref, w_ref, gain_ref, dmid_ref, col_ref,
+    x_ref, dq_ref, dk_ref, dv_ref, w_ref, gain_ref, dmid_ref, col_ref, sums0_ref,
     back_ref, gin_ref, sums_ref, df_ref,
 ):
     rows, width = x_ref.shape
@@ -627,7 +687,7 @@
             df_ref[...] += term
 
     def step(i, c):
-        at = pl.ds(pl.multiple_of(i * 16, 16), 16)
+        at = strip(i, STRIP)
         center, r = norm_stats(x_ref[at, :].astype(F32))
         n = center * r
         u = df_ref[at, :]
@@ -639,39 +699,54 @@
         q = dq_ref[at, :].astype(F32)
         v = dv_ref[at, :].astype(F32)
         return (
-            c[0] + un[0:8] + un[8:16],
-            c[1] + u[0:8] + u[8:16],
-            c[2] + q[0:8] + q[8:16],
-            c[3] + v[0:8] + v[8:16],
+            c[0] + fold8(un),
+            c[1] + fold8(u),
+            c[2] + fold8(q),
+            c[3] + fold8(v),
         )
 
     zero = jnp.zeros((8, width), F32)
-    total = lax.fori_loop(0, rows // 16, step, (zero,) * 4)
+    total = lax.fori_loop(0, rows // STRIP, step, (zero,) * 4)
+    sums_ref[0:16, :] = sums0_ref[...]
+    sums_ref[16:24, :] = jnp.zeros((8, width), F32)
     for i in range(4):
-        sums_ref[i : i + 1, :] = jnp.sum(total[i], axis=0, keepdims=True)
+        sums_ref[16 + i : 17 + i, :] = jnp.sum(total[i], axis=0, keepdims=True)
     back_ref[...] = give_back(col_ref, gin_ref)
 
 
-def wgrad_kernel(first_ref, dq_ref, dk_ref, dv_ref, gwa_ref, gwb_ref):
+def wgrad_kernel(run, own_ref, first_ref, dq_ref, dk_ref, dv_ref, att_ref, dmid_ref, *refs):
     width = first_ref.shape[1]
-    half = width // 2
     first = first_ref[...]
-    gwa_ref[:, :width] = dot_tn(first, dq_ref[...]).astype(BF16)
-    gw = dot_tn(first, dk_ref[...]).astype(BF16)
-    gwa_ref[:, width:] = gw[:, :half]
-    gwb_ref[:, :half] = gw[:, half:]
-    gwb_ref[:, half:] = dot_tn(first, dv_ref[...]).astype(BF16)
-
-
-def wgrad(first, dq, dk, dv):
+    each = 2 if run else 1
+    ends = refs[:each], refs[each:]
+
+    def put(half, at, value):
+        cols = slice(at * width, (at + 1) * width)
+        value = value.astype(BF16)
+        if run:
+            split_rows(own_ref[0], value, run, *(r.at[:, cols] for r in ends[half]))
+        else:
+            ends[half][0][:, cols] = value
+
+    put(0, 0, dot_tn(first, dq_ref[...]))
+    put(0, 1, dot_tn(first, dk_ref[...]))
+    put(1, 0, dot_tn(first, dv_ref[...]))
+    put(1, 1, dot_tn(att_ref[...], dmid_ref[...]))
+
+
+def wgrad(run, own, first, dq, dk, dv, att, dmid):
     rows, width = first.shape
-    return pl.pallas_call(
-        wgrad_kernel,
-        out_shape=(jax.ShapeDtypeStruct((width, width + width // 2), BF16),) * 2,
-        compiler_params=params(BIG),
-        cost_estimate=cost(6 * rows * width * width),
+    each = 2 if run else 1
+    vmem = pl.BlockSpec(memory_space=VMEM)
+    out = pl.pallas_call(
+        functools.partial(wgrad_kernel, run),
+        in_specs=[pl.BlockSpec(memory_space=pltpu.SMEM)] + [vmem] * 6,
+        out_shape=(jax.ShapeDtypeStruct((width // each, 2 * width), BF16),) * (2 * each),
+        compiler_params=params(BIG),
+        cost_estimate=cost(8 * rows * width * width),
         name="wgrad",
-    )(first, dq, dk, dv)
+    )(own, first, dq, dk, dv, att, dmid)
+    return out[:each], out[each:]
 
 
 def give_back(col_ref, value_ref):
@@ -680,20 +755,20 @@
     return dot_nn(pick.astype(BF16), value_ref[...]).astype(BF16)
 
 
-def last(x, dq, dk, dv, w, gain, dmid, col):
+def last(x, dq, dk, dv, w, gain, dmid, col, sums):
     rows, width = x.shape
     return pl.pallas_call(
         last_kernel,
         out_shape=(
             jax.ShapeDtypeStruct((col.shape[0], width), BF16),
             jax.ShapeDtypeStruct((rows, width), BF16),
-            jax.ShapeDtypeStruct((8, width), F32),
+            jax.ShapeDtypeStruct((24, width), F32),
         ),
         scratch_shapes=[VMEM((rows, width), F32)],
         compiler_params=params(BIG),
         cost_estimate=cost(2 * rows * width * w.shape[1]),
         name="last",
-    )(x, dq, dk, dv, w, gain, dmid, col)
+    )(x, dq, dk, dv, w, gain, dmid, col, sums)
 
 
 def back_kernel(col_ref, value_ref, out_ref):
@@ -726,10 +801,15 @@
 
 
 class Shards:
-    def __init__(self, value, left):
-        self.value, self.left = value, list(left)
+    def __init__(self, values, left):
+        self.ready = values if len(values) == 2 else None
+        self.value, self.left = values[0], list(left)
 
     def cut(self, key):
+        if self.ready:
+            send, self.ready = self.ready[1], None
+            self.left.remove(key)
+            return send
         above = 1 << self.left.index(key)
         rows, cols = self.value.shape
         parts = self.value.reshape(above, 2, rows // (2 * above), cols)
@@ -746,6 +826,7 @@
 
 class Joined(Shards):
     def __init__(self, first, second):
+        self.ready = None
         self.pair, self.left = (first.value, second.value), list(first.left)
 
     def cut(self, key):
@@ -754,17 +835,6 @@
         own = pair_bit(*key) == 0
         self.value = jnp.where(own, *self.pair)
         return jnp.where(own, *self.pair[::-1])
-
-
-class Whole:
-    def __init__(self, value):
-        self.value = value
-
-    def cut(self, key):
-        return self.value
-
-    def add(self, got):
-        self.value = self.value + got
 
 
 def launch(moves, *tied):
@@ -813,15 +883,17 @@
     send_g = pack_more(ways, places, grad_out)
     pos_row, pos_col, flag = index(ways, per, recv_t)
     over = flag[0, 0] > 0.5
-    enter = lambda value, recv: lax.cond(
+    side = lambda a, b: jnp.concatenate([a, b], axis=1)
+    apart = lambda v: (v[:, :width], v[:, width:])
+    x, spare = lax.cond(
         over,
-        lambda v, r, p: slow_in(v, *labels, ways, per),
-        lambda v, r, p: place(rows, p, r),
-        value,
-        recv,
+        lambda t, g, r, p: apart(slow_in(side(t, g), *labels, ways, per)),
+        lambda t, g, r, p: tuple(place(rows, p, r)),
+        tokens,
+        grad_out,
+        recv_t,
         pos_row,
     )
-    x = enter(tokens, recv_t)
     x, send_g = tie((x, send_g))
     recv_g = swap(send_g).reshape(ways * SLOTS, width)
     first, qkv = qkv_call(
@@ -829,7 +901,7 @@
     )
     att, lse = attn_fwd(per, qkv)
     att, recv_g = tie((att, recv_g))
-    g = enter(grad_out, recv_g)
+    g = place_or(over.astype(jnp.int32).reshape(1), pos_row, recv_g, spare)
     weights = (
         out_weight, row(out_bias), row(ln2_gain), row(ln2_bias),
         up_weight, up_bias, down_weight, down_bias,
@@ -841,106 +913,122 @@
     low_first = mids + [top]
     high_first = [top] + mids
 
-    mixed0, dmid0, datt0, g_up0, g_down0, g_ub0, sums0 = ffn(0, bounds[0], att, x, g, *weights)
-    up0, down0 = Shards(g_up0, every), Shards(g_down0, every[1:])
-    air1, (prev,) = launch(
-        [(up0, core), (down0, core)], (mixed0, dmid0, datt0, sums0)
-    )
-    mixed_s, dmid, d_att, g_up1, g_down1, g_ub1, sums2, g_wo = ffn(
-        1, bounds[1], att, x, g, *weights, prev=prev
-    )
-    d_att, mixed_s, g_up1, g_down1, g_wo = settle(air1, d_att, mixed_s, g_up1, g_down1, g_wo)
-    up1, down1, wo = Shards(g_up1, every), Shards(g_down1, every[1:]), Shards(g_wo, every)
+    own = pair_bit(*core).reshape(1)
+    hidden = up_weight.shape[2]
+    run = ways * (width // world)
+    if run % 16 or ways * 2 * hidden // world != width:
+        run = 0
+    each = 2 if run else 1
+    pieces = lambda v: (v[:each], v[each:])
+    along_seq = lambda v: swap(v.reshape(ways, -1, v.shape[-1]))
+    all_of = lambda v: jnp.sum(v.astype(F32), axis=0)
+
+    mixed0, dmid0, datt0, sums0, *grads = ffn(0, bounds[0], run, own, att, x, g, *weights)
+    g_up, g_down = pieces(grads)
+    up0, down0 = Shards(g_up, every), Shards(g_down, every[1:])
+    air1, (prev,) = launch([(up0, core), (down0, core)], (mixed0, dmid0, datt0, sums0))
+    mixed_s, dmid, d_att, sums2, *grads = ffn(
+        1, bounds[1], run, own, att, x, g, *weights, prev=prev
+    )
+    d_att, mixed_s, grads = settle(air1, d_att, mixed_s, grads)
+    g_up, g_down = pieces(grads)
+    up1, down1 = Shards(g_up, every), Shards(g_down, every[1:])
     back_m = back(pos_col, mixed_s)
     air2, (d_att, back_m) = launch(
-        [(up0, high_first[0]), (down0, low_first[0]), (up1, core), (down1, core), (wo, core)],
+        [(up0, high_first[0]), (down0, low_first[0]), (up1, core), (down1, core)],
         d_att,
         back_m,
     )
-    ret_m = swap(back_m.reshape(ways, SLOTS, width))
+    ret_m = along_seq(back_m)
     d_qkv = attn_bwd(per, qkv, d_att, lse)
     (d_qkv,) = settle(air2, d_qkv)
     for key in mids[1:]:
         air, (d_qkv,) = launch([(down0, key)], d_qkv)
         (d_qkv,) = settle(air, d_qkv)
-    air3, (d_qkv,) = launch(
-        [(up0, high_first[1]), (up1, high_first[0]), (down1, low_first[0]), (wo, low_first[0])],
-        d_qkv,
-    )
-    back_g, gin_s, sums1 = last(x, *d_qkv, qkv_weight, row(ln1_gain), dmid, pos_col)
-    back_g, d_qkv, sums1, ret_m = settle(air3, back_g, d_qkv, sums1, ret_m)
+    air3, (d_qkv,) = launch([(up0, high_first[1]), (up1, high_first[0])], d_qkv)
+    g_wa, g_wb = wgrad(run, own, first, *d_qkv, att, dmid)
+    wa, wb = Shards(g_wa, every), Shards(g_wb, every)
+    d_qkv, g_wa = settle(air3[:1], d_qkv, g_wa)
     for key in mids[1:]:
-        air, (d_qkv,) = launch([(down1, key), (up0, key)], d_qkv)
+        air, (d_qkv,) = launch([(up0, key)], d_qkv)
         (d_qkv,) = settle(air, d_qkv)
+    airc, (d_qkv, up0_all) = launch(
+        [(down1, low_first[0]), (wa, core), (wb, core)], d_qkv, up0.value
+    )
+    up0_all = along_seq(up0_all)
+    back_g, gin_s, vec = last(
+        x, *d_qkv, qkv_weight, row(ln1_gain), dmid, pos_col, sums2
+    )
+    back_g, vec, ret_m, up0_all = settle(air3[1:] + airc, back_g, vec, ret_m, up0_all)
+    for key in mids[1:]:
+        air, (back_g,) = launch([(down1, key)], back_g)
+        (back_g,) = settle(air, back_g)
     down = Joined(down0, down1)
-    vec = Whole(
-        jnp.concatenate(
-            [sums1[0:4], sums2[0:5], g_ub0.reshape(-1, width), g_ub1.reshape(-1, width)], axis=0
-        )
-    )
-    air4, (d_qkv, back_g) = launch(
-        [(up0, z0), (up1, high_first[1]), (down, top), (wo, low_first[1]), (vec, core)],
-        d_qkv,
-        back_g,
-    )
-    ret_g = swap(back_g.reshape(ways, SLOTS, width))
-    g_wa, g_wb = wgrad(first, *d_qkv)
-    g_wa, g_wb = settle(air4, g_wa, g_wb)
-    wa, wb = Shards(g_wa, every), Shards(g_wb, every)
+
+    air4, (back_g, vec) = launch(
+        [(up1, high_first[1]), (down, top), (wa, low_first[0]), (wb, high_first[0])], back_g, vec
+    )
+    ret_g = along_seq(back_g)
+    m_fast = choose(slot_col, ret_m.reshape(-1, width))
+    vec = vec + pass_on(vec, *core)
+    for key in low_first[:-1]:
+        vec = vec + pass_on(vec, *key)
+    vec, m_fast, ret_g = settle(air4, vec, m_fast, ret_g)
     for key in mids[1:]:
-        air, () = launch([(up1, key), (wo, low_first[low_first.index(key) + 1])])
+        air, () = launch([(up1, key)])
         settle(air)
-    air5, () = launch(
-        [(wa, core), (wb, core), (up0, z1), (up1, z0), (down, z0), (wo, z0), (vec, low_first[0])]
-    )
-    (ret_g,) = settle(air5, ret_g)
-    air6, () = launch(
-        [(wa, low_first[0]), (wb, high_first[0]), (up1, z1), (down, z1), (wo, z1)]
-        + [(vec, low_first[1])]
-    )
-    settle(air6)
-    air7, () = launch([(wa, low_first[1]), (wb, high_first[1]), (vec, z0)])
-    settle(air7)
+    air5, (vec, up1_all, ret_g) = launch(
+        [(wa, low_first[1]), (wb, high_first[1])], vec, up1.value, ret_g
+    )
+    up1_all = along_seq(up1_all)
+    i_fast = choose(slot_col, ret_g.reshape(-1, width))
+    vec = vec + pass_on(vec, *top)
+    vec, up1_all, i_fast = settle(air5, vec, up1_all, i_fast)
+    down_all = along_seq(down.value)
+    vec = vec + pass_on(vec, *z0)
     for lo_key, hi_key in zip(low_first[2:], high_first[2:]):
-        air, () = launch([(wa, lo_key), (wb, hi_key), (vec, lo_key)])
+        air, () = launch([(wa, lo_key), (wb, hi_key)])
         settle(air)
-    air8, () = launch([(wa, z0), (wb, z0), (vec, z1)])
-    settle(air8)
-    air9, () = launch([(wa, z1), (wb, z1)])
-    mixed_s, gin_s, ret_m, ret_g = settle(air9, mixed_s, gin_s, ret_m, ret_g)
-    flat2 = lambda r: r.reshape(-1, width)
+    down_all, vec, both = tie((down_all, vec, side(wa.value, wb.value)))
+    both = along_seq(both)
+    vec = vec + pass_on(vec, *z1)
+    up = jnp.stack([all_of(up0_all), all_of(up1_all)])
+    down = all_of(down_all)
+    up, down, vec, both, m_fast, i_fast, mixed_s, gin_s = tie(
+        (up, down, vec, both, m_fast, i_fast, mixed_s, gin_s)
+    )
+    both = all_of(both)
     mixed, grad_in = lax.cond(
         over,
-        lambda m, i, rm, rg, c: tuple(slow_out(v, *labels, ways, per) for v in (m, i)),
-        lambda m, i, rm, rg, c: (choose(c, flat2(rm)), choose(c, flat2(rg))),
+        lambda m, i, mf, gf: apart(slow_out(side(m, i), *labels, ways, per)),
+        lambda m, i, mf, gf: (mf, gf),
         mixed_s,
         gin_s,
-        ret_m,
-        ret_g,
-        slot_col,
+        m_fast,
+        i_fast,
     )
 
     piece = width // world
     me = lax.axis_index("dp") * ways + lax.axis_index("seq")
-    mine = lax.dynamic_slice_in_dim(vec.value[:9], me * piece, piece, 1)
-    flat = vec.value[9:].reshape(-1)
+    mine = lax.dynamic_slice_in_dim(vec, me * piece, piece, 1)
+    flat = vec[8:16].reshape(-1)
     ub_piece = flat.shape[0] // world
     return (
         mixed,
         grad_in,
+        mine[16],
+        mine[17],
+        both[:, : 3 * width],
+        mine[18],
+        mine[19],
+        both[:, 3 * width :],
+        mine[2],
         mine[0],
         mine[1],
-        jnp.concatenate([wa.value, wb.value], axis=1).astype(F32),
-        mine[2],
-        mine[3],
-        wo.value.astype(F32),
-        mine[6],
-        mine[4],
-        mine[5],
-        jnp.stack([up0.value, up1.value]).astype(F32),
+        up,
         lax.dynamic_slice_in_dim(flat, me * ub_piece, ub_piece, 0),
-        down.value.astype(F32),
-        mine[7:9],
+        down,
+        mine[3:5],
     )
 
 

time: 496 us -> 435 us (0.88)
  Pallas kernels: 214 us -> 191 us
  local copies, waits for them, and re-layouts: 47.2 us -> 26.1 us
  waiting for transfers between devices: 120 us -> 108 us
  loops' own time: 12.4 us -> 4.24 us
  starting transfers between devices: 51 us -> 56.9 us
    ppermute x37 -> x22, waiting for transfers between devices: 83.1 us -> 48.1 us  [pass_on(): return lax.ppermute(value, axis, [(i, i ^ 1 << bit) for i in range(n)])]
    all_to_all x4 -> x8, waiting for transfers between devices: 37.1 us -> 60.2 us  [swap(): lax.all_to_all(blocks, 'seq', split_axis=0, concat_axis=0, tiled=True)]
    all_to_all x4 -> x8, starting transfers between devices: 19.8 us -> 36.1 us  [swap(): lax.all_to_all(blocks, 'seq', split_axis=0, concat_axis=0, tiled=True)]
    squeeze x30 -> x10, local copies, waits for them, and re-layouts: 22.5 us -> 8.71 us  [cut(): take = lambda k: lax.dynamic_index_in_dim(parts, k, 1, keepdims=False)]
    pallas_call x5, Pallas kernels: 95.7 us -> 83.6 us  [the longest x2 64.9 us: ffn(): pl.pallas_call(functools.partial(ffn_kernel, expert, lo, hi, run), grid=(...]
    ppermute x37 -> x22, starting transfers between devices: 31.2 us -> 20.7 us  [pass_on(): return lax.ppermute(value, axis, [(i, i ^ 1 << bit) for i in range(n)])]
    another operation x3 -> x2, loops' own time: 12.4 us -> 4.24 us  [the longest x1 4.23 us: body(): lax.cond(over, lambda t, g, r, p: apart(slow_in(side(t, g), *labels, ways...]
    pallas_call x1, Pallas kernels: 28.5 us -> 21.5 us  [last(): pl.pallas_call(last_kernel, out_shape=(jax.ShapeDtypeStruct((col.shape[0]...]
  transfers between devices with their start and end apart: 41 -> 30, of which waited for: 13 -> 12; matrix products, arithmetic and copies ran while one was open for 8% -> 7% of each run, Pallas kernels for 31% -> 33%
where the time goes in v3:
time: 435 us; the launch traced here: 428 us
  Pallas kernels  191 us (44%)
  waiting for transfers between devices  108 us (25%)
  starting transfers between devices  56.9 us (13%)
  other arithmetic  39.3 us (9%)
  local copies, waits for them, and re-layouts  26.1 us (6%)
    pallas_call x2, Pallas kernels, ffn(): pl.pallas_call(functools.partial(ffn_kernel, expert, lo, hi, run), grid=(...  64.9 us
    all_to_all x8, waiting for transfers between devices, swap(): lax.all_to_all(blocks, 'seq', split_axis=0, concat_axis=0, tiled=True)  60.2 us
    ppermute x22, waiting for transfers between devices, pass_on(): return lax.ppermute(value, axis, [(i, i ^ 1 << bit) for i in range(n)])  48.1 us
    all_to_all x8, starting transfers between devices, swap(): lax.all_to_all(blocks, 'seq', split_axis=0, concat_axis=0, tiled=True)  36.1 us
    pallas_call x1, Pallas kernels, attn_bwd(): pl.pallas_call(functools.partial(attn_bwd_kernel, per), grid=(steps,), in...  27 us
    add x11, other arithmetic, add(): total = self.value + got  25.5 us
    pallas_call x1, Pallas kernels, last(): pl.pallas_call(last_kernel, out_shape=(jax.ShapeDtypeStruct((col.shape[0]...  21.5 us
    ppermute x22, starting transfers between devices, pass_on(): return lax.ppermute(value, axis, [(i, i ^ 1 << bit) for i in range(n)])  20.7 us
  transfers between devices with their start and end apart: 30, of which 12 were waited for; matrix products, arithmetic and copies ran while one was open for 7% of the time, Pallas kernels for 33%

profile of v3, /device:TPU:0, one launch (start us, length us, event | category | flops | bytes accessed | tf_op | source)
XLA Modules:
  0.0 428.1 jit_solution(8945875435207395040)
XLA Ops:
  0.6 5.8 %pack.1 = (bf16[4,288,768]{2,1,0:T(8,128)(2,1)}, s32[8,906]{1,0:T(8,128)}, s32[906,1]{1,0:T(8,128)}) custom-call(s32[1,906]{1,0:T(1,128)} %bitcast.133, s32[1,906]{1,0:T(1,128)} %bitcast.134, bf16[906,768]{1,0:T(8,128)(2,1)} %tok_ref.1), custom_call_target="tpu_custom_call" | custom-call | tf_op jit(solution)/shard_map/pack/pallas_call | solution.py:87
  6.5 6.3 %all-to-all-start.4 = ((bf16[4,288,768]{2,1,0:T(8,128)(2,1)}), bf16[4,288,768]{2,1,0:T(8,128)(2,1)S(1)}, u32[]{:S(2)}, u32[]{:S(2)}) async-start(bf16[4,288,768]{2,1,0:T(8,128)(2,1)} %get-tuple-element.190), calls=%async_computation.4 | async-start | bytes 3538944 | tf_op jit(solution)/shard_map/all_to_all | solution.py:222
  12.8 4.6 %pack_more.1 = bf16[4,288,768]{2,1,0:T(8,128)(2,1)} custom-call(s32[8,906]{1,0:T(8,128)} %get-tuple-element.194.row_ref, bf16[906,768]{1,0:T(8,128)(2,1)} %value_ref.1), custom_call_target="tpu_custom_call" | custom-call | flops 4809424896 | bytes 1048576 | tf_op jit(solution)/shard_map/pack_more/pallas_call | solution.py:107
  17.4 36.6 %all-to-all-done.4 = bf16[4,288,768]{2,1,0:T(8,128)(2,1)S(1)} async-done(((bf16[4,288,768]{2,1,0:T(8,128)(2,1)}), bf16[4,288,768]{2,1,0:T(8,128)(2,1)S(1)}, u32[]{:S(2)}, u32[]{:S(2)}) %all-to-all-start.4) | async-done | bytes 1769504 | tf_op jit(solution)/shard_map/all_to_all | solution.py:222
  57.2 7.3 %conditional.2 = ((bf16[928,768]{1,0:T(8,128)(2,1)}, bf16[928,768]{1,0:T(8,128)(2,1)})) conditional(s32[]{:T(128)} %bitcast.4, (s32[8,1152]{1,0:T(8,128)S(1)}, bf16[1152,768]{1,0:T(8,128)(2,1)S(1)}) %tuple.80, (s32[906]{0:T(1024)}, (), s32[906]{0:T(1024)S(1)}, s32[906]{0:T(1024)S(1)}, bf16[906,768]{1,0:T(8,128)(2,1)}, ...), branch_computations={%region_0.0_spmd, %region_1.4_spmd} | conditional | flops 7015282 | bytes 95208872 | solution.py:888
  57.2 3.1 place.1
  64.6 3.7 all-to-all-start.5
  72.5 12.7 %qkv.1 = (bf16[928,768]{1,0:T(8,128)(2,1)}, bf16[928,2304]{1,0:T(8,128)(2,1)}) custom-call(bf16[928,768]{1,0:T(8,128)(2,1)} %get-tuple-element.195.x_ref.refs_1_, f32[1,768]{1,0:T(1,128)} %reshape.188.gain_ref, f32[1,768]{1,0:T(1,128)} %reshape.189.shift_ref, bf16[768,2304]{1,0:T(8,128)(2,1)} %w_ref.3, f32[1,768]{1,0:T(1,128)} %reshape.190.qb_ref, ...), custom_call_target="tpu_custom_call" | custom-call | flops 9852420096 | bytes 1048576 | tf_op jit(solution)/shard_map/qkv/pallas_call | solution.py:301
  85.2 20.4 %attn_fwd.1 = (bf16[928,768]{1,0:T(8,128)(2,1)}, f32[6,8,1024]{2,1,0:T(8,128)}) custom-call(bf16[928,2304]{1,0:T(8,128)(2,1)} %get-tuple-element.196.q_ref.k_ref.v_ref, bf16[928,2304]{1,0:T(8,128)(2,1)} %get-tuple-element.196.q_ref.k_ref.v_ref, bf16[928,2304]{1,0:T(8,128)(2,1)} %get-tuple-element.196.q_ref.k_ref.v_ref), custom_call_target="tpu_custom_call" | custom-call | flops 11494490112 | bytes 1048576 | tf_op jit(solution)/shard_map/attn_fwd/pallas_call | solution.py:393
  105.7 3.4 all-to-all-done.5
  110.3 5.6 %place_or.1.refs_2_ = bf16[928,768]{1,0:T(8,128)(2,1)} custom-call(s32[1]{0:T(128)} %bitcast.7.flag_ref, s32[8,1152]{1,0:T(8,128)S(1)} %get-tuple-element.192.pos_ref, bf16[1152,768]{1,0:T(8,128)(2,1)} %bitcast.116, bf16[928,768]{1,0:T(8,128)(2,1)} %get-tuple-element.201.other_ref), custom_call_target="tpu_custom_call" | custom-call | tf_op jit(solution)/shard_map/place_or/pallas_call | solution.py:197
  115.9 31.5 %ffn0.1 = (bf16[416,768]{1,0:T(8,128)(2,1)}, bf16[416,768]{1,0:T(8,128)(2,1)}, bf16[416,768]{1,0:T(8,128)(2,1)}, f32[16,768]{1,0:T(8,128)}, bf16[384,3072]{1,0:T...) custom-call(s32[1]{0:T(128)} %bitcast.5.own_ref, ...), custom_call_target="tpu_custom_call" | custom-call | flops 35332816896 | bytes 1048576 | tf_op jit(solution)/shard_map/ffn0/pallas_call | solution.py:641
  147.9 33.5 %ffn1.1 = (bf16[928,768]{1,0:T(8,128)(2,1)S(1)}, bf16[928,768]{1,0:T(8,128)(2,1)}, bf16[928,768]{1,0:T(8,128)(2,1)}, f32[16,768]{1,0:T(8,128)}, bf16[384,3072]{1...) custom-call(s32[1]{0:T(128)} %bitcast.5.own_ref, ...), custom_call_target="tpu_custom_call" | custom-call | flops 43486543872 | bytes 1048576 | tf_op jit(solution)/shard_map/ffn1/pallas_call | solution.py:641
  182.9 3.0 add.155
  187.0 4.4 %back.1 = bf16[1152,768]{1,0:T(8,128)(2,1)} custom-call(s32[1152,1]{1,0:T(8,128)} %get-tuple-element.227.col_ref, bf16[928,768]{1,0:T(8,128)(2,1)S(1)} %get-tuple-element.311.value_ref), custom_call_target="tpu_custom_call" | custom-call | tf_op jit(solution)/shard_map/back/pallas_call | solution.py:779
  191.4 3.3 add.152
  197.7 1.5 collective-permute-start.2
  200.7 4.4 %all-to-all-start.6 = ((bf16[4,288,768]{2,1,0:T(8,128)(2,1)}), bf16[4,288,768]{2,1,0:T(8,128)(2,1)}, u32[]{:S(2)}, u32[]{:S(2)}) async-start(bf16[4,288,768]{2,1,0:T(8,128)(2,1)} %bitcast.115), calls=%async_computation.6 | async-start | bytes 3538944 | tf_op jit(solution)/shard_map/all_to_all | solution.py:222
  205.1 27.0 %attn_bwd.1 = (bf16[928,768]{1,0:T(8,128)(2,1)}, bf16[928,768]{1,0:T(8,128)(2,1)}, bf16[928,768]{1,0:T(8,128)(2,1)}) custom-call(bf16[928,2304]{1,0:T(8,128)(2,1)} %get-tuple-element.196.q_ref.k_ref.v_ref, bf16[928,2304]{1,0:T(8,128)(2,1)} %get-tuple-element.196.q_ref.k_ref.v_ref, bf16[928,2304]{1,0:T(8,128)(2,1)} %get-tuple-element.196.q_ref.k_ref.v_ref, ...), custom_call_target="tpu_custom_call" | custom-call | flops 14778630144 | bytes 1048576 | tf_op jit(solution)/shard_map/attn_bwd/pallas_call | solution.py:473
  232.1 3.7 add.158
  237.0 1.8 copy-done.6
  241.4 9.9 %wgrad.1 = (bf16[384,1536]{1,0:T(8,128)(2,1)}, bf16[384,1536]{1,0:T(8,128)(2,1)}, bf16[384,1536]{1,0:T(8,128)(2,1)}, bf16[384,1536]{1,0:T(8,128)(2,1)}) custom-call(s32[1]{0:T(128)} %bitcast.5.own_ref, bf16[928,768]{1,0:T(8,128)(2,1)} %get-tuple-element.247.first_ref, bf16[928,768]{1,0:T(8,128)(2,1)} %get-tuple-element.263.dq_ref, ...), custom_call_target="tpu_custom_call" | custom-call | flops 13136560128 | bytes 1048576 | tf_op jit(solution)/shard_map/wgrad/pallas_call | solution.py:741
  251.3 3.0 add.159
  255.5 1.9 fusion.16
  259.2 5.2 %all-to-all-start.7 = ((bf16[4,24,3072]{2,1,0:T(8,128)(2,1)}), bf16[4,24,3072]{2,1,0:T(8,128)(2,1)}, u32[]{:S(2)}, u32[]{:S(2)}) async-start(bf16[4,24,3072]{2,1,0:T(8,128)(2,1)} %bitcast.126), calls=%async_computation.7 | async-start | bytes 1179648 | tf_op jit(solution)/shard_map/all_to_all | solution.py:222
  264.4 21.5 %last.1 = (bf16[1152,768]{1,0:T(8,128)(2,1)}, bf16[928,768]{1,0:T(8,128)(2,1)}, f32[24,768]{1,0:T(8,128)}) custom-call(bf16[928,768]{1,0:T(8,128)(2,1)} %get-tuple-element.195.x_ref.refs_1_, bf16[928,768]{1,0:T(8,128)(2,1)} %get-tuple-element.263.dq_ref, bf16[928,768]{1,0:T(8,128)(2,1)} %get-tuple-element.264.dk_ref, ...), custom_call_target="tpu_custom_call" | custom-call | flops 9852420096 | bytes 1048576 | tf_op jit(solution)/shard_map/last/pallas_call | solution.py:760
  286.0 2.3 add.166
  290.3 1.7 add.162
  292.9 1.6 bitcast_add_fusion.3
  297.6 5.0 %all-to-all-start.8 = ((bf16[4,288,768]{2,1,0:T(8,128)(2,1)}), bf16[4,288,768]{2,1,0:T(8,128)(2,1)}, u32[]{:S(2)}, u32[]{:S(2)}) async-start(bf16[4,288,768]{2,1,0:T(8,128)(2,1)} %bitcast.130), calls=%async_computation.8 | async-start | bytes 3538944 | tf_op jit(solution)/shard_map/all_to_all | solution.py:222
  302.7 1.5 collective-permute-start.12
  309.1 1.6 collective-permute-start.16
  310.6 4.7 %choose.2 = bf16[906,768]{1,0:T(8,128)(2,1)} custom-call(s32[906,1]{1,0:T(8,128)} %get-tuple-element.285.col_ref, bf16[1152,768]{1,0:T(8,128)(2,1)} %bitcast.35.value_ref), custom_call_target="tpu_custom_call" | custom-call | tf_op jit(solution)/shard_map/choose/pallas_call | solution.py:213
  315.4 17.6 %collective-permute-done.16 = f32[24,768]{1,0:T(8,128)S(1)} collective-permute-done((f32[24,768]{1,0:T(8,128)S(1)}, f32[24,768]{1,0:T(8,128)S(1)}, u32[]{:S(2)}, u32[]{:S(2)}) %collective-permute-start.16) | collective-permute-done | bytes 73760 | tf_op jit(solution)/shard_map/ppermute | solution.py:797
  333.6 9.3 %collective-permute-done.14 = bf16[1,192,1536]{2,1,0:T(8,128)(2,1)} collective-permute-done((bf16[1,192,1536]{2,1,0:T(8,128)(2,1)}, bf16[1,192,1536]{2,1,0:T(8,128)(2,1)}, u32[]{:S(2)}, u32[]{:S(2)}) %collective-permute-start.14) | collective-permute-done | bytes 589856 | tf_op jit(solution)/shard_map/ppermute | solution.py:797
  343.8 2.2 fusion.15
  350.7 4.2 all-to-all-start.9
  354.9 3.3 bitcast_add_fusion
  358.2 12.2 %all-to-all-done.9 = bf16[4,24,3072]{2,1,0:T(8,128)(2,1)} async-done(((bf16[4,24,3072]{2,1,0:T(8,128)(2,1)}), bf16[4,24,3072]{2,1,0:T(8,128)(2,1)}, u32[]{:S(2)}, u32[]{:S(2)}) %all-to-all-start.9) | async-done | bytes 589856 | tf_op jit(solution)/shard_map/all_to_all | solution.py:222
  370.4 3.5 all-to-all-start.10
  373.9 1.6 collective-permute-start.17
  377.5 4.8 %choose.3 = bf16[906,768]{1,0:T(8,128)(2,1)} custom-call(s32[906,1]{1,0:T(8,128)} %get-tuple-element.285.col_ref, bf16[1152,768]{1,0:T(8,128)(2,1)} %bitcast.43.value_ref), custom_call_target="tpu_custom_call" | custom-call | tf_op jit(solution)/shard_map/choose/pallas_call | solution.py:213
  383.6 1.7 collective-permute-start.20
  387.2 7.0 %collective-permute-done.20 = f32[24,768]{1,0:T(8,128)S(1)} collective-permute-done((f32[24,768]{1,0:T(8,128)S(1)}, f32[24,768]{1,0:T(8,128)S(1)}, u32[]{:S(2)}, u32[]{:S(2)}) %collective-permute-start.20) | collective-permute-done | bytes 73760 | tf_op jit(solution)/shard_map/ppermute | solution.py:797
  394.8 7.1 %all-to-all-done.10 = bf16[4,192,768]{2,1,0:T(8,128)(2,1)S(1)} async-done(((bf16[4,192,768]{2,1,0:T(8,128)(2,1)}), bf16[4,192,768]{2,1,0:T(8,128)(2,1)S(1)}, u32[]{:S(2)}, u32[]{:S(2)}) %all-to-all-start.10) | async-done | bytes 1179680 | tf_op jit(solution)/shard_map/all_to_all | solution.py:222
  402.0 3.7 all-to-all-start.11
  409.0 3.0 collective-permute-start.21
  412.9 11.3 %collective-permute-done.21 = f32[24,768]{1,0:T(8,128)S(1)} collective-permute-done((f32[24,768]{1,0:T(8,128)S(1)}, f32[24,768]{1,0:T(8,128)S(1)}, u32[]{:S(2)}, u32[]{:S(2)}) %collective-permute-start.21) | collective-permute-done | bytes 73760 | tf_op jit(solution)/shard_map/ppermute | solution.py:797
  (160 shorter events, 52.8 us)
Async XLA Ops:
  6.5 47.5 %all-to-all-start.4 = ((bf16[4,288,768]{2,1,0:T(8,128)(2,1)}), bf16[4,288,768]{2,1,0:T(8,128)(2,1)S(1)}, u32[]{:S(2)}, u32[]{:S(2)}) async-start(bf16[4,288,768]{2,1,0:T(8,128)(2,1)} %get-tuple-element.190), calls=%async_computation.4 | async-start | bytes 3538944 | tf_op jit(solution)/shard_map/all_to_all | solution.py:222
  17.4 39.8 %copy-start.28 = (s32[906]{0:T(1024)S(1)}, s32[906]{0:T(1024)}, u32[]{:S(2)}) copy-start(s32[906]{0:T(1024)} %param.27) | copy-start | bytes 10876
  17.4 39.8 %copy-start.30 = (s32[906]{0:T(1024)S(1)}, s32[906]{0:T(1024)}, u32[]{:S(2)}) copy-start(s32[906]{0:T(1024)} %param.28) | copy-start | bytes 10876
  64.6 5.0 %copy-start.34 = (f32[768]{0:T(1024)S(1)}, f32[768]{0:T(1024)}, u32[]{:S(2)}) copy-start(f32[768]{0:T(1024)} %param.32) | copy-start | bytes 9220
  64.6 5.6 %copy-start.35 = (f32[768]{0:T(1024)S(1)}, f32[768]{0:T(1024)}, u32[]{:S(2)}) copy-start(f32[768]{0:T(1024)} %param.33) | copy-start | bytes 9220
  64.6 6.1 %copy-start.36 = (f32[768]{0:T(1024)S(1)}, f32[768]{0:T(1024)}, u32[]{:S(2)}) copy-start(f32[768]{0:T(1024)} %param.35) | copy-start | bytes 9220
  64.6 6.7 %copy-start.37 = (f32[768]{0:T(1024)S(1)}, f32[768]{0:T(1024)}, u32[]{:S(2)}) copy-start(f32[768]{0:T(1024)} %param.36) | copy-start | bytes 9220
  64.6 7.2 %copy-start.38 = (f32[768]{0:T(1024)S(1)}, f32[768]{0:T(1024)}, u32[]{:S(2)}) copy-start(f32[768]{0:T(1024)} %param.37) | copy-start | bytes 9220
  64.6 44.4 %all-to-all-start.5 = ((bf16[4,288,768]{2,1,0:T(8,128)(2,1)}), bf16[4,288,768]{2,1,0:T(8,128)(2,1)S(1)}, u32[]{:S(2)}, u32[]{:S(2)}) async-start(bf16[4,288,768]{2,1,0:T(8,128)(2,1)} %pack_more.1), calls=%async_computation.5 | async-start | bytes 3538944 | tf_op jit(solution)/shard_map/all_to_all | solution.py:222
  110.3 5.6 %copy-start.39 = (bf16[928,768]{1,0:T(8,128)(2,1)S(1)}, bf16[928,768]{1,0:T(8,128)(2,1)}, u32[]{:S(2)}) copy-start(bf16[928,768]{1,0:T(8,128)(2,1)} %get-tuple-element.195.x_ref.refs_1_) | copy-start | bytes 4276228
  147.4 34.1 %collective-permute-start = (bf16[384,3072]{1,0:T(8,128)(2,1)}, bf16[384,3072]{1,0:T(8,128)(2,1)S(1)}, u32[]{:S(2)}, u32[]{:S(2)}) collective-permute-start(bf16[384,3072]{1,0:T(8,128)(2,1)} %get-tuple-element.209), channel_id=1, source_target_pairs={{0,4},{4,0},{8,12},{12,8},{16,20},{20,16},{24,28},{28,24},{1,5},{5... | collective-permute-start | bytes 7077896 | tf_op jit(solution)/shard_map/ppermute | solution.py:797
  147.4 34.0 %collective-permute-start.1 = (bf16[1536,768]{1,0:T(8,128)(2,1)}, bf16[1536,768]{1,0:T(8,128)(2,1)}, u32[]{:S(2)}, u32[]{:S(2)}) collective-permute-start(bf16[1536,768]{1,0:T(8,128)(2,1)} %get-tuple-element.210), channel_id=1, source_target_pairs={{0,4},{4,0},{8,12},{12,8},{16,20},{20,16},{24,28},{28,24},{1,5},{5... | collective-permute-start | bytes 7077896 | tf_op jit(solution)/shard_map/ppermute | solution.py:797
  181.4 5.6 %copy-start.8 = (bf16[928,768]{1,0:T(8,128)(2,1)}, bf16[928,768]{1,0:T(8,128)(2,1)S(1)}, u32[]{:S(2)}) copy-start(bf16[928,768]{1,0:T(8,128)(2,1)S(1)} %get-tuple-element.311.value_ref) | copy-start | bytes 4276228
  197.2 34.9 %collective-permute-start.4 = (bf16[384,3072]{1,0:T(8,128)(2,1)}, bf16[384,3072]{1,0:T(8,128)(2,1)}, u32[]{:S(2)}, u32[]{:S(2)}) collective-permute-start(bf16[384,3072]{1,0:T(8,128)(2,1)} %get-tuple-element.231), channel_id=1, source_target_pairs={{0,4},{4,0},{8,12},{12,8},{16,20},{20,16},{24,28},{28,24},{1,5},{5... | collective-permute-start | bytes 7077896 | tf_op jit(solution)/shard_map/ppermute | solution.py:797
  197.3 34.8 %collective-permute-start.5 = (bf16[1536,768]{1,0:T(8,128)(2,1)}, bf16[1536,768]{1,0:T(8,128)(2,1)}, u32[]{:S(2)}, u32[]{:S(2)}) collective-permute-start(bf16[1536,768]{1,0:T(8,128)(2,1)} %get-tuple-element.232), channel_id=1, source_target_pairs={{0,4},{4,0},{8,12},{12,8},{16,20},{20,16},{24,28},{28,24},{1,5},{5... | collective-permute-start | bytes 7077896 | tf_op jit(solution)/shard_map/ppermute | solution.py:797
  197.7 34.4 %collective-permute-start.2 = (bf16[1,192,3072]{2,1,0:T(8,128)(2,1)}, bf16[1,192,3072]{2,1,0:T(8,128)(2,1)}, u32[]{:S(2)}, u32[]{:S(2)}) collective-permute-start(bf16[1,192,3072]{2,1,0:T(8,128)(2,1)} %dynamic-slice_bitcast_fusion.3), channel_id=1, source_target_pairs={{0,16},{4,20},{8,24},{12,28},{16,0},{20,4},{24,8},{28,12},{1,17},{... | collective-permute-start | bytes 3538952 | tf_op jit(solution)/shard_map/ppermute | solution.py:797
  199.2 32.9 %collective-permute-start.3 = (bf16[1,768,768]{2,1,0:T(8,128)(2,1)}, bf16[1,768,768]{2,1,0:T(8,128)(2,1)S(1)}, u32[]{:S(2)}, u32[]{:S(2)}) collective-permute-start(bf16[1,768,768]{2,1,0:T(8,128)(2,1)} %dynamic-slice_bitcast_fusion.2), channel_id=1, source_target_pairs={{0,8},{4,12},{8,0},{12,4},{16,24},{20,28},{24,16},{28,20},{1,9},{5... | collective-permute-start | bytes 3538952 | tf_op jit(solution)/shard_map/ppermute | solution.py:797
  200.7 58.5 %all-to-all-start.6 = ((bf16[4,288,768]{2,1,0:T(8,128)(2,1)}), bf16[4,288,768]{2,1,0:T(8,128)(2,1)}, u32[]{:S(2)}, u32[]{:S(2)}) async-start(bf16[4,288,768]{2,1,0:T(8,128)(2,1)} %bitcast.115), calls=%async_computation.6 | async-start | bytes 3538944 | tf_op jit(solution)/shard_map/all_to_all | solution.py:222
  240.3 15.2 %collective-permute-start.7 = (bf16[1,96,3072]{2,1,0:T(8,128)(2,1)S(1)}, bf16[1,96,3072]{2,1,0:T(8,128)(2,1)}, u32[]{:S(2)}, u32[]{:S(2)}) collective-permute-start(bf16[1,96,3072]{2,1,0:T(8,128)(2,1)S(1)} %dynamic-slice_bitcast_fusion.7), channel_id=1, source_target_pairs={{0,8},{4,12},{8,0},{12,4},{16,24},{20,28},{24,16},{28,20},{1,9},{5... | collective-permute-start | bytes 1769480 | tf_op jit(solution)/shard_map/ppermute | solution.py:797
  240.9 45.0 %collective-permute-start.6 = (bf16[1,192,3072]{2,1,0:T(8,128)(2,1)}, bf16[1,192,3072]{2,1,0:T(8,128)(2,1)}, u32[]{:S(2)}, u32[]{:S(2)}) collective-permute-start(bf16[1,192,3072]{2,1,0:T(8,128)(2,1)} %dynamic-slice_bitcast_fusion.1), channel_id=1, source_target_pairs={{0,16},{4,20},{8,24},{12,28},{16,0},{20,4},{24,8},{28,12},{1,17},{... | collective-permute-start | bytes 3538952 | tf_op jit(solution)/shard_map/ppermute | solution.py:797
  257.4 28.5 %collective-permute-start.10 = (bf16[384,1536]{1,0:T(8,128)(2,1)}, bf16[384,1536]{1,0:T(8,128)(2,1)}, u32[]{:S(2)}, u32[]{:S(2)}) collective-permute-start(bf16[384,1536]{1,0:T(8,128)(2,1)} %get-tuple-element.262), channel_id=1, source_target_pairs={{0,4},{4,0},{8,12},{12,8},{16,20},{20,16},{24,28},{28,24},{1,5},{5... | collective-permute-start | bytes 3538952 | tf_op jit(solution)/shard_map/ppermute | solution.py:797
  257.4 28.6 %collective-permute-start.8 = (bf16[1,768,768]{2,1,0:T(8,128)(2,1)}, bf16[1,768,768]{2,1,0:T(8,128)(2,1)S(1)}, u32[]{:S(2)}, u32[]{:S(2)}) collective-permute-start(bf16[1,768,768]{2,1,0:T(8,128)(2,1)} %dynamic-slice_bitcast_fusion), channel_id=1, source_target_pairs={{0,8},{4,12},{8,0},{12,4},{16,24},{20,28},{24,16},{28,20},{1,9},{5... | collective-permute-start | bytes 3538952 | tf_op jit(solution)/shard_map/ppermute | solution.py:797
  259.0 27.1 %collective-permute-start.9 = (bf16[384,1536]{1,0:T(8,128)(2,1)}, bf16[384,1536]{1,0:T(8,128)(2,1)}, u32[]{:S(2)}, u32[]{:S(2)}) collective-permute-start(bf16[384,1536]{1,0:T(8,128)(2,1)} %get-tuple-element.261), channel_id=1, source_target_pairs={{0,4},{4,0},{8,12},{12,8},{16,20},{20,16},{24,28},{28,24},{1,5},{5... | collective-permute-start | bytes 3538952 | tf_op jit(solution)/shard_map/ppermute | solution.py:797
  259.2 26.7 %all-to-all-start.7 = ((bf16[4,24,3072]{2,1,0:T(8,128)(2,1)}), bf16[4,24,3072]{2,1,0:T(8,128)(2,1)}, u32[]{:S(2)}, u32[]{:S(2)}) async-start(bf16[4,24,3072]{2,1,0:T(8,128)(2,1)} %bitcast.126), calls=%async_computation.7 | async-start | bytes 1179648 | tf_op jit(solution)/shard_map/all_to_all | solution.py:222
  297.6 46.2 %all-to-all-start.8 = ((bf16[4,288,768]{2,1,0:T(8,128)(2,1)}), bf16[4,288,768]{2,1,0:T(8,128)(2,1)}, u32[]{:S(2)}, u32[]{:S(2)}) async-start(bf16[4,288,768]{2,1,0:T(8,128)(2,1)} %bitcast.130), calls=%async_computation.8 | async-start | bytes 3538944 | tf_op jit(solution)/shard_map/all_to_all | solution.py:222
  302.7 40.2 %collective-permute-start.12 = (bf16[768,768]{1,0:T(8,128)(2,1)}, bf16[768,768]{1,0:T(8,128)(2,1)}, u32[]{:S(2)}, u32[]{:S(2)}) collective-permute-start(bf16[768,768]{1,0:T(8,128)(2,1)} %select_bitcast_fusion), channel_id=1, source_target_pairs={{0,16},{4,20},{8,24},{12,28},{16,0},{20,4},{24,8},{28,12},{1,17},{... | collective-permute-start | bytes 3538952 | tf_op jit(solution)/shard_map/ppermute | solution.py:797
  304.2 29.4 %collective-permute-start.11 = (bf16[1,96,3072]{2,1,0:T(8,128)(2,1)}, bf16[1,96,3072]{2,1,0:T(8,128)(2,1)}, u32[]{:S(2)}, u32[]{:S(2)}) collective-permute-start(bf16[1,96,3072]{2,1,0:T(8,128)(2,1)} %dynamic-slice_bitcast_fusion.6), channel_id=1, source_target_pairs={{0,8},{4,12},{8,0},{12,4},{16,24},{20,28},{24,16},{28,20},{1,9},{5... | collective-permute-start | bytes 1769480 | tf_op jit(solution)/shard_map/ppermute | solution.py:797
  305.7 28.0 %collective-permute-start.13 = (bf16[2,96,1536]{2,1,0:T(8,128)(2,1)}, bf16[2,96,1536]{2,1,0:T(8,128)(2,1)}, u32[]{:S(2)}, u32[]{:S(2)}) collective-permute-start(bf16[2,96,1536]{2,1,0:T(8,128)(2,1)} %dynamic-slice_bitcast_fusion.5), channel_id=1, source_target_pairs={{0,8},{4,12},{8,0},{12,4},{16,24},{20,28},{24,16},{28,20},{1,9},{5... | collective-permute-start | bytes 1769480 | tf_op jit(solution)/shard_map/ppermute | solution.py:797
  306.2 36.7 %collective-permute-start.14 = (bf16[1,192,1536]{2,1,0:T(8,128)(2,1)}, bf16[1,192,1536]{2,1,0:T(8,128)(2,1)}, u32[]{:S(2)}, u32[]{:S(2)}) collective-permute-start(bf16[1,192,1536]{2,1,0:T(8,128)(2,1)} %dynamic-slice_bitcast_fusion.4), channel_id=1, source_target_pairs={{0,16},{4,20},{8,24},{12,28},{16,0},{20,4},{24,8},{28,12},{1,17},{... | collective-permute-start | bytes 1769480 | tf_op jit(solution)/shard_map/ppermute | solution.py:797
  306.7 1.5 collective-permute-start.15
  309.1 23.9 %collective-permute-start.16 = (f32[24,768]{1,0:T(8,128)S(1)}, f32[24,768]{1,0:T(8,128)S(1)}, u32[]{:S(2)}, u32[]{:S(2)}) collective-permute-start(f32[24,768]{1,0:T(8,128)S(1)} %add.167), channel_id=1, source_target_pairs={{0,8},{4,12},{8,0},{12,4},{16,24},{20,28},{24,16},{28,20},{1,9},{5... | collective-permute-start | bytes 221192 | tf_op jit(solution)/shard_map/ppermute | solution.py:797
  350.7 19.7 %all-to-all-start.9 = ((bf16[4,24,3072]{2,1,0:T(8,128)(2,1)}), bf16[4,24,3072]{2,1,0:T(8,128)(2,1)}, u32[]{:S(2)}, u32[]{:S(2)}) async-start(bf16[4,24,3072]{2,1,0:T(8,128)(2,1)} %bitcast.127), calls=%async_computation.9 | async-start | bytes 1179648 | tf_op jit(solution)/shard_map/all_to_all | solution.py:222
  358.1 15.7 %copy-start.27 = (bf16[1,96,1536]{2,1,0:T(8,128)(2,1)S(1)}, bf16[1,96,1536]{2,1,0:T(8,128)(2,1)}, u32[]{:S(2)}) copy-start(bf16[1,96,1536]{2,1,0:T(8,128)(2,1)} %constant_dynamic-slice_fusion.1) | copy-start | bytes 884740
  358.1 17.3 %copy-start.26 = (bf16[1,96,1536]{2,1,0:T(8,128)(2,1)S(1)}, bf16[1,96,1536]{2,1,0:T(8,128)(2,1)}, u32[]{:S(2)}) copy-start(bf16[1,96,1536]{2,1,0:T(8,128)(2,1)} %dynamic-slice_bitcast_fusion.8) | copy-start | bytes 884740
  358.2 18.8 %copy-start.24 = (f32[24,768]{1,0:T(8,128)S(1)}, f32[24,768]{1,0:T(8,128)}, u32[]{:S(2)}) copy-start(f32[24,768]{1,0:T(8,128)} %add.168) | copy-start | bytes 221188
  370.4 31.6 %all-to-all-start.10 = ((bf16[4,192,768]{2,1,0:T(8,128)(2,1)}), bf16[4,192,768]{2,1,0:T(8,128)(2,1)S(1)}, u32[]{:S(2)}, u32[]{:S(2)}) async-start(bf16[4,192,768]{2,1,0:T(8,128)(2,1)} %bitcast.125), calls=%async_computation.10 | async-start | bytes 2359296 | tf_op jit(solution)/shard_map/all_to_all | solution.py:222
  373.9 9.7 %collective-permute-start.17 = (bf16[1,96,1536]{2,1,0:T(8,128)(2,1)S(1)}, bf16[1,96,1536]{2,1,0:T(8,128)(2,1)S(1)}, u32[]{:S(2)}, u32[]{:S(2)}) collective-permute-start(bf16[1,96,1536]{2,1,0:T(8,128)(2,1)S(1)} %copy-done.27), channel_id=1, source_target_pairs={{0,16},{4,20},{8,24},{12,28},{16,0},{20,4},{24,8},{28,12},{1,17},{... | collective-permute-start | bytes 884744 | tf_op jit(solution)/shard_map/ppermute | solution.py:797
  375.5 8.1 %collective-permute-start.18 = (bf16[1,96,1536]{2,1,0:T(8,128)(2,1)S(1)}, bf16[1,96,1536]{2,1,0:T(8,128)(2,1)}, u32[]{:S(2)}, u32[]{:S(2)}) collective-permute-start(bf16[1,96,1536]{2,1,0:T(8,128)(2,1)S(1)} %copy-done.26), channel_id=1, source_target_pairs={{0,8},{4,12},{8,0},{12,4},{16,24},{20,28},{24,16},{28,20},{1,9},{5... | collective-permute-start | bytes 884744 | tf_op jit(solution)/shard_map/ppermute | solution.py:797
  376.9 6.6 %collective-permute-start.19 = (f32[24,768]{1,0:T(8,128)S(1)}, f32[24,768]{1,0:T(8,128)S(1)}, u32[]{:S(2)}, u32[]{:S(2)}) collective-permute-start(f32[24,768]{1,0:T(8,128)S(1)} %copy-done.24), channel_id=1, source_target_pairs={{0,16},{4,20},{8,24},{12,28},{16,0},{20,4},{24,8},{28,12},{1,17},{... | collective-permute-start | bytes 221192 | tf_op jit(solution)/shard_map/ppermute | solution.py:797
  377.5 7.9 %copy-start.20 = (bf16[1,192,1536]{2,1,0:T(8,128)(2,1)S(1)}, bf16[1,192,1536]{2,1,0:T(8,128)(2,1)}, u32[]{:S(2)}) copy-start(bf16[1,192,1536]{2,1,0:T(8,128)(2,1)} %copy-done.19) | copy-start | bytes 1769476
  377.5 7.9 %copy-start.22 = (bf16[2,96,1536]{2,1,0:T(8,128)(2,1)S(1)}, bf16[2,96,1536]{2,1,0:T(8,128)(2,1)}, u32[]{:S(2)}) copy-start(bf16[2,96,1536]{2,1,0:T(8,128)(2,1)} %copy-done.21) | copy-start | bytes 1769476
  383.6 10.6 %collective-permute-start.20 = (f32[24,768]{1,0:T(8,128)S(1)}, f32[24,768]{1,0:T(8,128)S(1)}, u32[]{:S(2)}, u32[]{:S(2)}) collective-permute-start(f32[24,768]{1,0:T(8,128)S(1)} %add.172), channel_id=1, source_target_pairs={{0,1},{1,0},{2,3},{3,2},{4,5},{5,4},{6,7},{7,6},{8,9},{9,8},{10,11... | collective-permute-start | bytes 221192 | tf_op jit(solution)/shard_map/ppermute | solution.py:797
  402.0 22.3 %all-to-all-start.11 = ((bf16[4,24,3072]{2,1,0:T(8,128)(2,1)}), bf16[4,24,3072]{2,1,0:T(8,128)(2,1)S(1)}, u32[]{:S(2)}, u32[]{:S(2)}) async-start(bf16[4,24,3072]{2,1,0:T(8,128)(2,1)} %bitcast.50), calls=%async_computation.11 | async-start | bytes 1179648 | tf_op jit(solution)/shard_map/all_to_all | solution.py:222
  409.0 16.8 %copy-start = (s32[906]{0:T(1024)S(1)}, s32[906]{0:T(1024)}, u32[]{:S(2)}) copy-start(s32[906]{0:T(1024)} %constant.179.clone) | copy-start | bytes 10876
  409.0 16.8 %copy-start.9 = (bf16[928,768]{1,0:T(8,128)(2,1)S(1)}, bf16[928,768]{1,0:T(8,128)(2,1)}, u32[]{:S(2)}) copy-start(bf16[928,768]{1,0:T(8,128)(2,1)} %copy-done.8) | copy-start | bytes 4276228
  409.0 16.8 %copy-start.29 = (s32[906]{0:T(1024)S(1)}, s32[906]{0:T(1024)}, u32[]{:S(2)}) copy-start(s32[906]{0:T(1024)} %param.27) | copy-start | bytes 10876
  409.0 16.8 %copy-start.31 = (s32[906]{0:T(1024)S(1)}, s32[906]{0:T(1024)}, u32[]{:S(2)}) copy-start(s32[906]{0:T(1024)} %param.28) | copy-start | bytes 10876
  409.0 15.3 %collective-permute-start.21 = (f32[24,768]{1,0:T(8,128)S(1)}, f32[24,768]{1,0:T(8,128)S(1)}, u32[]{:S(2)}, u32[]{:S(2)}) collective-permute-start(f32[24,768]{1,0:T(8,128)S(1)} %copy-done.25), channel_id=1, source_target_pairs={{0,2},{1,3},{2,0},{3,1},{4,6},{5,7},{6,4},{7,5},{8,10},{9,11},{10,... | collective-permute-start | bytes 221192 | tf_op jit(solution)/shard_map/ppermute | solution.py:797
  (22 other events, 59.1 us)

commit v4 on v3

--- a/solution.py
+++ b/solution.py
@@ -16,7 +16,7 @@
 SEGS = CAPTIONS + 1
 IMG = 208
 CAP = CAPTIONS * CAP_LEN
-SLOTS = 288
+SLOTS = 272
 ROOM = SLOTS - 1
 EPS = 1e-05
 F32 = jnp.float32
@@ -504,10 +504,12 @@
     up_ref, ub_ref, down_ref, db_ref = refs[7:11]
     refs = refs[11:]
     if lo:
-        mixed0_ref, dmid0_ref, datt0_ref, sums0_ref = refs[:4]
-        refs = refs[4:]
+        mixed0_ref, dmid0_ref, datt0_ref, sums0_ref, col_ref = refs[:5]
+        refs = refs[5:]
     mixed_ref, dmid_ref, datt_ref, sums_ref = refs[:4]
     refs = refs[4:]
+    if lo:
+        back_ref, refs = refs[0], refs[1:]
     each = 2 if run else 1
     gup_refs, gdown_refs = refs[:each], refs[each : 2 * each]
     refs = refs[2 * each :]
@@ -609,6 +611,7 @@
             mixed_ref[:lo, :] = mixed0_ref[...]
             dmid_ref[:lo, :] = dmid0_ref[...]
             datt_ref[:lo, :] = datt0_ref[...]
+            back_ref[...] = give_back(col_ref, mixed_ref)
             datt_ref[part, :] = dot_nt(dmid_ref[part, :], wo_ref[...]).astype(BF16)
         else:
             datt_ref[...] = dot_nt(dmid_ref[...], wo_ref[...]).astype(BF16)
@@ -629,12 +632,14 @@
     out_specs = (
         [full(done, width)] * 3
         + [full(16, width)]
+        + [full(p.shape[0], width) for p in prev[4:]]
         + [pl.BlockSpec((width // each, chunk), lambda j: (0, j))] * each
         + [pl.BlockSpec((chunk, width), lambda j: (j // each, 0))] * each
     )
     out_shape = (
         [shape((done, width), BF16)] * 3
         + [shape((16, width), F32)]
+        + [shape((p.shape[0], width), BF16) for p in prev[4:]]
         + [shape((width // each, hidden), BF16)] * each
         + [shape((hidden // each, width), BF16)] * each
     )
@@ -771,19 +776,6 @@
     )(x, dq, dk, dv, w, gain, dmid, col, sums)
 
 
-def back_kernel(col_ref, value_ref, out_ref):
-    out_ref[...] = give_back(col_ref, value_ref)
-
-
-def back(col, value):
-    return pl.pallas_call(
-        back_kernel,
-        out_shape=jax.ShapeDtypeStruct((col.shape[0], value.shape[1]), BF16),
-        compiler_params=params(BIG),
-        name="back",
-    )(col, value)
-
-
 def bits_of(axis):
     return [(axis, b) for b in reversed(range(lax.axis_size(axis).bit_length() - 1))]
 
@@ -800,41 +792,61 @@
 tie = lax.optimization_barrier
 
 
+class Term:
+    def __init__(self, value, bits):
+        self.value, self.bits = value, bits
+
+    def rows(self, fixed):
+        rows, cols = self.value.shape
+        count = len(self.bits)
+        parts = self.value.reshape((2,) * count + (rows >> count, cols))
+        zero = jnp.int32(0)
+        start = [fixed.get(b, zero) for b in self.bits] + [zero, zero]
+        sizes = [1 if b in fixed else 2 for b in self.bits] + list(parts.shape[count:])
+        return lax.dynamic_slice(parts, start, sizes).reshape(-1, cols).astype(F32)
+
+
 class Shards:
-    def __init__(self, values, left):
-        self.ready = values if len(values) == 2 else None
-        self.value, self.left = values[0], list(left)
+    def __init__(self, values, bits):
+        self.bits, self.fixed = list(bits), {}
+        self.ready = values[1] if len(values) == 2 else None
+        start = self.bits[:]
+        if self.ready is not None:
+            start.remove(core_bit())
+        self.terms = [Term(values[0], start)]
+
+    def total(self, **extra):
+        return sum(t.rows({**self.fixed, **extra.get("more", {})}) for t in self.terms)
 
     def cut(self, key):
-        if self.ready:
-            send, self.ready = self.ready[1], None
-            self.left.remove(key)
-            return send
-        above = 1 << self.left.index(key)
-        rows, cols = self.value.shape
-        parts = self.value.reshape(above, 2, rows // (2 * above), cols)
-        own = pair_bit(*key)
-        take = lambda k: lax.dynamic_index_in_dim(parts, k, 1, keepdims=False)
-        self.left.remove(key)
-        self.value = take(own)
-        return take(1 - own)
+        if self.ready is not None:
+            send, self.ready = self.ready, None
+        else:
+            send = self.total(more={key: 1 - pair_bit(*key)}).astype(BF16)
+            self.fixed[key] = pair_bit(*key)
+        self.bits.remove(key)
+        return send
 
     def add(self, got):
-        total = self.value + got
-        self.value = total.reshape(-1, total.shape[-1])
+        self.terms.append(Term(got, self.bits[:]))
 
 
 class Joined(Shards):
     def __init__(self, first, second):
-        self.ready = None
-        self.pair, self.left = (first.value, second.value), list(first.left)
+        self.pair, self.bits, self.terms = (first, second), first.bits, []
 
     def cut(self, key):
-        if key in self.left:
-            return super().cut(key)
-        own = pair_bit(*key) == 0
-        self.value = jnp.where(own, *self.pair)
-        return jnp.where(own, *self.pair[::-1])
+        self.low = pair_bit(*key) == 0
+        first, second = (s.total() for s in self.pair)
+        return jnp.where(self.low, second, first).astype(BF16)
+
+    def total(self):
+        first, second = (s.total() for s in self.pair)
+        return jnp.where(self.low, first, second) + self.terms[0].value.astype(F32)
+
+
+def core_bit():
+    return ("dp", 0)
 
 
 def launch(moves, *tied):
@@ -880,7 +892,12 @@
     labels = (group_ids, segment_ids)
     send_t, places, slot_col = pack(ways, per, group_ids, segment_ids, tokens)
     recv_t = swap(send_t).reshape(ways * SLOTS, width)
+    vectors = [row(v) for v in (ln1_gain, ln1_bias, q_bias, v_bias, out_bias, ln2_gain, ln2_bias)]
+    recv_t, vectors = tie((recv_t, vectors))
+    ln1_gain, ln1_bias, q_bias, v_bias, out_bias, ln2_gain, ln2_bias = vectors
     send_g = pack_more(ways, places, grad_out)
+    recv_t, send_g = tie((recv_t, send_g))
+    recv_g = swap(send_g).reshape(ways * SLOTS, width)
     pos_row, pos_col, flag = index(ways, per, recv_t)
     over = flag[0, 0] > 0.5
     side = lambda a, b: jnp.concatenate([a, b], axis=1)
@@ -894,8 +911,6 @@
         recv_t,
         pos_row,
     )
-    x, send_g = tie((x, send_g))
-    recv_g = swap(send_g).reshape(ways * SLOTS, width)
     first, qkv = qkv_call(
         x, row(ln1_gain), row(ln1_bias), qkv_weight, row(q_bias), row(v_bias)
     )
@@ -922,18 +937,18 @@
     pieces = lambda v: (v[:each], v[each:])
     along_seq = lambda v: swap(v.reshape(ways, -1, v.shape[-1]))
     all_of = lambda v: jnp.sum(v.astype(F32), axis=0)
+    whole = lambda s: s.total().astype(BF16)
 
     mixed0, dmid0, datt0, sums0, *grads = ffn(0, bounds[0], run, own, att, x, g, *weights)
     g_up, g_down = pieces(grads)
     up0, down0 = Shards(g_up, every), Shards(g_down, every[1:])
     air1, (prev,) = launch([(up0, core), (down0, core)], (mixed0, dmid0, datt0, sums0))
-    mixed_s, dmid, d_att, sums2, *grads = ffn(
-        1, bounds[1], run, own, att, x, g, *weights, prev=prev
-    )
-    d_att, mixed_s, grads = settle(air1, d_att, mixed_s, grads)
+    mixed_s, dmid, d_att, sums2, back_m, *grads = ffn(
+        1, bounds[1], run, own, att, x, g, *weights, prev=prev + (pos_col,)
+    )
+    d_att, back_m, grads = settle(air1, d_att, back_m, grads)
     g_up, g_down = pieces(grads)
     up1, down1 = Shards(g_up, every), Shards(g_down, every[1:])
-    back_m = back(pos_col, mixed_s)
     air2, (d_att, back_m) = launch(
         [(up0, high_first[0]), (down0, low_first[0]), (up1, core), (down1, core)],
         d_att,
@@ -953,7 +968,7 @@
         air, (d_qkv,) = launch([(up0, key)], d_qkv)
         (d_qkv,) = settle(air, d_qkv)
     airc, (d_qkv, up0_all) = launch(
-        [(down1, low_first[0]), (wa, core), (wb, core)], d_qkv, up0.value
+        [(down1, low_first[0]), (wa, core), (wb, core)], d_qkv, whole(up0)
     )
     up0_all = along_seq(up0_all)
     back_g, gin_s, vec = last(
@@ -973,31 +988,34 @@
     vec = vec + pass_on(vec, *core)
     for key in low_first[:-1]:
         vec = vec + pass_on(vec, *key)
-    vec, m_fast, ret_g = settle(air4, vec, m_fast, ret_g)
+    (m_fast,) = settle(air4[1:2], m_fast)
+    down_in = whole(down)
+    vec, down_in = settle(air4[:1] + air4[2:], vec, down_in)
     for key in mids[1:]:
         air, () = launch([(up1, key)])
         settle(air)
-    air5, (vec, up1_all, ret_g) = launch(
-        [(wa, low_first[1]), (wb, high_first[1])], vec, up1.value, ret_g
-    )
-    up1_all = along_seq(up1_all)
+    air5, (vec, down_in) = launch([(wa, low_first[1]), (wb, high_first[1])], vec, down_in)
+    ret_g, down_in = tie((ret_g, down_in))
+    down_all = along_seq(down_in)
     i_fast = choose(slot_col, ret_g.reshape(-1, width))
     vec = vec + pass_on(vec, *top)
-    vec, up1_all, i_fast = settle(air5, vec, up1_all, i_fast)
-    down_all = along_seq(down.value)
     vec = vec + pass_on(vec, *z0)
+    vec, i_fast = settle(air5, vec, i_fast)
     for lo_key, hi_key in zip(low_first[2:], high_first[2:]):
         air, () = launch([(wa, lo_key), (wb, hi_key)])
         settle(air)
-    down_all, vec, both = tie((down_all, vec, side(wa.value, wb.value)))
-    both = along_seq(both)
+    rest, down_all, vec, i_fast = tie(
+        (jnp.concatenate([whole(up1), whole(wa), whole(wb)], axis=1), down_all, vec, i_fast)
+    )
+    rest = along_seq(rest)
     vec = vec + pass_on(vec, *z1)
-    up = jnp.stack([all_of(up0_all), all_of(up1_all)])
     down = all_of(down_all)
-    up, down, vec, both, m_fast, i_fast, mixed_s, gin_s = tie(
-        (up, down, vec, both, m_fast, i_fast, mixed_s, gin_s)
-    )
-    both = all_of(both)
+    down, vec, up0_sum, rest, m_fast, i_fast, mixed_s, gin_s = tie(
+        (down, vec, all_of(up0_all), rest, m_fast, i_fast, mixed_s, gin_s)
+    )
+    rest = all_of(rest)
+    up = jnp.stack([up0_sum, rest[:, :hidden]])
+    both = rest[:, hidden:]
     mixed, grad_in = lax.cond(
         over,
         lambda m, i, mf, gf: apart(slow_out(side(m, i), *labels, ways, per)),

time: 435 us -> 423 us (0.972)
  waiting for transfers between devices: 108 us -> 97.1 us
  other arithmetic: 39.3 us -> 50 us
  local copies, waits for them, and re-layouts: 26.1 us -> 20.3 us
    convert_element_type x0 -> x14, other arithmetic: none -> 25.8 us  [the longest x8 13.3 us: cut(): send = self.total(more={key: 1 - pair_bit(*key)}).astype(BF16)]
    all_to_all x8 -> x7, waiting for transfers between devices: 60.2 us -> 51.2 us  [swap(): lax.all_to_all(blocks, 'seq', split_axis=0, concat_axis=0, tiled=True)]
    add x11 -> x5, other arithmetic: 25.5 us -> 16.7 us  [total(): sum((t.rows({**self.fixed, **extra.get('more', {})}) for t in self.terms))]
    squeeze x10 -> x0, local copies, waits for them, and re-layouts: 8.71 us -> none  [cut(): take = lambda k: lax.dynamic_index_in_dim(parts, k, 1, keepdims=False)]
    dynamic_slice x0 -> x4, local copies, waits for them, and re-layouts: none -> 8.59 us  [rows(): return lax.dynamic_slice(parts, start, sizes).reshape(-1, cols).astype(F32)]
    unnamed x80 -> x76, local copies, waits for them, and re-layouts: 8.95 us -> 3.19 us
    reshape x3 -> x0, other arithmetic: 5.19 us -> none  [add(): self.value = total.reshape(-1, total.shape[-1])]
    pallas_call x1 -> x0, Pallas kernels: 4.42 us -> none  [back(): pl.pallas_call(back_kernel, out_shape=jax.ShapeDtypeStruct((col.shape[0],...]
  transfers between devices with their start and end apart: 30 -> 29, of which waited for: 12 -> 6; matrix products, arithmetic and copies ran while one was open for 7% -> 11% of each run, Pallas kernels for 33% -> 34%
where the time goes in v4:
time: 423 us; the launch traced here: 415 us
  Pallas kernels  189 us (45%)
  waiting for transfers between devices  97.1 us (23%)
  starting transfers between devices  52.8 us (12%)
  other arithmetic  50 us (12%)
  local copies, waits for them, and re-layouts  20.3 us (5%)
    pallas_call x2, Pallas kernels, ffn(): pl.pallas_call(functools.partial(ffn_kernel, expert, lo, hi, run), grid=(...  68 us
    all_to_all x7, waiting for transfers between devices, swap(): lax.all_to_all(blocks, 'seq', split_axis=0, concat_axis=0, tiled=True)  51.2 us
    ppermute x22, waiting for transfers between devices, pass_on(): return lax.ppermute(value, axis, [(i, i ^ 1 << bit) for i in range(n)])  46 us
    all_to_all x7, starting transfers between devices, swap(): lax.all_to_all(blocks, 'seq', split_axis=0, concat_axis=0, tiled=True)  32.4 us
    pallas_call x1, Pallas kernels, attn_bwd(): pl.pallas_call(functools.partial(attn_bwd_kernel, per), grid=(steps,), in...  26.9 us
    pallas_call x1, Pallas kernels, last(): pl.pallas_call(last_kernel, out_shape=(jax.ShapeDtypeStruct((col.shape[0]...  21.7 us
    pallas_call x1, Pallas kernels, attn_fwd(): pl.pallas_call(functools.partial(attn_fwd_kernel, per), grid=(steps,), in...  20.4 us
    ppermute x22, starting transfers between devices, pass_on(): return lax.ppermute(value, axis, [(i, i ^ 1 << bit) for i in range(n)])  20.3 us
  transfers between devices with their start and end apart: 29, of which 6 were waited for; matrix products, arithmetic and copies ran while one was open for 11% of the time, Pallas kernels for 34%

profile of v4, /device:TPU:0, one launch (start us, length us, event | category | flops | bytes accessed | tf_op | source)
XLA Modules:
  0.0 415.5 jit_solution(17200436068665389)
XLA Ops:
  0.6 5.6 %pack.1 = (bf16[4,272,768]{2,1,0:T(8,128)(2,1)}, s32[8,906]{1,0:T(8,128)}, s32[906,1]{1,0:T(8,128)}) custom-call(s32[1,906]{1,0:T(1,128)} %bitcast.124, s32[1,906]{1,0:T(1,128)} %bitcast.125, bf16[906,768]{1,0:T(8,128)(2,1)} %tok_ref.1), custom_call_target="tpu_custom_call" | custom-call | tf_op jit(solution)/shard_map/pack/pallas_call | solution.py:87
  6.3 6.5 %all-to-all-start.4 = ((bf16[4,272,768]{2,1,0:T(8,128)(2,1)}), bf16[4,272,768]{2,1,0:T(8,128)(2,1)S(1)}, u32[]{:S(2)}, u32[]{:S(2)}) async-start(bf16[4,272,768]{2,1,0:T(8,128)(2,1)} %get-tuple-element.200), calls=%async_computation.4 | async-start | bytes 3342336 | tf_op jit(solution)/shard_map/all_to_all | solution.py:222
  16.9 3.9 pack_more.1
  20.8 31.1 %all-to-all-done.4 = bf16[4,272,768]{2,1,0:T(8,128)(2,1)S(1)} async-done(((bf16[4,272,768]{2,1,0:T(8,128)(2,1)}), bf16[4,272,768]{2,1,0:T(8,128)(2,1)S(1)}, u32[]{:S(2)}, u32[]{:S(2)}) %all-to-all-start.4) | async-done | bytes 1671200 | tf_op jit(solution)/shard_map/all_to_all | solution.py:222
  55.2 7.3 %conditional.2 = ((bf16[928,768]{1,0:T(8,128)(2,1)}, bf16[928,768]{1,0:T(8,128)(2,1)})) conditional(s32[]{:T(128)} %bitcast.4, (s32[8,1088]{1,0:T(8,128)S(1)}, bf16[1088,768]{1,0:T(8,128)(2,1)S(1)}) %tuple.97, (s32[906]{0:T(1024)}, (), s32[906]{0:T(1024)S(1)}, s32[906]{0:T(1024)S(1)}, bf16[906,768]{1,0:T(8,128)(2,1)}, ...), branch_computations={%region_0.0_spmd, %region_1.4_spmd} | conditional | flops 7015282 | bytes 100775368 | solution.py:905
  55.2 3.1 place.1
  62.5 3.6 all-to-all-start.5
  66.1 12.7 %qkv.1 = (bf16[928,768]{1,0:T(8,128)(2,1)}, bf16[928,2304]{1,0:T(8,128)(2,1)}) custom-call(bf16[928,768]{1,0:T(8,128)(2,1)} %get-tuple-element.206.x_ref.refs_1_, f32[1,768]{1,0:T(1,128)} %reshape.333.gain_ref, f32[1,768]{1,0:T(1,128)} %reshape.334.shift_ref, bf16[768,2304]{1,0:T(8,128)(2,1)} %w_ref.3, f32[1,768]{1,0:T(1,128)} %reshape.335.qb_ref, ...), custom_call_target="tpu_custom_call" | custom-call | flops 9852420096 | bytes 1048576 | tf_op jit(solution)/shard_map/qkv/pallas_call | solution.py:301
  78.8 20.4 %attn_fwd.1 = (bf16[928,768]{1,0:T(8,128)(2,1)}, f32[6,8,1024]{2,1,0:T(8,128)}) custom-call(bf16[928,2304]{1,0:T(8,128)(2,1)} %get-tuple-element.211.q_ref.k_ref.v_ref, bf16[928,2304]{1,0:T(8,128)(2,1)} %get-tuple-element.211.q_ref.k_ref.v_ref, bf16[928,2304]{1,0:T(8,128)(2,1)} %get-tuple-element.211.q_ref.k_ref.v_ref), custom_call_target="tpu_custom_call" | custom-call | flops 11494490112 | bytes 1048576 | tf_op jit(solution)/shard_map/attn_fwd/pallas_call | solution.py:393
  99.3 5.4 %all-to-all-done.5 = bf16[4,272,768]{2,1,0:T(8,128)(2,1)S(1)} async-done(((bf16[4,272,768]{2,1,0:T(8,128)(2,1)}), bf16[4,272,768]{2,1,0:T(8,128)(2,1)S(1)}, u32[]{:S(2)}, u32[]{:S(2)}) %all-to-all-start.5) | async-done | bytes 1671200 | tf_op jit(solution)/shard_map/all_to_all | solution.py:222
  105.9 5.5 %place_or.1.refs_2_ = bf16[928,768]{1,0:T(8,128)(2,1)} custom-call(s32[1]{0:T(128)} %bitcast.7.flag_ref, s32[8,1088]{1,0:T(8,128)S(1)} %get-tuple-element.205.pos_ref, bf16[1088,768]{1,0:T(8,128)(2,1)} %bitcast.108, bf16[928,768]{1,0:T(8,128)(2,1)} %get-tuple-element.216.other_ref), custom_call_target="tpu_custom_call" | custom-call | tf_op jit(solution)/shard_map/place_or/pallas_call | solution.py:197
  111.4 32.0 %ffn0.1 = (bf16[416,768]{1,0:T(8,128)(2,1)}, bf16[416,768]{1,0:T(8,128)(2,1)}, bf16[416,768]{1,0:T(8,128)(2,1)}, f32[16,768]{1,0:T(8,128)}, bf16[384,3072]{1,0:T...) custom-call(s32[1]{0:T(128)} %bitcast.5.own_ref, ...), custom_call_target="tpu_custom_call" | custom-call | flops 35332816896 | bytes 1048576 | tf_op jit(solution)/shard_map/ffn0/pallas_call | solution.py:646
  144.0 36.0 %ffn1.1 = (bf16[928,768]{1,0:T(8,128)(2,1)}, bf16[928,768]{1,0:T(8,128)(2,1)}, bf16[928,768]{1,0:T(8,128)(2,1)}, f32[16,768]{1,0:T(8,128)}, bf16[1088,768]{1,0:T...) custom-call(s32[1]{0:T(128)} %bitcast.5.own_ref, ...), custom_call_target="tpu_custom_call" | custom-call | flops 43486543872 | bytes 1048576 | tf_op jit(solution)/shard_map/ffn1/pallas_call | solution.py:646
  180.1 2.8 add_convert_fusion.4
  182.9 3.2 convert_add_fusion
  186.6 1.5 collective-permute-start.2
  189.6 4.3 %all-to-all-start.6 = ((bf16[4,272,768]{2,1,0:T(8,128)(2,1)}), bf16[4,272,768]{2,1,0:T(8,128)(2,1)}, u32[]{:S(2)}, u32[]{:S(2)}) async-start(bf16[4,272,768]{2,1,0:T(8,128)(2,1)} %bitcast.117), calls=%async_computation.6 | async-start | bytes 3342336 | tf_op jit(solution)/shard_map/all_to_all | solution.py:222
  194.0 26.9 %attn_bwd.1 = (bf16[928,768]{1,0:T(8,128)(2,1)}, bf16[928,768]{1,0:T(8,128)(2,1)}, bf16[928,768]{1,0:T(8,128)(2,1)}) custom-call(bf16[928,2304]{1,0:T(8,128)(2,1)} %get-tuple-element.211.q_ref.k_ref.v_ref, bf16[928,2304]{1,0:T(8,128)(2,1)} %get-tuple-element.211.q_ref.k_ref.v_ref, bf16[928,2304]{1,0:T(8,128)(2,1)} %get-tuple-element.211.q_ref.k_ref.v_ref, ...), custom_call_target="tpu_custom_call" | custom-call | flops 14778630144 | bytes 1048576 | tf_op jit(solution)/shard_map/attn_bwd/pallas_call | solution.py:473
  220.9 2.6 constant_dynamic-slice_fusion.6
  223.5 4.2 %convert_add_fusion.7 = (f32[1,1,2,2,24,3072]{5,4,3,2,1,0:T(8,128)}, f32[1,1,2,2,24,3072]{5,4,3,2,1,0:T(8,128)S(1)}, f32[1,1,2,2,24,3072]{5,4,3,2,1,0:T(8,128)S(1)}, f32[1,1,2,2,24,3072]{5,4,3,2,1,0:T(8,128)}) fusion(bf16[2,2,2,2,24,3072]{5,4,3,2,1,0:T(8,128)(2,1)} %bitcast.10, s32[]{:T(128)S(6)} %select_n.59, s32[]{:T(128)S(6)} %select_n.60, ...), kind=kLoop, calls=%fused_computation.63 | loop fusion | flops 3538944 | bytes 9437196 | tf_op jit(solution)/shard_map/add | solution.py:819
  229.6 2.7 add_convert_fusion.2
  233.3 10.0 %wgrad.1 = (bf16[384,1536]{1,0:T(8,128)(2,1)}, bf16[384,1536]{1,0:T(8,128)(2,1)}, bf16[384,1536]{1,0:T(8,128)(2,1)}, bf16[384,1536]{1,0:T(8,128)(2,1)}) custom-call(s32[1]{0:T(128)} %bitcast.5.own_ref, bf16[928,768]{1,0:T(8,128)(2,1)} %get-tuple-element.265.first_ref, bf16[928,768]{1,0:T(8,128)(2,1)} %get-tuple-element.281.dq_ref, ...), custom_call_target="tpu_custom_call" | custom-call | flops 13136560128 | bytes 1048576 | tf_op jit(solution)/shard_map/wgrad/pallas_call | solution.py:746
  243.3 4.8 %convert_add_fusion.1 = (f32[1,2,2,192,768]{4,3,2,1,0:T(8,128)}, bf16[1,2,2,192,768]{4,3,2,1,0:T(8,128)(2,1)}) fusion(bf16[2,2,2,192,768]{4,3,2,1,0:T(8,128)(2,1)} %bitcast.22, s32[]{:T(128)S(6)} %select_n.60, bf16[2,2,2,192,768]{4,3,2,1,0:T(8,128)(2,1)} %bitcast.114, s32[]{:T(128)S(6)} %select_n.62), kind=kLoop, calls=%fused_computation.43 | loop fusion | flops 4128768 | bytes 8257544 | tf_op jit(solution)/shard_map/add | solution.py:819
  248.1 2.1 fusion.19
  251.9 5.3 %all-to-all-start.7 = ((bf16[4,24,3072]{2,1,0:T(8,128)(2,1)}), bf16[4,24,3072]{2,1,0:T(8,128)(2,1)}, u32[]{:S(2)}, u32[]{:S(2)}) async-start(bf16[4,24,3072]{2,1,0:T(8,128)(2,1)} %bitcast.113), calls=%async_computation.7 | async-start | bytes 1179648 | tf_op jit(solution)/shard_map/all_to_all | solution.py:222
  257.2 21.7 %last.1 = (bf16[1088,768]{1,0:T(8,128)(2,1)}, bf16[928,768]{1,0:T(8,128)(2,1)}, f32[24,768]{1,0:T(8,128)}) custom-call(bf16[928,768]{1,0:T(8,128)(2,1)} %get-tuple-element.206.x_ref.refs_1_, bf16[928,768]{1,0:T(8,128)(2,1)} %get-tuple-element.281.dq_ref, bf16[928,768]{1,0:T(8,128)(2,1)} %get-tuple-element.282.dk_ref, ...), custom_call_target="tpu_custom_call" | custom-call | flops 9852420096 | bytes 1048576 | tf_op jit(solution)/shard_map/last/pallas_call | solution.py:765
  278.9 2.3 constant_dynamic-slice_fusion.5
  281.2 2.1 add_convert_fusion.5
  283.3 2.1 add_convert_fusion.6
  287.3 2.8 select_convert_fusion
  290.1 1.5 collective-permute-start.16
  291.7 5.2 %all-to-all-start.8 = ((bf16[4,272,768]{2,1,0:T(8,128)(2,1)}), bf16[4,272,768]{2,1,0:T(8,128)(2,1)}, u32[]{:S(2)}, u32[]{:S(2)}) async-start(bf16[4,272,768]{2,1,0:T(8,128)(2,1)} %bitcast.116), calls=%async_computation.8 | async-start | bytes 3342336 | tf_op jit(solution)/shard_map/all_to_all | solution.py:222
  296.9 2.3 convert_add_fusion.15
  304.1 2.2 convert_add_fusion.17
  306.3 4.8 %choose.2 = bf16[906,768]{1,0:T(8,128)(2,1)} custom-call(s32[906,1]{1,0:T(8,128)} %get-tuple-element.302.col_ref, bf16[1088,768]{1,0:T(8,128)(2,1)} %bitcast.40.value_ref), custom_call_target="tpu_custom_call" | custom-call | tf_op jit(solution)/shard_map/choose/pallas_call | solution.py:213
  311.1 18.0 %collective-permute-done.15 = f32[24,768]{1,0:T(8,128)S(1)} collective-permute-done((f32[24,768]{1,0:T(8,128)S(1)}, f32[24,768]{1,0:T(8,128)S(1)}, u32[]{:S(2)}, u32[]{:S(2)}) %collective-permute-start.15) | collective-permute-done | bytes 73760 | tf_op jit(solution)/shard_map/ppermute | solution.py:789
  329.1 4.0 add_convert_fusion
  333.2 1.9 constant_dynamic-slice_fusion.8
  335.0 1.9 constant_dynamic-slice_fusion.1
  341.9 1.8 collective-permute-done.19
  344.3 1.7 collective-permute-start.20
  346.0 3.9 all-to-all-start.9
  351.3 1.6 add.311
  352.8 4.8 %choose.3 = bf16[906,768]{1,0:T(8,128)(2,1)} custom-call(s32[906,1]{1,0:T(8,128)} %get-tuple-element.302.col_ref, bf16[1088,768]{1,0:T(8,128)(2,1)} %bitcast.50.value_ref), custom_call_target="tpu_custom_call" | custom-call | tf_op jit(solution)/shard_map/choose/pallas_call | solution.py:213
  361.1 14.7 %all-to-all-done.9 = bf16[4,192,768]{2,1,0:T(8,128)(2,1)S(1)} async-done(((bf16[4,192,768]{2,1,0:T(8,128)(2,1)}), bf16[4,192,768]{2,1,0:T(8,128)(2,1)S(1)}, u32[]{:S(2)}, u32[]{:S(2)}) %all-to-all-start.9) | async-done | bytes 1179680 | tf_op jit(solution)/shard_map/all_to_all | solution.py:222
  375.7 3.7 all-to-all-start.10
  380.6 2.9 collective-permute-start.21
  384.5 26.1 %collective-permute-done.21 = f32[24,768]{1,0:T(8,128)S(1)} collective-permute-done((f32[24,768]{1,0:T(8,128)S(1)}, f32[24,768]{1,0:T(8,128)S(1)}, u32[]{:S(2)}, u32[]{:S(2)}) %collective-permute-start.21) | collective-permute-done | bytes 73760 | tf_op jit(solution)/shard_map/ppermute | solution.py:789
  (151 shorter events, 38.9 us)
Async XLA Ops:
  6.3 6.6 %copy-start.31 = (f32[768]{0:T(1024)S(1)}, f32[768]{0:T(1024)}, u32[]{:S(2)}) copy-start(f32[768]{0:T(1024)} %param.29) | copy-start | bytes 9220
  6.3 7.1 %copy-start.32 = (f32[768]{0:T(1024)S(1)}, f32[768]{0:T(1024)}, u32[]{:S(2)}) copy-start(f32[768]{0:T(1024)} %param.30) | copy-start | bytes 9220
  6.3 7.7 %copy-start.33 = (f32[768]{0:T(1024)S(1)}, f32[768]{0:T(1024)}, u32[]{:S(2)}) copy-start(f32[768]{0:T(1024)} %param.32) | copy-start | bytes 9220
  6.3 8.3 %copy-start.34 = (f32[768]{0:T(1024)S(1)}, f32[768]{0:T(1024)}, u32[]{:S(2)}) copy-start(f32[768]{0:T(1024)} %param.33) | copy-start | bytes 9220
  6.3 8.9 %copy-start.35 = (f32[768]{0:T(1024)S(1)}, f32[768]{0:T(1024)}, u32[]{:S(2)}) copy-start(f32[768]{0:T(1024)} %param.35) | copy-start | bytes 9220
  6.3 9.4 %copy-start.36 = (f32[768]{0:T(1024)S(1)}, f32[768]{0:T(1024)}, u32[]{:S(2)}) copy-start(f32[768]{0:T(1024)} %param.36) | copy-start | bytes 9220
  6.3 10.0 %copy-start.37 = (f32[768]{0:T(1024)S(1)}, f32[768]{0:T(1024)}, u32[]{:S(2)}) copy-start(f32[768]{0:T(1024)} %param.37) | copy-start | bytes 9220
  6.3 10.6 %copy-start.18 = (bf16[906,768]{1,0:T(8,128)(2,1)S(1)}, bf16[906,768]{1,0:T(8,128)(2,1)}, u32[]{:S(2)}) copy-start(bf16[906,768]{1,0:T(8,128)(2,1)} %value_ref.1) | copy-start | bytes 4174852
  6.3 45.6 %all-to-all-start.4 = ((bf16[4,272,768]{2,1,0:T(8,128)(2,1)}), bf16[4,272,768]{2,1,0:T(8,128)(2,1)S(1)}, u32[]{:S(2)}, u32[]{:S(2)}) async-start(bf16[4,272,768]{2,1,0:T(8,128)(2,1)} %get-tuple-element.200), calls=%async_computation.4 | async-start | bytes 3342336 | tf_op jit(solution)/shard_map/all_to_all | solution.py:222
  20.8 34.4 %copy-start.27 = (s32[906]{0:T(1024)S(1)}, s32[906]{0:T(1024)}, u32[]{:S(2)}) copy-start(s32[906]{0:T(1024)} %param.27) | copy-start | bytes 10876
  20.8 34.4 %copy-start.29 = (s32[906]{0:T(1024)S(1)}, s32[906]{0:T(1024)}, u32[]{:S(2)}) copy-start(s32[906]{0:T(1024)} %param.28) | copy-start | bytes 10876
  62.5 42.2 %all-to-all-start.5 = ((bf16[4,272,768]{2,1,0:T(8,128)(2,1)}), bf16[4,272,768]{2,1,0:T(8,128)(2,1)S(1)}, u32[]{:S(2)}, u32[]{:S(2)}) async-start(bf16[4,272,768]{2,1,0:T(8,128)(2,1)} %pack_more.1), calls=%async_computation.5 | async-start | bytes 3342336 | tf_op jit(solution)/shard_map/all_to_all | solution.py:222
  111.4 32.6 %copy-start.38 = (bf16[928,768]{1,0:T(8,128)(2,1)S(1)}, bf16[928,768]{1,0:T(8,128)(2,1)}, u32[]{:S(2)}) copy-start(bf16[928,768]{1,0:T(8,128)(2,1)} %get-tuple-element.206.x_ref.refs_1_) | copy-start | bytes 4276228
  143.4 36.6 %collective-permute-start = (bf16[384,3072]{1,0:T(8,128)(2,1)}, bf16[384,3072]{1,0:T(8,128)(2,1)}, u32[]{:S(2)}, u32[]{:S(2)}) collective-permute-start(bf16[384,3072]{1,0:T(8,128)(2,1)} %get-tuple-element.226), channel_id=1, source_target_pairs={{0,4},{4,0},{8,12},{12,8},{16,20},{20,16},{24,28},{28,24},{1,5},{5... | collective-permute-start | bytes 7077896 | tf_op jit(solution)/shard_map/ppermute | solution.py:789
  143.5 36.5 %collective-permute-start.1 = (bf16[1536,768]{1,0:T(8,128)(2,1)}, bf16[1536,768]{1,0:T(8,128)(2,1)}, u32[]{:S(2)}, u32[]{:S(2)}) collective-permute-start(bf16[1536,768]{1,0:T(8,128)(2,1)} %get-tuple-element.227), channel_id=1, source_target_pairs={{0,4},{4,0},{8,12},{12,8},{16,20},{20,16},{24,28},{28,24},{1,5},{5... | collective-permute-start | bytes 7077896 | tf_op jit(solution)/shard_map/ppermute | solution.py:789
  144.0 36.1 %copy-start.8 = (bf16[384,3072]{1,0:T(8,128)(2,1)S(1)}, bf16[384,3072]{1,0:T(8,128)(2,1)}, u32[]{:S(2)}) copy-start(bf16[384,3072]{1,0:T(8,128)(2,1)} %get-tuple-element.240) | copy-start | bytes 7077892
  186.1 34.8 %collective-permute-start.4 = (bf16[384,3072]{1,0:T(8,128)(2,1)}, bf16[384,3072]{1,0:T(8,128)(2,1)}, u32[]{:S(2)}, u32[]{:S(2)}) collective-permute-start(bf16[384,3072]{1,0:T(8,128)(2,1)} %get-tuple-element.250), channel_id=1, source_target_pairs={{0,4},{4,0},{8,12},{12,8},{16,20},{20,16},{24,28},{28,24},{1,5},{5... | collective-permute-start | bytes 7077896 | tf_op jit(solution)/shard_map/ppermute | solution.py:789
  186.1 34.8 %collective-permute-start.5 = (bf16[1536,768]{1,0:T(8,128)(2,1)}, bf16[1536,768]{1,0:T(8,128)(2,1)}, u32[]{:S(2)}, u32[]{:S(2)}) collective-permute-start(bf16[1536,768]{1,0:T(8,128)(2,1)} %get-tuple-element.251), channel_id=1, source_target_pairs={{0,4},{4,0},{8,12},{12,8},{16,20},{20,16},{24,28},{28,24},{1,5},{5... | collective-permute-start | bytes 7077896 | tf_op jit(solution)/shard_map/ppermute | solution.py:789
  186.6 34.3 %collective-permute-start.2 = (bf16[192,3072]{1,0:T(8,128)(2,1)}, bf16[192,3072]{1,0:T(8,128)(2,1)}, u32[]{:S(2)}, u32[]{:S(2)}) collective-permute-start(bf16[192,3072]{1,0:T(8,128)(2,1)} %bitcast.11), channel_id=1, source_target_pairs={{0,16},{4,20},{8,24},{12,28},{16,0},{20,4},{24,8},{28,12},{1,17},{... | collective-permute-start | bytes 3538952 | tf_op jit(solution)/shard_map/ppermute | solution.py:789
  188.1 32.8 %collective-permute-start.3 = (bf16[768,768]{1,0:T(8,128)(2,1)}, bf16[768,768]{1,0:T(8,128)(2,1)S(1)}, u32[]{:S(2)}, u32[]{:S(2)}) collective-permute-start(bf16[768,768]{1,0:T(8,128)(2,1)} %bitcast.118), channel_id=1, source_target_pairs={{0,8},{4,12},{8,0},{12,4},{16,24},{20,28},{24,16},{28,20},{1,9},{5... | collective-permute-start | bytes 3538952 | tf_op jit(solution)/shard_map/ppermute | solution.py:789
  189.6 62.3 %all-to-all-start.6 = ((bf16[4,272,768]{2,1,0:T(8,128)(2,1)}), bf16[4,272,768]{2,1,0:T(8,128)(2,1)}, u32[]{:S(2)}, u32[]{:S(2)}) async-start(bf16[4,272,768]{2,1,0:T(8,128)(2,1)} %bitcast.117), calls=%async_computation.6 | async-start | bytes 3342336 | tf_op jit(solution)/shard_map/all_to_all | solution.py:222
  232.3 15.8 %collective-permute-start.7 = (bf16[96,3072]{1,0:T(8,128)(2,1)}, bf16[96,3072]{1,0:T(8,128)(2,1)}, u32[]{:S(2)}, u32[]{:S(2)}) collective-permute-start(bf16[96,3072]{1,0:T(8,128)(2,1)} %fusion.20), channel_id=1, source_target_pairs={{0,8},{4,12},{8,0},{12,4},{16,24},{20,28},{24,16},{28,20},{1,9},{5... | collective-permute-start | bytes 1769480 | tf_op jit(solution)/shard_map/ppermute | solution.py:789
  232.8 46.1 %collective-permute-start.6 = (bf16[192,3072]{1,0:T(8,128)(2,1)}, bf16[192,3072]{1,0:T(8,128)(2,1)}, u32[]{:S(2)}, u32[]{:S(2)}) collective-permute-start(bf16[192,3072]{1,0:T(8,128)(2,1)} %bitcast.20), channel_id=1, source_target_pairs={{0,16},{4,20},{8,24},{12,28},{16,0},{20,4},{24,8},{28,12},{1,17},{... | collective-permute-start | bytes 3538952 | tf_op jit(solution)/shard_map/ppermute | solution.py:789
  250.2 28.7 %collective-permute-start.10 = (bf16[384,1536]{1,0:T(8,128)(2,1)}, bf16[384,1536]{1,0:T(8,128)(2,1)}, u32[]{:S(2)}, u32[]{:S(2)}) collective-permute-start(bf16[384,1536]{1,0:T(8,128)(2,1)} %get-tuple-element.280), channel_id=1, source_target_pairs={{0,4},{4,0},{8,12},{12,8},{16,20},{20,16},{24,28},{28,24},{1,5},{5... | collective-permute-start | bytes 3538952 | tf_op jit(solution)/shard_map/ppermute | solution.py:789
  250.2 28.7 %collective-permute-start.8 = (bf16[768,768]{1,0:T(8,128)(2,1)}, bf16[768,768]{1,0:T(8,128)(2,1)}, u32[]{:S(2)}, u32[]{:S(2)}) collective-permute-start(bf16[768,768]{1,0:T(8,128)(2,1)} %bitcast.23), channel_id=1, source_target_pairs={{0,8},{4,12},{8,0},{12,4},{16,24},{20,28},{24,16},{28,20},{1,9},{5... | collective-permute-start | bytes 3538952 | tf_op jit(solution)/shard_map/ppermute | solution.py:789
  251.7 27.2 %collective-permute-start.9 = (bf16[384,1536]{1,0:T(8,128)(2,1)}, bf16[384,1536]{1,0:T(8,128)(2,1)}, u32[]{:S(2)}, u32[]{:S(2)}) collective-permute-start(bf16[384,1536]{1,0:T(8,128)(2,1)} %get-tuple-element.279), channel_id=1, source_target_pairs={{0,4},{4,0},{8,12},{12,8},{16,20},{20,16},{24,28},{28,24},{1,5},{5... | collective-permute-start | bytes 3538952 | tf_op jit(solution)/shard_map/ppermute | solution.py:789
  251.9 27.0 %all-to-all-start.7 = ((bf16[4,24,3072]{2,1,0:T(8,128)(2,1)}), bf16[4,24,3072]{2,1,0:T(8,128)(2,1)}, u32[]{:S(2)}, u32[]{:S(2)}) async-start(bf16[4,24,3072]{2,1,0:T(8,128)(2,1)} %bitcast.113), calls=%async_computation.7 | async-start | bytes 1179648 | tf_op jit(solution)/shard_map/all_to_all | solution.py:222
  290.1 39.0 %collective-permute-start.16 = (bf16[768,768]{1,0:T(8,128)(2,1)}, bf16[768,768]{1,0:T(8,128)(2,1)}, u32[]{:S(2)}, u32[]{:S(2)}) collective-permute-start(bf16[768,768]{1,0:T(8,128)(2,1)} %select_convert_fusion), channel_id=1, source_target_pairs={{0,16},{4,20},{8,24},{12,28},{16,0},{20,4},{24,8},{28,12},{1,17},{... | collective-permute-start | bytes 3538952 | tf_op jit(solution)/shard_map/ppermute | solution.py:789
  291.6 10.1 %collective-permute-start.14 = (f32[24,768]{1,0:T(8,128)}, f32[24,768]{1,0:T(8,128)}, u32[]{:S(2)}, u32[]{:S(2)}) collective-permute-start(f32[24,768]{1,0:T(8,128)} %get-tuple-element.300), channel_id=1, source_target_pairs={{0,4},{4,0},{8,12},{12,8},{16,20},{20,16},{24,28},{28,24},{1,5},{5... | collective-permute-start | bytes 221192 | tf_op jit(solution)/shard_map/ppermute | solution.py:789
  291.7 5.2 %copy-start.23 = (bf16[384,1536]{1,0:T(8,128)(2,1)S(1)}, bf16[384,1536]{1,0:T(8,128)(2,1)}, u32[]{:S(2)}) copy-start(bf16[384,1536]{1,0:T(8,128)(2,1)} %get-tuple-element.293) | copy-start | bytes 3538948
  291.7 54.4 %all-to-all-start.8 = ((bf16[4,272,768]{2,1,0:T(8,128)(2,1)}), bf16[4,272,768]{2,1,0:T(8,128)(2,1)}, u32[]{:S(2)}, u32[]{:S(2)}) async-start(bf16[4,272,768]{2,1,0:T(8,128)(2,1)} %bitcast.116), calls=%async_computation.8 | async-start | bytes 3342336 | tf_op jit(solution)/shard_map/all_to_all | solution.py:222
  296.9 7.2 %copy-start.21 = (bf16[384,1536]{1,0:T(8,128)(2,1)S(1)}, bf16[384,1536]{1,0:T(8,128)(2,1)}, u32[]{:S(2)}) copy-start(bf16[384,1536]{1,0:T(8,128)(2,1)} %get-tuple-element.273) | copy-start | bytes 3538948
  299.2 34.0 %collective-permute-start.11 = (bf16[96,3072]{1,0:T(8,128)(2,1)}, bf16[96,3072]{1,0:T(8,128)(2,1)}, u32[]{:S(2)}, u32[]{:S(2)}) collective-permute-start(bf16[96,3072]{1,0:T(8,128)(2,1)} %fusion.15), channel_id=1, source_target_pairs={{0,8},{4,12},{8,0},{12,4},{16,24},{20,28},{24,16},{28,20},{1,9},{5... | collective-permute-start | bytes 1769480 | tf_op jit(solution)/shard_map/ppermute | solution.py:789
  300.5 32.6 %collective-permute-start.12 = (bf16[192,1536]{1,0:T(8,128)(2,1)}, bf16[192,1536]{1,0:T(8,128)(2,1)}, u32[]{:S(2)}, u32[]{:S(2)}) collective-permute-start(bf16[192,1536]{1,0:T(8,128)(2,1)} %bitcast.36), channel_id=1, source_target_pairs={{0,8},{4,12},{8,0},{12,4},{16,24},{20,28},{24,16},{28,20},{1,9},{5... | collective-permute-start | bytes 1769480 | tf_op jit(solution)/shard_map/ppermute | solution.py:789
  301.2 31.9 %collective-permute-start.13 = (bf16[192,1536]{1,0:T(8,128)(2,1)}, bf16[192,1536]{1,0:T(8,128)(2,1)}, u32[]{:S(2)}, u32[]{:S(2)}) collective-permute-start(bf16[192,1536]{1,0:T(8,128)(2,1)} %bitcast.39), channel_id=1, source_target_pairs={{0,16},{4,20},{8,24},{12,28},{16,0},{20,4},{24,8},{28,12},{1,17},{... | collective-permute-start | bytes 1769480 | tf_op jit(solution)/shard_map/ppermute | solution.py:789
  302.7 26.4 %collective-permute-start.15 = (f32[24,768]{1,0:T(8,128)S(1)}, f32[24,768]{1,0:T(8,128)S(1)}, u32[]{:S(2)}, u32[]{:S(2)}) collective-permute-start(f32[24,768]{1,0:T(8,128)S(1)} %add.297), channel_id=1, source_target_pairs={{0,8},{4,12},{8,0},{12,4},{16,24},{20,28},{24,16},{28,20},{1,9},{5... | collective-permute-start | bytes 221192 | tf_op jit(solution)/shard_map/ppermute | solution.py:789
  306.3 22.8 %copy-start.6 = (bf16[768,768]{1,0:T(8,128)(2,1)S(1)}, bf16[768,768]{1,0:T(8,128)(2,1)}, u32[]{:S(2)}) copy-start(bf16[768,768]{1,0:T(8,128)(2,1)} %copy-done.4) | copy-start | bytes 3538948
  338.5 11.4 %copy-start.3 = (f32[1,1,2,2,24,3072]{5,4,3,2,1,0:T(8,128)S(1)}, f32[1,1,2,2,24,3072]{5,4,3,2,1,0:T(8,128)}, u32[]{:S(2)}) copy-start(f32[1,1,2,2,24,3072]{5,4,3,2,1,0:T(8,128)} %get-tuple-element.378) | copy-start | bytes 3538948
  338.5 11.4 %copy-start.15 = (bf16[1,2,2,24,3072]{4,3,2,1,0:T(8,128)(2,1)S(1)}, bf16[1,2,2,24,3072]{4,3,2,1,0:T(8,128)(2,1)}, u32[]{:S(2)}) copy-start(bf16[1,2,2,24,3072]{4,3,2,1,0:T(8,128)(2,1)} %get-tuple-element.362) | copy-start | bytes 1769476
  338.5 5.1 %collective-permute-start.19 = (f32[24,768]{1,0:T(8,128)S(1)}, f32[24,768]{1,0:T(8,128)S(1)}, u32[]{:S(2)}, u32[]{:S(2)}) collective-permute-start(f32[24,768]{1,0:T(8,128)S(1)} %add.298), channel_id=1, source_target_pairs={{0,16},{4,20},{8,24},{12,28},{16,0},{20,4},{24,8},{28,12},{1,17},{... | collective-permute-start | bytes 221192 | tf_op jit(solution)/shard_map/ppermute | solution.py:789
  339.0 18.6 %collective-permute-start.17 = (bf16[96,1536]{1,0:T(8,128)(2,1)}, bf16[96,1536]{1,0:T(8,128)(2,1)}, u32[]{:S(2)}, u32[]{:S(2)}) collective-permute-start(bf16[96,1536]{1,0:T(8,128)(2,1)} %fusion.24), channel_id=1, source_target_pairs={{0,16},{4,20},{8,24},{12,28},{16,0},{20,4},{24,8},{28,12},{1,17},{... | collective-permute-start | bytes 884744 | tf_op jit(solution)/shard_map/ppermute | solution.py:789
  340.5 17.1 %collective-permute-start.18 = (bf16[96,1536]{1,0:T(8,128)(2,1)}, bf16[96,1536]{1,0:T(8,128)(2,1)}, u32[]{:S(2)}, u32[]{:S(2)}) collective-permute-start(bf16[96,1536]{1,0:T(8,128)(2,1)} %fusion.23), channel_id=1, source_target_pairs={{0,8},{4,12},{8,0},{12,4},{16,24},{20,28},{24,16},{28,20},{1,9},{5... | collective-permute-start | bytes 884744 | tf_op jit(solution)/shard_map/ppermute | solution.py:789
  344.3 7.0 %collective-permute-start.20 = (f32[24,768]{1,0:T(8,128)}, f32[24,768]{1,0:T(8,128)}, u32[]{:S(2)}, u32[]{:S(2)}) collective-permute-start(f32[24,768]{1,0:T(8,128)} %add.310), channel_id=1, source_target_pairs={{0,1},{1,0},{2,3},{3,2},{4,5},{5,4},{6,7},{7,6},{8,9},{9,8},{10,11... | collective-permute-start | bytes 221192 | tf_op jit(solution)/shard_map/ppermute | solution.py:789
  346.0 29.7 %all-to-all-start.9 = ((bf16[4,192,768]{2,1,0:T(8,128)(2,1)}), bf16[4,192,768]{2,1,0:T(8,128)(2,1)S(1)}, u32[]{:S(2)}, u32[]{:S(2)}) async-start(bf16[4,192,768]{2,1,0:T(8,128)(2,1)} %bitcast.53), calls=%async_computation.9 | async-start | bytes 2359296 | tf_op jit(solution)/shard_map/all_to_all | solution.py:222
  352.8 4.8 %copy-start.25 = (bf16[1,2,2,24,1536]{4,3,2,1,0:T(8,128)(2,1)S(1)}, bf16[1,2,2,24,1536]{4,3,2,1,0:T(8,128)(2,1)}, u32[]{:S(2)}) copy-start(bf16[1,2,2,24,1536]{4,3,2,1,0:T(8,128)(2,1)} %get-tuple-element.366) | copy-start | bytes 884740
  375.7 4.9 %copy-start.26 = (f32[24,768]{1,0:T(8,128)S(1)}, f32[24,768]{1,0:T(8,128)}, u32[]{:S(2)}) copy-start(f32[24,768]{1,0:T(8,128)} %add.311) | copy-start | bytes 221188
  375.7 34.9 %all-to-all-start.10 = ((bf16[4,24,6144]{2,1,0:T(8,128)(2,1)}), bf16[4,24,6144]{2,1,0:T(8,128)(2,1)S(1)}, u32[]{:S(2)}, u32[]{:S(2)}) async-start(bf16[4,24,6144]{2,1,0:T(8,128)(2,1)} %bitcast.54), calls=%async_computation.10 | async-start | bytes 2359296 | tf_op jit(solution)/shard_map/all_to_all | solution.py:222
  380.6 30.0 %collective-permute-start.21 = (f32[24,768]{1,0:T(8,128)S(1)}, f32[24,768]{1,0:T(8,128)S(1)}, u32[]{:S(2)}, u32[]{:S(2)}) collective-permute-start(f32[24,768]{1,0:T(8,128)S(1)} %copy-done.26), channel_id=1, source_target_pairs={{0,2},{1,3},{2,0},{3,1},{4,6},{5,7},{6,4},{7,5},{8,10},{9,11},{10,... | collective-permute-start | bytes 221192 | tf_op jit(solution)/shard_map/ppermute | solution.py:789
  (19 other events, 50.7 us)

commit v5 on v4

--- a/solution.py
+++ b/solution.py
@@ -16,6 +16,7 @@
 SEGS = CAPTIONS + 1
 IMG = 208
 CAP = CAPTIONS * CAP_LEN
+LSE = 512
 SLOTS = 272
 ROOM = SLOTS - 1
 EPS = 1e-05
@@ -339,49 +340,53 @@
     return (iota((n, n), 0) < CAP_LEN) == (iota((n, n), 1) < CAP_LEN)
 
 
+def both_heads(value):
+    return jnp.concatenate([only(head_lanes(h), value) for h in range(2)], axis=0)
+
+
+def by_head(value):
+    n = value.shape[0] // 2
+    return jnp.where(head_lanes(0), value[:n], value[n:])
+
+
 def attn_fwd_kernel(per, q_ref, k_ref, v_ref, o_ref, lse_ref):
     n = 2 * CAP_LEN
+    count = CAP // n
     scale = HEAD_DIM ** (-0.5)
     diag = same_caption()
+    real = real_keys(1)
     for g in range(per):
         ia = pl.ds(g * IMG, IMG)
         ca = pl.ds(per * IMG + g * CAP, CAP)
-        qi, qc = q_ref[ia, :] * scale, q_ref[ca, :] * scale
-        ki, kc = k_ref[ia, :], k_ref[ca, :]
-        vi, vc = v_ref[ia, :], v_ref[ca, :]
-        out_i = jnp.zeros((n, IMG), F32)
-        out_c = [jnp.zeros((n, n), F32) for _ in range(CAP // n)]
+        q = jnp.concatenate([q_ref[ca, :], q_ref[ia, :]], axis=0) * scale
+        kc, vc = k_ref[ca, :], v_ref[ca, :]
+        parts = [slice(p * n, p * n + n) for p in range(count)]
+        s_all = dot_nt(both_heads(k_ref[ia, :]), q)
+        s_own = [dot_nt(both_heads(kc[pa]), q[pa]) for pa in parts]
+        probs, probs_own = [], [[] for _ in parts]
         for h in range(2):
-            sel = head_lanes(h)
-            kim, vim = only(sel, ki), only(sel, vi)
-            kcm, vcm = only(sel, kc), only(sel, vc)
-            s = jnp.where(real_keys(IMG), dot_nt(kim, qi), -1e30)
-            peak = jnp.max(s, axis=0, keepdims=True)
-            e = jnp.exp(s - peak)
-            total = jnp.sum(e, axis=0, keepdims=True)
-            probs = (e * (1.0 / total)).astype(BF16)
-            out_i = out_i + dot_tn(vim, probs)
-            lse_ref[0, h : h + 1, g * 256 : g * 256 + IMG] = peak + jnp.log(total)
-            for p in range(CAP // n):
-                pa = slice(p * n, p * n + n)
-                sa = jnp.where(real_keys(n), dot_nt(kim, qc[pa]), -1e30)
-                sb = jnp.where(diag, dot_nt(kcm[pa], qc[pa]), -1e30)
-                peak = jnp.maximum(
-                    jnp.max(sa, axis=0, keepdims=True), jnp.max(sb, axis=0, keepdims=True)
-                )
-                ea, eb = jnp.exp(sa - peak), jnp.exp(sb - peak)
-                total = jnp.sum(ea, axis=0, keepdims=True) + jnp.sum(eb, axis=0, keepdims=True)
-                inv = 1.0 / total
-                out_c[p] = (
-                    out_c[p]
-                    + dot_tn(vim, (ea * inv).astype(BF16))
-                    + dot_tn(vcm[pa], (eb * inv).astype(BF16))
-                )
-                at = (per + g) * 256 + p * n
-                lse_ref[0, h : h + 1, at : at + n] = peak + jnp.log(total)
-        o_ref[ia, :] = out_i.T.astype(BF16)
-        for p in range(CAP // n):
-            o_ref[pl.ds(per * IMG + g * CAP + p * n, n), :] = out_c[p].T.astype(BF16)
+            si = jnp.where(real, s_all[h * IMG : h * IMG + IMG], -1e30)
+            sb = [jnp.where(diag, s[h * n : h * n + n], -1e30) for s in s_own]
+            sb = jnp.concatenate(sb, axis=1)
+            peak = jnp.max(si, axis=0, keepdims=True)
+            peak_c = jnp.maximum(peak[:, :CAP], jnp.max(sb, axis=0, keepdims=True))
+            peak = jnp.concatenate([peak_c, peak[:, CAP:]], axis=1)
+            ei = jnp.exp(si - peak)
+            eb = jnp.exp(sb - peak_c)
+            total = jnp.sum(ei, axis=0, keepdims=True)
+            total_c = total[:, :CAP] + jnp.sum(eb, axis=0, keepdims=True)
+            total = jnp.concatenate([total_c, total[:, CAP:]], axis=1)
+            inv = 1.0 / total
+            probs.append((ei * inv).astype(BF16))
+            pb = (eb * inv[:, :CAP]).astype(BF16)
+            for own, pa in zip(probs_own, parts):
+                own.append(pb[:, pa])
+            lse_ref[0, h : h + 1, g * LSE : g * LSE + CAP + IMG] = peak + jnp.log(total)
+        out = dot_tn(both_heads(v_ref[ia, :]), jnp.concatenate(probs, axis=0))
+        o_ref[ia, :] = out[:, CAP:].T.astype(BF16)
+        for p, pa in enumerate(parts):
+            own = dot_tn(both_heads(vc[pa]), jnp.concatenate(probs_own[p], axis=0))
+            o_ref[pl.ds(per * IMG + g * CAP + p * n, n), :] = (out[:, pa] + own).T.astype(BF16)
 
 
 def attn_fwd(per, qkv):
@@ -394,10 +399,10 @@
         functools.partial(attn_fwd_kernel, per),
         grid=(steps,),
         in_specs=[col(0), col(1), col(2)],
-        out_specs=[col(0), pl.BlockSpec((1, 8, 2 * per * 256), lambda j: (j, 0, 0))],
+        out_specs=[col(0), pl.BlockSpec((1, 8, per * LSE), lambda j: (j, 0, 0))],
         out_shape=(
             jax.ShapeDtypeStruct((rows, width), BF16),
-            jax.ShapeDtypeStruct((steps, 8, 2 * per * 256), F32),
+            jax.ShapeDtypeStruct((steps, 8, per * LSE), F32),
         ),
         compiler_params=params(BIG),
         cost_estimate=cost(7 * rows * width * width),
@@ -407,61 +412,56 @@
 
 def attn_bwd_kernel(per, q_ref, k_ref, v_ref, do_ref, lse_ref, dq_ref, dk_ref, dv_ref):
     n = 2 * CAP_LEN
+    count = CAP // n
     scale = HEAD_DIM ** (-0.5)
     diag = same_caption()
+    real = real_keys(1)
     for g in range(per):
         ia = pl.ds(g * IMG, IMG)
         ca = pl.ds(per * IMG + g * CAP, CAP)
-        qi, qc = q_ref[ia, :] * scale, q_ref[ca, :] * scale
-        ki, kc = k_ref[ia, :] * scale, k_ref[ca, :] * scale
-        vi, vc = v_ref[ia, :], v_ref[ca, :]
-        doi, doc = do_ref[ia, :], do_ref[ca, :]
-        dq_i = jnp.zeros((n, IMG), F32)
-        dk_i = jnp.zeros((IMG, n), F32)
-        dv_i = jnp.zeros((IMG, n), F32)
-        dq_c = [jnp.zeros((n, n), F32) for _ in range(CAP // n)]
-        dk_c = [jnp.zeros((n, n), F32) for _ in range(CAP // n)]
-        dv_c = [jnp.zeros((n, n), F32) for _ in range(CAP // n)]
+        q = jnp.concatenate([q_ref[ca, :], q_ref[ia, :]], axis=0) * scale
+        do = jnp.concatenate([do_ref[ca, :], do_ref[ia, :]], axis=0)
+        parts = [slice(p * n, p * n + n) for p in range(count)]
+        ki, vi = both_heads(k_ref[ia, :]), both_heads(v_ref[ia, :])
+        kc, vc = k_ref[ca, :], v_ref[ca, :]
+        kc = [both_heads(kc[pa]) for pa in parts]
+        vc = [both_heads(vc[pa]) for pa in parts]
+        s_all, dp_all = dot_nt(ki, q), dot_nt(vi, do)
+        s_own = [dot_nt(k, q[pa]) for k, pa in zip(kc, parts)]
+        dp_own = [dot_nt(v, do[pa]) for v, pa in zip(vc, parts)]
+        probs, grads = [], []
+        probs_own, grads_own = [[] for _ in parts], [[] for _ in parts]
         for h in range(2):
-            sel = head_lanes(h)
-            kim, vim, qim, doim = only(sel, ki), only(sel, vi), only(sel, qi), only(sel, doi)
-            kcm, vcm, qcm, docm = only(sel, kc), only(sel, vc), only(sel, qc), only(sel, doc)
-            kun = only(sel, k_ref[ia, :])
-            kcun = only(sel, k_ref[ca, :])
-            lse = lse_ref[0, h : h + 1, g * 256 : g * 256 + IMG]
-            p_ = jnp.where(real_keys(IMG), jnp.exp(dot_nt(kun, qi) - lse), 0.0)
-            dp = dot_nt(vim, doi)
-            delta = jnp.sum(dp * p_, axis=0, keepdims=True)
-            ds = (p_ * (dp - delta)).astype(BF16)
-            dq_i = dq_i + dot_tn(kim, ds)
-            dk_i = dk_i + dot_nn(ds, qim)
-            dv_i = dv_i + dot_nn(p_.astype(BF16), doim)
-            for p in range(CAP // n):
-                pa = slice(p * n, p * n + n)
-                at = (per + g) * 256 + p * n
-                lse = lse_ref[0, h : h + 1, at : at + n]
-                wa = jnp.where(real_keys(n), jnp.exp(dot_nt(kun, qc[pa]) - lse), 0.0)
-                wb = jnp.where(diag, jnp.exp(dot_nt(kcun[pa], qc[pa]) - lse), 0.0)
-                da = dot_nt(vim, doc[pa])
-                db = dot_nt(vcm[pa], doc[pa])
-                delta = jnp.sum(da * wa, axis=0, keepdims=True) + jnp.sum(
-                    db * wb, axis=0, keepdims=True
-                )
-                sa = (wa * (da - delta)).astype(BF16)
-                sb = (wb * (db - delta)).astype(BF16)
-                dq_c[p] = dq_c[p] + dot_tn(kim, sa) + dot_tn(kcm[pa], sb)
-                dk_i = dk_i + dot_nn(sa, qcm[pa])
-                dv_i = dv_i + dot_nn(wa.astype(BF16), docm[pa])
-                dk_c[p] = dk_c[p] + dot_nn(sb, qcm[pa])
-                dv_c[p] = dv_c[p] + dot_nn(wb.astype(BF16), docm[pa])
-        dq_ref[ia, :] = dq_i.T.astype(BF16)
-        dk_ref[ia, :] = dk_i.astype(BF16)
-        dv_ref[ia, :] = dv_i.astype(BF16)
-        for p in range(CAP // n):
+            rows, own = slice(h * IMG, h * IMG + IMG), slice(h * n, h * n + n)
+            lse = lse_ref[0, h : h + 1, g * LSE : g * LSE + CAP + IMG]
+            lse_c = lse[:, :CAP]
+            wi = jnp.where(real, jnp.exp(s_all[rows] - lse), 0.0)
+            dpi = dp_all[rows]
+            wb = [jnp.where(diag, jnp.exp(s[own] - lse_c[:, pa]), 0.0) for s, pa in zip(s_own, parts)]
+            dpb = [d[own] for d in dp_own]
+            delta = jnp.sum(dpi * wi, axis=0, keepdims=True)
+            delta_b = [
+                delta[:, pa] + jnp.sum(d * w, axis=0, keepdims=True)
+                for d, w, pa in zip(dpb, wb, parts)
+            ]
+            delta = jnp.concatenate(delta_b + [delta[:, CAP:]], axis=1)
+            probs.append(wi.astype(BF16))
+            grads.append((wi * (dpi - delta)).astype(BF16))
+            for p in range(count):
+                probs_own[p].append(wb[p].astype(BF16))
+                grads_own[p].append((wb[p] * (dpb[p] - delta_b[p])).astype(BF16))
+        stack = lambda v: jnp.concatenate(v, axis=0)
+        grads, probs = stack(grads), stack(probs)
+        dq = dot_tn(ki, grads)
+        dk_ref[ia, :] = by_head(dot_nn(grads, q)).astype(BF16)
+        dv_ref[ia, :] = by_head(dot_nn(probs, do)).astype(BF16)
+        dq_ref[ia, :] = (dq[:, CAP:] * scale).T.astype(BF16)
+        for p, pa in enumerate(parts):
             at = pl.ds(per * IMG + g * CAP + p * n, n)
-            dq_ref[at, :] = dq_c[p].T.astype(BF16)
-            dk_ref[at, :] = dk_c[p].astype(BF16)
-            dv_ref[at, :] = dv_c[p].astype(BF16)
+            grad, prob = stack(grads_own[p]), stack(probs_own[p])
+            dq_ref[at, :] = ((dq[:, pa] + dot_tn(kc[p], grad)) * scale).T.astype(BF16)
+            dk_ref[at, :] = by_head(dot_nn(grad, q[pa])).astype(BF16)
+            dv_ref[at, :] = by_head(dot_nn(prob, do[pa])).astype(BF16)
 
 
 def attn_bwd(per, qkv, d_att, lse):
@@ -956,56 +956,54 @@
     )
     ret_m = along_seq(back_m)
     d_qkv = attn_bwd(per, qkv, d_att, lse)
-    (d_qkv,) = settle(air2, d_qkv)
+    g_wa, g_wb = wgrad(run, own, first, *d_qkv, att, dmid)
+    d_qkv, g_wa, g_wb = settle(air2, d_qkv, g_wa, g_wb)
+    wa, wb = Shards(g_wa, every), Shards(g_wb, every)
     for key in mids[1:]:
         air, (d_qkv,) = launch([(down0, key)], d_qkv)
         (d_qkv,) = settle(air, d_qkv)
-    air3, (d_qkv,) = launch([(up0, high_first[1]), (up1, high_first[0])], d_qkv)
-    g_wa, g_wb = wgrad(run, own, first, *d_qkv, att, dmid)
-    wa, wb = Shards(g_wa, every), Shards(g_wb, every)
-    d_qkv, g_wa = settle(air3[:1], d_qkv, g_wa)
-    for key in mids[1:]:
-        air, (d_qkv,) = launch([(up0, key)], d_qkv)
-        (d_qkv,) = settle(air, d_qkv)
-    airc, (d_qkv, up0_all) = launch(
-        [(down1, low_first[0]), (wa, core), (wb, core)], d_qkv, whole(up0)
-    )
-    up0_all = along_seq(up0_all)
+    air3, (d_qkv,) = launch(
+        [(up0, high_first[1]), (up1, high_first[0]), (down1, low_first[0]), (wa, core), (wb, core)],
+        d_qkv,
+    )
     back_g, gin_s, vec = last(
         x, *d_qkv, qkv_weight, row(ln1_gain), dmid, pos_col, sums2
     )
-    back_g, vec, ret_m, up0_all = settle(air3[1:] + airc, back_g, vec, ret_m, up0_all)
-    for key in mids[1:]:
-        air, (back_g,) = launch([(down1, key)], back_g)
-        (back_g,) = settle(air, back_g)
-    down = Joined(down0, down1)
-
-    air4, (back_g, vec) = launch(
-        [(up1, high_first[1]), (down, top), (wa, low_first[0]), (wb, high_first[0])], back_g, vec
-    )
+    back_g, ret_m = tie((back_g, ret_m))
     ret_g = along_seq(back_g)
     m_fast = choose(slot_col, ret_m.reshape(-1, width))
+    vec, m_fast = settle(air3, vec, m_fast)
+    for key in mids[1:]:
+        air, () = launch([(down1, key), (up0, key)])
+        settle(air)
+    down = Joined(down0, down1)
+    air4, (vec, up0_all) = launch(
+        [(up1, high_first[1]), (down, top), (wa, low_first[0]), (wb, high_first[0])],
+        vec,
+        whole(up0),
+    )
     vec = vec + pass_on(vec, *core)
     for key in low_first[:-1]:
         vec = vec + pass_on(vec, *key)
-    (m_fast,) = settle(air4[1:2], m_fast)
+    vec, ret_g, up0_all = settle(air4[::2], vec, ret_g, up0_all)
+    up0_all = along_seq(up0_all)
+    i_fast = choose(slot_col, ret_g.reshape(-1, width))
+    (i_fast,) = settle(air4[1:2], i_fast)
     down_in = whole(down)
-    vec, down_in = settle(air4[:1] + air4[2:], vec, down_in)
+    vec, down_in, up0_all = settle(air4[3:], vec, down_in, up0_all)
     for key in mids[1:]:
         air, () = launch([(up1, key)])
         settle(air)
     air5, (vec, down_in) = launch([(wa, low_first[1]), (wb, high_first[1])], vec, down_in)
-    ret_g, down_in = tie((ret_g, down_in))
     down_all = along_seq(down_in)
-    i_fast = choose(slot_col, ret_g.reshape(-1, width))
     vec = vec + pass_on(vec, *top)
     vec = vec + pass_on(vec, *z0)
-    vec, i_fast = settle(air5, vec, i_fast)
+    (vec,) = settle(air5, vec)
     for lo_key, hi_key in zip(low_first[2:], high_first[2:]):
         air, () = launch([(wa, lo_key), (wb, hi_key)])
         settle(air)
-    rest, down_all, vec, i_fast = tie(
-        (jnp.concatenate([whole(up1), whole(wa), whole(wb)], axis=1), down_all, vec, i_fast)
+    rest, down_all, vec = tie(
+        (jnp.concatenate([whole(up1), whole(wa), whole(wb)], axis=1), down_all, vec)
     )
     rest = along_seq(rest)
     vec = vec + pass_on(vec, *z1)

time: 423 us -> 418 us (0.988)
  waiting for transfers between devices: 97.1 us -> 124 us
  Pallas kernels: 189 us -> 166 us
    ppermute x22, waiting for transfers between devices: 46 us -> 64.5 us  [pass_on(): return lax.ppermute(value, axis, [(i, i ^ 1 << bit) for i in range(n)])]
    pallas_call x1, Pallas kernels: 26.9 us -> 14.2 us  [attn_bwd(): pl.pallas_call(functools.partial(attn_bwd_kernel, per), grid=(steps,), in...]
    pallas_call x1, Pallas kernels: 20.4 us -> 10.5 us  [attn_fwd(): pl.pallas_call(functools.partial(attn_fwd_kernel, per), grid=(steps,), in...]
    all_to_all x7, waiting for transfers between devices: 51.2 us -> 59.1 us  [swap(): lax.all_to_all(blocks, 'seq', split_axis=0, concat_axis=0, tiled=True)]
    convert_element_type x8 -> x7, other arithmetic: 13.3 us -> 11.5 us  [cut(): send = self.total(more={key: 1 - pair_bit(*key)}).astype(BF16)]
  transfers between devices with their start and end apart: 29 -> 29, of which waited for: 6 -> 9; matrix products, arithmetic and copies ran while one was open for 11% -> 11% of each run, Pallas kernels for 34% -> 29%
where the time goes in v5:
time: 418 us; the launch traced here: 411 us
  Pallas kernels  166 us (40%)
  waiting for transfers between devices  124 us (30%)
  starting transfers between devices  50.4 us (12%)
  other arithmetic  46.8 us (11%)
  local copies, waits for them, and re-layouts  18 us (4%)
    pallas_call x2, Pallas kernels, ffn(): pl.pallas_call(functools.partial(ffn_kernel, expert, lo, hi, run), grid=(...  68.2 us
    ppermute x22, waiting for transfers between devices, pass_on(): return lax.ppermute(value, axis, [(i, i ^ 1 << bit) for i in range(n)])  64.5 us
    all_to_all x7, waiting for transfers between devices, swap(): lax.all_to_all(blocks, 'seq', split_axis=0, concat_axis=0, tiled=True)  59.1 us
    all_to_all x7, starting transfers between devices, swap(): lax.all_to_all(blocks, 'seq', split_axis=0, concat_axis=0, tiled=True)  31 us
    pallas_call x1, Pallas kernels, last(): pl.pallas_call(last_kernel, out_shape=(jax.ShapeDtypeStruct((col.shape[0]...  21.9 us
    ppermute x22, starting transfers between devices, pass_on(): return lax.ppermute(value, axis, [(i, i ^ 1 << bit) for i in range(n)])  19.4 us
    add x5, other arithmetic, total(): sum((t.rows({**self.fixed, **extra.get('more', {})}) for t in self.terms))  16.5 us
    pallas_call x1, Pallas kernels, attn_bwd(): pl.pallas_call(functools.partial(attn_bwd_kernel, per), grid=(steps,), in...  14.2 us
  transfers between devices with their start and end apart: 29, of which 9 were waited for; matrix products, arithmetic and copies ran while one was open for 11% of the time, Pallas kernels for 29%

profile of v5, /device:TPU:0, one launch (start us, length us, event | category | flops | bytes accessed | tf_op | source)
XLA Modules:
  0.0 410.9 jit_solution(7476277566510132700)
XLA Ops:
  0.6 5.6 %pack.1 = (bf16[4,272,768]{2,1,0:T(8,128)(2,1)}, s32[8,906]{1,0:T(8,128)}, s32[906,1]{1,0:T(8,128)}) custom-call(s32[1,906]{1,0:T(1,128)} %bitcast.124, s32[1,906]{1,0:T(1,128)} %bitcast.125, bf16[906,768]{1,0:T(8,128)(2,1)} %tok_ref.1), custom_call_target="tpu_custom_call" | custom-call | tf_op jit(solution)/shard_map/pack/pallas_call | solution.py:88
  6.3 6.5 %all-to-all-start.4 = ((bf16[4,272,768]{2,1,0:T(8,128)(2,1)}), bf16[4,272,768]{2,1,0:T(8,128)(2,1)S(1)}, u32[]{:S(2)}, u32[]{:S(2)}) async-start(bf16[4,272,768]{2,1,0:T(8,128)(2,1)} %get-tuple-element.197), calls=%async_computation.4 | async-start | bytes 3342336 | tf_op jit(solution)/shard_map/all_to_all | solution.py:223
  16.9 3.8 pack_more.1
  20.8 31.1 %all-to-all-done.4 = bf16[4,272,768]{2,1,0:T(8,128)(2,1)S(1)} async-done(((bf16[4,272,768]{2,1,0:T(8,128)(2,1)}), bf16[4,272,768]{2,1,0:T(8,128)(2,1)S(1)}, u32[]{:S(2)}, u32[]{:S(2)}) %all-to-all-start.4) | async-done | bytes 1671200 | tf_op jit(solution)/shard_map/all_to_all | solution.py:223
  55.2 6.7 %conditional.2 = ((bf16[928,768]{1,0:T(8,128)(2,1)}, bf16[928,768]{1,0:T(8,128)(2,1)})) conditional(s32[]{:T(128)} %bitcast.4, (s32[8,1088]{1,0:T(8,128)S(1)}, bf16[1088,768]{1,0:T(8,128)(2,1)S(1)}) %tuple.96, (s32[906]{0:T(1024)}, (), s32[906]{0:T(1024)S(1)}, s32[906]{0:T(1024)S(1)}, bf16[906,768]{1,0:T(8,128)(2,1)}, ...), branch_computations={%region_0.0_spmd, %region_1.4_spmd} | conditional | flops 7015282 | bytes 100775368 | solution.py:905
  55.2 3.1 place.1
  61.9 3.6 all-to-all-start.5
  65.5 12.7 %qkv.1 = (bf16[928,768]{1,0:T(8,128)(2,1)}, bf16[928,2304]{1,0:T(8,128)(2,1)}) custom-call(bf16[928,768]{1,0:T(8,128)(2,1)} %get-tuple-element.203.x_ref.refs_1_, f32[1,768]{1,0:T(1,128)} %reshape.333.gain_ref, f32[1,768]{1,0:T(1,128)} %reshape.334.shift_ref, bf16[768,2304]{1,0:T(8,128)(2,1)} %w_ref.3, f32[1,768]{1,0:T(1,128)} %reshape.335.qb_ref, ...), custom_call_target="tpu_custom_call" | custom-call | flops 9852420096 | bytes 1048576 | tf_op jit(solution)/shard_map/qkv/pallas_call | solution.py:302
  78.3 10.5 %attn_fwd.1 = (bf16[928,768]{1,0:T(8,128)(2,1)}, f32[6,8,1024]{2,1,0:T(8,128)}) custom-call(bf16[928,2304]{1,0:T(8,128)(2,1)} %get-tuple-element.208.q_ref.k_ref.v_ref, bf16[928,2304]{1,0:T(8,128)(2,1)} %get-tuple-element.208.q_ref.k_ref.v_ref, bf16[928,2304]{1,0:T(8,128)(2,1)} %get-tuple-element.208.q_ref.k_ref.v_ref), custom_call_target="tpu_custom_call" | custom-call | flops 11494490112 | bytes 1048576 | tf_op jit(solution)/shard_map/attn_fwd/pallas_call | solution.py:398
  88.7 15.4 %all-to-all-done.5 = bf16[4,272,768]{2,1,0:T(8,128)(2,1)S(1)} async-done(((bf16[4,272,768]{2,1,0:T(8,128)(2,1)}), bf16[4,272,768]{2,1,0:T(8,128)(2,1)S(1)}, u32[]{:S(2)}, u32[]{:S(2)}) %all-to-all-start.5) | async-done | bytes 1671200 | tf_op jit(solution)/shard_map/all_to_all | solution.py:223
  105.3 5.5 %place_or.1.refs_2_ = bf16[928,768]{1,0:T(8,128)(2,1)} custom-call(s32[1]{0:T(128)} %bitcast.7.flag_ref, s32[8,1088]{1,0:T(8,128)S(1)} %get-tuple-element.202.pos_ref, bf16[1088,768]{1,0:T(8,128)(2,1)} %bitcast.108, bf16[928,768]{1,0:T(8,128)(2,1)} %get-tuple-element.213.other_ref), custom_call_target="tpu_custom_call" | custom-call | tf_op jit(solution)/shard_map/place_or/pallas_call | solution.py:198
  110.8 32.0 %ffn0.1 = (bf16[416,768]{1,0:T(8,128)(2,1)}, bf16[416,768]{1,0:T(8,128)(2,1)}, bf16[416,768]{1,0:T(8,128)(2,1)}, f32[16,768]{1,0:T(8,128)}, bf16[384,3072]{1,0:T...) custom-call(s32[1]{0:T(128)} %bitcast.5.own_ref, ...), custom_call_target="tpu_custom_call" | custom-call | flops 35332816896 | bytes 1048576 | tf_op jit(solution)/shard_map/ffn0/pallas_call | solution.py:646
  143.3 36.2 %ffn1.1 = (bf16[928,768]{1,0:T(8,128)(2,1)}, bf16[928,768]{1,0:T(8,128)(2,1)}, bf16[928,768]{1,0:T(8,128)(2,1)}, f32[16,768]{1,0:T(8,128)}, bf16[1088,768]{1,0:T...) custom-call(s32[1]{0:T(128)} %bitcast.5.own_ref, ...), custom_call_target="tpu_custom_call" | custom-call | flops 43486543872 | bytes 1048576 | tf_op jit(solution)/shard_map/ffn1/pallas_call | solution.py:646
  179.6 2.7 add_convert_fusion.4
  182.3 3.1 convert_add_fusion.6
  185.4 3.2 convert_add_fusion
  188.6 1.5 collective-permute-start.2
  192.2 4.4 %all-to-all-start.6 = ((bf16[4,272,768]{2,1,0:T(8,128)(2,1)}), bf16[4,272,768]{2,1,0:T(8,128)(2,1)}, u32[]{:S(2)}, u32[]{:S(2)}) async-start(bf16[4,272,768]{2,1,0:T(8,128)(2,1)} %bitcast.116), calls=%async_computation.6 | async-start | bytes 3342336 | tf_op jit(solution)/shard_map/all_to_all | solution.py:223
  196.5 14.2 %attn_bwd.1 = (bf16[928,768]{1,0:T(8,128)(2,1)}, bf16[928,768]{1,0:T(8,128)(2,1)}, bf16[928,768]{1,0:T(8,128)(2,1)}) custom-call(bf16[928,2304]{1,0:T(8,128)(2,1)} %get-tuple-element.208.q_ref.k_ref.v_ref, bf16[928,2304]{1,0:T(8,128)(2,1)} %get-tuple-element.208.q_ref.k_ref.v_ref, bf16[928,2304]{1,0:T(8,128)(2,1)} %get-tuple-element.208.q_ref.k_ref.v_ref, ...), custom_call_target="tpu_custom_call" | custom-call | flops 14778630144 | bytes 1048576 | tf_op jit(solution)/shard_map/attn_bwd/pallas_call | solution.py:473
  210.8 10.0 %wgrad.1 = (bf16[384,1536]{1,0:T(8,128)(2,1)}, bf16[384,1536]{1,0:T(8,128)(2,1)}, bf16[384,1536]{1,0:T(8,128)(2,1)}, bf16[384,1536]{1,0:T(8,128)(2,1)}) custom-call(s32[1]{0:T(128)} %bitcast.5.own_ref, bf16[928,768]{1,0:T(8,128)(2,1)} %get-tuple-element.254.first_ref, bf16[928,768]{1,0:T(8,128)(2,1)} %get-tuple-element.274.dq_ref, ...), custom_call_target="tpu_custom_call" | custom-call | flops 13136560128 | bytes 1048576 | tf_op jit(solution)/shard_map/wgrad/pallas_call | solution.py:746
  220.8 2.3 constant_dynamic-slice_fusion.3
  223.1 4.1 convert_add_fusion.1
  227.2 2.8 add_convert_fusion.2
  232.0 1.5 collective-permute-start.8
  234.1 21.9 %last.1 = (bf16[1088,768]{1,0:T(8,128)(2,1)}, bf16[928,768]{1,0:T(8,128)(2,1)}, f32[24,768]{1,0:T(8,128)}) custom-call(bf16[928,768]{1,0:T(8,128)(2,1)} %get-tuple-element.203.x_ref.refs_1_, bf16[928,768]{1,0:T(8,128)(2,1)} %get-tuple-element.274.dq_ref, bf16[928,768]{1,0:T(8,128)(2,1)} %get-tuple-element.275.dk_ref, ...), custom_call_target="tpu_custom_call" | custom-call | flops 9852420096 | bytes 1048576 | tf_op jit(solution)/shard_map/last/pallas_call | solution.py:765
  255.9 3.3 convert_add_fusion.9
  259.2 5.0 %all-to-all-start.7 = ((bf16[4,272,768]{2,1,0:T(8,128)(2,1)}), bf16[4,272,768]{2,1,0:T(8,128)(2,1)}, u32[]{:S(2)}, u32[]{:S(2)}) async-start(bf16[4,272,768]{2,1,0:T(8,128)(2,1)} %bitcast.117), calls=%async_computation.7 | async-start | bytes 3342336 | tf_op jit(solution)/shard_map/all_to_all | solution.py:223
  264.3 4.7 %choose.2 = bf16[906,768]{1,0:T(8,128)(2,1)} custom-call(s32[906,1]{1,0:T(8,128)} %get-tuple-element.279.col_ref, bf16[1088,768]{1,0:T(8,128)(2,1)} %bitcast.25.value_ref), custom_call_target="tpu_custom_call" | custom-call | tf_op jit(solution)/shard_map/choose/pallas_call | solution.py:214
  269.0 2.8 collective-permute-done.8
  271.8 2.1 constant_dynamic-slice_fusion.6
  275.4 2.1 add_convert_fusion.5
  277.5 3.0 select_convert_fusion
  280.5 2.3 fusion.16
  283.9 1.5 collective-permute-start.12
  287.3 2.8 convert_add_fusion.15
  290.1 1.5 collective-permute-start.15
  291.6 20.1 %collective-permute-done.14 = f32[24,768]{1,0:T(8,128)S(1)} collective-permute-done((f32[24,768]{1,0:T(8,128)S(1)}, f32[24,768]{1,0:T(8,128)S(1)}, u32[]{:S(2)}, u32[]{:S(2)}) %collective-permute-start.14) | collective-permute-done | bytes 73760 | tf_op jit(solution)/shard_map/ppermute | solution.py:789
  312.4 4.7 %choose.3 = bf16[906,768]{1,0:T(8,128)(2,1)} custom-call(s32[906,1]{1,0:T(8,128)} %get-tuple-element.279.col_ref, bf16[1088,768]{1,0:T(8,128)(2,1)} %bitcast.47.value_ref), custom_call_target="tpu_custom_call" | custom-call | tf_op jit(solution)/shard_map/choose/pallas_call | solution.py:214
  317.1 4.5 %all-to-all-start.8 = ((bf16[4,24,3072]{2,1,0:T(8,128)(2,1)}), bf16[4,24,3072]{2,1,0:T(8,128)(2,1)}, u32[]{:S(2)}, u32[]{:S(2)}) async-start(bf16[4,24,3072]{2,1,0:T(8,128)(2,1)} %bitcast.109), calls=%async_computation.8 | async-start | bytes 1179648 | tf_op jit(solution)/shard_map/all_to_all | solution.py:223
  321.5 4.0 add_convert_fusion
  327.6 8.2 %all-to-all-done.8 = bf16[4,24,3072]{2,1,0:T(8,128)(2,1)} async-done(((bf16[4,24,3072]{2,1,0:T(8,128)(2,1)}), bf16[4,24,3072]{2,1,0:T(8,128)(2,1)}, u32[]{:S(2)}, u32[]{:S(2)}) %all-to-all-start.8) | async-done | bytes 589856 | tf_op jit(solution)/shard_map/all_to_all | solution.py:223
  340.2 3.5 all-to-all-start.9
  344.7 2.0 collective-permute-start.20
  348.1 14.1 %collective-permute-done.20 = f32[24,768]{1,0:T(8,128)S(1)} collective-permute-done((f32[24,768]{1,0:T(8,128)S(1)}, f32[24,768]{1,0:T(8,128)S(1)}, u32[]{:S(2)}, u32[]{:S(2)}) %collective-permute-start.20) | collective-permute-done | bytes 73760 | tf_op jit(solution)/shard_map/ppermute | solution.py:789
  365.6 4.5 %all-to-all-done.9 = bf16[4,192,768]{2,1,0:T(8,128)(2,1)S(1)} async-done(((bf16[4,192,768]{2,1,0:T(8,128)(2,1)}), bf16[4,192,768]{2,1,0:T(8,128)(2,1)S(1)}, u32[]{:S(2)}, u32[]{:S(2)}) %all-to-all-start.9) | async-done | bytes 1179680 | tf_op jit(solution)/shard_map/all_to_all | solution.py:223
  370.1 3.5 all-to-all-start.10
  374.8 2.9 collective-permute-start.21
  378.7 26.1 %collective-permute-done.21 = f32[24,768]{1,0:T(8,128)S(1)} collective-permute-done((f32[24,768]{1,0:T(8,128)S(1)}, f32[24,768]{1,0:T(8,128)S(1)}, u32[]{:S(2)}, u32[]{:S(2)}) %collective-permute-start.21) | collective-permute-done | bytes 73760 | tf_op jit(solution)/shard_map/ppermute | solution.py:789
  (140 shorter events, 38.0 us)
Async XLA Ops:
  6.2 6.6 %copy-start.26 = (f32[768]{0:T(1024)S(1)}, f32[768]{0:T(1024)}, u32[]{:S(2)}) copy-start(f32[768]{0:T(1024)} %param.29) | copy-start | bytes 9220
  6.2 7.2 %copy-start.27 = (f32[768]{0:T(1024)S(1)}, f32[768]{0:T(1024)}, u32[]{:S(2)}) copy-start(f32[768]{0:T(1024)} %param.30) | copy-start | bytes 9220
  6.2 7.7 %copy-start.28 = (f32[768]{0:T(1024)S(1)}, f32[768]{0:T(1024)}, u32[]{:S(2)}) copy-start(f32[768]{0:T(1024)} %param.32) | copy-start | bytes 9220
  6.3 8.3 %copy-start.29 = (f32[768]{0:T(1024)S(1)}, f32[768]{0:T(1024)}, u32[]{:S(2)}) copy-start(f32[768]{0:T(1024)} %param.33) | copy-start | bytes 9220
  6.3 8.9 %copy-start.30 = (f32[768]{0:T(1024)S(1)}, f32[768]{0:T(1024)}, u32[]{:S(2)}) copy-start(f32[768]{0:T(1024)} %param.35) | copy-start | bytes 9220
  6.3 9.5 %copy-start.31 = (f32[768]{0:T(1024)S(1)}, f32[768]{0:T(1024)}, u32[]{:S(2)}) copy-start(f32[768]{0:T(1024)} %param.36) | copy-start | bytes 9220
  6.3 10.1 %copy-start.32 = (f32[768]{0:T(1024)S(1)}, f32[768]{0:T(1024)}, u32[]{:S(2)}) copy-start(f32[768]{0:T(1024)} %param.37) | copy-start | bytes 9220
  6.3 10.6 %copy-start.17 = (bf16[906,768]{1,0:T(8,128)(2,1)S(1)}, bf16[906,768]{1,0:T(8,128)(2,1)}, u32[]{:S(2)}) copy-start(bf16[906,768]{1,0:T(8,128)(2,1)} %value_ref.1) | copy-start | bytes 4174852
  6.3 45.6 %all-to-all-start.4 = ((bf16[4,272,768]{2,1,0:T(8,128)(2,1)}), bf16[4,272,768]{2,1,0:T(8,128)(2,1)S(1)}, u32[]{:S(2)}, u32[]{:S(2)}) async-start(bf16[4,272,768]{2,1,0:T(8,128)(2,1)} %get-tuple-element.197), calls=%async_computation.4 | async-start | bytes 3342336 | tf_op jit(solution)/shard_map/all_to_all | solution.py:223
  20.8 34.4 %copy-start.22 = (s32[906]{0:T(1024)S(1)}, s32[906]{0:T(1024)}, u32[]{:S(2)}) copy-start(s32[906]{0:T(1024)} %param.27) | copy-start | bytes 10876
  20.8 34.4 %copy-start.24 = (s32[906]{0:T(1024)S(1)}, s32[906]{0:T(1024)}, u32[]{:S(2)}) copy-start(s32[906]{0:T(1024)} %param.28) | copy-start | bytes 10876
  61.9 42.2 %all-to-all-start.5 = ((bf16[4,272,768]{2,1,0:T(8,128)(2,1)}), bf16[4,272,768]{2,1,0:T(8,128)(2,1)S(1)}, u32[]{:S(2)}, u32[]{:S(2)}) async-start(bf16[4,272,768]{2,1,0:T(8,128)(2,1)} %pack_more.1), calls=%async_computation.5 | async-start | bytes 3342336 | tf_op jit(solution)/shard_map/all_to_all | solution.py:223
  110.8 32.6 %copy-start.33 = (bf16[928,768]{1,0:T(8,128)(2,1)S(1)}, bf16[928,768]{1,0:T(8,128)(2,1)}, u32[]{:S(2)}) copy-start(bf16[928,768]{1,0:T(8,128)(2,1)} %get-tuple-element.203.x_ref.refs_1_) | copy-start | bytes 4276228
  142.8 36.8 %collective-permute-start = (bf16[384,3072]{1,0:T(8,128)(2,1)}, bf16[384,3072]{1,0:T(8,128)(2,1)}, u32[]{:S(2)}, u32[]{:S(2)}) collective-permute-start(bf16[384,3072]{1,0:T(8,128)(2,1)} %get-tuple-element.223), channel_id=1, source_target_pairs={{0,4},{4,0},{8,12},{12,8},{16,20},{20,16},{24,28},{28,24},{1,5},{5... | collective-permute-start | bytes 7077896 | tf_op jit(solution)/shard_map/ppermute | solution.py:789
  142.8 36.7 %collective-permute-start.1 = (bf16[1536,768]{1,0:T(8,128)(2,1)}, bf16[1536,768]{1,0:T(8,128)(2,1)}, u32[]{:S(2)}, u32[]{:S(2)}) collective-permute-start(bf16[1536,768]{1,0:T(8,128)(2,1)} %get-tuple-element.224), channel_id=1, source_target_pairs={{0,4},{4,0},{8,12},{12,8},{16,20},{20,16},{24,28},{28,24},{1,5},{5... | collective-permute-start | bytes 7077896 | tf_op jit(solution)/shard_map/ppermute | solution.py:789
  143.3 36.2 %copy-start.12 = (bf16[384,3072]{1,0:T(8,128)(2,1)S(1)}, bf16[384,3072]{1,0:T(8,128)(2,1)}, u32[]{:S(2)}) copy-start(bf16[384,3072]{1,0:T(8,128)(2,1)} %get-tuple-element.237) | copy-start | bytes 7077892
  188.6 32.1 %collective-permute-start.2 = (bf16[192,3072]{1,0:T(8,128)(2,1)}, bf16[192,3072]{1,0:T(8,128)(2,1)}, u32[]{:S(2)}, u32[]{:S(2)}) collective-permute-start(bf16[192,3072]{1,0:T(8,128)(2,1)} %bitcast.11), channel_id=1, source_target_pairs={{0,16},{4,20},{8,24},{12,28},{16,0},{20,4},{24,8},{28,12},{1,17},{... | collective-permute-start | bytes 3538952 | tf_op jit(solution)/shard_map/ppermute | solution.py:789
  190.2 30.6 %collective-permute-start.3 = (bf16[768,768]{1,0:T(8,128)(2,1)}, bf16[768,768]{1,0:T(8,128)(2,1)S(1)}, u32[]{:S(2)}, u32[]{:S(2)}) collective-permute-start(bf16[768,768]{1,0:T(8,128)(2,1)} %bitcast.14), channel_id=1, source_target_pairs={{0,8},{4,12},{8,0},{12,4},{16,24},{20,28},{24,16},{28,20},{1,9},{5... | collective-permute-start | bytes 3538952 | tf_op jit(solution)/shard_map/ppermute | solution.py:789
  191.7 29.1 %collective-permute-start.4 = (bf16[384,3072]{1,0:T(8,128)(2,1)}, bf16[384,3072]{1,0:T(8,128)(2,1)}, u32[]{:S(2)}, u32[]{:S(2)}) collective-permute-start(bf16[384,3072]{1,0:T(8,128)(2,1)} %get-tuple-element.247), channel_id=1, source_target_pairs={{0,4},{4,0},{8,12},{12,8},{16,20},{20,16},{24,28},{28,24},{1,5},{5... | collective-permute-start | bytes 7077896 | tf_op jit(solution)/shard_map/ppermute | solution.py:789
  191.7 29.1 %collective-permute-start.5 = (bf16[1536,768]{1,0:T(8,128)(2,1)}, bf16[1536,768]{1,0:T(8,128)(2,1)}, u32[]{:S(2)}, u32[]{:S(2)}) collective-permute-start(bf16[1536,768]{1,0:T(8,128)(2,1)} %get-tuple-element.248), channel_id=1, source_target_pairs={{0,4},{4,0},{8,12},{12,8},{16,20},{20,16},{24,28},{28,24},{1,5},{5... | collective-permute-start | bytes 7077896 | tf_op jit(solution)/shard_map/ppermute | solution.py:789
  192.2 67.1 %all-to-all-start.6 = ((bf16[4,272,768]{2,1,0:T(8,128)(2,1)}), bf16[4,272,768]{2,1,0:T(8,128)(2,1)}, u32[]{:S(2)}, u32[]{:S(2)}) async-start(bf16[4,272,768]{2,1,0:T(8,128)(2,1)} %bitcast.116), calls=%async_computation.6 | async-start | bytes 3342336 | tf_op jit(solution)/shard_map/all_to_all | solution.py:223
  231.0 38.0 %collective-permute-start.6 = (bf16[96,3072]{1,0:T(8,128)(2,1)}, bf16[96,3072]{1,0:T(8,128)(2,1)}, u32[]{:S(2)}, u32[]{:S(2)}) collective-permute-start(bf16[96,3072]{1,0:T(8,128)(2,1)} %fusion.20), channel_id=1, source_target_pairs={{0,8},{4,12},{8,0},{12,4},{16,24},{20,28},{24,16},{28,20},{1,9},{5... | collective-permute-start | bytes 1769480 | tf_op jit(solution)/shard_map/ppermute | solution.py:789
  231.6 37.4 %collective-permute-start.7 = (bf16[192,3072]{1,0:T(8,128)(2,1)}, bf16[192,3072]{1,0:T(8,128)(2,1)}, u32[]{:S(2)}, u32[]{:S(2)}) collective-permute-start(bf16[192,3072]{1,0:T(8,128)(2,1)} %bitcast.20), channel_id=1, source_target_pairs={{0,16},{4,20},{8,24},{12,28},{16,0},{20,4},{24,8},{28,12},{1,17},{... | collective-permute-start | bytes 3538952 | tf_op jit(solution)/shard_map/ppermute | solution.py:789
  232.0 39.8 %collective-permute-start.8 = (bf16[768,768]{1,0:T(8,128)(2,1)}, bf16[768,768]{1,0:T(8,128)(2,1)}, u32[]{:S(2)}, u32[]{:S(2)}) collective-permute-start(bf16[768,768]{1,0:T(8,128)(2,1)} %bitcast.23), channel_id=1, source_target_pairs={{0,8},{4,12},{8,0},{12,4},{16,24},{20,28},{24,16},{28,20},{1,9},{5... | collective-permute-start | bytes 3538952 | tf_op jit(solution)/shard_map/ppermute | solution.py:789
  233.6 38.3 %collective-permute-start.9 = (bf16[384,1536]{1,0:T(8,128)(2,1)}, bf16[384,1536]{1,0:T(8,128)(2,1)}, u32[]{:S(2)}, u32[]{:S(2)}) collective-permute-start(bf16[384,1536]{1,0:T(8,128)(2,1)} %get-tuple-element.272), channel_id=1, source_target_pairs={{0,4},{4,0},{8,12},{12,8},{16,20},{20,16},{24,28},{28,24},{1,5},{5... | collective-permute-start | bytes 3538952 | tf_op jit(solution)/shard_map/ppermute | solution.py:789
  233.6 38.3 %collective-permute-start.10 = (bf16[384,1536]{1,0:T(8,128)(2,1)}, bf16[384,1536]{1,0:T(8,128)(2,1)}, u32[]{:S(2)}, u32[]{:S(2)}) collective-permute-start(bf16[384,1536]{1,0:T(8,128)(2,1)} %get-tuple-element.273), channel_id=1, source_target_pairs={{0,4},{4,0},{8,12},{12,8},{16,20},{20,16},{24,28},{28,24},{1,5},{5... | collective-permute-start | bytes 3538952 | tf_op jit(solution)/shard_map/ppermute | solution.py:789
  259.2 53.1 %all-to-all-start.7 = ((bf16[4,272,768]{2,1,0:T(8,128)(2,1)}), bf16[4,272,768]{2,1,0:T(8,128)(2,1)}, u32[]{:S(2)}, u32[]{:S(2)}) async-start(bf16[4,272,768]{2,1,0:T(8,128)(2,1)} %bitcast.117), calls=%async_computation.7 | async-start | bytes 3342336 | tf_op jit(solution)/shard_map/all_to_all | solution.py:223
  269.0 5.0 %copy-start.19 = (bf16[384,1536]{1,0:T(8,128)(2,1)S(1)}, bf16[384,1536]{1,0:T(8,128)(2,1)}, u32[]{:S(2)}) copy-start(bf16[384,1536]{1,0:T(8,128)(2,1)} %get-tuple-element.286) | copy-start | bytes 3538948
  280.5 4.9 %copy-start.21 = (f32[24,768]{1,0:T(8,128)S(1)}, f32[24,768]{1,0:T(8,128)}, u32[]{:S(2)}) copy-start(f32[24,768]{1,0:T(8,128)} %get-tuple-element.294) | copy-start | bytes 221188
  282.9 34.2 %collective-permute-start.16 = (bf16[768,768]{1,0:T(8,128)(2,1)}, bf16[768,768]{1,0:T(8,128)(2,1)}, u32[]{:S(2)}, u32[]{:S(2)}) collective-permute-start(bf16[768,768]{1,0:T(8,128)(2,1)} %select_convert_fusion), channel_id=1, source_target_pairs={{0,16},{4,20},{8,24},{12,28},{16,0},{20,4},{24,8},{28,12},{1,17},{... | collective-permute-start | bytes 3538952 | tf_op jit(solution)/shard_map/ppermute | solution.py:789
  283.4 29.0 %collective-permute-start.11 = (bf16[96,3072]{1,0:T(8,128)(2,1)S(1)}, bf16[96,3072]{1,0:T(8,128)(2,1)}, u32[]{:S(2)}, u32[]{:S(2)}) collective-permute-start(bf16[96,3072]{1,0:T(8,128)(2,1)S(1)} %get-tuple-element.292), channel_id=1, source_target_pairs={{0,8},{4,12},{8,0},{12,4},{16,24},{20,28},{24,16},{28,20},{1,9},{5... | collective-permute-start | bytes 1769480 | tf_op jit(solution)/shard_map/ppermute | solution.py:789
  283.9 28.5 %collective-permute-start.12 = (bf16[192,1536]{1,0:T(8,128)(2,1)S(1)}, bf16[192,1536]{1,0:T(8,128)(2,1)}, u32[]{:S(2)}, u32[]{:S(2)}) collective-permute-start(bf16[192,1536]{1,0:T(8,128)(2,1)S(1)} %bitcast.123), channel_id=1, source_target_pairs={{0,8},{4,12},{8,0},{12,4},{16,24},{20,28},{24,16},{28,20},{1,9},{5... | collective-permute-start | bytes 1769480 | tf_op jit(solution)/shard_map/ppermute | solution.py:789
  285.4 1.3 collective-permute-start.13
  286.7 25.0 %collective-permute-start.14 = (f32[24,768]{1,0:T(8,128)S(1)}, f32[24,768]{1,0:T(8,128)S(1)}, u32[]{:S(2)}, u32[]{:S(2)}) collective-permute-start(f32[24,768]{1,0:T(8,128)S(1)} %add.297), channel_id=1, source_target_pairs={{0,8},{4,12},{8,0},{12,4},{16,24},{20,28},{24,16},{28,20},{1,9},{5... | collective-permute-start | bytes 221192 | tf_op jit(solution)/shard_map/ppermute | solution.py:789
  290.1 37.5 %collective-permute-start.15 = (bf16[192,1536]{1,0:T(8,128)(2,1)}, bf16[192,1536]{1,0:T(8,128)(2,1)}, u32[]{:S(2)}, u32[]{:S(2)}) collective-permute-start(bf16[192,1536]{1,0:T(8,128)(2,1)} %bitcast.37), channel_id=1, source_target_pairs={{0,16},{4,20},{8,24},{12,28},{16,0},{20,4},{24,8},{28,12},{1,17},{... | collective-permute-start | bytes 1769480 | tf_op jit(solution)/shard_map/ppermute | solution.py:789
  317.1 18.7 %all-to-all-start.8 = ((bf16[4,24,3072]{2,1,0:T(8,128)(2,1)}), bf16[4,24,3072]{2,1,0:T(8,128)(2,1)}, u32[]{:S(2)}, u32[]{:S(2)}) async-start(bf16[4,24,3072]{2,1,0:T(8,128)(2,1)} %bitcast.109), calls=%async_computation.8 | async-start | bytes 1179648 | tf_op jit(solution)/shard_map/all_to_all | solution.py:223
  326.7 10.1 %copy-start.7 = (f32[1,1,2,2,24,1536]{5,4,3,2,1,0:T(8,128)S(1)}, f32[1,1,2,2,24,1536]{5,4,3,2,1,0:T(8,128)}, u32[]{:S(2)}) copy-start(f32[1,1,2,2,24,1536]{5,4,3,2,1,0:T(8,128)} %get-tuple-element.354) | copy-start | bytes 1769476
  337.7 9.1 %copy-start.4 = (f32[1,1,2,2,24,3072]{5,4,3,2,1,0:T(8,128)S(1)}, f32[1,1,2,2,24,3072]{5,4,3,2,1,0:T(8,128)}, u32[]{:S(2)}) copy-start(f32[1,1,2,2,24,3072]{5,4,3,2,1,0:T(8,128)} %get-tuple-element.344) | copy-start | bytes 3538948
  337.7 9.1 %copy-start.13 = (bf16[1,2,2,24,3072]{4,3,2,1,0:T(8,128)(2,1)S(1)}, bf16[1,2,2,24,3072]{4,3,2,1,0:T(8,128)(2,1)}, u32[]{:S(2)}) copy-start(bf16[1,2,2,24,3072]{4,3,2,1,0:T(8,128)(2,1)} %get-tuple-element.356) | copy-start | bytes 1769476
  337.7 6.1 %collective-permute-start.19 = (f32[24,768]{1,0:T(8,128)}, f32[24,768]{1,0:T(8,128)}, u32[]{:S(2)}, u32[]{:S(2)}) collective-permute-start(f32[24,768]{1,0:T(8,128)} %add.298), channel_id=1, source_target_pairs={{0,16},{4,20},{8,24},{12,28},{16,0},{20,4},{24,8},{28,12},{1,17},{... | collective-permute-start | bytes 221192 | tf_op jit(solution)/shard_map/ppermute | solution.py:789
  339.2 23.1 %collective-permute-start.17 = (bf16[96,1536]{1,0:T(8,128)(2,1)}, bf16[96,1536]{1,0:T(8,128)(2,1)}, u32[]{:S(2)}, u32[]{:S(2)}) collective-permute-start(bf16[96,1536]{1,0:T(8,128)(2,1)} %fusion.24), channel_id=1, source_target_pairs={{0,16},{4,20},{8,24},{12,28},{16,0},{20,4},{24,8},{28,12},{1,17},{... | collective-permute-start | bytes 884744 | tf_op jit(solution)/shard_map/ppermute | solution.py:789
  339.7 22.6 %collective-permute-start.18 = (bf16[96,1536]{1,0:T(8,128)(2,1)}, bf16[96,1536]{1,0:T(8,128)(2,1)}, u32[]{:S(2)}, u32[]{:S(2)}) collective-permute-start(bf16[96,1536]{1,0:T(8,128)(2,1)} %fusion.23), channel_id=1, source_target_pairs={{0,8},{4,12},{8,0},{12,4},{16,24},{20,28},{24,16},{28,20},{1,9},{5... | collective-permute-start | bytes 884744 | tf_op jit(solution)/shard_map/ppermute | solution.py:789
  340.2 29.9 %all-to-all-start.9 = ((bf16[4,192,768]{2,1,0:T(8,128)(2,1)}), bf16[4,192,768]{2,1,0:T(8,128)(2,1)S(1)}, u32[]{:S(2)}, u32[]{:S(2)}) async-start(bf16[4,192,768]{2,1,0:T(8,128)(2,1)} %bitcast.53), calls=%async_computation.9 | async-start | bytes 2359296 | tf_op jit(solution)/shard_map/all_to_all | solution.py:223
  344.7 17.6 %collective-permute-start.20 = (f32[24,768]{1,0:T(8,128)S(1)}, f32[24,768]{1,0:T(8,128)S(1)}, u32[]{:S(2)}, u32[]{:S(2)}) collective-permute-start(f32[24,768]{1,0:T(8,128)S(1)} %add.310), channel_id=1, source_target_pairs={{0,1},{1,0},{2,3},{3,2},{4,5},{5,4},{6,7},{7,6},{8,9},{9,8},{10,11... | collective-permute-start | bytes 221192 | tf_op jit(solution)/shard_map/ppermute | solution.py:789
  346.7 15.6 %copy-start.15 = (f32[1,1,2,2,24,1536]{5,4,3,2,1,0:T(8,128)S(1)}, f32[1,1,2,2,24,1536]{5,4,3,2,1,0:T(8,128)}, u32[]{:S(2)}) copy-start(f32[1,1,2,2,24,1536]{5,4,3,2,1,0:T(8,128)} %get-tuple-element.355) | copy-start | bytes 1769476
  348.1 15.3 %copy-start.14 = (f32[1,1,2,2,24,1536]{5,4,3,2,1,0:T(8,128)S(1)}, f32[1,1,2,2,24,1536]{5,4,3,2,1,0:T(8,128)}, u32[]{:S(2)}) copy-start(f32[1,1,2,2,24,1536]{5,4,3,2,1,0:T(8,128)} %get-tuple-element.372) | copy-start | bytes 1769476
  370.1 34.8 %all-to-all-start.10 = ((bf16[4,24,6144]{2,1,0:T(8,128)(2,1)}), bf16[4,24,6144]{2,1,0:T(8,128)(2,1)S(1)}, u32[]{:S(2)}, u32[]{:S(2)}) async-start(bf16[4,24,6144]{2,1,0:T(8,128)(2,1)} %bitcast.54), calls=%async_computation.10 | async-start | bytes 2359296 | tf_op jit(solution)/shard_map/all_to_all | solution.py:223
  374.8 30.0 %collective-permute-start.21 = (f32[24,768]{1,0:T(8,128)S(1)}, f32[24,768]{1,0:T(8,128)S(1)}, u32[]{:S(2)}, u32[]{:S(2)}) collective-permute-start(f32[24,768]{1,0:T(8,128)S(1)} %add.311), channel_id=1, source_target_pairs={{0,2},{1,3},{2,0},{3,1},{4,6},{5,7},{6,4},{7,5},{8,10},{9,11},{10,... | collective-permute-start | bytes 221192 | tf_op jit(solution)/shard_map/ppermute | solution.py:789
  (14 other events, 35.3 us)

commit v6 on v5

--- a/solution.py
+++ b/solution.py
@@ -963,39 +963,45 @@
         air, (d_qkv,) = launch([(down0, key)], d_qkv)
         (d_qkv,) = settle(air, d_qkv)
     air3, (d_qkv,) = launch(
-        [(up0, high_first[1]), (up1, high_first[0]), (down1, low_first[0]), (wa, core), (wb, core)],
+        [(up1, high_first[0]), (down1, low_first[0]), (wa, core), (wb, core)],
         d_qkv,
     )
+    up0_in = whole(up0).reshape(1 << len(mids), ways, -1, hidden)
+    up0_in = up0_in.transpose(1, 0, 2, 3).reshape(-1, hidden)
+    ret_m, up0_in, d_qkv = tie((ret_m, up0_in, d_qkv))
+    up0_all = along_seq(up0_in)
     back_g, gin_s, vec = last(
         x, *d_qkv, qkv_weight, row(ln1_gain), dmid, pos_col, sums2
     )
-    back_g, ret_m = tie((back_g, ret_m))
+    back_g, ret_m, up0_all = tie((back_g, ret_m, up0_all))
     ret_g = along_seq(back_g)
-    m_fast = choose(slot_col, ret_m.reshape(-1, width))
-    vec, m_fast = settle(air3, vec, m_fast)
+    (vec,) = settle(air3, vec)
     for key in mids[1:]:
-        air, () = launch([(down1, key), (up0, key)])
+        air, () = launch([(down1, key)])
         settle(air)
     down = Joined(down0, down1)
-    air4, (vec, up0_all) = launch(
+    air4, (vec, ret_m, up0_all) = launch(
         [(up1, high_first[1]), (down, top), (wa, low_first[0]), (wb, high_first[0])],
         vec,
-        whole(up0),
-    )
+        ret_m,
+        up0_all,
+    )
+    m_fast = choose(slot_col, ret_m.reshape(-1, width))
+    up0 = Shards((all_of(up0_all).astype(BF16),), dp_bits[1:-1])
     vec = vec + pass_on(vec, *core)
     for key in low_first[:-1]:
         vec = vec + pass_on(vec, *key)
-    vec, ret_g, up0_all = settle(air4[::2], vec, ret_g, up0_all)
-    up0_all = along_seq(up0_all)
+    vec, ret_g, m_fast = settle(air4[:3], vec, ret_g, m_fast)
+    down_in = whole(down)
+    vec, down_in = settle(air4[3:], vec, down_in)
+    for key in mids[1:]:
+        air, () = launch([(up1, key), (up0, key)])
+        settle(air)
+    air5, (vec, down_in) = launch(
+        [(wa, low_first[1]), (wb, high_first[1]), (up0, mids[0])], vec, down_in
+    )
+    down_all = along_seq(down_in)
     i_fast = choose(slot_col, ret_g.reshape(-1, width))
-    (i_fast,) = settle(air4[1:2], i_fast)
-    down_in = whole(down)
-    vec, down_in, up0_all = settle(air4[3:], vec, down_in, up0_all)
-    for key in mids[1:]:
-        air, () = launch([(up1, key)])
-        settle(air)
-    air5, (vec, down_in) = launch([(wa, low_first[1]), (wb, high_first[1])], vec, down_in)
-    down_all = along_seq(down_in)
     vec = vec + pass_on(vec, *top)
     vec = vec + pass_on(vec, *z0)
     (vec,) = settle(air5, vec)
@@ -1009,7 +1015,7 @@
     vec = vec + pass_on(vec, *z1)
     down = all_of(down_all)
     down, vec, up0_sum, rest, m_fast, i_fast, mixed_s, gin_s = tie(
-        (down, vec, all_of(up0_all), rest, m_fast, i_fast, mixed_s, gin_s)
+        (down, vec, up0.total(), rest, m_fast, i_fast, mixed_s, gin_s)
     )
     rest = all_of(rest)
     up = jnp.stack([up0_sum, rest[:, :hidden]])

time: 418 us -> 404 us (0.967)
  waiting for transfers between devices: 124 us -> 105 us
    ppermute x22, waiting for transfers between devices: 64.5 us -> 51.4 us  [pass_on(): return lax.ppermute(value, axis, [(i, i ^ 1 << bit) for i in range(n)])]
    all_to_all x7, waiting for transfers between devices: 59.1 us -> 53.1 us  [swap(): lax.all_to_all(blocks, 'seq', split_axis=0, concat_axis=0, tiled=True)]
    convert_element_type x7 -> x6, other arithmetic: 11.5 us -> 9.73 us  [cut(): send = self.total(more={key: 1 - pair_bit(*key)}).astype(BF16)]
    add x5 -> x6, other arithmetic: 16.5 us -> 17.8 us  [total(): sum((t.rows({**self.fixed, **extra.get('more', {})}) for t in self.terms))]
  transfers between devices with their start and end apart: 29 -> 29, of which waited for: 9 -> 8; matrix products, arithmetic and copies ran while one was open for 11% -> 12% of each run, Pallas kernels for 29% -> 30%
where the time goes in v6:
time: 404 us; the launch traced here: 397 us
  Pallas kernels  166 us (41%)
  waiting for transfers between devices  105 us (26%)
  starting transfers between devices  52 us (13%)
  other arithmetic  49 us (12%)
  local copies, waits for them, and re-layouts  19.6 us (5%)
    pallas_call x2, Pallas kernels, ffn(): pl.pallas_call(functools.partial(ffn_kernel, expert, lo, hi, run), grid=(...  67.8 us
    all_to_all x7, waiting for transfers between devices, swap(): lax.all_to_all(blocks, 'seq', split_axis=0, concat_axis=0, tiled=True)  53.1 us
    ppermute x22, waiting for transfers between devices, pass_on(): return lax.ppermute(value, axis, [(i, i ^ 1 << bit) for i in range(n)])  51.4 us
    all_to_all x7, starting transfers between devices, swap(): lax.all_to_all(blocks, 'seq', split_axis=0, concat_axis=0, tiled=True)  32.6 us
    pallas_call x1, Pallas kernels, last(): pl.pallas_call(last_kernel, out_shape=(jax.ShapeDtypeStruct((col.shape[0]...  21.6 us
    ppermute x22, starting transfers between devices, pass_on(): return lax.ppermute(value, axis, [(i, i ^ 1 << bit) for i in range(n)])  19.4 us
    add x6, other arithmetic, total(): sum((t.rows({**self.fixed, **extra.get('more', {})}) for t in self.terms))  17.8 us
    pallas_call x1, Pallas kernels, attn_bwd(): pl.pallas_call(functools.partial(attn_bwd_kernel, per), grid=(steps,), in...  14.3 us
  transfers between devices with their start and end apart: 29, of which 8 were waited for; matrix products, arithmetic and copies ran while one was open for 12% of the time, Pallas kernels for 30%

profile of v6, /device:TPU:0, one launch (start us, length us, event | category | flops | bytes accessed | tf_op | source)
XLA Modules:
  0.0 396.6 jit_solution(8279886926332809089)
XLA Ops:
  0.6 5.6 %pack.1 = (bf16[4,272,768]{2,1,0:T(8,128)(2,1)}, s32[8,906]{1,0:T(8,128)}, s32[906,1]{1,0:T(8,128)}) custom-call(s32[1,906]{1,0:T(1,128)} %bitcast.129, s32[1,906]{1,0:T(1,128)} %bitcast.130, bf16[906,768]{1,0:T(8,128)(2,1)} %tok_ref.1), custom_call_target="tpu_custom_call" | custom-call | tf_op jit(solution)/shard_map/pack/pallas_call | solution.py:88
  6.3 6.5 %all-to-all-start.4 = ((bf16[4,272,768]{2,1,0:T(8,128)(2,1)}), bf16[4,272,768]{2,1,0:T(8,128)(2,1)S(1)}, u32[]{:S(2)}, u32[]{:S(2)}) async-start(bf16[4,272,768]{2,1,0:T(8,128)(2,1)} %get-tuple-element.201), calls=%async_computation.4 | async-start | bytes 3342336 | tf_op jit(solution)/shard_map/all_to_all | solution.py:223
  16.9 3.9 pack_more.1
  20.8 31.1 %all-to-all-done.4 = bf16[4,272,768]{2,1,0:T(8,128)(2,1)S(1)} async-done(((bf16[4,272,768]{2,1,0:T(8,128)(2,1)}), bf16[4,272,768]{2,1,0:T(8,128)(2,1)S(1)}, u32[]{:S(2)}, u32[]{:S(2)}) %all-to-all-start.4) | async-done | bytes 1671200 | tf_op jit(solution)/shard_map/all_to_all | solution.py:223
  55.2 6.7 %conditional.2 = ((bf16[928,768]{1,0:T(8,128)(2,1)}, bf16[928,768]{1,0:T(8,128)(2,1)})) conditional(s32[]{:T(128)} %bitcast.4, (s32[8,1088]{1,0:T(8,128)S(1)}, bf16[1088,768]{1,0:T(8,128)(2,1)S(1)}) %tuple.94, (s32[906]{0:T(1024)}, (), s32[906]{0:T(1024)S(1)}, s32[906]{0:T(1024)S(1)}, bf16[906,768]{1,0:T(8,128)(2,1)}, ...), branch_computations={%region_0.0_spmd, %region_1.4_spmd} | conditional | flops 7015282 | bytes 100775368 | solution.py:905
  55.2 3.1 place.1
  61.9 3.6 all-to-all-start.5
  65.5 12.7 %qkv.1 = (bf16[928,768]{1,0:T(8,128)(2,1)}, bf16[928,2304]{1,0:T(8,128)(2,1)}) custom-call(bf16[928,768]{1,0:T(8,128)(2,1)} %get-tuple-element.207.x_ref.refs_1_, f32[1,768]{1,0:T(1,128)} %reshape.332.gain_ref, f32[1,768]{1,0:T(1,128)} %reshape.333.shift_ref, bf16[768,2304]{1,0:T(8,128)(2,1)} %w_ref.3, f32[1,768]{1,0:T(1,128)} %reshape.334.qb_ref, ...), custom_call_target="tpu_custom_call" | custom-call | flops 9852420096 | bytes 1048576 | tf_op jit(solution)/shard_map/qkv/pallas_call | solution.py:302
  78.2 10.5 %attn_fwd.1 = (bf16[928,768]{1,0:T(8,128)(2,1)}, f32[6,8,1024]{2,1,0:T(8,128)}) custom-call(bf16[928,2304]{1,0:T(8,128)(2,1)} %get-tuple-element.212.q_ref.k_ref.v_ref, bf16[928,2304]{1,0:T(8,128)(2,1)} %get-tuple-element.212.q_ref.k_ref.v_ref, bf16[928,2304]{1,0:T(8,128)(2,1)} %get-tuple-element.212.q_ref.k_ref.v_ref), custom_call_target="tpu_custom_call" | custom-call | flops 11494490112 | bytes 1048576 | tf_op jit(solution)/shard_map/attn_fwd/pallas_call | solution.py:398
  88.7 15.4 %all-to-all-done.5 = bf16[4,272,768]{2,1,0:T(8,128)(2,1)S(1)} async-done(((bf16[4,272,768]{2,1,0:T(8,128)(2,1)}), bf16[4,272,768]{2,1,0:T(8,128)(2,1)S(1)}, u32[]{:S(2)}, u32[]{:S(2)}) %all-to-all-start.5) | async-done | bytes 1671200 | tf_op jit(solution)/shard_map/all_to_all | solution.py:223
  105.3 5.5 %place_or.1.refs_2_ = bf16[928,768]{1,0:T(8,128)(2,1)} custom-call(s32[1]{0:T(128)} %bitcast.7.flag_ref, s32[8,1088]{1,0:T(8,128)S(1)} %get-tuple-element.206.pos_ref, bf16[1088,768]{1,0:T(8,128)(2,1)} %bitcast.111, bf16[928,768]{1,0:T(8,128)(2,1)} %get-tuple-element.217.other_ref), custom_call_target="tpu_custom_call" | custom-call | tf_op jit(solution)/shard_map/place_or/pallas_call | solution.py:198
  110.8 31.9 %ffn0.1 = (bf16[416,768]{1,0:T(8,128)(2,1)}, bf16[416,768]{1,0:T(8,128)(2,1)}, bf16[416,768]{1,0:T(8,128)(2,1)}, f32[16,768]{1,0:T(8,128)}, bf16[384,3072]{1,0:T...) custom-call(s32[1]{0:T(128)} %bitcast.5.own_ref, ...), custom_call_target="tpu_custom_call" | custom-call | flops 35332816896 | bytes 1048576 | tf_op jit(solution)/shard_map/ffn0/pallas_call | solution.py:646
  143.3 35.9 %ffn1.1 = (bf16[928,768]{1,0:T(8,128)(2,1)}, bf16[928,768]{1,0:T(8,128)(2,1)}, bf16[928,768]{1,0:T(8,128)(2,1)}, f32[16,768]{1,0:T(8,128)}, bf16[1088,768]{1,0:T...) custom-call(s32[1]{0:T(128)} %bitcast.5.own_ref, ...), custom_call_target="tpu_custom_call" | custom-call | flops 43486543872 | bytes 1048576 | tf_op jit(solution)/shard_map/ffn1/pallas_call | solution.py:646
  180.6 4.1 %convert_add_fusion = (f32[1,2,2,192,768]{4,3,2,1,0:T(8,128)S(1)}, bf16[1,2,2,192,768]{4,3,2,1,0:T(8,128)(2,1)}) fusion(bf16[2,2,2,192,768]{4,3,2,1,0:T(8,128)(2,1)} %bitcast.13, s32[]{:T(128)S(6)} %select_n.60, bf16[2,2,2,192,768]{4,3,2,1,0:T(8,128)(2,1)} %bitcast.119, s32[]{:T(128)S(6)} %select_n.62), kind=kLoop, calls=%fused_computation.44 | loop fusion | flops 4128768 | bytes 8257544 | tf_op jit(solution)/shard_map/add | solution.py:819
  184.7 2.6 convert_add_fusion.2
  187.8 1.5 collective-permute-start.2
  189.4 1.5 collective-permute-start.3
  190.9 4.4 %all-to-all-start.6 = ((bf16[4,272,768]{2,1,0:T(8,128)(2,1)}), bf16[4,272,768]{2,1,0:T(8,128)(2,1)}, u32[]{:S(2)}, u32[]{:S(2)}) async-start(bf16[4,272,768]{2,1,0:T(8,128)(2,1)} %bitcast.120), calls=%async_computation.6 | async-start | bytes 3342336 | tf_op jit(solution)/shard_map/all_to_all | solution.py:223
  195.2 14.3 %attn_bwd.1 = (bf16[928,768]{1,0:T(8,128)(2,1)}, bf16[928,768]{1,0:T(8,128)(2,1)}, bf16[928,768]{1,0:T(8,128)(2,1)}) custom-call(bf16[928,2304]{1,0:T(8,128)(2,1)} %get-tuple-element.212.q_ref.k_ref.v_ref, bf16[928,2304]{1,0:T(8,128)(2,1)} %get-tuple-element.212.q_ref.k_ref.v_ref, bf16[928,2304]{1,0:T(8,128)(2,1)} %get-tuple-element.212.q_ref.k_ref.v_ref, ...), custom_call_target="tpu_custom_call" | custom-call | flops 14778630144 | bytes 1048576 | tf_op jit(solution)/shard_map/attn_bwd/pallas_call | solution.py:473
  209.5 9.9 %wgrad.1 = (bf16[384,1536]{1,0:T(8,128)(2,1)}, bf16[384,1536]{1,0:T(8,128)(2,1)}, bf16[384,1536]{1,0:T(8,128)(2,1)}, bf16[384,1536]{1,0:T(8,128)(2,1)}) custom-call(s32[1]{0:T(128)} %bitcast.5.own_ref, bf16[928,768]{1,0:T(8,128)(2,1)} %get-tuple-element.258.first_ref, bf16[928,768]{1,0:T(8,128)(2,1)} %get-tuple-element.281.dq_ref, ...), custom_call_target="tpu_custom_call" | custom-call | flops 13136560128 | bytes 1048576 | tf_op jit(solution)/shard_map/wgrad/pallas_call | solution.py:746
  219.5 2.2 fusion.15
  223.8 4.1 %convert_add_fusion.1 = (f32[1,2,2,192,768]{4,3,2,1,0:T(8,128)}, bf16[1,2,2,192,768]{4,3,2,1,0:T(8,128)(2,1)}) fusion(bf16[2,2,2,192,768]{4,3,2,1,0:T(8,128)(2,1)} %bitcast.19, s32[]{:T(128)S(6)} %select_n.60, bf16[2,2,2,192,768]{4,3,2,1,0:T(8,128)(2,1)S(1)} %bitcast.116, s32[]{:T(128)S(6)} %select_n.62), kind=kLoop, calls=%fused_computation.45 | loop fusion | flops 4128768 | bytes 8257544 | tf_op jit(solution)/shard_map/add | solution.py:819
  227.9 2.7 add_convert_fusion.2
  232.1 2.2 all-to-all-done.6
  234.3 4.5 %all-to-all-start.7 = ((bf16[4,48,3072]{2,1,0:T(8,128)(2,1)}), bf16[4,48,3072]{2,1,0:T(8,128)(2,1)}, u32[]{:S(2)}, u32[]{:S(2)}) async-start(bf16[4,48,3072]{2,1,0:T(8,128)(2,1)} %bitcast.112), calls=%async_computation.7 | async-start | bytes 2359296 | tf_op jit(solution)/shard_map/all_to_all | solution.py:223
  238.8 3.4 convert_add_fusion.6
  242.2 21.6 %last.1 = (bf16[1088,768]{1,0:T(8,128)(2,1)}, bf16[928,768]{1,0:T(8,128)(2,1)}, f32[24,768]{1,0:T(8,128)}) custom-call(bf16[928,768]{1,0:T(8,128)(2,1)} %get-tuple-element.207.x_ref.refs_1_, bf16[928,768]{1,0:T(8,128)(2,1)} %get-tuple-element.281.dq_ref, bf16[928,768]{1,0:T(8,128)(2,1)} %get-tuple-element.282.dk_ref, ...), custom_call_target="tpu_custom_call" | custom-call | flops 9852420096 | bytes 1048576 | tf_op jit(solution)/shard_map/last/pallas_call | solution.py:765
  263.9 2.2 add_convert_fusion.5
  266.1 2.3 constant_dynamic-slice_fusion.6
  268.4 5.1 %all-to-all-start.8 = ((bf16[4,272,768]{2,1,0:T(8,128)(2,1)}), bf16[4,272,768]{2,1,0:T(8,128)(2,1)}, u32[]{:S(2)}, u32[]{:S(2)}) async-start(bf16[4,272,768]{2,1,0:T(8,128)(2,1)} %bitcast.121), calls=%async_computation.8 | async-start | bytes 3342336 | tf_op jit(solution)/shard_map/all_to_all | solution.py:223
  273.5 2.2 add_convert_fusion.6
  275.7 3.7 select_convert_fusion
  282.9 2.8 convert_add_fusion.12
  285.7 1.5 collective-permute-start.15
  287.2 2.3 reduce_sum.30
  291.0 1.6 dynamic-slice_bitcast_fusion
  292.6 4.7 %choose.2 = bf16[906,768]{1,0:T(8,128)(2,1)} custom-call(s32[906,1]{1,0:T(8,128)} %get-tuple-element.304.col_ref, bf16[1088,768]{1,0:T(8,128)(2,1)} %bitcast.40.value_ref), custom_call_target="tpu_custom_call" | custom-call | tf_op jit(solution)/shard_map/choose/pallas_call | solution.py:214
  297.3 13.8 %collective-permute-done.14 = f32[24,768]{1,0:T(8,128)S(1)} collective-permute-done((f32[24,768]{1,0:T(8,128)S(1)}, f32[24,768]{1,0:T(8,128)S(1)}, u32[]{:S(2)}, u32[]{:S(2)}) %collective-permute-start.14) | collective-permute-done | bytes 73760 | tf_op jit(solution)/shard_map/ppermute | solution.py:789
  311.7 4.0 %add_convert_fusion = bf16[768,768]{1,0:T(8,128)(2,1)} fusion(bf16[768,768]{1,0:T(8,128)(2,1)} %collective-permute-done.11, bf16[768,768]{1,0:T(8,128)(2,1)} %collective-permute-done.7, f32[1,2,2,192,768]{4,3,2,1,0:T(8,128)} %get-tuple-element.356, bf16[768,768]{1,0:T(8,128)(2,1)S(1)} %collective-permute-done.3, ...), kind=kLoop, calls=%fused_computation.42 | loop fusion | flops 4718592 | bytes 9437185 | tf_op jit(solution)/shard_map/convert_element_type | solution.py:940
  315.7 4.0 %collective-permute-done.15 = bf16[192,1536]{1,0:T(8,128)(2,1)} collective-permute-done((bf16[192,1536]{1,0:T(8,128)(2,1)}, bf16[192,1536]{1,0:T(8,128)(2,1)}, u32[]{:S(2)}, u32[]{:S(2)}) %collective-permute-start.15) | collective-permute-done | bytes 589856 | tf_op jit(solution)/shard_map/ppermute | solution.py:789
  327.7 4.8 %all-to-all-start.9 = ((bf16[4,192,768]{2,1,0:T(8,128)(2,1)}), bf16[4,192,768]{2,1,0:T(8,128)(2,1)S(1)}, u32[]{:S(2)}, u32[]{:S(2)}) async-start(bf16[4,192,768]{2,1,0:T(8,128)(2,1)} %bitcast.53), calls=%async_computation.9 | async-start | bytes 2359296 | tf_op jit(solution)/shard_map/all_to_all | solution.py:223
  333.5 2.1 collective-permute-start.20
  337.0 12.7 %collective-permute-done.20 = f32[24,768]{1,0:T(8,128)S(1)} collective-permute-done((f32[24,768]{1,0:T(8,128)S(1)}, f32[24,768]{1,0:T(8,128)S(1)}, u32[]{:S(2)}, u32[]{:S(2)}) %collective-permute-start.20) | collective-permute-done | bytes 73760 | tf_op jit(solution)/shard_map/ppermute | solution.py:789
  353.1 4.4 %all-to-all-done.9 = bf16[4,192,768]{2,1,0:T(8,128)(2,1)S(1)} async-done(((bf16[4,192,768]{2,1,0:T(8,128)(2,1)}), bf16[4,192,768]{2,1,0:T(8,128)(2,1)S(1)}, u32[]{:S(2)}, u32[]{:S(2)}) %all-to-all-start.9) | async-done | bytes 1179680 | tf_op jit(solution)/shard_map/all_to_all | solution.py:223
  357.5 3.8 all-to-all-start.10
  361.3 4.7 %choose.3 = bf16[906,768]{1,0:T(8,128)(2,1)} custom-call(s32[906,1]{1,0:T(8,128)} %get-tuple-element.304.col_ref, bf16[1088,768]{1,0:T(8,128)(2,1)} %bitcast.56.value_ref), custom_call_target="tpu_custom_call" | custom-call | tf_op jit(solution)/shard_map/choose/pallas_call | solution.py:214
  367.0 2.9 collective-permute-start.21
  370.9 20.8 %collective-permute-done.21 = f32[24,768]{1,0:T(8,128)S(1)} collective-permute-done((f32[24,768]{1,0:T(8,128)S(1)}, f32[24,768]{1,0:T(8,128)S(1)}, u32[]{:S(2)}, u32[]{:S(2)}) %collective-permute-start.21) | collective-permute-done | bytes 73760 | tf_op jit(solution)/shard_map/ppermute | solution.py:789
  (137 shorter events, 39.7 us)
Async XLA Ops:
  6.2 6.6 %copy-start.24 = (f32[768]{0:T(1024)S(1)}, f32[768]{0:T(1024)}, u32[]{:S(2)}) copy-start(f32[768]{0:T(1024)} %param.29) | copy-start | bytes 9220
  6.2 7.1 %copy-start.25 = (f32[768]{0:T(1024)S(1)}, f32[768]{0:T(1024)}, u32[]{:S(2)}) copy-start(f32[768]{0:T(1024)} %param.30) | copy-start | bytes 9220
  6.2 7.7 %copy-start.26 = (f32[768]{0:T(1024)S(1)}, f32[768]{0:T(1024)}, u32[]{:S(2)}) copy-start(f32[768]{0:T(1024)} %param.32) | copy-start | bytes 9220
  6.2 8.3 %copy-start.27 = (f32[768]{0:T(1024)S(1)}, f32[768]{0:T(1024)}, u32[]{:S(2)}) copy-start(f32[768]{0:T(1024)} %param.33) | copy-start | bytes 9220
  6.2 8.9 %copy-start.28 = (f32[768]{0:T(1024)S(1)}, f32[768]{0:T(1024)}, u32[]{:S(2)}) copy-start(f32[768]{0:T(1024)} %param.35) | copy-start | bytes 9220
  6.3 9.5 %copy-start.29 = (f32[768]{0:T(1024)S(1)}, f32[768]{0:T(1024)}, u32[]{:S(2)}) copy-start(f32[768]{0:T(1024)} %param.36) | copy-start | bytes 9220
  6.3 10.0 %copy-start.30 = (f32[768]{0:T(1024)S(1)}, f32[768]{0:T(1024)}, u32[]{:S(2)}) copy-start(f32[768]{0:T(1024)} %param.37) | copy-start | bytes 9220
  6.3 10.6 %copy-start.15 = (bf16[906,768]{1,0:T(8,128)(2,1)S(1)}, bf16[906,768]{1,0:T(8,128)(2,1)}, u32[]{:S(2)}) copy-start(bf16[906,768]{1,0:T(8,128)(2,1)} %value_ref.1) | copy-start | bytes 4174852
  6.3 45.6 %all-to-all-start.4 = ((bf16[4,272,768]{2,1,0:T(8,128)(2,1)}), bf16[4,272,768]{2,1,0:T(8,128)(2,1)S(1)}, u32[]{:S(2)}, u32[]{:S(2)}) async-start(bf16[4,272,768]{2,1,0:T(8,128)(2,1)} %get-tuple-element.201), calls=%async_computation.4 | async-start | bytes 3342336 | tf_op jit(solution)/shard_map/all_to_all | solution.py:223
  20.8 34.4 %copy-start.20 = (s32[906]{0:T(1024)S(1)}, s32[906]{0:T(1024)}, u32[]{:S(2)}) copy-start(s32[906]{0:T(1024)} %param.27) | copy-start | bytes 10876
  20.8 34.4 %copy-start.22 = (s32[906]{0:T(1024)S(1)}, s32[906]{0:T(1024)}, u32[]{:S(2)}) copy-start(s32[906]{0:T(1024)} %param.28) | copy-start | bytes 10876
  61.9 42.2 %all-to-all-start.5 = ((bf16[4,272,768]{2,1,0:T(8,128)(2,1)}), bf16[4,272,768]{2,1,0:T(8,128)(2,1)S(1)}, u32[]{:S(2)}, u32[]{:S(2)}) async-start(bf16[4,272,768]{2,1,0:T(8,128)(2,1)} %pack_more.1), calls=%async_computation.5 | async-start | bytes 3342336 | tf_op jit(solution)/shard_map/all_to_all | solution.py:223
  110.8 32.5 %copy-start.31 = (bf16[928,768]{1,0:T(8,128)(2,1)S(1)}, bf16[928,768]{1,0:T(8,128)(2,1)}, u32[]{:S(2)}) copy-start(bf16[928,768]{1,0:T(8,128)(2,1)} %get-tuple-element.207.x_ref.refs_1_) | copy-start | bytes 4276228
  142.7 36.5 %collective-permute-start = (bf16[384,3072]{1,0:T(8,128)(2,1)}, bf16[384,3072]{1,0:T(8,128)(2,1)S(1)}, u32[]{:S(2)}, u32[]{:S(2)}) collective-permute-start(bf16[384,3072]{1,0:T(8,128)(2,1)} %get-tuple-element.227), channel_id=1, source_target_pairs={{0,4},{4,0},{8,12},{12,8},{16,20},{20,16},{24,28},{28,24},{1,5},{5... | collective-permute-start | bytes 7077896 | tf_op jit(solution)/shard_map/ppermute | solution.py:789
  142.8 36.4 %collective-permute-start.1 = (bf16[1536,768]{1,0:T(8,128)(2,1)}, bf16[1536,768]{1,0:T(8,128)(2,1)}, u32[]{:S(2)}, u32[]{:S(2)}) collective-permute-start(bf16[1536,768]{1,0:T(8,128)(2,1)} %get-tuple-element.228), channel_id=1, source_target_pairs={{0,4},{4,0},{8,12},{12,8},{16,20},{20,16},{24,28},{28,24},{1,5},{5... | collective-permute-start | bytes 7077896 | tf_op jit(solution)/shard_map/ppermute | solution.py:789
  180.6 4.1 %copy-start.8 = (bf16[384,3072]{1,0:T(8,128)(2,1)S(1)}, bf16[384,3072]{1,0:T(8,128)(2,1)}, u32[]{:S(2)}) copy-start(bf16[384,3072]{1,0:T(8,128)(2,1)} %get-tuple-element.241) | copy-start | bytes 7077892
  180.6 4.1 %copy-start.10 = (bf16[384,3072]{1,0:T(8,128)(2,1)S(1)}, bf16[384,3072]{1,0:T(8,128)(2,1)}, u32[]{:S(2)}) copy-start(bf16[384,3072]{1,0:T(8,128)(2,1)} %copy-done.9) | copy-start | bytes 7077892
  187.3 32.1 %collective-permute-start.4 = (bf16[384,3072]{1,0:T(8,128)(2,1)}, bf16[384,3072]{1,0:T(8,128)(2,1)}, u32[]{:S(2)}, u32[]{:S(2)}) collective-permute-start(bf16[384,3072]{1,0:T(8,128)(2,1)} %get-tuple-element.251), channel_id=1, source_target_pairs={{0,4},{4,0},{8,12},{12,8},{16,20},{20,16},{24,28},{28,24},{1,5},{5... | collective-permute-start | bytes 7077896 | tf_op jit(solution)/shard_map/ppermute | solution.py:789
  187.4 32.1 %collective-permute-start.5 = (bf16[1536,768]{1,0:T(8,128)(2,1)}, bf16[1536,768]{1,0:T(8,128)(2,1)}, u32[]{:S(2)}, u32[]{:S(2)}) collective-permute-start(bf16[1536,768]{1,0:T(8,128)(2,1)} %get-tuple-element.252), channel_id=1, source_target_pairs={{0,4},{4,0},{8,12},{12,8},{16,20},{20,16},{24,28},{28,24},{1,5},{5... | collective-permute-start | bytes 7077896 | tf_op jit(solution)/shard_map/ppermute | solution.py:789
  187.8 31.6 %collective-permute-start.2 = (bf16[192,3072]{1,0:T(8,128)(2,1)}, bf16[192,3072]{1,0:T(8,128)(2,1)}, u32[]{:S(2)}, u32[]{:S(2)}) collective-permute-start(bf16[192,3072]{1,0:T(8,128)(2,1)} %bitcast.11), channel_id=1, source_target_pairs={{0,16},{4,20},{8,24},{12,28},{16,0},{20,4},{24,8},{28,12},{1,17},{... | collective-permute-start | bytes 3538952 | tf_op jit(solution)/shard_map/ppermute | solution.py:789
  189.4 30.1 %collective-permute-start.3 = (bf16[768,768]{1,0:T(8,128)(2,1)}, bf16[768,768]{1,0:T(8,128)(2,1)S(1)}, u32[]{:S(2)}, u32[]{:S(2)}) collective-permute-start(bf16[768,768]{1,0:T(8,128)(2,1)} %bitcast.14), channel_id=1, source_target_pairs={{0,8},{4,12},{8,0},{12,4},{16,24},{20,28},{24,16},{28,20},{1,9},{5... | collective-permute-start | bytes 3538952 | tf_op jit(solution)/shard_map/ppermute | solution.py:789
  190.9 43.5 %all-to-all-start.6 = ((bf16[4,272,768]{2,1,0:T(8,128)(2,1)}), bf16[4,272,768]{2,1,0:T(8,128)(2,1)}, u32[]{:S(2)}, u32[]{:S(2)}) async-start(bf16[4,272,768]{2,1,0:T(8,128)(2,1)} %bitcast.120), calls=%async_computation.6 | async-start | bytes 3342336 | tf_op jit(solution)/shard_map/all_to_all | solution.py:223
  230.6 33.3 %collective-permute-start.6 = (bf16[192,3072]{1,0:T(8,128)(2,1)}, bf16[192,3072]{1,0:T(8,128)(2,1)}, u32[]{:S(2)}, u32[]{:S(2)}) collective-permute-start(bf16[192,3072]{1,0:T(8,128)(2,1)} %bitcast.17), channel_id=1, source_target_pairs={{0,16},{4,20},{8,24},{12,28},{16,0},{20,4},{24,8},{28,12},{1,17},{... | collective-permute-start | bytes 3538952 | tf_op jit(solution)/shard_map/ppermute | solution.py:789
  231.1 32.8 %collective-permute-start.7 = (bf16[768,768]{1,0:T(8,128)(2,1)}, bf16[768,768]{1,0:T(8,128)(2,1)}, u32[]{:S(2)}, u32[]{:S(2)}) collective-permute-start(bf16[768,768]{1,0:T(8,128)(2,1)} %bitcast.20), channel_id=1, source_target_pairs={{0,8},{4,12},{8,0},{12,4},{16,24},{20,28},{24,16},{28,20},{1,9},{5... | collective-permute-start | bytes 3538952 | tf_op jit(solution)/shard_map/ppermute | solution.py:789
  231.6 32.3 %collective-permute-start.8 = (bf16[384,1536]{1,0:T(8,128)(2,1)}, bf16[384,1536]{1,0:T(8,128)(2,1)}, u32[]{:S(2)}, u32[]{:S(2)}) collective-permute-start(bf16[384,1536]{1,0:T(8,128)(2,1)} %get-tuple-element.274), channel_id=1, source_target_pairs={{0,4},{4,0},{8,12},{12,8},{16,20},{20,16},{24,28},{28,24},{1,5},{5... | collective-permute-start | bytes 3538952 | tf_op jit(solution)/shard_map/ppermute | solution.py:789
  231.6 32.3 %collective-permute-start.9 = (bf16[384,1536]{1,0:T(8,128)(2,1)}, bf16[384,1536]{1,0:T(8,128)(2,1)}, u32[]{:S(2)}, u32[]{:S(2)}) collective-permute-start(bf16[384,1536]{1,0:T(8,128)(2,1)} %get-tuple-element.275), channel_id=1, source_target_pairs={{0,4},{4,0},{8,12},{12,8},{16,20},{20,16},{24,28},{28,24},{1,5},{5... | collective-permute-start | bytes 3538952 | tf_op jit(solution)/shard_map/ppermute | solution.py:789
  234.3 34.1 %all-to-all-start.7 = ((bf16[4,48,3072]{2,1,0:T(8,128)(2,1)}), bf16[4,48,3072]{2,1,0:T(8,128)(2,1)}, u32[]{:S(2)}, u32[]{:S(2)}) async-start(bf16[4,48,3072]{2,1,0:T(8,128)(2,1)} %bitcast.112), calls=%async_computation.7 | async-start | bytes 2359296 | tf_op jit(solution)/shard_map/all_to_all | solution.py:223
  268.4 43.3 %all-to-all-start.8 = ((bf16[4,272,768]{2,1,0:T(8,128)(2,1)}), bf16[4,272,768]{2,1,0:T(8,128)(2,1)}, u32[]{:S(2)}, u32[]{:S(2)}) async-start(bf16[4,272,768]{2,1,0:T(8,128)(2,1)} %bitcast.121), calls=%async_computation.8 | async-start | bytes 3342336 | tf_op jit(solution)/shard_map/all_to_all | solution.py:223
  280.4 31.3 %collective-permute-start.11 = (bf16[768,768]{1,0:T(8,128)(2,1)}, bf16[768,768]{1,0:T(8,128)(2,1)}, u32[]{:S(2)}, u32[]{:S(2)}) collective-permute-start(bf16[768,768]{1,0:T(8,128)(2,1)} %select_convert_fusion), channel_id=1, source_target_pairs={{0,16},{4,20},{8,24},{12,28},{16,0},{20,4},{24,8},{28,12},{1,17},{... | collective-permute-start | bytes 3538952 | tf_op jit(solution)/shard_map/ppermute | solution.py:789
  280.9 8.6 %collective-permute-start.13 = (f32[24,768]{1,0:T(8,128)}, f32[24,768]{1,0:T(8,128)}, u32[]{:S(2)}, u32[]{:S(2)}) collective-permute-start(f32[24,768]{1,0:T(8,128)} %get-tuple-element.302), channel_id=1, source_target_pairs={{0,4},{4,0},{8,12},{12,8},{16,20},{20,16},{24,28},{28,24},{1,5},{5... | collective-permute-start | bytes 221192 | tf_op jit(solution)/shard_map/ppermute | solution.py:789
  280.9 30.8 %collective-permute-start.10 = (bf16[96,3072]{1,0:T(8,128)(2,1)}, bf16[96,3072]{1,0:T(8,128)(2,1)}, u32[]{:S(2)}, u32[]{:S(2)}) collective-permute-start(bf16[96,3072]{1,0:T(8,128)(2,1)} %fusion.16), channel_id=1, source_target_pairs={{0,8},{4,12},{8,0},{12,4},{16,24},{20,28},{24,16},{28,20},{1,9},{5... | collective-permute-start | bytes 1769480 | tf_op jit(solution)/shard_map/ppermute | solution.py:789
  282.0 29.8 %collective-permute-start.12 = (bf16[192,1536]{1,0:T(8,128)(2,1)}, bf16[192,1536]{1,0:T(8,128)(2,1)}, u32[]{:S(2)}, u32[]{:S(2)}) collective-permute-start(bf16[192,1536]{1,0:T(8,128)(2,1)} %bitcast.34), channel_id=1, source_target_pairs={{0,8},{4,12},{8,0},{12,4},{16,24},{20,28},{24,16},{28,20},{1,9},{5... | collective-permute-start | bytes 1769480 | tf_op jit(solution)/shard_map/ppermute | solution.py:789
  285.7 34.1 %collective-permute-start.15 = (bf16[192,1536]{1,0:T(8,128)(2,1)}, bf16[192,1536]{1,0:T(8,128)(2,1)}, u32[]{:S(2)}, u32[]{:S(2)}) collective-permute-start(bf16[192,1536]{1,0:T(8,128)(2,1)} %bitcast.37), channel_id=1, source_target_pairs={{0,16},{4,20},{8,24},{12,28},{16,0},{20,4},{24,8},{28,12},{1,17},{... | collective-permute-start | bytes 1769480 | tf_op jit(solution)/shard_map/ppermute | solution.py:789
  290.4 20.7 %collective-permute-start.14 = (f32[24,768]{1,0:T(8,128)S(1)}, f32[24,768]{1,0:T(8,128)S(1)}, u32[]{:S(2)}, u32[]{:S(2)}) collective-permute-start(f32[24,768]{1,0:T(8,128)S(1)} %add.278), channel_id=1, source_target_pairs={{0,8},{4,12},{8,0},{12,4},{16,24},{20,28},{24,16},{28,20},{1,9},{5... | collective-permute-start | bytes 221192 | tf_op jit(solution)/shard_map/ppermute | solution.py:789
  315.7 6.3 %copy-start.5 = (f32[1,1,2,2,24,1536]{5,4,3,2,1,0:T(8,128)S(1)}, f32[1,1,2,2,24,1536]{5,4,3,2,1,0:T(8,128)}, u32[]{:S(2)}) copy-start(f32[1,1,2,2,24,1536]{5,4,3,2,1,0:T(8,128)} %get-tuple-element.362) | copy-start | bytes 1769476
  322.9 12.8 %copy-start.3 = (f32[1,1,2,2,24,3072]{5,4,3,2,1,0:T(8,128)S(1)}, f32[1,1,2,2,24,3072]{5,4,3,2,1,0:T(8,128)}, u32[]{:S(2)}) copy-start(f32[1,1,2,2,24,3072]{5,4,3,2,1,0:T(8,128)} %get-tuple-element.352) | copy-start | bytes 3538948
  322.9 12.8 %copy-start.11 = (bf16[1,2,2,24,3072]{4,3,2,1,0:T(8,128)(2,1)S(1)}, bf16[1,2,2,24,3072]{4,3,2,1,0:T(8,128)(2,1)}, u32[]{:S(2)}) copy-start(bf16[1,2,2,24,3072]{4,3,2,1,0:T(8,128)(2,1)} %get-tuple-element.364) | copy-start | bytes 1769476
  323.7 8.9 %collective-permute-start.19 = (f32[24,768]{1,0:T(8,128)}, f32[24,768]{1,0:T(8,128)}, u32[]{:S(2)}, u32[]{:S(2)}) collective-permute-start(f32[24,768]{1,0:T(8,128)} %add.279), channel_id=1, source_target_pairs={{0,16},{4,20},{8,24},{12,28},{16,0},{20,4},{24,8},{28,12},{1,17},{... | collective-permute-start | bytes 221192 | tf_op jit(solution)/shard_map/ppermute | solution.py:789
  324.3 25.4 %collective-permute-start.16 = (bf16[96,1536]{1,0:T(8,128)(2,1)}, bf16[96,1536]{1,0:T(8,128)(2,1)}, u32[]{:S(2)}, u32[]{:S(2)}) collective-permute-start(bf16[96,1536]{1,0:T(8,128)(2,1)} %fusion.22), channel_id=1, source_target_pairs={{0,16},{4,20},{8,24},{12,28},{16,0},{20,4},{24,8},{28,12},{1,17},{... | collective-permute-start | bytes 884744 | tf_op jit(solution)/shard_map/ppermute | solution.py:789
  325.7 24.1 %collective-permute-start.17 = (bf16[96,1536]{1,0:T(8,128)(2,1)}, bf16[96,1536]{1,0:T(8,128)(2,1)}, u32[]{:S(2)}, u32[]{:S(2)}) collective-permute-start(bf16[96,1536]{1,0:T(8,128)(2,1)} %fusion.21), channel_id=1, source_target_pairs={{0,8},{4,12},{8,0},{12,4},{16,24},{20,28},{24,16},{28,20},{1,9},{5... | collective-permute-start | bytes 884744 | tf_op jit(solution)/shard_map/ppermute | solution.py:789
  326.3 23.4 %collective-permute-start.18 = (bf16[24,3072]{1,0:T(8,128)(2,1)}, bf16[24,3072]{1,0:T(8,128)(2,1)}, u32[]{:S(2)}, u32[]{:S(2)}) collective-permute-start(bf16[24,3072]{1,0:T(8,128)(2,1)} %dynamic-slice_bitcast_fusion), channel_id=1, source_target_pairs={{0,8},{4,12},{8,0},{12,4},{16,24},{20,28},{24,16},{28,20},{1,9},{5... | collective-permute-start | bytes 442376 | tf_op jit(solution)/shard_map/ppermute | solution.py:789
  327.7 29.8 %all-to-all-start.9 = ((bf16[4,192,768]{2,1,0:T(8,128)(2,1)}), bf16[4,192,768]{2,1,0:T(8,128)(2,1)S(1)}, u32[]{:S(2)}, u32[]{:S(2)}) async-start(bf16[4,192,768]{2,1,0:T(8,128)(2,1)} %bitcast.53), calls=%async_computation.9 | async-start | bytes 2359296 | tf_op jit(solution)/shard_map/all_to_all | solution.py:223
  332.5 17.2 %copy-start.13 = (f32[1,1,2,2,24,1536]{5,4,3,2,1,0:T(8,128)S(1)}, f32[1,1,2,2,24,1536]{5,4,3,2,1,0:T(8,128)}, u32[]{:S(2)}) copy-start(f32[1,1,2,2,24,1536]{5,4,3,2,1,0:T(8,128)} %get-tuple-element.378) | copy-start | bytes 1769476
  333.5 16.2 %collective-permute-start.20 = (f32[24,768]{1,0:T(8,128)S(1)}, f32[24,768]{1,0:T(8,128)S(1)}, u32[]{:S(2)}, u32[]{:S(2)}) collective-permute-start(f32[24,768]{1,0:T(8,128)S(1)} %add.291), channel_id=1, source_target_pairs={{0,1},{1,0},{2,3},{3,2},{4,5},{5,4},{6,7},{7,6},{8,9},{9,8},{10,11... | collective-permute-start | bytes 221192 | tf_op jit(solution)/shard_map/ppermute | solution.py:789
  335.6 15.3 %copy-start.12 = (f32[1,1,2,2,24,1536]{5,4,3,2,1,0:T(8,128)S(1)}, f32[1,1,2,2,24,1536]{5,4,3,2,1,0:T(8,128)}, u32[]{:S(2)}) copy-start(f32[1,1,2,2,24,1536]{5,4,3,2,1,0:T(8,128)} %get-tuple-element.363) | copy-start | bytes 1769476
  357.5 34.2 %all-to-all-start.10 = ((bf16[4,24,6144]{2,1,0:T(8,128)(2,1)}), bf16[4,24,6144]{2,1,0:T(8,128)(2,1)S(1)}, u32[]{:S(2)}, u32[]{:S(2)}) async-start(bf16[4,24,6144]{2,1,0:T(8,128)(2,1)} %bitcast.55), calls=%async_computation.10 | async-start | bytes 2359296 | tf_op jit(solution)/shard_map/all_to_all | solution.py:223
  361.3 4.8 %copy-start.17 = (bf16[48,3072]{1,0:T(8,128)(2,1)S(1)}, bf16[48,3072]{1,0:T(8,128)(2,1)}, u32[]{:S(2)}) copy-start(bf16[48,3072]{1,0:T(8,128)(2,1)} %reduce_sum.30) | copy-start | bytes 884740
  367.0 24.7 %collective-permute-start.21 = (f32[24,768]{1,0:T(8,128)S(1)}, f32[24,768]{1,0:T(8,128)S(1)}, u32[]{:S(2)}, u32[]{:S(2)}) collective-permute-start(f32[24,768]{1,0:T(8,128)S(1)} %add.292), channel_id=1, source_target_pairs={{0,2},{1,3},{2,0},{3,1},{4,6},{5,7},{6,4},{7,5},{8,10},{9,11},{10,... | collective-permute-start | bytes 221192 | tf_op jit(solution)/shard_map/ppermute | solution.py:789
  (12 other events, 33.2 us)

commit v7 on v6

--- a/solution.py
+++ b/solution.py
@@ -516,7 +516,7 @@
     mid_ref, second_ref, mix_ref, ds_ref, pre_ref, dh_ref, hid_ref, dpre_ref = refs
     width = x_ref.shape[1]
     span = hi - lo
-    size = 64 if span % 64 == 0 else STRIP
+    size = 64 if span % 64 == 0 else span // 2
     steps = span // size
     part = slice(lo, hi)
     here = lambda i: strip(i, size)

time: 404 us -> 402 us (level)
  Pallas kernels: 166 us -> 161 us
    pallas_call x2, Pallas kernels: 67.8 us -> 63.1 us  [ffn(): pl.pallas_call(functools.partial(ffn_kernel, expert, lo, hi, run), grid=(...]
where the time goes in v7:
time: 402 us; the launch traced here: 395 us
  Pallas kernels  161 us (40%)
  waiting for transfers between devices  105 us (26%)
  starting transfers between devices  52.1 us (13%)
  other arithmetic  49 us (12%)
  local copies, waits for them, and re-layouts  19.6 us (5%)
  loops' own time  7.13 us (2%)
    pallas_call x2, Pallas kernels, ffn(): pl.pallas_call(functools.partial(ffn_kernel, expert, lo, hi, run), grid=(...  63.1 us
    all_to_all x7, waiting for transfers between devices, swap(): lax.all_to_all(blocks, 'seq', split_axis=0, concat_axis=0, tiled=True)  53.1 us
    ppermute x22, waiting for transfers between devices, pass_on(): return lax.ppermute(value, axis, [(i, i ^ 1 << bit) for i in range(n)])  51.4 us
    all_to_all x7, starting transfers between devices, swap(): lax.all_to_all(blocks, 'seq', split_axis=0, concat_axis=0, tiled=True)  32.8 us
    pallas_call x1, Pallas kernels, last(): pl.pallas_call(last_kernel, out_shape=(jax.ShapeDtypeStruct((col.shape[0]...  21.6 us
    ppermute x22, starting transfers between devices, pass_on(): return lax.ppermute(value, axis, [(i, i ^ 1 << bit) for i in range(n)])  19.4 us
    add x6, other arithmetic, total(): sum((t.rows({**self.fixed, **extra.get('more', {})}) for t in self.terms))  17.8 us
    pallas_call x1, Pallas kernels, attn_bwd(): pl.pallas_call(functools.partial(attn_bwd_kernel, per), grid=(steps,), in...  14.3 us
  transfers between devices with their start and end apart: 29, of which 8 were waited for; matrix products, arithmetic and copies ran while one was open for 12% of the time, Pallas kernels for 30%

profile of v7, /device:TPU:0, one launch (start us, length us, event | category | flops | bytes accessed | tf_op | source)
XLA Modules:
  0.0 395.2 jit_solution(17155280861108598474)
XLA Ops:
  0.6 5.6 %pack.1 = (bf16[4,272,768]{2,1,0:T(8,128)(2,1)}, s32[8,906]{1,0:T(8,128)}, s32[906,1]{1,0:T(8,128)}) custom-call(s32[1,906]{1,0:T(1,128)} %bitcast.129, s32[1,906]{1,0:T(1,128)} %bitcast.130, bf16[906,768]{1,0:T(8,128)(2,1)} %tok_ref.1), custom_call_target="tpu_custom_call" | custom-call | tf_op jit(solution)/shard_map/pack/pallas_call | solution.py:88
  6.3 6.5 %all-to-all-start.4 = ((bf16[4,272,768]{2,1,0:T(8,128)(2,1)}), bf16[4,272,768]{2,1,0:T(8,128)(2,1)S(1)}, u32[]{:S(2)}, u32[]{:S(2)}) async-start(bf16[4,272,768]{2,1,0:T(8,128)(2,1)} %get-tuple-element.201), calls=%async_computation.4 | async-start | bytes 3342336 | tf_op jit(solution)/shard_map/all_to_all | solution.py:223
  16.9 3.9 pack_more.1
  20.8 31.1 %all-to-all-done.4 = bf16[4,272,768]{2,1,0:T(8,128)(2,1)S(1)} async-done(((bf16[4,272,768]{2,1,0:T(8,128)(2,1)}), bf16[4,272,768]{2,1,0:T(8,128)(2,1)S(1)}, u32[]{:S(2)}, u32[]{:S(2)}) %all-to-all-start.4) | async-done | bytes 1671200 | tf_op jit(solution)/shard_map/all_to_all | solution.py:223
  55.2 10.3 %conditional.2 = ((bf16[928,768]{1,0:T(8,128)(2,1)}, bf16[928,768]{1,0:T(8,128)(2,1)})) conditional(s32[]{:T(128)} %bitcast.4, (s32[8,1088]{1,0:T(8,128)S(1)}, bf16[1088,768]{1,0:T(8,128)(2,1)S(1)}) %tuple.94, (s32[906]{0:T(1024)}, (), s32[906]{0:T(1024)S(1)}, s32[906]{0:T(1024)S(1)}, bf16[906,768]{1,0:T(8,128)(2,1)}, ...), branch_computations={%region_0.0_spmd, %region_1.4_spmd} | conditional | flops 7015282 | bytes 100775368 | solution.py:905
  55.2 3.1 place.1
  65.4 3.6 all-to-all-start.5
  69.0 12.7 %qkv.1 = (bf16[928,768]{1,0:T(8,128)(2,1)}, bf16[928,2304]{1,0:T(8,128)(2,1)}) custom-call(bf16[928,768]{1,0:T(8,128)(2,1)} %get-tuple-element.207.x_ref.refs_1_, f32[1,768]{1,0:T(1,128)} %reshape.332.gain_ref, f32[1,768]{1,0:T(1,128)} %reshape.333.shift_ref, bf16[768,2304]{1,0:T(8,128)(2,1)} %w_ref.3, f32[1,768]{1,0:T(1,128)} %reshape.334.qb_ref, ...), custom_call_target="tpu_custom_call" | custom-call | flops 9852420096 | bytes 1048576 | tf_op jit(solution)/shard_map/qkv/pallas_call | solution.py:302
  81.8 10.5 %attn_fwd.1 = (bf16[928,768]{1,0:T(8,128)(2,1)}, f32[6,8,1024]{2,1,0:T(8,128)}) custom-call(bf16[928,2304]{1,0:T(8,128)(2,1)} %get-tuple-element.212.q_ref.k_ref.v_ref, bf16[928,2304]{1,0:T(8,128)(2,1)} %get-tuple-element.212.q_ref.k_ref.v_ref, bf16[928,2304]{1,0:T(8,128)(2,1)} %get-tuple-element.212.q_ref.k_ref.v_ref), custom_call_target="tpu_custom_call" | custom-call | flops 11494490112 | bytes 1048576 | tf_op jit(solution)/shard_map/attn_fwd/pallas_call | solution.py:398
  92.2 15.4 %all-to-all-done.5 = bf16[4,272,768]{2,1,0:T(8,128)(2,1)S(1)} async-done(((bf16[4,272,768]{2,1,0:T(8,128)(2,1)}), bf16[4,272,768]{2,1,0:T(8,128)(2,1)S(1)}, u32[]{:S(2)}, u32[]{:S(2)}) %all-to-all-start.5) | async-done | bytes 1671200 | tf_op jit(solution)/shard_map/all_to_all | solution.py:223
  108.9 5.0 %place_or.1.refs_2_ = bf16[928,768]{1,0:T(8,128)(2,1)} custom-call(s32[1]{0:T(128)} %bitcast.7.flag_ref, s32[8,1088]{1,0:T(8,128)S(1)} %get-tuple-element.206.pos_ref, bf16[1088,768]{1,0:T(8,128)(2,1)} %bitcast.111, bf16[928,768]{1,0:T(8,128)(2,1)} %get-tuple-element.217.other_ref), custom_call_target="tpu_custom_call" | custom-call | tf_op jit(solution)/shard_map/place_or/pallas_call | solution.py:198
  113.9 26.9 %ffn0.1 = (bf16[416,768]{1,0:T(8,128)(2,1)}, bf16[416,768]{1,0:T(8,128)(2,1)}, bf16[416,768]{1,0:T(8,128)(2,1)}, f32[16,768]{1,0:T(8,128)}, bf16[384,3072]{1,0:T...) custom-call(s32[1]{0:T(128)} %bitcast.5.own_ref, ...), custom_call_target="tpu_custom_call" | custom-call | flops 35332816896 | bytes 1048576 | tf_op jit(solution)/shard_map/ffn0/pallas_call | solution.py:646
  141.4 36.2 %ffn1.1 = (bf16[928,768]{1,0:T(8,128)(2,1)}, bf16[928,768]{1,0:T(8,128)(2,1)}, bf16[928,768]{1,0:T(8,128)(2,1)}, f32[16,768]{1,0:T(8,128)}, bf16[1088,768]{1,0:T...) custom-call(s32[1]{0:T(128)} %bitcast.5.own_ref, ...), custom_call_target="tpu_custom_call" | custom-call | flops 43486543872 | bytes 1048576 | tf_op jit(solution)/shard_map/ffn1/pallas_call | solution.py:646
  179.0 4.1 %convert_add_fusion = (f32[1,2,2,192,768]{4,3,2,1,0:T(8,128)S(1)}, bf16[1,2,2,192,768]{4,3,2,1,0:T(8,128)(2,1)}) fusion(bf16[2,2,2,192,768]{4,3,2,1,0:T(8,128)(2,1)} %bitcast.13, s32[]{:T(128)S(6)} %select_n.60, bf16[2,2,2,192,768]{4,3,2,1,0:T(8,128)(2,1)} %bitcast.119, s32[]{:T(128)S(6)} %select_n.62), kind=kLoop, calls=%fused_computation.44 | loop fusion | flops 4128768 | bytes 8257544 | tf_op jit(solution)/shard_map/add | solution.py:819
  183.1 2.6 convert_add_fusion.2
  186.2 1.5 collective-permute-start.2
  187.7 1.5 collective-permute-start.3
  189.2 4.5 %all-to-all-start.6 = ((bf16[4,272,768]{2,1,0:T(8,128)(2,1)}), bf16[4,272,768]{2,1,0:T(8,128)(2,1)}, u32[]{:S(2)}, u32[]{:S(2)}) async-start(bf16[4,272,768]{2,1,0:T(8,128)(2,1)} %bitcast.120), calls=%async_computation.6 | async-start | bytes 3342336 | tf_op jit(solution)/shard_map/all_to_all | solution.py:223
  193.8 14.3 %attn_bwd.1 = (bf16[928,768]{1,0:T(8,128)(2,1)}, bf16[928,768]{1,0:T(8,128)(2,1)}, bf16[928,768]{1,0:T(8,128)(2,1)}) custom-call(bf16[928,2304]{1,0:T(8,128)(2,1)} %get-tuple-element.212.q_ref.k_ref.v_ref, bf16[928,2304]{1,0:T(8,128)(2,1)} %get-tuple-element.212.q_ref.k_ref.v_ref, bf16[928,2304]{1,0:T(8,128)(2,1)} %get-tuple-element.212.q_ref.k_ref.v_ref, ...), custom_call_target="tpu_custom_call" | custom-call | flops 14778630144 | bytes 1048576 | tf_op jit(solution)/shard_map/attn_bwd/pallas_call | solution.py:473
  208.1 9.9 %wgrad.1 = (bf16[384,1536]{1,0:T(8,128)(2,1)}, bf16[384,1536]{1,0:T(8,128)(2,1)}, bf16[384,1536]{1,0:T(8,128)(2,1)}, bf16[384,1536]{1,0:T(8,128)(2,1)}) custom-call(s32[1]{0:T(128)} %bitcast.5.own_ref, bf16[928,768]{1,0:T(8,128)(2,1)} %get-tuple-element.258.first_ref, bf16[928,768]{1,0:T(8,128)(2,1)} %get-tuple-element.281.dq_ref, ...), custom_call_target="tpu_custom_call" | custom-call | flops 13136560128 | bytes 1048576 | tf_op jit(solution)/shard_map/wgrad/pallas_call | solution.py:746
  218.0 2.2 fusion.15
  222.4 4.1 %convert_add_fusion.1 = (f32[1,2,2,192,768]{4,3,2,1,0:T(8,128)}, bf16[1,2,2,192,768]{4,3,2,1,0:T(8,128)(2,1)}) fusion(bf16[2,2,2,192,768]{4,3,2,1,0:T(8,128)(2,1)} %bitcast.19, s32[]{:T(128)S(6)} %select_n.60, bf16[2,2,2,192,768]{4,3,2,1,0:T(8,128)(2,1)S(1)} %bitcast.116, s32[]{:T(128)S(6)} %select_n.62), kind=kLoop, calls=%fused_computation.45 | loop fusion | flops 4128768 | bytes 8257544 | tf_op jit(solution)/shard_map/add | solution.py:819
  226.4 2.7 add_convert_fusion.2
  230.7 2.2 all-to-all-done.6
  232.9 4.5 %all-to-all-start.7 = ((bf16[4,48,3072]{2,1,0:T(8,128)(2,1)}), bf16[4,48,3072]{2,1,0:T(8,128)(2,1)}, u32[]{:S(2)}, u32[]{:S(2)}) async-start(bf16[4,48,3072]{2,1,0:T(8,128)(2,1)} %bitcast.112), calls=%async_computation.7 | async-start | bytes 2359296 | tf_op jit(solution)/shard_map/all_to_all | solution.py:223
  237.4 3.4 convert_add_fusion.6
  240.8 21.6 %last.1 = (bf16[1088,768]{1,0:T(8,128)(2,1)}, bf16[928,768]{1,0:T(8,128)(2,1)}, f32[24,768]{1,0:T(8,128)}) custom-call(bf16[928,768]{1,0:T(8,128)(2,1)} %get-tuple-element.207.x_ref.refs_1_, bf16[928,768]{1,0:T(8,128)(2,1)} %get-tuple-element.281.dq_ref, bf16[928,768]{1,0:T(8,128)(2,1)} %get-tuple-element.282.dk_ref, ...), custom_call_target="tpu_custom_call" | custom-call | flops 9852420096 | bytes 1048576 | tf_op jit(solution)/shard_map/last/pallas_call | solution.py:765
  262.4 2.2 add_convert_fusion.5
  264.7 2.3 constant_dynamic-slice_fusion.6
  267.0 5.1 %all-to-all-start.8 = ((bf16[4,272,768]{2,1,0:T(8,128)(2,1)}), bf16[4,272,768]{2,1,0:T(8,128)(2,1)}, u32[]{:S(2)}, u32[]{:S(2)}) async-start(bf16[4,272,768]{2,1,0:T(8,128)(2,1)} %bitcast.121), calls=%async_computation.8 | async-start | bytes 3342336 | tf_op jit(solution)/shard_map/all_to_all | solution.py:223
  272.0 2.2 add_convert_fusion.6
  274.3 3.7 select_convert_fusion
  281.5 2.8 convert_add_fusion.12
  284.3 1.5 collective-permute-start.15
  285.8 2.3 reduce_sum.30
  289.6 1.6 dynamic-slice_bitcast_fusion
  291.1 4.7 %choose.2 = bf16[906,768]{1,0:T(8,128)(2,1)} custom-call(s32[906,1]{1,0:T(8,128)} %get-tuple-element.304.col_ref, bf16[1088,768]{1,0:T(8,128)(2,1)} %bitcast.40.value_ref), custom_call_target="tpu_custom_call" | custom-call | tf_op jit(solution)/shard_map/choose/pallas_call | solution.py:214
  295.9 13.8 %collective-permute-done.14 = f32[24,768]{1,0:T(8,128)S(1)} collective-permute-done((f32[24,768]{1,0:T(8,128)S(1)}, f32[24,768]{1,0:T(8,128)S(1)}, u32[]{:S(2)}, u32[]{:S(2)}) %collective-permute-start.14) | collective-permute-done | bytes 73760 | tf_op jit(solution)/shard_map/ppermute | solution.py:789
  310.3 4.0 %add_convert_fusion = bf16[768,768]{1,0:T(8,128)(2,1)} fusion(bf16[768,768]{1,0:T(8,128)(2,1)} %collective-permute-done.11, bf16[768,768]{1,0:T(8,128)(2,1)} %collective-permute-done.7, f32[1,2,2,192,768]{4,3,2,1,0:T(8,128)} %get-tuple-element.356, bf16[768,768]{1,0:T(8,128)(2,1)S(1)} %collective-permute-done.3, ...), kind=kLoop, calls=%fused_computation.42 | loop fusion | flops 4718592 | bytes 9437185 | tf_op jit(solution)/shard_map/convert_element_type | solution.py:940
  314.3 4.0 %collective-permute-done.15 = bf16[192,1536]{1,0:T(8,128)(2,1)} collective-permute-done((bf16[192,1536]{1,0:T(8,128)(2,1)}, bf16[192,1536]{1,0:T(8,128)(2,1)}, u32[]{:S(2)}, u32[]{:S(2)}) %collective-permute-start.15) | collective-permute-done | bytes 589856 | tf_op jit(solution)/shard_map/ppermute | solution.py:789
  326.3 4.8 %all-to-all-start.9 = ((bf16[4,192,768]{2,1,0:T(8,128)(2,1)}), bf16[4,192,768]{2,1,0:T(8,128)(2,1)S(1)}, u32[]{:S(2)}, u32[]{:S(2)}) async-start(bf16[4,192,768]{2,1,0:T(8,128)(2,1)} %bitcast.53), calls=%async_computation.9 | async-start | bytes 2359296 | tf_op jit(solution)/shard_map/all_to_all | solution.py:223
  332.1 2.1 collective-permute-start.20
  335.6 12.8 %collective-permute-done.20 = f32[24,768]{1,0:T(8,128)S(1)} collective-permute-done((f32[24,768]{1,0:T(8,128)S(1)}, f32[24,768]{1,0:T(8,128)S(1)}, u32[]{:S(2)}, u32[]{:S(2)}) %collective-permute-start.20) | collective-permute-done | bytes 73760 | tf_op jit(solution)/shard_map/ppermute | solution.py:789
  351.7 4.4 %all-to-all-done.9 = bf16[4,192,768]{2,1,0:T(8,128)(2,1)S(1)} async-done(((bf16[4,192,768]{2,1,0:T(8,128)(2,1)}), bf16[4,192,768]{2,1,0:T(8,128)(2,1)S(1)}, u32[]{:S(2)}, u32[]{:S(2)}) %all-to-all-start.9) | async-done | bytes 1179680 | tf_op jit(solution)/shard_map/all_to_all | solution.py:223
  356.1 3.8 all-to-all-start.10
  359.9 4.7 %choose.3 = bf16[906,768]{1,0:T(8,128)(2,1)} custom-call(s32[906,1]{1,0:T(8,128)} %get-tuple-element.304.col_ref, bf16[1088,768]{1,0:T(8,128)(2,1)} %bitcast.56.value_ref), custom_call_target="tpu_custom_call" | custom-call | tf_op jit(solution)/shard_map/choose/pallas_call | solution.py:214
  365.6 2.9 collective-permute-start.21
  369.5 20.8 %collective-permute-done.21 = f32[24,768]{1,0:T(8,128)S(1)} collective-permute-done((f32[24,768]{1,0:T(8,128)S(1)}, f32[24,768]{1,0:T(8,128)S(1)}, u32[]{:S(2)}, u32[]{:S(2)}) %collective-permute-start.21) | collective-permute-done | bytes 73760 | tf_op jit(solution)/shard_map/ppermute | solution.py:789
  (137 shorter events, 39.8 us)
Async XLA Ops:
  6.2 6.6 %copy-start.24 = (f32[768]{0:T(1024)S(1)}, f32[768]{0:T(1024)}, u32[]{:S(2)}) copy-start(f32[768]{0:T(1024)} %param.29) | copy-start | bytes 9220
  6.2 7.1 %copy-start.25 = (f32[768]{0:T(1024)S(1)}, f32[768]{0:T(1024)}, u32[]{:S(2)}) copy-start(f32[768]{0:T(1024)} %param.30) | copy-start | bytes 9220
  6.2 7.7 %copy-start.26 = (f32[768]{0:T(1024)S(1)}, f32[768]{0:T(1024)}, u32[]{:S(2)}) copy-start(f32[768]{0:T(1024)} %param.32) | copy-start | bytes 9220
  6.2 8.3 %copy-start.27 = (f32[768]{0:T(1024)S(1)}, f32[768]{0:T(1024)}, u32[]{:S(2)}) copy-start(f32[768]{0:T(1024)} %param.33) | copy-start | bytes 9220
  6.2 8.9 %copy-start.28 = (f32[768]{0:T(1024)S(1)}, f32[768]{0:T(1024)}, u32[]{:S(2)}) copy-start(f32[768]{0:T(1024)} %param.35) | copy-start | bytes 9220
  6.3 9.5 %copy-start.29 = (f32[768]{0:T(1024)S(1)}, f32[768]{0:T(1024)}, u32[]{:S(2)}) copy-start(f32[768]{0:T(1024)} %param.36) | copy-start | bytes 9220
  6.3 10.0 %copy-start.30 = (f32[768]{0:T(1024)S(1)}, f32[768]{0:T(1024)}, u32[]{:S(2)}) copy-start(f32[768]{0:T(1024)} %param.37) | copy-start | bytes 9220
  6.3 10.6 %copy-start.15 = (bf16[906,768]{1,0:T(8,128)(2,1)S(1)}, bf16[906,768]{1,0:T(8,128)(2,1)}, u32[]{:S(2)}) copy-start(bf16[906,768]{1,0:T(8,128)(2,1)} %value_ref.1) | copy-start | bytes 4174852
  6.3 45.6 %all-to-all-start.4 = ((bf16[4,272,768]{2,1,0:T(8,128)(2,1)}), bf16[4,272,768]{2,1,0:T(8,128)(2,1)S(1)}, u32[]{:S(2)}, u32[]{:S(2)}) async-start(bf16[4,272,768]{2,1,0:T(8,128)(2,1)} %get-tuple-element.201), calls=%async_computation.4 | async-start | bytes 3342336 | tf_op jit(solution)/shard_map/all_to_all | solution.py:223
  20.8 34.4 %copy-start.20 = (s32[906]{0:T(1024)S(1)}, s32[906]{0:T(1024)}, u32[]{:S(2)}) copy-start(s32[906]{0:T(1024)} %param.27) | copy-start | bytes 10876
  20.8 34.4 %copy-start.22 = (s32[906]{0:T(1024)S(1)}, s32[906]{0:T(1024)}, u32[]{:S(2)}) copy-start(s32[906]{0:T(1024)} %param.28) | copy-start | bytes 10876
  65.4 42.2 %all-to-all-start.5 = ((bf16[4,272,768]{2,1,0:T(8,128)(2,1)}), bf16[4,272,768]{2,1,0:T(8,128)(2,1)S(1)}, u32[]{:S(2)}, u32[]{:S(2)}) async-start(bf16[4,272,768]{2,1,0:T(8,128)(2,1)} %pack_more.1), calls=%async_computation.5 | async-start | bytes 3342336 | tf_op jit(solution)/shard_map/all_to_all | solution.py:223
  113.9 27.5 %copy-start.31 = (bf16[928,768]{1,0:T(8,128)(2,1)S(1)}, bf16[928,768]{1,0:T(8,128)(2,1)}, u32[]{:S(2)}) copy-start(bf16[928,768]{1,0:T(8,128)(2,1)} %get-tuple-element.207.x_ref.refs_1_) | copy-start | bytes 4276228
  140.8 36.8 %collective-permute-start = (bf16[384,3072]{1,0:T(8,128)(2,1)}, bf16[384,3072]{1,0:T(8,128)(2,1)S(1)}, u32[]{:S(2)}, u32[]{:S(2)}) collective-permute-start(bf16[384,3072]{1,0:T(8,128)(2,1)} %get-tuple-element.227), channel_id=1, source_target_pairs={{0,4},{4,0},{8,12},{12,8},{16,20},{20,16},{24,28},{28,24},{1,5},{5... | collective-permute-start | bytes 7077896 | tf_op jit(solution)/shard_map/ppermute | solution.py:789
  140.9 36.7 %collective-permute-start.1 = (bf16[1536,768]{1,0:T(8,128)(2,1)}, bf16[1536,768]{1,0:T(8,128)(2,1)}, u32[]{:S(2)}, u32[]{:S(2)}) collective-permute-start(bf16[1536,768]{1,0:T(8,128)(2,1)} %get-tuple-element.228), channel_id=1, source_target_pairs={{0,4},{4,0},{8,12},{12,8},{16,20},{20,16},{24,28},{28,24},{1,5},{5... | collective-permute-start | bytes 7077896 | tf_op jit(solution)/shard_map/ppermute | solution.py:789
  179.0 4.1 %copy-start.8 = (bf16[384,3072]{1,0:T(8,128)(2,1)S(1)}, bf16[384,3072]{1,0:T(8,128)(2,1)}, u32[]{:S(2)}) copy-start(bf16[384,3072]{1,0:T(8,128)(2,1)} %get-tuple-element.241) | copy-start | bytes 7077892
  179.0 4.1 %copy-start.10 = (bf16[384,3072]{1,0:T(8,128)(2,1)S(1)}, bf16[384,3072]{1,0:T(8,128)(2,1)}, u32[]{:S(2)}) copy-start(bf16[384,3072]{1,0:T(8,128)(2,1)} %copy-done.9) | copy-start | bytes 7077892
  185.7 32.3 %collective-permute-start.4 = (bf16[384,3072]{1,0:T(8,128)(2,1)}, bf16[384,3072]{1,0:T(8,128)(2,1)}, u32[]{:S(2)}, u32[]{:S(2)}) collective-permute-start(bf16[384,3072]{1,0:T(8,128)(2,1)} %get-tuple-element.251), channel_id=1, source_target_pairs={{0,4},{4,0},{8,12},{12,8},{16,20},{20,16},{24,28},{28,24},{1,5},{5... | collective-permute-start | bytes 7077896 | tf_op jit(solution)/shard_map/ppermute | solution.py:789
  185.8 32.2 %collective-permute-start.5 = (bf16[1536,768]{1,0:T(8,128)(2,1)}, bf16[1536,768]{1,0:T(8,128)(2,1)}, u32[]{:S(2)}, u32[]{:S(2)}) collective-permute-start(bf16[1536,768]{1,0:T(8,128)(2,1)} %get-tuple-element.252), channel_id=1, source_target_pairs={{0,4},{4,0},{8,12},{12,8},{16,20},{20,16},{24,28},{28,24},{1,5},{5... | collective-permute-start | bytes 7077896 | tf_op jit(solution)/shard_map/ppermute | solution.py:789
  186.2 31.8 %collective-permute-start.2 = (bf16[192,3072]{1,0:T(8,128)(2,1)}, bf16[192,3072]{1,0:T(8,128)(2,1)}, u32[]{:S(2)}, u32[]{:S(2)}) collective-permute-start(bf16[192,3072]{1,0:T(8,128)(2,1)} %bitcast.11), channel_id=1, source_target_pairs={{0,16},{4,20},{8,24},{12,28},{16,0},{20,4},{24,8},{28,12},{1,17},{... | collective-permute-start | bytes 3538952 | tf_op jit(solution)/shard_map/ppermute | solution.py:789
  187.7 30.3 %collective-permute-start.3 = (bf16[768,768]{1,0:T(8,128)(2,1)}, bf16[768,768]{1,0:T(8,128)(2,1)S(1)}, u32[]{:S(2)}, u32[]{:S(2)}) collective-permute-start(bf16[768,768]{1,0:T(8,128)(2,1)} %bitcast.14), channel_id=1, source_target_pairs={{0,8},{4,12},{8,0},{12,4},{16,24},{20,28},{24,16},{28,20},{1,9},{5... | collective-permute-start | bytes 3538952 | tf_op jit(solution)/shard_map/ppermute | solution.py:789
  189.2 43.6 %all-to-all-start.6 = ((bf16[4,272,768]{2,1,0:T(8,128)(2,1)}), bf16[4,272,768]{2,1,0:T(8,128)(2,1)}, u32[]{:S(2)}, u32[]{:S(2)}) async-start(bf16[4,272,768]{2,1,0:T(8,128)(2,1)} %bitcast.120), calls=%async_computation.6 | async-start | bytes 3342336 | tf_op jit(solution)/shard_map/all_to_all | solution.py:223
  229.1 33.3 %collective-permute-start.6 = (bf16[192,3072]{1,0:T(8,128)(2,1)}, bf16[192,3072]{1,0:T(8,128)(2,1)}, u32[]{:S(2)}, u32[]{:S(2)}) collective-permute-start(bf16[192,3072]{1,0:T(8,128)(2,1)} %bitcast.17), channel_id=1, source_target_pairs={{0,16},{4,20},{8,24},{12,28},{16,0},{20,4},{24,8},{28,12},{1,17},{... | collective-permute-start | bytes 3538952 | tf_op jit(solution)/shard_map/ppermute | solution.py:789
  229.6 32.8 %collective-permute-start.7 = (bf16[768,768]{1,0:T(8,128)(2,1)}, bf16[768,768]{1,0:T(8,128)(2,1)}, u32[]{:S(2)}, u32[]{:S(2)}) collective-permute-start(bf16[768,768]{1,0:T(8,128)(2,1)} %bitcast.20), channel_id=1, source_target_pairs={{0,8},{4,12},{8,0},{12,4},{16,24},{20,28},{24,16},{28,20},{1,9},{5... | collective-permute-start | bytes 3538952 | tf_op jit(solution)/shard_map/ppermute | solution.py:789
  230.2 32.3 %collective-permute-start.8 = (bf16[384,1536]{1,0:T(8,128)(2,1)}, bf16[384,1536]{1,0:T(8,128)(2,1)}, u32[]{:S(2)}, u32[]{:S(2)}) collective-permute-start(bf16[384,1536]{1,0:T(8,128)(2,1)} %get-tuple-element.274), channel_id=1, source_target_pairs={{0,4},{4,0},{8,12},{12,8},{16,20},{20,16},{24,28},{28,24},{1,5},{5... | collective-permute-start | bytes 3538952 | tf_op jit(solution)/shard_map/ppermute | solution.py:789
  230.2 32.3 %collective-permute-start.9 = (bf16[384,1536]{1,0:T(8,128)(2,1)}, bf16[384,1536]{1,0:T(8,128)(2,1)}, u32[]{:S(2)}, u32[]{:S(2)}) collective-permute-start(bf16[384,1536]{1,0:T(8,128)(2,1)} %get-tuple-element.275), channel_id=1, source_target_pairs={{0,4},{4,0},{8,12},{12,8},{16,20},{20,16},{24,28},{28,24},{1,5},{5... | collective-permute-start | bytes 3538952 | tf_op jit(solution)/shard_map/ppermute | solution.py:789
  232.9 34.1 %all-to-all-start.7 = ((bf16[4,48,3072]{2,1,0:T(8,128)(2,1)}), bf16[4,48,3072]{2,1,0:T(8,128)(2,1)}, u32[]{:S(2)}, u32[]{:S(2)}) async-start(bf16[4,48,3072]{2,1,0:T(8,128)(2,1)} %bitcast.112), calls=%async_computation.7 | async-start | bytes 2359296 | tf_op jit(solution)/shard_map/all_to_all | solution.py:223
  267.0 43.3 %all-to-all-start.8 = ((bf16[4,272,768]{2,1,0:T(8,128)(2,1)}), bf16[4,272,768]{2,1,0:T(8,128)(2,1)}, u32[]{:S(2)}, u32[]{:S(2)}) async-start(bf16[4,272,768]{2,1,0:T(8,128)(2,1)} %bitcast.121), calls=%async_computation.8 | async-start | bytes 3342336 | tf_op jit(solution)/shard_map/all_to_all | solution.py:223
  279.0 31.3 %collective-permute-start.11 = (bf16[768,768]{1,0:T(8,128)(2,1)}, bf16[768,768]{1,0:T(8,128)(2,1)}, u32[]{:S(2)}, u32[]{:S(2)}) collective-permute-start(bf16[768,768]{1,0:T(8,128)(2,1)} %select_convert_fusion), channel_id=1, source_target_pairs={{0,16},{4,20},{8,24},{12,28},{16,0},{20,4},{24,8},{28,12},{1,17},{... | collective-permute-start | bytes 3538952 | tf_op jit(solution)/shard_map/ppermute | solution.py:789
  279.5 8.6 %collective-permute-start.13 = (f32[24,768]{1,0:T(8,128)}, f32[24,768]{1,0:T(8,128)}, u32[]{:S(2)}, u32[]{:S(2)}) collective-permute-start(f32[24,768]{1,0:T(8,128)} %get-tuple-element.302), channel_id=1, source_target_pairs={{0,4},{4,0},{8,12},{12,8},{16,20},{20,16},{24,28},{28,24},{1,5},{5... | collective-permute-start | bytes 221192 | tf_op jit(solution)/shard_map/ppermute | solution.py:789
  279.5 30.8 %collective-permute-start.10 = (bf16[96,3072]{1,0:T(8,128)(2,1)}, bf16[96,3072]{1,0:T(8,128)(2,1)}, u32[]{:S(2)}, u32[]{:S(2)}) collective-permute-start(bf16[96,3072]{1,0:T(8,128)(2,1)} %fusion.16), channel_id=1, source_target_pairs={{0,8},{4,12},{8,0},{12,4},{16,24},{20,28},{24,16},{28,20},{1,9},{5... | collective-permute-start | bytes 1769480 | tf_op jit(solution)/shard_map/ppermute | solution.py:789
  280.6 29.7 %collective-permute-start.12 = (bf16[192,1536]{1,0:T(8,128)(2,1)}, bf16[192,1536]{1,0:T(8,128)(2,1)}, u32[]{:S(2)}, u32[]{:S(2)}) collective-permute-start(bf16[192,1536]{1,0:T(8,128)(2,1)} %bitcast.34), channel_id=1, source_target_pairs={{0,8},{4,12},{8,0},{12,4},{16,24},{20,28},{24,16},{28,20},{1,9},{5... | collective-permute-start | bytes 1769480 | tf_op jit(solution)/shard_map/ppermute | solution.py:789
  284.3 34.1 %collective-permute-start.15 = (bf16[192,1536]{1,0:T(8,128)(2,1)}, bf16[192,1536]{1,0:T(8,128)(2,1)}, u32[]{:S(2)}, u32[]{:S(2)}) collective-permute-start(bf16[192,1536]{1,0:T(8,128)(2,1)} %bitcast.37), channel_id=1, source_target_pairs={{0,16},{4,20},{8,24},{12,28},{16,0},{20,4},{24,8},{28,12},{1,17},{... | collective-permute-start | bytes 1769480 | tf_op jit(solution)/shard_map/ppermute | solution.py:789
  289.0 20.7 %collective-permute-start.14 = (f32[24,768]{1,0:T(8,128)S(1)}, f32[24,768]{1,0:T(8,128)S(1)}, u32[]{:S(2)}, u32[]{:S(2)}) collective-permute-start(f32[24,768]{1,0:T(8,128)S(1)} %add.278), channel_id=1, source_target_pairs={{0,8},{4,12},{8,0},{12,4},{16,24},{20,28},{24,16},{28,20},{1,9},{5... | collective-permute-start | bytes 221192 | tf_op jit(solution)/shard_map/ppermute | solution.py:789
  314.3 6.3 %copy-start.5 = (f32[1,1,2,2,24,1536]{5,4,3,2,1,0:T(8,128)S(1)}, f32[1,1,2,2,24,1536]{5,4,3,2,1,0:T(8,128)}, u32[]{:S(2)}) copy-start(f32[1,1,2,2,24,1536]{5,4,3,2,1,0:T(8,128)} %get-tuple-element.362) | copy-start | bytes 1769476
  321.4 12.8 %copy-start.3 = (f32[1,1,2,2,24,3072]{5,4,3,2,1,0:T(8,128)S(1)}, f32[1,1,2,2,24,3072]{5,4,3,2,1,0:T(8,128)}, u32[]{:S(2)}) copy-start(f32[1,1,2,2,24,3072]{5,4,3,2,1,0:T(8,128)} %get-tuple-element.352) | copy-start | bytes 3538948
  321.4 12.8 %copy-start.11 = (bf16[1,2,2,24,3072]{4,3,2,1,0:T(8,128)(2,1)S(1)}, bf16[1,2,2,24,3072]{4,3,2,1,0:T(8,128)(2,1)}, u32[]{:S(2)}) copy-start(bf16[1,2,2,24,3072]{4,3,2,1,0:T(8,128)(2,1)} %get-tuple-element.364) | copy-start | bytes 1769476
  322.2 8.9 %collective-permute-start.19 = (f32[24,768]{1,0:T(8,128)}, f32[24,768]{1,0:T(8,128)}, u32[]{:S(2)}, u32[]{:S(2)}) collective-permute-start(f32[24,768]{1,0:T(8,128)} %add.279), channel_id=1, source_target_pairs={{0,16},{4,20},{8,24},{12,28},{16,0},{20,4},{24,8},{28,12},{1,17},{... | collective-permute-start | bytes 221192 | tf_op jit(solution)/shard_map/ppermute | solution.py:789
  322.9 25.4 %collective-permute-start.16 = (bf16[96,1536]{1,0:T(8,128)(2,1)}, bf16[96,1536]{1,0:T(8,128)(2,1)}, u32[]{:S(2)}, u32[]{:S(2)}) collective-permute-start(bf16[96,1536]{1,0:T(8,128)(2,1)} %fusion.22), channel_id=1, source_target_pairs={{0,16},{4,20},{8,24},{12,28},{16,0},{20,4},{24,8},{28,12},{1,17},{... | collective-permute-start | bytes 884744 | tf_op jit(solution)/shard_map/ppermute | solution.py:789
  324.3 24.1 %collective-permute-start.17 = (bf16[96,1536]{1,0:T(8,128)(2,1)}, bf16[96,1536]{1,0:T(8,128)(2,1)}, u32[]{:S(2)}, u32[]{:S(2)}) collective-permute-start(bf16[96,1536]{1,0:T(8,128)(2,1)} %fusion.21), channel_id=1, source_target_pairs={{0,8},{4,12},{8,0},{12,4},{16,24},{20,28},{24,16},{28,20},{1,9},{5... | collective-permute-start | bytes 884744 | tf_op jit(solution)/shard_map/ppermute | solution.py:789
  324.9 23.4 %collective-permute-start.18 = (bf16[24,3072]{1,0:T(8,128)(2,1)}, bf16[24,3072]{1,0:T(8,128)(2,1)}, u32[]{:S(2)}, u32[]{:S(2)}) collective-permute-start(bf16[24,3072]{1,0:T(8,128)(2,1)} %dynamic-slice_bitcast_fusion), channel_id=1, source_target_pairs={{0,8},{4,12},{8,0},{12,4},{16,24},{20,28},{24,16},{28,20},{1,9},{5... | collective-permute-start | bytes 442376 | tf_op jit(solution)/shard_map/ppermute | solution.py:789
  326.3 29.8 %all-to-all-start.9 = ((bf16[4,192,768]{2,1,0:T(8,128)(2,1)}), bf16[4,192,768]{2,1,0:T(8,128)(2,1)S(1)}, u32[]{:S(2)}, u32[]{:S(2)}) async-start(bf16[4,192,768]{2,1,0:T(8,128)(2,1)} %bitcast.53), calls=%async_computation.9 | async-start | bytes 2359296 | tf_op jit(solution)/shard_map/all_to_all | solution.py:223
  331.1 17.3 %copy-start.13 = (f32[1,1,2,2,24,1536]{5,4,3,2,1,0:T(8,128)S(1)}, f32[1,1,2,2,24,1536]{5,4,3,2,1,0:T(8,128)}, u32[]{:S(2)}) copy-start(f32[1,1,2,2,24,1536]{5,4,3,2,1,0:T(8,128)} %get-tuple-element.378) | copy-start | bytes 1769476
  332.1 16.2 %collective-permute-start.20 = (f32[24,768]{1,0:T(8,128)S(1)}, f32[24,768]{1,0:T(8,128)S(1)}, u32[]{:S(2)}, u32[]{:S(2)}) collective-permute-start(f32[24,768]{1,0:T(8,128)S(1)} %add.291), channel_id=1, source_target_pairs={{0,1},{1,0},{2,3},{3,2},{4,5},{5,4},{6,7},{7,6},{8,9},{9,8},{10,11... | collective-permute-start | bytes 221192 | tf_op jit(solution)/shard_map/ppermute | solution.py:789
  334.2 15.3 %copy-start.12 = (f32[1,1,2,2,24,1536]{5,4,3,2,1,0:T(8,128)S(1)}, f32[1,1,2,2,24,1536]{5,4,3,2,1,0:T(8,128)}, u32[]{:S(2)}) copy-start(f32[1,1,2,2,24,1536]{5,4,3,2,1,0:T(8,128)} %get-tuple-element.363) | copy-start | bytes 1769476
  356.1 34.2 %all-to-all-start.10 = ((bf16[4,24,6144]{2,1,0:T(8,128)(2,1)}), bf16[4,24,6144]{2,1,0:T(8,128)(2,1)S(1)}, u32[]{:S(2)}, u32[]{:S(2)}) async-start(bf16[4,24,6144]{2,1,0:T(8,128)(2,1)} %bitcast.55), calls=%async_computation.10 | async-start | bytes 2359296 | tf_op jit(solution)/shard_map/all_to_all | solution.py:223
  359.9 4.8 %copy-start.17 = (bf16[48,3072]{1,0:T(8,128)(2,1)S(1)}, bf16[48,3072]{1,0:T(8,128)(2,1)}, u32[]{:S(2)}) copy-start(bf16[48,3072]{1,0:T(8,128)(2,1)} %reduce_sum.30) | copy-start | bytes 884740
  365.6 24.7 %collective-permute-start.21 = (f32[24,768]{1,0:T(8,128)S(1)}, f32[24,768]{1,0:T(8,128)S(1)}, u32[]{:S(2)}, u32[]{:S(2)}) collective-permute-start(f32[24,768]{1,0:T(8,128)S(1)} %add.292), channel_id=1, source_target_pairs={{0,2},{1,3},{2,0},{3,1},{4,6},{5,7},{6,4},{7,5},{8,10},{9,11},{10,... | collective-permute-start | bytes 221192 | tf_op jit(solution)/shard_map/ppermute | solution.py:789
  (12 other events, 33.2 us)
